TPU v7x, 256 devices: a whole 4x4x8 slice. The times are simulated.
256 devices in a mesh: mem: 32 (over x, z_hi, core), gx: 4 (over y), gy: 2 (over z_lo).
Axes of the slice: x: 4, y: 4, z: 8 (z_hi: 4, z_lo: 2; z = z_hi * 2 + z_lo), core: 2. Of those that a mesh axis runs over, the one named last changes fastest.
Arguments:
- perturbations: float32 [32, 32, 128, 512], P('mem', None, 'gx', 'gy'), may hold values from -9 to 9
- control: float32 [32, 128, 512], P(None, 'gx', 'gy'), may hold values from -6 to 6
Outputs:
- increment: float32 [32, 128, 512], P('mem', 'gx', 'gy')
All inputs are finite; a program needn't handle non-finite values.
Results may differ from a plain program's by a relative error of at most 0.0001.
Values sent between devices are 32-bit elements; how exact they have to be, the bound alone decides.
No kernel may reach another device: no remote copies, remote signals or barrier semaphores. Data moves between devices by JAX's collectives and lax.ppermute only.
A program may use at most 64 MiB of HBM per device.

v0:
```python
import jax
import jax.numpy as jnp
import numpy as np
from jax import lax
from jax.experimental import pallas as pl
from jax.experimental.pallas import tpu as pltpu
from jax.sharding import PartitionSpec as P

F32, BF16 = jnp.float32, jnp.bfloat16
HALO = 16
VMEM = pl.BlockSpec(memory_space=pltpu.VMEM)


def line_terms(size):
    offsets = np.arange(-4, 5)
    taps = np.exp(-offsets * offsets / 18.0)
    taps = taps / np.sqrt(np.sum(taps * taps))

    def banded(count):
        return sum(t * np.eye(count, k=o) for t, o in zip(taps, offsets))

    pairs = np.repeat(np.eye(size // 2), 2, axis=1) * np.sqrt(0.5)
    return banded(size), pairs.T @ banded(size // 2) @ pairs


def split(values):
    high = values.astype(BF16)
    return high, (values - high.astype(values.dtype)).astype(BF16)


def left_table(size, parts):
    fine, pair = line_terms(size)
    rows = size // parts
    tables = []
    for part in range(parts):
        terms = []
        for term in (fine @ fine, fine @ pair, pair @ fine, pair @ pair):
            wide = np.zeros((rows, rows + 2 * HALO))
            for e in range(rows + 2 * HALO):
                source = part * rows - HALO + e
                if 0 <= source < size:
                    wide[:, e] = term[part * rows : (part + 1) * rows, source]
            segments = wide.reshape(rows, 4, 1, HALO)
            terms.append(np.broadcast_to(segments, (rows, 4, 4, HALO)).reshape(rows, 256))
        tables.append(np.concatenate(terms))
    return np.stack(tables)


def right_table(size, parts):
    fine, pair = line_terms(size)
    columns = size // parts
    tables = []
    for part in range(parts):
        own = slice(part * columns, (part + 1) * columns)
        edge = slice(columns, columns + HALO) if part == 0 else slice(columns - HALO, columns)
        terms = (fine @ fine, pair @ fine, fine @ pair, pair @ pair)
        rows = [term[own, own] for term in terms] + [term[edge, own] for term in terms]
        rows.append(np.zeros((64, columns)))
        tables.append(np.concatenate(rows))
    return np.stack(tables)


def halves(table):
    high = table.astype(np.float32).astype(BF16)
    low = (table - high.astype(np.float64)).astype(np.float32).astype(BF16)
    return np.stack([high, low], axis=1)


def dot3(left, right):
    (lh, ll), (rh, rl) = left, right
    dot = lambda a, b: jnp.dot(a, b, preferred_element_type=F32)
    return dot(lh, rh) + (dot(lh, rl) + dot(ll, rh))


def product_kernel(where, p_ref, c_ref, top_ref, bottom_ref, edge_top_ref, edge_bottom_ref):
    gy = where[4]
    lane = lax.broadcasted_iota(jnp.int32, (1, 1, 128), 2)
    edges = jnp.zeros((4, 32, 128), F32)
    for g in range(8):
        v = p_ref[0, 4 * g : 4 * g + 4] * c_ref[4 * g : 4 * g + 4]
        top_ref[4 * g : 4 * g + 4] = v[:, :HALO]
        bottom_ref[4 * g : 4 * g + 4] = v[:, HALO:]
        last = v[:, :, 128:].reshape(128, 128)
        first = v[:, :, :128].reshape(128, 128)
        edge = jnp.where(gy == 0, pltpu.roll(last, 16, 1), first)
        if g:
            edge = pltpu.roll(edge, 16 * g, 1)
        edges = jnp.where(lane // 16 == g, edge.reshape(4, 32, 128), edges)
    edge_top_ref[...] = edges[:, :HALO]
    edge_bottom_ref[...] = edges[:, HALO:]


def filter_kernel(
    where, p_ref, above_ref, top_ref, bottom_ref, below_ref,
    side_above_ref, side_top_ref, side_bottom_ref, side_below_ref,
    left_ref, right_ref, keep_ref, send_ref, xh_ref, xl_ref, sh_ref, sl_ref,
):
    core, gx, gy = where[2], where[3], where[4]
    lane = lax.broadcasted_iota(jnp.int32, (1, 256), 1)
    for t in range(4):
        for f in range(4):
            mine = (lane // 16) % 4 == f
            rows = slice(32 * t, 32 * t + 32)
            at = slice(128 * t + 32 * f, 128 * t + 32 * f + 32)
            zero = jnp.zeros((32, 256), F32)
            xh_ref[at] = jnp.where(mine, left_ref[gx, 0, rows].astype(F32), zero).astype(BF16)
            xl_ref[at] = jnp.where(mine, left_ref[gx, 1, rows].astype(F32), zero).astype(BF16)
    left = (xh_ref[...], xl_ref[...])

    sides = [r[...].reshape(64, 128) for r in (side_above_ref, side_top_ref, side_bottom_ref, side_below_ref)]
    side = dot3(left, split(jnp.concatenate(sides)))
    narrow = lax.broadcasted_iota(jnp.int32, (1, 128), 1)
    for g in range(8):
        packed = jnp.zeros((128, 128), F32)
        for t in range(4):
            moved = side[128 * t : 128 * t + 128]
            if t != g:
                moved = pltpu.roll(moved, (16 * (t - g)) % 128, 1)
            packed = jnp.where(narrow // 16 == t, moved, packed)
        sh_ref[g], sl_ref[g] = split(packed)

    def group(g, carry):
        fields = pl.ds(4 * g, 4)
        v = [r[fields].reshape(64, 256) for r in (above_ref, top_ref, bottom_ref, below_ref)]
        u = dot3((xh_ref[...], xl_ref[...]), split(jnp.concatenate(v)))
        parts = [split(u[128 * t : 128 * t + 128]) for t in range(4)]
        uh = jnp.concatenate([h for h, _ in parts] + [sh_ref[g]], axis=1)
        ul = jnp.concatenate([l for _, l in parts] + [sl_ref[g]], axis=1)
        alpha = dot3((uh, ul), (right_ref[gy, 0], right_ref[gy, 1]))
        q = p_ref[0, fields] * alpha.reshape(4, 32, 256)
        for j in range(2):
            keep_ref[2 * g + j] = jnp.where(core == 0, q[2 * j], q[2 * j + 1])
            send_ref[2 * g + j] = jnp.where(core == 0, q[2 * j + 1], q[2 * j])
        return carry

    lax.fori_loop(0, 8, group, 0)


def core_sum_kernel(where, keep_ref, got_ref, *out_refs):
    for d, out_ref in enumerate(out_refs):
        at = pl.ds(4 * lax.rem(where[0] + d, 4), 4)
        out_ref[...] = keep_ref[at] + got_ref[at]


def row_sum_kernel(where, a_ref, b_ref, c_ref, d_ref, *out_refs):
    for e, out_ref in enumerate(out_refs):
        at = lax.rem(where[1] + e, 4)
        out_ref[0] = (a_ref[at] + b_ref[at]) + (c_ref[at] + d_ref[at])


def last_sum_kernel(a_ref, b_ref, c_ref, d_ref, out_ref):
    out_ref[...] = ((a_ref[...] + b_ref[...]) + (c_ref[...] + d_ref[...])) * (1.0 / 31.0)


def call(kernel, outs, *args, scalars=True, scratch=(), cost=0):
    specs = ([pl.BlockSpec(memory_space=pltpu.SMEM)] if scalars else []) + [VMEM] * (len(args) - scalars)
    return pl.pallas_call(
        kernel,
        out_shape=[jax.ShapeDtypeStruct(s, F32) for s in outs],
        in_specs=specs,
        out_specs=[VMEM] * len(outs),
        scratch_shapes=scratch,
        cost_estimate=pl.CostEstimate(flops=cost, bytes_accessed=1 << 20, transcendentals=0),
    )(*args)


def body(perturbations, control):
    mem, gx, gy = lax.axis_index("mem"), lax.axis_index("gx"), lax.axis_index("gy")
    where = jnp.stack([mem // 8, (mem // 2) % 4, mem % 2, gx, gy]).astype(jnp.int32)
    left = jnp.asarray(halves(left_table(128, 4)))
    right = jnp.asarray(halves(right_table(512, 2)))

    top, bottom, edge_top, edge_bottom = call(
        product_kernel, [(32, 16, 256)] * 2 + [(4, 16, 128)] * 2, where, perturbations, control
    )
    down = [(i, i + 1) for i in range(3)]
    up = [(i + 1, i) for i in range(3)]
    cross = lambda pairs: [(2 * a + s, 2 * b + 1 - s) for a, b in pairs for s in range(2)]
    above = lax.ppermute(bottom, "gx", down)
    below = lax.ppermute(top, "gx", up)
    side_top = lax.ppermute(edge_top, "gy", [(0, 1), (1, 0)])
    side_bottom = lax.ppermute(edge_bottom, "gy", [(0, 1), (1, 0)])
    side_above = lax.ppermute(edge_bottom, ("gx", "gy"), cross(down))
    side_below = lax.ppermute(edge_top, ("gx", "gy"), cross(up))

    keep, send = call(
        filter_kernel, [(16, 32, 256)] * 2, where, perturbations, above, top, bottom, below,
        side_above, side_top, side_bottom, side_below, left, right,
        scratch=[pltpu.VMEM((512, 256), BF16)] * 2 + [pltpu.VMEM((8, 128, 128), BF16)] * 2,
        cost=4 * 10**9,
    )
    got = lax.ppermute(send, "mem", [(m, m ^ 1) for m in range(32)])
    pieces = call(core_sum_kernel, [(4, 32, 256)] * 4, where, keep, got)
    along_x = lambda d: [(m, (m + 8 * d) % 32) for m in range(32)]
    along_z = lambda e: [(m, m - m % 8 + (m % 8 + 2 * e) % 8) for m in range(32)]
    got_x = {d: lax.ppermute(pieces[d], "mem", along_x(d)) for d in (2, 1, 3)}
    cells = call(row_sum_kernel, [(1, 32, 256)] * 4, where, pieces[0], got_x[1], got_x[2], got_x[3])
    got_z = {e: lax.ppermute(cells[e], "mem", along_z(e)) for e in (2, 1, 3)}
    return call(last_sum_kernel, [(1, 32, 256)], cells[0], got_z[1], got_z[2], got_z[3], scalars=False)[0]


def solution(mesh):
    placed = (P("mem", None, "gx", "gy"), P(None, "gx", "gy"))
    return jax.shard_map(
        body, mesh=mesh, in_specs=placed, out_specs=P("mem", "gx", "gy"), check_vma=False
    )
```

profile of v0, /device:TPU:8, one launch (start us, length us, event | category | flops | bytes accessed | tf_op | source)
XLA Modules:
  0.0 71.1 jit_solution(7839285693246224692)
XLA Ops:
  0.0 0.7 stack.23.where
  0.7 3.0 %shard_map.46 = (f32[32,16,256]{2,1,0:T(8,128)}, f32[32,16,256]{2,1,0:T(8,128)}, f32[4,16,128]{2,1,0:T(8,128)}, f32[4,16,128]{2,1,0:T(8,128)}) custom-call(s32[5]{0:T(128)} %stack.23.where, f32[1,32,32,256]{3,2,1,0:T(8,128)} %p_ref.3, f32[32,32,256]{2,1,0:T(8,128)} %c_ref.1), custom_call_target="tpu_custom_call" | custom-call | bytes 1048576 | tf_op jit(solution)/shard_map/pallas_call | solution.py:157
  3.6 3.5 %collective-permute-start = (f32[32,16,256]{2,1,0:T(8,128)}, f32[32,16,256]{2,1,0:T(8,128)S(1)}, u32[]{:S(2)}, u32[]{:S(2)}) collective-permute-start(f32[32,16,256]{2,1,0:T(8,128)} %get-tuple-element.19.bottom_ref), channel_id=1, source_target_pairs={{0,2},{2,4},{4,6},{1,3},{3,5},{5,7},{8,10},{10,12},{12,14},{9,11},... | collective-permute-start | bytes 1572872 | tf_op jit(solution)/shard_map/ppermute | solution.py:179
  7.1 2.4 %collective-permute-start.1 = (f32[32,16,256]{2,1,0:T(8,128)}, f32[32,16,256]{2,1,0:T(8,128)S(1)}, u32[]{:S(2)}, u32[]{:S(2)}) collective-permute-start(f32[32,16,256]{2,1,0:T(8,128)} %get-tuple-element.20.top_ref), channel_id=1, source_target_pairs={{2,0},{4,2},{6,4},{3,1},{5,3},{7,5},{10,8},{12,10},{14,12},{11,9},... | collective-permute-start | bytes 1572872 | tf_op jit(solution)/shard_map/ppermute | solution.py:180
  9.5 2.0 %collective-permute-start.4 = (f32[4,16,128]{2,1,0:T(8,128)}, f32[4,16,128]{2,1,0:T(8,128)S(1)}, u32[]{:S(2)}, u32[]{:S(2)}) collective-permute-start(f32[4,16,128]{2,1,0:T(8,128)} %get-tuple-element.21), channel_id=1, source_target_pairs={{0,1},{1,0},{2,3},{3,2},{4,5},{5,4},{6,7},{7,6},{8,9},{9,8},{10,11... | collective-permute-start | bytes 98312 | tf_op jit(solution)/shard_map/ppermute | solution.py:182
  11.5 3.0 %collective-permute-start.2 = (f32[4,16,128]{2,1,0:T(8,128)}, f32[4,16,128]{2,1,0:T(8,128)S(1)}, u32[]{:S(2)}, u32[]{:S(2)}) collective-permute-start(f32[4,16,128]{2,1,0:T(8,128)} %get-tuple-element.21), channel_id=1, source_target_pairs={{0,3},{1,2},{2,5},{3,4},{4,7},{5,6},{8,11},{9,10},{10,13},{11,12},... | collective-permute-start | bytes 98312 | tf_op jit(solution)/shard_map/ppermute | solution.py:183
  14.5 3.7 %collective-permute-start.5 = (f32[4,16,128]{2,1,0:T(8,128)}, f32[4,16,128]{2,1,0:T(8,128)S(1)}, u32[]{:S(2)}, u32[]{:S(2)}) collective-permute-start(f32[4,16,128]{2,1,0:T(8,128)} %get-tuple-element.22), channel_id=1, source_target_pairs={{2,1},{3,0},{4,3},{5,2},{6,5},{7,4},{10,9},{11,8},{12,11},{13,10},... | collective-permute-start | bytes 98312 | tf_op jit(solution)/shard_map/ppermute | solution.py:184
  18.2 0.0 collective-permute-done.4.side_bottom_ref
  18.3 0.0 copy-start.9
  18.3 0.2 collective-permute-start.3
  18.5 0.0 collective-permute-done.2.side_above_ref
  18.5 0.0 copy-start.10
  18.5 3.0 %collective-permute-done.5.side_below_ref = f32[4,16,128]{2,1,0:T(8,128)S(1)} collective-permute-done((f32[4,16,128]{2,1,0:T(8,128)}, f32[4,16,128]{2,1,0:T(8,128)S(1)}, u32[]{:S(2)}, u32[]{:S(2)}) %collective-permute-start.5) | collective-permute-done | bytes 32800 | tf_op jit(solution)/shard_map/ppermute | solution.py:184
  21.5 1.0 %collective-permute-done.3.side_top_ref = f32[4,16,128]{2,1,0:T(8,128)S(1)} collective-permute-done((f32[4,16,128]{2,1,0:T(8,128)}, f32[4,16,128]{2,1,0:T(8,128)S(1)}, u32[]{:S(2)}, u32[]{:S(2)}) %collective-permute-start.3) | collective-permute-done | bytes 32800 | tf_op jit(solution)/shard_map/ppermute | solution.py:181
  22.5 0.0 collective-permute-done.above_ref
  22.5 0.8 %collective-permute-done.1.below_ref = f32[32,16,256]{2,1,0:T(8,128)S(1)} collective-permute-done((f32[32,16,256]{2,1,0:T(8,128)}, f32[32,16,256]{2,1,0:T(8,128)S(1)}, u32[]{:S(2)}, u32[]{:S(2)}) %collective-permute-start.1) | collective-permute-done | bytes 524320 | tf_op jit(solution)/shard_map/ppermute | solution.py:180
  23.3 0.0 copy-done.9
  23.3 0.0 copy-done.10
  23.3 0.0 copy-done.11
  23.3 0.0 copy-done.12
  23.3 0.0 copy-done.7
  23.3 0.0 copy-start.8
  23.3 0.8 %copy-done.8 = f32[32,16,256]{2,1,0:T(8,128)} copy-done((f32[32,16,256]{2,1,0:T(8,128)}, f32[32,16,256]{2,1,0:T(8,128)S(1)}, u32[]{:S(2)}) %copy-start.8) | copy-done | bytes 524312
  24.1 13.1 %shard_map.47 = (f32[16,32,256]{2,1,0:T(8,128)}, f32[16,32,256]{2,1,0:T(8,128)}) custom-call(s32[5]{0:T(128)} %stack.23.where, f32[1,32,32,256]{3,2,1,0:T(8,128)} %p_ref.3, f32[32,16,256]{2,1,0:T(8,128)} %copy-done.7, f32[32,16,256]{2,1,0:T(8,128)} %get-tuple-element.20.top_ref, f32[32,16,256]{2,1,0:T(8,128)} %get-tuple-element.19.bottom_ref, ...), custom_call_target="tpu_custom_call" | custom-call | flops 4000000000 | bytes 1048576 | tf_op jit(solution)/shard_map/pallas_call | solution.py:157
  37.2 0.0 collective-permute-start.6
  37.2 2.1 %collective-permute-done.6.got_ref = f32[16,32,256]{2,1,0:T(8,128)S(1)} collective-permute-done((f32[16,32,256]{2,1,0:T(8,128)}, f32[16,32,256]{2,1,0:T(8,128)S(1)}, u32[]{:S(2)}, u32[]{:S(2)}) %collective-permute-start.6) | collective-permute-done | bytes 524320 | tf_op jit(solution)/shard_map/ppermute | solution.py:192
  39.3 0.8 %copy-done = f32[16,32,256]{2,1,0:T(8,128)} copy-done((f32[16,32,256]{2,1,0:T(8,128)}, f32[16,32,256]{2,1,0:T(8,128)S(1)}, u32[]{:S(2)}) %copy-start) | copy-done | bytes 524312
  40.1 2.1 %shard_map.48 = (f32[4,32,256]{2,1,0:T(8,128)}, f32[4,32,256]{2,1,0:T(8,128)}, f32[4,32,256]{2,1,0:T(8,128)}, f32[4,32,256]{2,1,0:T(8,128)}) custom-call(s32[5]{0:T(128)} %stack.23.where, f32[16,32,256]{2,1,0:T(8,128)} %get-tuple-element.23.keep_ref, f32[16,32,256]{2,1,0:T(8,128)} %copy-done), custom_call_target="tpu_custom_call" | custom-call | bytes 1048576 | tf_op jit(solution)/shard_map/pallas_call | solution.py:157
  42.2 1.5 %collective-permute-start.7 = (f32[4,32,256]{2,1,0:T(8,128)}, f32[4,32,256]{2,1,0:T(8,128)S(1)}, u32[]{:S(2)}, u32[]{:S(2)}) collective-permute-start(f32[4,32,256]{2,1,0:T(8,128)} %get-tuple-element.26), channel_id=1, source_target_pairs={{0,64},{8,72},{16,80},{24,88},{32,96},{40,104},{48,112},{56,120},{... | collective-permute-start | bytes 393224 | tf_op jit(solution)/shard_map/ppermute | solution.py:196
  43.7 2.7 %collective-permute-start.8 = (f32[4,32,256]{2,1,0:T(8,128)}, f32[4,32,256]{2,1,0:T(8,128)S(1)}, u32[]{:S(2)}, u32[]{:S(2)}) collective-permute-start(f32[4,32,256]{2,1,0:T(8,128)} %get-tuple-element.27), channel_id=1, source_target_pairs={{0,128},{8,136},{16,144},{24,152},{32,160},{40,168},{48,176},{56,1... | collective-permute-start | bytes 393224 | tf_op jit(solution)/shard_map/ppermute | solution.py:196
  46.4 1.4 %collective-permute-start.9 = (f32[4,32,256]{2,1,0:T(8,128)}, f32[4,32,256]{2,1,0:T(8,128)S(1)}, u32[]{:S(2)}, u32[]{:S(2)}) collective-permute-start(f32[4,32,256]{2,1,0:T(8,128)} %get-tuple-element.28), channel_id=1, source_target_pairs={{0,192},{8,200},{16,208},{24,216},{32,224},{40,232},{48,240},{56,2... | collective-permute-start | bytes 393224 | tf_op jit(solution)/shard_map/ppermute | solution.py:196
  47.9 1.3 %collective-permute-done.7.b_ref = f32[4,32,256]{2,1,0:T(8,128)S(1)} collective-permute-done((f32[4,32,256]{2,1,0:T(8,128)}, f32[4,32,256]{2,1,0:T(8,128)S(1)}, u32[]{:S(2)}, u32[]{:S(2)}) %collective-permute-start.7) | collective-permute-done | bytes 131104 | tf_op jit(solution)/shard_map/ppermute | solution.py:196
  49.2 3.8 %collective-permute-done.8.c_ref = f32[4,32,256]{2,1,0:T(8,128)S(1)} collective-permute-done((f32[4,32,256]{2,1,0:T(8,128)}, f32[4,32,256]{2,1,0:T(8,128)S(1)}, u32[]{:S(2)}, u32[]{:S(2)}) %collective-permute-start.8) | collective-permute-done | bytes 131104 | tf_op jit(solution)/shard_map/ppermute | solution.py:196
  53.0 0.0 collective-permute-done.9.d_ref
  53.0 0.0 copy-done.1
  53.0 0.6 copy-done.2
  53.6 0.0 copy-done.3
  53.6 1.8 %shard_map.49 = (f32[1,32,256]{2,1,0:T(8,128)}, f32[1,32,256]{2,1,0:T(8,128)}, f32[1,32,256]{2,1,0:T(8,128)}, f32[1,32,256]{2,1,0:T(8,128)}) custom-call(s32[5]{0:T(128)} %stack.23.where, f32[4,32,256]{2,1,0:T(8,128)} %get-tuple-element.25.a_ref, f32[4,32,256]{2,1,0:T(8,128)} %copy-done.1, f32[4,32,256]{2,1,0:T(8,128)} %copy-done.2, f32[4,32,256]{2,1,0:T(8,128)} %copy-done.3), custom_call_target="tpu_custom_call" | custom-call | bytes 1048576 | tf_op jit(solution)/shard_map/pallas_call | solution.py:157
  55.4 3.3 %collective-permute-start.10 = (f32[1,32,256]{2,1,0:T(8,128)}, f32[1,32,256]{2,1,0:T(8,128)S(1)}, u32[]{:S(2)}, u32[]{:S(2)}) collective-permute-start(f32[1,32,256]{2,1,0:T(8,128)} %get-tuple-element.30), channel_id=1, source_target_pairs={{0,16},{8,24},{16,32},{24,40},{32,48},{40,56},{48,0},{56,8},{64,80... | collective-permute-start | bytes 98312 | tf_op jit(solution)/shard_map/ppermute | solution.py:198
  58.7 5.4 %collective-permute-start.11 = (f32[1,32,256]{2,1,0:T(8,128)}, f32[1,32,256]{2,1,0:T(8,128)S(1)}, u32[]{:S(2)}, u32[]{:S(2)}) collective-permute-start(f32[1,32,256]{2,1,0:T(8,128)} %get-tuple-element.31), channel_id=1, source_target_pairs={{0,32},{8,40},{16,48},{24,56},{32,0},{40,8},{48,16},{56,24},{64,96... | collective-permute-start | bytes 98312 | tf_op jit(solution)/shard_map/ppermute | solution.py:198
  64.1 2.7 %collective-permute-start.12 = (f32[1,32,256]{2,1,0:T(8,128)}, f32[1,32,256]{2,1,0:T(8,128)S(1)}, u32[]{:S(2)}, u32[]{:S(2)}) collective-permute-start(f32[1,32,256]{2,1,0:T(8,128)} %get-tuple-element.32), channel_id=1, source_target_pairs={{0,48},{8,56},{16,0},{24,8},{32,16},{40,24},{48,32},{56,40},{64,11... | collective-permute-start | bytes 98312 | tf_op jit(solution)/shard_map/ppermute | solution.py:198
  66.7 0.0 collective-permute-done.10.b_ref
  66.7 0.1 collective-permute-done.11.c_ref
  66.9 2.2 %collective-permute-done.12.d_ref = f32[1,32,256]{2,1,0:T(8,128)S(1)} collective-permute-done((f32[1,32,256]{2,1,0:T(8,128)}, f32[1,32,256]{2,1,0:T(8,128)S(1)}, u32[]{:S(2)}, u32[]{:S(2)}) %collective-permute-start.12) | collective-permute-done | bytes 32800 | tf_op jit(solution)/shard_map/ppermute | solution.py:198
  69.1 0.0 copy-done.4
  69.1 0.0 copy-done.5
  69.1 0.6 copy-done.6
  69.7 1.4 %shard_map.50 = f32[1,32,256]{2,1,0:T(8,128)} custom-call(f32[1,32,256]{2,1,0:T(8,128)} %get-tuple-element.29.a_ref, f32[1,32,256]{2,1,0:T(8,128)} %copy-done.4, f32[1,32,256]{2,1,0:T(8,128)} %copy-done.5, f32[1,32,256]{2,1,0:T(8,128)} %copy-done.6), custom_call_target="tpu_custom_call" | custom-call | bytes 1048576 | tf_op jit(solution)/shard_map/pallas_call | solution.py:157
  (10 shorter events, 0.0 us)
Async XLA Ops:
  3.6 18.9 %collective-permute-start = (f32[32,16,256]{2,1,0:T(8,128)}, f32[32,16,256]{2,1,0:T(8,128)S(1)}, u32[]{:S(2)}, u32[]{:S(2)}) collective-permute-start(f32[32,16,256]{2,1,0:T(8,128)} %get-tuple-element.19.bottom_ref), channel_id=1, source_target_pairs={{0,2},{2,4},{4,6},{1,3},{3,5},{5,7},{8,10},{10,12},{12,14},{9,11},... | collective-permute-start | bytes 1572872 | tf_op jit(solution)/shard_map/ppermute | solution.py:179
  7.1 16.2 %collective-permute-start.1 = (f32[32,16,256]{2,1,0:T(8,128)}, f32[32,16,256]{2,1,0:T(8,128)S(1)}, u32[]{:S(2)}, u32[]{:S(2)}) collective-permute-start(f32[32,16,256]{2,1,0:T(8,128)} %get-tuple-element.20.top_ref), channel_id=1, source_target_pairs={{2,0},{4,2},{6,4},{3,1},{5,3},{7,5},{10,8},{12,10},{14,12},{11,9},... | collective-permute-start | bytes 1572872 | tf_op jit(solution)/shard_map/ppermute | solution.py:180
  9.5 8.7 %collective-permute-start.4 = (f32[4,16,128]{2,1,0:T(8,128)}, f32[4,16,128]{2,1,0:T(8,128)S(1)}, u32[]{:S(2)}, u32[]{:S(2)}) collective-permute-start(f32[4,16,128]{2,1,0:T(8,128)} %get-tuple-element.21), channel_id=1, source_target_pairs={{0,1},{1,0},{2,3},{3,2},{4,5},{5,4},{6,7},{7,6},{8,9},{9,8},{10,11... | collective-permute-start | bytes 98312 | tf_op jit(solution)/shard_map/ppermute | solution.py:182
  11.5 7.0 %collective-permute-start.2 = (f32[4,16,128]{2,1,0:T(8,128)}, f32[4,16,128]{2,1,0:T(8,128)S(1)}, u32[]{:S(2)}, u32[]{:S(2)}) collective-permute-start(f32[4,16,128]{2,1,0:T(8,128)} %get-tuple-element.21), channel_id=1, source_target_pairs={{0,3},{1,2},{2,5},{3,4},{4,7},{5,6},{8,11},{9,10},{10,13},{11,12},... | collective-permute-start | bytes 98312 | tf_op jit(solution)/shard_map/ppermute | solution.py:183
  14.5 7.0 %collective-permute-start.5 = (f32[4,16,128]{2,1,0:T(8,128)}, f32[4,16,128]{2,1,0:T(8,128)S(1)}, u32[]{:S(2)}, u32[]{:S(2)}) collective-permute-start(f32[4,16,128]{2,1,0:T(8,128)} %get-tuple-element.22), channel_id=1, source_target_pairs={{2,1},{3,0},{4,3},{5,2},{6,5},{7,4},{10,9},{11,8},{12,11},{13,10},... | collective-permute-start | bytes 98312 | tf_op jit(solution)/shard_map/ppermute | solution.py:184
  18.3 5.0 %copy-start.9 = (f32[4,16,128]{2,1,0:T(8,128)}, f32[4,16,128]{2,1,0:T(8,128)S(1)}, u32[]{:S(2)}) copy-start(f32[4,16,128]{2,1,0:T(8,128)S(1)} %collective-permute-done.4.side_bottom_ref) | copy-start | bytes 98308
  18.3 4.2 %collective-permute-start.3 = (f32[4,16,128]{2,1,0:T(8,128)}, f32[4,16,128]{2,1,0:T(8,128)S(1)}, u32[]{:S(2)}, u32[]{:S(2)}) collective-permute-start(f32[4,16,128]{2,1,0:T(8,128)} %get-tuple-element.22), channel_id=1, source_target_pairs={{0,1},{1,0},{2,3},{3,2},{4,5},{5,4},{6,7},{7,6},{8,9},{9,8},{10,11... | collective-permute-start | bytes 98312 | tf_op jit(solution)/shard_map/ppermute | solution.py:181
  18.5 4.8 %copy-start.10 = (f32[4,16,128]{2,1,0:T(8,128)}, f32[4,16,128]{2,1,0:T(8,128)S(1)}, u32[]{:S(2)}) copy-start(f32[4,16,128]{2,1,0:T(8,128)S(1)} %collective-permute-done.2.side_above_ref) | copy-start | bytes 98308
  21.5 1.8 %copy-start.11 = (f32[4,16,128]{2,1,0:T(8,128)}, f32[4,16,128]{2,1,0:T(8,128)S(1)}, u32[]{:S(2)}) copy-start(f32[4,16,128]{2,1,0:T(8,128)S(1)} %collective-permute-done.5.side_below_ref) | copy-start | bytes 98308
  22.5 0.8 %copy-start.12 = (f32[4,16,128]{2,1,0:T(8,128)}, f32[4,16,128]{2,1,0:T(8,128)S(1)}, u32[]{:S(2)}) copy-start(f32[4,16,128]{2,1,0:T(8,128)S(1)} %collective-permute-done.3.side_top_ref) | copy-start | bytes 98308
  22.5 0.8 %copy-start.7 = (f32[32,16,256]{2,1,0:T(8,128)}, f32[32,16,256]{2,1,0:T(8,128)S(1)}, u32[]{:S(2)}) copy-start(f32[32,16,256]{2,1,0:T(8,128)S(1)} %collective-permute-done.above_ref) | copy-start | bytes 1572868
  23.3 0.8 %copy-start.8 = (f32[32,16,256]{2,1,0:T(8,128)}, f32[32,16,256]{2,1,0:T(8,128)S(1)}, u32[]{:S(2)}) copy-start(f32[32,16,256]{2,1,0:T(8,128)S(1)} %collective-permute-done.1.below_ref) | copy-start | bytes 1572868
  37.2 2.1 %collective-permute-start.6 = (f32[16,32,256]{2,1,0:T(8,128)}, f32[16,32,256]{2,1,0:T(8,128)S(1)}, u32[]{:S(2)}, u32[]{:S(2)}) collective-permute-start(f32[16,32,256]{2,1,0:T(8,128)} %get-tuple-element.24), channel_id=1, source_target_pairs={{0,8},{8,0},{16,24},{24,16},{32,40},{40,32},{48,56},{56,48},{64,72... | collective-permute-start | bytes 1572872 | tf_op jit(solution)/shard_map/ppermute | solution.py:192
  39.3 0.8 %copy-start = (f32[16,32,256]{2,1,0:T(8,128)}, f32[16,32,256]{2,1,0:T(8,128)S(1)}, u32[]{:S(2)}) copy-start(f32[16,32,256]{2,1,0:T(8,128)S(1)} %collective-permute-done.6.got_ref) | copy-start | bytes 1572868
  42.2 7.0 %collective-permute-start.7 = (f32[4,32,256]{2,1,0:T(8,128)}, f32[4,32,256]{2,1,0:T(8,128)S(1)}, u32[]{:S(2)}, u32[]{:S(2)}) collective-permute-start(f32[4,32,256]{2,1,0:T(8,128)} %get-tuple-element.26), channel_id=1, source_target_pairs={{0,64},{8,72},{16,80},{24,88},{32,96},{40,104},{48,112},{56,120},{... | collective-permute-start | bytes 393224 | tf_op jit(solution)/shard_map/ppermute | solution.py:196
  43.7 9.3 %collective-permute-start.8 = (f32[4,32,256]{2,1,0:T(8,128)}, f32[4,32,256]{2,1,0:T(8,128)S(1)}, u32[]{:S(2)}, u32[]{:S(2)}) collective-permute-start(f32[4,32,256]{2,1,0:T(8,128)} %get-tuple-element.27), channel_id=1, source_target_pairs={{0,128},{8,136},{16,144},{24,152},{32,160},{40,168},{48,176},{56,1... | collective-permute-start | bytes 393224 | tf_op jit(solution)/shard_map/ppermute | solution.py:196
  46.4 6.5 %collective-permute-start.9 = (f32[4,32,256]{2,1,0:T(8,128)}, f32[4,32,256]{2,1,0:T(8,128)S(1)}, u32[]{:S(2)}, u32[]{:S(2)}) collective-permute-start(f32[4,32,256]{2,1,0:T(8,128)} %get-tuple-element.28), channel_id=1, source_target_pairs={{0,192},{8,200},{16,208},{24,216},{32,224},{40,232},{48,240},{56,2... | collective-permute-start | bytes 393224 | tf_op jit(solution)/shard_map/ppermute | solution.py:196
  49.2 3.8 %copy-start.1 = (f32[4,32,256]{2,1,0:T(8,128)}, f32[4,32,256]{2,1,0:T(8,128)S(1)}, u32[]{:S(2)}) copy-start(f32[4,32,256]{2,1,0:T(8,128)S(1)} %collective-permute-done.7.b_ref) | copy-start | bytes 393220
  53.0 0.6 copy-start.2
  53.0 0.7 copy-start.3
  55.4 11.3 %collective-permute-start.10 = (f32[1,32,256]{2,1,0:T(8,128)}, f32[1,32,256]{2,1,0:T(8,128)S(1)}, u32[]{:S(2)}, u32[]{:S(2)}) collective-permute-start(f32[1,32,256]{2,1,0:T(8,128)} %get-tuple-element.30), channel_id=1, source_target_pairs={{0,16},{8,24},{16,32},{24,40},{32,48},{40,56},{48,0},{56,8},{64,80... | collective-permute-start | bytes 98312 | tf_op jit(solution)/shard_map/ppermute | solution.py:198
  58.7 8.2 %collective-permute-start.11 = (f32[1,32,256]{2,1,0:T(8,128)}, f32[1,32,256]{2,1,0:T(8,128)S(1)}, u32[]{:S(2)}, u32[]{:S(2)}) collective-permute-start(f32[1,32,256]{2,1,0:T(8,128)} %get-tuple-element.31), channel_id=1, source_target_pairs={{0,32},{8,40},{16,48},{24,56},{32,0},{40,8},{48,16},{56,24},{64,96... | collective-permute-start | bytes 98312 | tf_op jit(solution)/shard_map/ppermute | solution.py:198
  64.1 5.0 %collective-permute-start.12 = (f32[1,32,256]{2,1,0:T(8,128)}, f32[1,32,256]{2,1,0:T(8,128)S(1)}, u32[]{:S(2)}, u32[]{:S(2)}) collective-permute-start(f32[1,32,256]{2,1,0:T(8,128)} %get-tuple-element.32), channel_id=1, source_target_pairs={{0,48},{8,56},{16,0},{24,8},{32,16},{40,24},{48,32},{56,40},{64,11... | collective-permute-start | bytes 98312 | tf_op jit(solution)/shard_map/ppermute | solution.py:198
  66.7 2.4 %copy-start.4 = (f32[1,32,256]{2,1,0:T(8,128)}, f32[1,32,256]{2,1,0:T(8,128)S(1)}, u32[]{:S(2)}) copy-start(f32[1,32,256]{2,1,0:T(8,128)S(1)} %collective-permute-done.10.b_ref) | copy-start | bytes 98308
  66.9 2.2 %copy-start.5 = (f32[1,32,256]{2,1,0:T(8,128)}, f32[1,32,256]{2,1,0:T(8,128)S(1)}, u32[]{:S(2)}) copy-start(f32[1,32,256]{2,1,0:T(8,128)S(1)} %collective-permute-done.11.c_ref) | copy-start | bytes 98308
  69.1 0.6 copy-start.6
where the time goes:
time: 71.5 us; the launch traced here: 71.1 us
  starting transfers between devices  31.8 us (44%)
  Pallas kernels  21.3 us (30%)
  waiting for transfers between devices  14.4 us (20%)
  local copies, waits for them, and re-layouts  3.59 us (5%)
    pallas_call x5, Pallas kernels, call(): pl.pallas_call(kernel, out_shape=[jax.ShapeDtypeStruct(s, F32) for s in o...  21.3 us
    ppermute x3, starting transfers between devices, body(): got_z = {e: lax.ppermute(cells[e], 'mem', along_z(e)) for e in (2, 1, 3)}  11.3 us
    ppermute x3, starting transfers between devices, body(): got_x = {d: lax.ppermute(pieces[d], 'mem', along_x(d)) for d in (2, 1, 3)}  5.66 us
    ppermute x3, waiting for transfers between devices, body(): got_x = {d: lax.ppermute(pieces[d], 'mem', along_x(d)) for d in (2, 1, 3)}  5.09 us
    ppermute x1, starting transfers between devices, body(): side_below = lax.ppermute(edge_top, ('gx', 'gy'), cross(up))  3.74 us
    ppermute x1, starting transfers between devices, body(): above = lax.ppermute(bottom, 'gx', down)  3.47 us
    ppermute x1, waiting for transfers between devices, body(): side_below = lax.ppermute(edge_top, ('gx', 'gy'), cross(up))  3.01 us
    ppermute x1, starting transfers between devices, body(): side_above = lax.ppermute(edge_bottom, ('gx', 'gy'), cross(down))  2.99 us
  transfers between devices with their start and end apart: 13, of which 8 were waited for; matrix products, arithmetic and copies ran while one was open for 0% of the time, Pallas kernels for 0%

commit v1 on v0

v1 whole, which is shorter than its diff:
```python
import jax
import jax.numpy as jnp
import numpy as np
from jax import lax
from jax.experimental import pallas as pl
from jax.experimental.pallas import tpu as pltpu
from jax.sharding import Mesh, PartitionSpec as P

F32, BF16 = jnp.float32, jnp.bfloat16
HALO = 16
VMEM = pl.BlockSpec(memory_space=pltpu.VMEM)


def line_terms(size):
    offsets = np.arange(-4, 5)
    taps = np.exp(-offsets * offsets / 18.0)
    taps = taps / np.sqrt(np.sum(taps * taps))

    def banded(count):
        return sum(t * np.eye(count, k=o) for t, o in zip(taps, offsets))

    pairs = np.repeat(np.eye(size // 2), 2, axis=1) * np.sqrt(0.5)
    coarse = np.sqrt(0.5) * banded(size // 2) @ pairs
    return banded(size), np.repeat(coarse, 2, axis=0), coarse


def split(values):
    high = values.astype(BF16)
    return high, (values - high.astype(values.dtype)).astype(BF16)


def left_table(size, parts):
    fine, pair, coarse = line_terms(size)
    rows = size // parts
    tables = []
    for part in range(parts):
        terms = []
        for term in (fine @ fine, fine @ pair, coarse @ fine, coarse @ pair):
            count = term.shape[0] // parts
            wide = np.zeros((count, rows + 2 * HALO))
            for e in range(rows + 2 * HALO):
                source = part * rows - HALO + e
                if 0 <= source < size:
                    wide[:, e] = term[part * count : (part + 1) * count, source]
            segments = wide.reshape(count, 4, 1, HALO)
            terms.append(np.broadcast_to(segments, (count, 4, 4, HALO)).reshape(count, 256))
        tables.append(np.concatenate(terms))
    return np.stack(tables)


def right_tables(size, parts):
    fine, pair, _ = line_terms(size)
    columns = size // parts
    owns, sides = [], []
    for part in range(parts):
        own = slice(part * columns, (part + 1) * columns)
        edge = slice(columns, columns + HALO) if part == 0 else slice(columns - HALO, columns)
        near = slice(columns - HALO, columns) if part == 0 else slice(columns, columns + HALO)
        terms = (fine @ fine, pair @ fine, fine @ pair, pair @ pair)
        owns.append(np.concatenate([term[own, own] for term in terms]))
        sides.append(np.concatenate([np.kron(np.eye(8), term[edge, near]) for term in terms]))
    return np.stack(owns), np.stack(sides)


def halves(table):
    high = table.astype(np.float32).astype(BF16)
    low = (table - high.astype(np.float64)).astype(np.float32).astype(BF16)
    return np.stack([high, low], axis=1)


def dot3(left, right):
    (lh, ll), (rh, rl) = left, right
    dot = lambda a, b: jnp.dot(a, b, preferred_element_type=F32)
    return dot(lh, rh) + (dot(lh, rl) + dot(ll, rh))


def product_kernel(where, p_ref, c_ref, top_ref, bottom_ref, edge_top_ref, edge_bottom_ref):
    gy = where[2]
    lane = lax.broadcasted_iota(jnp.int32, (1, 1, 128), 2)
    edges = jnp.zeros((4, 32, 128), F32)
    for g in range(8):
        v = p_ref[0, 4 * g : 4 * g + 4] * c_ref[4 * g : 4 * g + 4]
        top_ref[4 * g : 4 * g + 4] = v[:, :HALO]
        bottom_ref[4 * g : 4 * g + 4] = v[:, HALO:]
        last = v[:, :, 128:].reshape(128, 128)
        first = v[:, :, :128].reshape(128, 128)
        edge = jnp.where(gy == 0, pltpu.roll(last, 16, 1), first)
        if g:
            edge = pltpu.roll(edge, 16 * g, 1)
        edges = jnp.where(lane // 16 == g, edge.reshape(4, 32, 128), edges)
    edge_top_ref[...] = edges[:, :HALO]
    edge_bottom_ref[...] = edges[:, HALO:]


def filter_kernel(
    where, p_ref, above_ref, top_ref, bottom_ref, below_ref,
    side_above_ref, side_top_ref, side_bottom_ref, side_below_ref,
    left_ref, right_ref, edge_ref, keep_ref, send_ref,
    xh_ref, xl_ref, fh_ref, fl_ref, ch_ref, cl_ref, alpha_ref, pairs_ref, near_ref,
):
    core, gx, gy = where[0], where[1], where[2]
    lane = lax.broadcasted_iota(jnp.int32, (1, 256), 1)
    row, start = 0, 0
    for count in (32, 32, 16, 16):
        for f in range(4):
            mine = (lane // 16) % 4 == f
            rows, at = slice(start, start + count), slice(row, row + count)
            zero = jnp.zeros((count, 256), F32)
            xh_ref[at] = jnp.where(mine, left_ref[gx, 0, rows].astype(F32), zero).astype(BF16)
            xl_ref[at] = jnp.where(mine, left_ref[gx, 1, rows].astype(F32), zero).astype(BF16)
            row += count
        start += count

    def by_rows(refs, pick):
        return dot3((xh_ref[...], xl_ref[...]), split(jnp.concatenate([pick(r) for r in refs])))

    side = by_rows((side_above_ref, side_top_ref, side_bottom_ref, side_below_ref), lambda r: r[...].reshape(64, 128))
    fine = split(jnp.concatenate([side[:128], side[128:256]], axis=1))
    pair = split(jnp.concatenate([side[256:320], side[320:]], axis=1))
    near = dot3(fine, (edge_ref[gy, 0, :256], edge_ref[gy, 1, :256]))
    near_pairs = dot3(pair, (edge_ref[gy, 0, 256:], edge_ref[gy, 1, 256:]))
    near_ref[pl.ds(0, 64, stride=2), :] = near_pairs
    near_ref[pl.ds(1, 64, stride=2), :] = near_pairs
    near = near + near_ref[...]
    near = jnp.where(gy == 0, pltpu.roll(near, 112, 1), near)
    narrow = lax.broadcasted_iota(jnp.int32, (1, 128), 1)
    on_left = (narrow < HALO) & (gy == 1)
    on_right = (narrow >= 128 - HALO) & (gy == 0)

    for g in range(8):
        u = by_rows((above_ref, top_ref, bottom_ref, below_ref), lambda r: r[4 * g : 4 * g + 4].reshape(64, 256))
        for t in range(2):
            at, lanes = slice(128 * g, 128 * g + 128), slice(256 * t, 256 * t + 256)
            fh_ref[at, lanes], fl_ref[at, lanes] = split(u[128 * t : 128 * t + 128])
            at = slice(64 * g, 64 * g + 64)
            ch_ref[at, lanes], cl_ref[at, lanes] = split(u[256 + 64 * t : 320 + 64 * t])

    alpha_ref[...] = dot3((fh_ref[...], fl_ref[...]), (right_ref[gy, 0, :512], right_ref[gy, 1, :512]))
    pairs = dot3((ch_ref[...], cl_ref[...]), (right_ref[gy, 0, 512:], right_ref[gy, 1, 512:]))
    for h in range(2):
        for s in range(2):
            pairs_ref[h, pl.ds(s, 512, stride=2), :] = pairs[:, 128 * h : 128 * h + 128]

    for g in range(8):
        at = slice(128 * g, 128 * g + 128)
        moved = pltpu.roll(near, (128 - 16 * g) % 128, 1) if g else near
        zero = jnp.zeros_like(moved)
        low = pairs_ref[0, at] + jnp.where(on_left, moved, zero)
        high = pairs_ref[1, at] + jnp.where(on_right, moved, zero)
        alpha = alpha_ref[at] + jnp.concatenate([low, high], axis=1)
        q = p_ref[0, 4 * g : 4 * g + 4] * alpha.reshape(4, 32, 256)
        for j in range(2):
            keep_ref[2 * g + j] = jnp.where(core == 0, q[2 * j], q[2 * j + 1])
            send_ref[2 * g + j] = jnp.where(core == 0, q[2 * j + 1], q[2 * j])


def call(kernel, outs, *args, scratch=(), cost=0, grant=16):
    specs = [pl.BlockSpec(memory_space=pltpu.SMEM)] + [VMEM] * (len(args) - 1)
    return pl.pallas_call(
        kernel,
        out_shape=[jax.ShapeDtypeStruct(s, F32) for s in outs],
        in_specs=specs,
        out_specs=[VMEM] * len(outs),
        scratch_shapes=scratch,
        cost_estimate=pl.CostEstimate(flops=cost, bytes_accessed=1 << 20, transcendentals=0),
        compiler_params=pltpu.CompilerParams(vmem_limit_bytes=grant << 20),
    )(*args)


def body(perturbations, control):
    core, gx, gy = lax.axis_index("core"), lax.axis_index("gx"), lax.axis_index("gy")
    where = jnp.stack([core, gx, gy]).astype(jnp.int32)
    left = jnp.asarray(halves(left_table(128, 4)))
    right, edge = (jnp.asarray(halves(t)) for t in right_tables(512, 2))

    top, bottom, edge_top, edge_bottom = call(
        product_kernel, [(32, 16, 256)] * 2 + [(4, 16, 128)] * 2, where, perturbations, control
    )
    down = [(i, i + 1) for i in range(3)]
    up = [(i + 1, i) for i in range(3)]
    cross = lambda pairs: [(2 * a + s, 2 * b + 1 - s) for a, b in pairs for s in range(2)]
    above = lax.ppermute(bottom, "gx", down)
    below = lax.ppermute(top, "gx", up)
    side_top = lax.ppermute(edge_top, "gy", [(0, 1), (1, 0)])
    side_bottom = lax.ppermute(edge_bottom, "gy", [(0, 1), (1, 0)])
    side_above = lax.ppermute(edge_bottom, ("gx", "gy"), cross(down))
    side_below = lax.ppermute(edge_top, ("gx", "gy"), cross(up))

    vmem, f32 = pltpu.VMEM, F32
    keep, send = call(
        filter_kernel, [(16, 32, 256)] * 2, where, perturbations, above, top, bottom, below,
        side_above, side_top, side_bottom, side_below, left, right, edge,
        scratch=[vmem((384, 256), BF16)] * 2 + [vmem((1024, 512), BF16)] * 2 + [vmem((512, 512), BF16)] * 2
        + [vmem((1024, 256), f32), vmem((2, 1024, 128), f32), vmem((128, 128), f32)],
        cost=4 * 10**9, grant=24,
    )
    got = lax.ppermute(send, "core", [(0, 1), (1, 0)])
    pieces = lax.all_to_all(keep + got, ("x", "z"), 0, 0, tiled=True)
    return jnp.sum(pieces, axis=0, keepdims=True) * (1.0 / 31.0)


def solution(mesh):
    grid = Mesh(mesh.devices.reshape(4, 4, 2, 4, 2), ("x", "z", "core", "gx", "gy"))
    mem = ("x", "z", "core")
    placed = (P(mem, None, "gx", "gy"), P(None, "gx", "gy"))
    return jax.shard_map(
        body, mesh=grid, in_specs=placed, out_specs=P(mem, "gx", "gy"), check_vma=False
    )
```

time: 71.5 us -> 60.6 us (0.85)
  blocking collectives: 0 us -> 28.8 us
  starting transfers between devices: 31.8 us -> 14.9 us
  Pallas kernels: 21.3 us -> 4.91 us
  waiting for transfers between devices: 14.4 us -> 6.53 us
  other arithmetic: 0 us -> 0.8 us
    all_to_all x0 -> x1, blocking collectives: none -> 28.8 us  [body(): pieces = lax.all_to_all(keep + got, ('x', 'z'), 0, 0, tiled=True)]
    ppermute x7 -> x1, starting transfers between devices: 17 us -> 0.09 us  [body(): got = lax.ppermute(send, 'core', [(0, 1), (1, 0)])]
    pallas_call x5 -> x2, Pallas kernels: 21.3 us -> 4.91 us  [call(): pl.pallas_call(kernel, out_shape=[jax.ShapeDtypeStruct(s, F32) for s in o...]
    ppermute x7 -> x1, waiting for transfers between devices: 9.57 us -> 1.9 us  [body(): got = lax.ppermute(send, 'core', [(0, 1), (1, 0)])]
    unnamed x26 -> x12, local copies, waits for them, and re-layouts: 2.92 us -> 4.05 us
  transfers between devices with their start and end apart: 13 -> 7, of which waited for: 8 -> 4; matrix products, arithmetic and copies ran while one was open for 0% -> 0% of each run, Pallas kernels for 0% -> 0%
where the time goes in v1:
time: 60.6 us; the launch traced here: 60.1 us
  blocking collectives  28.8 us (48%)
  starting transfers between devices  14.9 us (25%)
  waiting for transfers between devices  6.53 us (11%)
  Pallas kernels  4.91 us (8%)
  local copies, waits for them, and re-layouts  4.05 us (7%)
  other arithmetic  0.8 us (1%)
    all_to_all x1, blocking collectives, body(): pieces = lax.all_to_all(keep + got, ('x', 'z'), 0, 0, tiled=True)  28.8 us
    pallas_call x2, Pallas kernels, call(): pl.pallas_call(kernel, out_shape=[jax.ShapeDtypeStruct(s, F32) for s in o...  4.91 us
    unnamed x12, local copies, waits for them, and re-layouts  4.05 us
    ppermute x1, starting transfers between devices, body(): side_below = lax.ppermute(edge_top, ('gx', 'gy'), cross(up))  3.74 us
    ppermute x1, starting transfers between devices, body(): above = lax.ppermute(bottom, 'gx', down)  3.48 us
    ppermute x1, starting transfers between devices, body(): side_above = lax.ppermute(edge_bottom, ('gx', 'gy'), cross(down))  2.99 us
    ppermute x1, waiting for transfers between devices, body(): side_below = lax.ppermute(edge_top, ('gx', 'gy'), cross(up))  2.86 us
    ppermute x1, starting transfers between devices, body(): below = lax.ppermute(top, 'gx', up)  2.39 us
  transfers between devices with their start and end apart: 7, of which 4 were waited for; matrix products, arithmetic and copies ran while one was open for 0% of the time, Pallas kernels for 0%

profile of v1, /device:TPU:8, one launch (start us, length us, event | category | flops | bytes accessed | tf_op | source)
XLA Modules:
  0.0 60.1 jit_solution(7703491445246125223)
XLA Ops:
  0.0 0.1 pad_add_fusion.where
  0.1 0.0 copy-start
  0.1 1.2 %copy-done = f32[32,32,256]{2,1,0:T(8,128)S(1)} copy-done((f32[32,32,256]{2,1,0:T(8,128)S(1)}, f32[32,32,256]{2,1,0:T(8,128)}, u32[]{:S(2)}) %copy-start) | copy-done | bytes 1048600
  1.3 0.0 copy-start.1
  1.3 1.2 %copy-done.1 = f32[1,32,32,256]{3,2,1,0:T(8,128)S(1)} copy-done((f32[1,32,32,256]{3,2,1,0:T(8,128)S(1)}, f32[1,32,32,256]{3,2,1,0:T(8,128)}, u32[]{:S(2)}) %copy-start.1) | copy-done | bytes 1048600
  2.5 0.0 copy-start.2
  2.5 0.0 copy-start.4
  2.5 0.0 copy-start.5
  2.5 1.1 %shard_map.55 = (f32[32,16,256]{2,1,0:T(8,128)S(1)}, f32[32,16,256]{2,1,0:T(8,128)S(1)}, f32[4,16,128]{2,1,0:T(8,128)S(1)}, f32[4,16,128]{2,1,0:T(8,128)S(1)}) custom-call(s32[3]{0:T(128)S(1)} %pad_add_fusion.where, f32[1,32,32,256]{3,2,1,0:T(8,128)S(1)} %copy-done.1, f32[32,32,256]{2,1,0:T(8,128)S(1)} %copy-done), custom_call_target="tpu_custom_call" | custom-call | bytes 1048576 | tf_op jit(solution)/shard_map/pallas_call | solution.py:159
  3.6 3.5 %collective-permute-start = (f32[32,16,256]{2,1,0:T(8,128)S(1)}, f32[32,16,256]{2,1,0:T(8,128)S(1)}, u32[]{:S(2)}, u32[]{:S(2)}) collective-permute-start(f32[32,16,256]{2,1,0:T(8,128)S(1)} %get-tuple-element.11.bottom_ref), channel_id=1, source_target_pairs={{0,2},{2,4},{4,6},{1,3},{3,5},{5,7},{8,10},{10,12},{12,14},{9,11},... | collective-permute-start | bytes 1572872 | tf_op jit(solution)/shard_map/ppermute | solution.py:182
  7.1 2.4 %collective-permute-start.1 = (f32[32,16,256]{2,1,0:T(8,128)S(1)}, f32[32,16,256]{2,1,0:T(8,128)S(1)}, u32[]{:S(2)}, u32[]{:S(2)}) collective-permute-start(f32[32,16,256]{2,1,0:T(8,128)S(1)} %get-tuple-element.12.top_ref), channel_id=1, source_target_pairs={{2,0},{4,2},{6,4},{3,1},{5,3},{7,5},{10,8},{12,10},{14,12},{11,9},... | collective-permute-start | bytes 1572872 | tf_op jit(solution)/shard_map/ppermute | solution.py:183
  9.5 2.0 %collective-permute-start.4 = (f32[4,16,128]{2,1,0:T(8,128)S(1)}, f32[4,16,128]{2,1,0:T(8,128)S(1)}, u32[]{:S(2)}, u32[]{:S(2)}) collective-permute-start(f32[4,16,128]{2,1,0:T(8,128)S(1)} %get-tuple-element.13), channel_id=1, source_target_pairs={{0,1},{1,0},{2,3},{3,2},{4,5},{5,4},{6,7},{7,6},{8,9},{9,8},{10,11... | collective-permute-start | bytes 98312 | tf_op jit(solution)/shard_map/ppermute | solution.py:185
  11.5 3.0 %collective-permute-start.2 = (f32[4,16,128]{2,1,0:T(8,128)S(1)}, f32[4,16,128]{2,1,0:T(8,128)S(1)}, u32[]{:S(2)}, u32[]{:S(2)}) collective-permute-start(f32[4,16,128]{2,1,0:T(8,128)S(1)} %get-tuple-element.13), channel_id=1, source_target_pairs={{0,3},{1,2},{2,5},{3,4},{4,7},{5,6},{8,11},{9,10},{10,13},{11,12},... | collective-permute-start | bytes 98312 | tf_op jit(solution)/shard_map/ppermute | solution.py:186
  14.5 3.7 %collective-permute-start.5 = (f32[4,16,128]{2,1,0:T(8,128)S(1)}, f32[4,16,128]{2,1,0:T(8,128)S(1)}, u32[]{:S(2)}, u32[]{:S(2)}) collective-permute-start(f32[4,16,128]{2,1,0:T(8,128)S(1)} %get-tuple-element.14), channel_id=1, source_target_pairs={{2,1},{3,0},{4,3},{5,2},{6,5},{7,4},{10,9},{11,8},{12,11},{13,10},... | collective-permute-start | bytes 98312 | tf_op jit(solution)/shard_map/ppermute | solution.py:187
  18.3 0.0 collective-permute-done.4.side_bottom_ref
  18.3 0.2 collective-permute-start.3
  18.5 0.0 collective-permute-done.2.side_above_ref
  18.5 2.9 %collective-permute-done.5.side_below_ref = f32[4,16,128]{2,1,0:T(8,128)S(1)} collective-permute-done((f32[4,16,128]{2,1,0:T(8,128)S(1)}, f32[4,16,128]{2,1,0:T(8,128)S(1)}, u32[]{:S(2)}, u32[]{:S(2)}) %collective-permute-start.5) | collective-permute-done | bytes 32800 | tf_op jit(solution)/shard_map/ppermute | solution.py:187
  21.3 0.9 %collective-permute-done.3.side_top_ref = f32[4,16,128]{2,1,0:T(8,128)S(1)} collective-permute-done((f32[4,16,128]{2,1,0:T(8,128)S(1)}, f32[4,16,128]{2,1,0:T(8,128)S(1)}, u32[]{:S(2)}, u32[]{:S(2)}) %collective-permute-start.3) | collective-permute-done | bytes 32800 | tf_op jit(solution)/shard_map/ppermute | solution.py:184
  22.3 0.0 collective-permute-done.above_ref
  22.3 0.8 %collective-permute-done.1.below_ref = f32[32,16,256]{2,1,0:T(8,128)S(1)} collective-permute-done((f32[32,16,256]{2,1,0:T(8,128)S(1)}, f32[32,16,256]{2,1,0:T(8,128)S(1)}, u32[]{:S(2)}, u32[]{:S(2)}) %collective-permute-start.1) | collective-permute-done | bytes 524320 | tf_op jit(solution)/shard_map/ppermute | solution.py:183
  23.1 0.0 copy-done.2
  23.1 0.0 copy-done.4
  23.1 0.0 copy-done.5
  23.1 0.0 copy-start.3
  23.1 1.6 %copy-done.3 = bf16[2,2,1024,256]{3,2,1,0:T(8,128)(2,1)S(1)} copy-done((bf16[2,2,1024,256]{3,2,1,0:T(8,128)(2,1)S(1)}, bf16[2,2,1024,256]{3,2,1,0:T(8,128)(2,1)}, u32[]{:S(2)}) %copy-start.3) | copy-done | bytes 2097176
  24.7 3.8 %shard_map.56 = (f32[16,32,256]{2,1,0:T(8,128)S(1)}, f32[16,32,256]{2,1,0:T(8,128)S(1)}) custom-call(s32[3]{0:T(128)S(1)} %pad_add_fusion.where, f32[1,32,32,256]{3,2,1,0:T(8,128)S(1)} %copy-done.2, f32[32,16,256]{2,1,0:T(8,128)S(1)} %collective-permute-done.above_ref, f32[32,16,256]{2,1,0:T(8,128)S(1)} %get-tuple-element.12.top_ref, ...), custom_call_target="tpu_custom_call" | custom-call | flops 4000000000 | bytes 1048576 | tf_op jit(solution)/shard_map/pallas_call | solution.py:159
  28.5 0.1 collective-permute-start.6
  28.6 1.9 %collective-permute-done.6 = f32[16,32,256]{2,1,0:T(8,128)S(1)} collective-permute-done((f32[16,32,256]{2,1,0:T(8,128)S(1)}, f32[16,32,256]{2,1,0:T(8,128)S(1)}, u32[]{:S(2)}, u32[]{:S(2)}) %collective-permute-start.6) | collective-permute-done | bytes 524320 | tf_op jit(solution)/shard_map/ppermute | solution.py:197
  30.5 0.1 add.3
  30.6 28.8 %all_to_all.5 = f32[16,32,256]{2,1,0:T(8,128)S(1)} all-to-all(f32[16,32,256]{2,1,0:T(8,128)S(1)} %add.3), channel_id=1, replica_groups=mesh['x'=4,'z'=4,'core'=2,'gx'=4,'gy'=2] {'x','z'}, dimensions={0} | all-to-all | bytes 1048576 | tf_op jit(solution)/shard_map/all_to_all | solution.py:198
  59.5 0.6 %multiply_bitcast_fusion = f32[1,32,256]{2,1,0:T(8,128)} fusion(f32[32,256]{1,0:T(8,128)S(1)} %reduce_sum.9), kind=kLoop, calls=%fused_computation | loop fusion | flops 8192 | bytes 65536 | tf_op jit(solution)/shard_map/mul | solution.py:199
  (1 shorter events, 0.0 us)
Async XLA Ops:
  0.1 1.2 %copy-start = (f32[32,32,256]{2,1,0:T(8,128)S(1)}, f32[32,32,256]{2,1,0:T(8,128)}, u32[]{:S(2)}) copy-start(f32[32,32,256]{2,1,0:T(8,128)} %c_ref.1) | copy-start | bytes 3145732
  1.3 1.2 %copy-start.1 = (f32[1,32,32,256]{3,2,1,0:T(8,128)S(1)}, f32[1,32,32,256]{3,2,1,0:T(8,128)}, u32[]{:S(2)}) copy-start(f32[1,32,32,256]{3,2,1,0:T(8,128)} %p_ref.3) | copy-start | bytes 3145732
  2.5 20.6 %copy-start.2 = (f32[1,32,32,256]{3,2,1,0:T(8,128)S(1)}, f32[1,32,32,256]{3,2,1,0:T(8,128)}, u32[]{:S(2)}) copy-start(f32[1,32,32,256]{3,2,1,0:T(8,128)} %p_ref.3) | copy-start | bytes 3145732
  2.5 20.6 %copy-start.4 = (bf16[2,2,512,128]{3,2,1,0:T(8,128)(2,1)S(1)}, bf16[2,2,512,128]{3,2,1,0:T(8,128)(2,1)}, u32[]{:S(2)}) copy-start(bf16[2,2,512,128]{3,2,1,0:T(8,128)(2,1)} %constant.23.clone.edge_ref) | copy-start | bytes 1572868
  2.5 20.6 %copy-start.5 = (bf16[4,2,96,256]{3,2,1,0:T(8,128)(2,1)S(1)}, bf16[4,2,96,256]{3,2,1,0:T(8,128)(2,1)}, u32[]{:S(2)}) copy-start(bf16[4,2,96,256]{3,2,1,0:T(8,128)(2,1)} %constant.21.clone.left_ref) | copy-start | bytes 1179652
  3.6 18.6 %collective-permute-start = (f32[32,16,256]{2,1,0:T(8,128)S(1)}, f32[32,16,256]{2,1,0:T(8,128)S(1)}, u32[]{:S(2)}, u32[]{:S(2)}) collective-permute-start(f32[32,16,256]{2,1,0:T(8,128)S(1)} %get-tuple-element.11.bottom_ref), channel_id=1, source_target_pairs={{0,2},{2,4},{4,6},{1,3},{3,5},{5,7},{8,10},{10,12},{12,14},{9,11},... | collective-permute-start | bytes 1572872 | tf_op jit(solution)/shard_map/ppermute | solution.py:182
  7.1 16.0 %collective-permute-start.1 = (f32[32,16,256]{2,1,0:T(8,128)S(1)}, f32[32,16,256]{2,1,0:T(8,128)S(1)}, u32[]{:S(2)}, u32[]{:S(2)}) collective-permute-start(f32[32,16,256]{2,1,0:T(8,128)S(1)} %get-tuple-element.12.top_ref), channel_id=1, source_target_pairs={{2,0},{4,2},{6,4},{3,1},{5,3},{7,5},{10,8},{12,10},{14,12},{11,9},... | collective-permute-start | bytes 1572872 | tf_op jit(solution)/shard_map/ppermute | solution.py:183
  9.5 8.8 %collective-permute-start.4 = (f32[4,16,128]{2,1,0:T(8,128)S(1)}, f32[4,16,128]{2,1,0:T(8,128)S(1)}, u32[]{:S(2)}, u32[]{:S(2)}) collective-permute-start(f32[4,16,128]{2,1,0:T(8,128)S(1)} %get-tuple-element.13), channel_id=1, source_target_pairs={{0,1},{1,0},{2,3},{3,2},{4,5},{5,4},{6,7},{7,6},{8,9},{9,8},{10,11... | collective-permute-start | bytes 98312 | tf_op jit(solution)/shard_map/ppermute | solution.py:185
  11.5 7.0 %collective-permute-start.2 = (f32[4,16,128]{2,1,0:T(8,128)S(1)}, f32[4,16,128]{2,1,0:T(8,128)S(1)}, u32[]{:S(2)}, u32[]{:S(2)}) collective-permute-start(f32[4,16,128]{2,1,0:T(8,128)S(1)} %get-tuple-element.13), channel_id=1, source_target_pairs={{0,3},{1,2},{2,5},{3,4},{4,7},{5,6},{8,11},{9,10},{10,13},{11,12},... | collective-permute-start | bytes 98312 | tf_op jit(solution)/shard_map/ppermute | solution.py:186
  14.5 6.8 %collective-permute-start.5 = (f32[4,16,128]{2,1,0:T(8,128)S(1)}, f32[4,16,128]{2,1,0:T(8,128)S(1)}, u32[]{:S(2)}, u32[]{:S(2)}) collective-permute-start(f32[4,16,128]{2,1,0:T(8,128)S(1)} %get-tuple-element.14), channel_id=1, source_target_pairs={{2,1},{3,0},{4,3},{5,2},{6,5},{7,4},{10,9},{11,8},{12,11},{13,10},... | collective-permute-start | bytes 98312 | tf_op jit(solution)/shard_map/ppermute | solution.py:187
  18.3 4.0 %collective-permute-start.3 = (f32[4,16,128]{2,1,0:T(8,128)S(1)}, f32[4,16,128]{2,1,0:T(8,128)S(1)}, u32[]{:S(2)}, u32[]{:S(2)}) collective-permute-start(f32[4,16,128]{2,1,0:T(8,128)S(1)} %get-tuple-element.14), channel_id=1, source_target_pairs={{0,1},{1,0},{2,3},{3,2},{4,5},{5,4},{6,7},{7,6},{8,9},{9,8},{10,11... | collective-permute-start | bytes 98312 | tf_op jit(solution)/shard_map/ppermute | solution.py:184
  23.1 1.6 %copy-start.3 = (bf16[2,2,1024,256]{3,2,1,0:T(8,128)(2,1)S(1)}, bf16[2,2,1024,256]{3,2,1,0:T(8,128)(2,1)}, u32[]{:S(2)}) copy-start(bf16[2,2,1024,256]{3,2,1,0:T(8,128)(2,1)} %constant.22.clone.right_ref) | copy-start | bytes 6291460
  28.5 2.0 %collective-permute-start.6 = (f32[16,32,256]{2,1,0:T(8,128)S(1)}, f32[16,32,256]{2,1,0:T(8,128)S(1)}, u32[]{:S(2)}, u32[]{:S(2)}) collective-permute-start(f32[16,32,256]{2,1,0:T(8,128)S(1)} %get-tuple-element.16), channel_id=1, source_target_pairs={{0,8},{8,0},{1,9},{9,1},{2,10},{10,2},{3,11},{11,3},{4,12},{12,4},... | collective-permute-start | bytes 1572872 | tf_op jit(solution)/shard_map/ppermute | solution.py:197

commit v2 on v1

--- a/solution.py
+++ b/solution.py
@@ -58,7 +58,7 @@
         near = slice(columns - HALO, columns) if part == 0 else slice(columns, columns + HALO)
         terms = (fine @ fine, pair @ fine, fine @ pair, pair @ pair)
         owns.append(np.concatenate([term[own, own] for term in terms]))
-        sides.append(np.concatenate([np.kron(np.eye(8), term[edge, near]) for term in terms]))
+        sides.append(np.concatenate([np.tile(term[edge, near], (1, 8)) for term in terms]))
     return np.stack(owns), np.stack(sides)
 
 
@@ -74,12 +74,21 @@
     return dot(lh, rh) + (dot(lh, rl) + dot(ll, rh))
 
 
-def product_kernel(where, p_ref, c_ref, top_ref, bottom_ref, edge_top_ref, edge_bottom_ref):
+def product_kernel(where, p_hbm, c_hbm, top_ref, bottom_ref, edge_ref, edge_top_ref, edge_bottom_ref, p_ref, c_ref, sems):
     gy = where[2]
+    copies = []
+    for g in range(8):
+        at = pl.ds(4 * g, 4)
+        copies.append(pltpu.make_async_copy(p_hbm.at[0, at], p_ref.at[at], sems.at[0, g]))
+        copies.append(pltpu.make_async_copy(c_hbm.at[at], c_ref.at[at], sems.at[1, g]))
+    for copy in copies:
+        copy.start()
     lane = lax.broadcasted_iota(jnp.int32, (1, 1, 128), 2)
     edges = jnp.zeros((4, 32, 128), F32)
     for g in range(8):
-        v = p_ref[0, 4 * g : 4 * g + 4] * c_ref[4 * g : 4 * g + 4]
+        copies[2 * g].wait()
+        copies[2 * g + 1].wait()
+        v = p_ref[4 * g : 4 * g + 4] * c_ref[4 * g : 4 * g + 4]
         top_ref[4 * g : 4 * g + 4] = v[:, :HALO]
         bottom_ref[4 * g : 4 * g + 4] = v[:, HALO:]
         last = v[:, :, 128:].reshape(128, 128)
@@ -88,17 +97,24 @@
         if g:
             edge = pltpu.roll(edge, 16 * g, 1)
         edges = jnp.where(lane // 16 == g, edge.reshape(4, 32, 128), edges)
+    edge_ref[...] = edges
     edge_top_ref[...] = edges[:, :HALO]
     edge_bottom_ref[...] = edges[:, HALO:]
 
 
 def filter_kernel(
     where, p_ref, above_ref, top_ref, bottom_ref, below_ref,
-    side_above_ref, side_top_ref, side_bottom_ref, side_below_ref,
-    left_ref, right_ref, edge_ref, keep_ref, send_ref,
-    xh_ref, xl_ref, fh_ref, fl_ref, ch_ref, cl_ref, alpha_ref, pairs_ref, near_ref,
+    side_above_ref, side_ref, side_below_ref, left_ref, edge_ref, right_hbm, keep_ref, send_ref,
+    xh_ref, xl_ref, fh_ref, fl_ref, ch_ref, cl_ref, alpha_ref, pairs_ref, near_ref, right_ref, sems,
 ):
     core, gx, gy = where[0], where[1], where[2]
+    copies = []
+    for h in range(2):
+        for k in range(4):
+            at = pl.ds(256 * k, 256)
+            copies.append(pltpu.make_async_copy(right_hbm.at[gy, h, at], right_ref.at[h, at], sems.at[h, k]))
+    for copy in copies:
+        copy.start()
     lane = lax.broadcasted_iota(jnp.int32, (1, 256), 1)
     row, start = 0, 0
     for count in (32, 32, 16, 16):
@@ -111,32 +127,40 @@
             row += count
         start += count
 
-    def by_rows(refs, pick):
-        return dot3((xh_ref[...], xl_ref[...]), split(jnp.concatenate([pick(r) for r in refs])))
-
-    side = by_rows((side_above_ref, side_top_ref, side_bottom_ref, side_below_ref), lambda r: r[...].reshape(64, 128))
+    def by_rows(parts):
+        return dot3((xh_ref[...], xl_ref[...]), split(jnp.concatenate(parts)))
+
+    sides = (side_above_ref[...], side_ref[:, :HALO], side_ref[:, HALO:], side_below_ref[...])
+    side = by_rows([s.reshape(64, 128) for s in sides])
     fine = split(jnp.concatenate([side[:128], side[128:256]], axis=1))
     pair = split(jnp.concatenate([side[256:320], side[320:]], axis=1))
-    near = dot3(fine, (edge_ref[gy, 0, :256], edge_ref[gy, 1, :256]))
-    near_pairs = dot3(pair, (edge_ref[gy, 0, 256:], edge_ref[gy, 1, 256:]))
+    narrow = lax.broadcasted_iota(jnp.int32, (1, 128), 1)
+
+    def edge(h, t):
+        rows = edge_ref[gy, h, 16 * t : 16 * t + 16].astype(F32)
+        return [jnp.where(narrow // 16 == g, rows, jnp.zeros_like(rows)).astype(BF16) for g in range(8)]
+
+    near = dot3(fine, [jnp.concatenate(edge(h, 0) + edge(h, 1)) for h in range(2)])
+    near_pairs = dot3(pair, [jnp.concatenate(edge(h, 2) + edge(h, 3)) for h in range(2)])
     near_ref[pl.ds(0, 64, stride=2), :] = near_pairs
     near_ref[pl.ds(1, 64, stride=2), :] = near_pairs
     near = near + near_ref[...]
     near = jnp.where(gy == 0, pltpu.roll(near, 112, 1), near)
-    narrow = lax.broadcasted_iota(jnp.int32, (1, 128), 1)
     on_left = (narrow < HALO) & (gy == 1)
     on_right = (narrow >= 128 - HALO) & (gy == 0)
 
     for g in range(8):
-        u = by_rows((above_ref, top_ref, bottom_ref, below_ref), lambda r: r[4 * g : 4 * g + 4].reshape(64, 256))
+        u = by_rows([r[4 * g : 4 * g + 4].reshape(64, 256) for r in (above_ref, top_ref, bottom_ref, below_ref)])
         for t in range(2):
             at, lanes = slice(128 * g, 128 * g + 128), slice(256 * t, 256 * t + 256)
             fh_ref[at, lanes], fl_ref[at, lanes] = split(u[128 * t : 128 * t + 128])
             at = slice(64 * g, 64 * g + 64)
             ch_ref[at, lanes], cl_ref[at, lanes] = split(u[256 + 64 * t : 320 + 64 * t])
 
-    alpha_ref[...] = dot3((fh_ref[...], fl_ref[...]), (right_ref[gy, 0, :512], right_ref[gy, 1, :512]))
-    pairs = dot3((ch_ref[...], cl_ref[...]), (right_ref[gy, 0, 512:], right_ref[gy, 1, 512:]))
+    for copy in copies:
+        copy.wait()
+    alpha_ref[...] = dot3((fh_ref[...], fl_ref[...]), (right_ref[0, :512], right_ref[1, :512]))
+    pairs = dot3((ch_ref[...], cl_ref[...]), (right_ref[0, 512:], right_ref[1, 512:]))
     for h in range(2):
         for s in range(2):
             pairs_ref[h, pl.ds(s, 512, stride=2), :] = pairs[:, 128 * h : 128 * h + 128]
@@ -148,14 +172,18 @@
         low = pairs_ref[0, at] + jnp.where(on_left, moved, zero)
         high = pairs_ref[1, at] + jnp.where(on_right, moved, zero)
         alpha = alpha_ref[at] + jnp.concatenate([low, high], axis=1)
-        q = p_ref[0, 4 * g : 4 * g + 4] * alpha.reshape(4, 32, 256)
+        q = p_ref[4 * g : 4 * g + 4] * alpha.reshape(4, 32, 256)
         for j in range(2):
-            keep_ref[2 * g + j] = jnp.where(core == 0, q[2 * j], q[2 * j + 1])
-            send_ref[2 * g + j] = jnp.where(core == 0, q[2 * j + 1], q[2 * j])
-
-
-def call(kernel, outs, *args, scratch=(), cost=0, grant=16):
-    specs = [pl.BlockSpec(memory_space=pltpu.SMEM)] + [VMEM] * (len(args) - 1)
+            at = 4 * lax.rem(g // 2 + 4 - where[3], 4) + lax.rem(2 * (g % 2) + j + 4 - where[4], 4)
+            keep_ref[at] = jnp.where(core == 0, q[2 * j], q[2 * j + 1])
+            send_ref[at] = jnp.where(core == 0, q[2 * j + 1], q[2 * j])
+
+
+def call(kernel, outs, *args, hbm=(), scratch=(), cost=0, grant=16):
+    args = [pltpu.with_memory_space_constraint(a, pltpu.HBM) if i in hbm else a for i, a in enumerate(args)]
+    specs = [pl.BlockSpec(memory_space=pltpu.SMEM)] + [
+        pl.BlockSpec(memory_space=pltpu.HBM) if i in hbm else VMEM for i in range(1, len(args))
+    ]
     return pl.pallas_call(
         kernel,
         out_shape=[jax.ShapeDtypeStruct(s, F32) for s in outs],
@@ -168,41 +196,45 @@
 
 
 def body(perturbations, control):
-    core, gx, gy = lax.axis_index("core"), lax.axis_index("gx"), lax.axis_index("gy")
-    where = jnp.stack([core, gx, gy]).astype(jnp.int32)
+    x, z, core, gx, gy = (lax.axis_index(a) for a in ("x", "z", "core", "gx", "gy"))
+    where = jnp.stack([core, gx, gy, x, z]).astype(jnp.int32)
     left = jnp.asarray(halves(left_table(128, 4)))
     right, edge = (jnp.asarray(halves(t)) for t in right_tables(512, 2))
-
-    top, bottom, edge_top, edge_bottom = call(
-        product_kernel, [(32, 16, 256)] * 2 + [(4, 16, 128)] * 2, where, perturbations, control
+    vmem, sems = pltpu.VMEM, pltpu.SemaphoreType.DMA
+
+    top, bottom, edges, edge_top, edge_bottom, near_p = call(
+        product_kernel, [(32, 16, 256)] * 2 + [(4, 32, 128)] + [(4, 16, 128)] * 2 + [(32, 32, 256)],
+        where, perturbations, control, hbm=(1, 2), scratch=[vmem((32, 32, 256), F32), sems((2, 8))],
     )
     down = [(i, i + 1) for i in range(3)]
     up = [(i + 1, i) for i in range(3)]
     cross = lambda pairs: [(2 * a + s, 2 * b + 1 - s) for a, b in pairs for s in range(2)]
+
+    side = lax.ppermute(edges, "gy", [(0, 1), (1, 0)])
+    side_above = lax.ppermute(edge_bottom, ("gx", "gy"), cross(down))
+    side_below = lax.ppermute(edge_top, ("gx", "gy"), cross(up))
     above = lax.ppermute(bottom, "gx", down)
     below = lax.ppermute(top, "gx", up)
-    side_top = lax.ppermute(edge_top, "gy", [(0, 1), (1, 0)])
-    side_bottom = lax.ppermute(edge_bottom, "gy", [(0, 1), (1, 0)])
-    side_above = lax.ppermute(edge_bottom, ("gx", "gy"), cross(down))
-    side_below = lax.ppermute(edge_top, ("gx", "gy"), cross(up))
-
-    vmem, f32 = pltpu.VMEM, F32
-    keep, send = call(
-        filter_kernel, [(16, 32, 256)] * 2, where, perturbations, above, top, bottom, below,
-        side_above, side_top, side_bottom, side_below, left, right, edge,
+
+    keep, give = call(
+        filter_kernel, [(16, 32, 256)] * 2, where, near_p, above, top, bottom, below,
+        side_above, side, side_below, left, edge, right, hbm=(11,),
         scratch=[vmem((384, 256), BF16)] * 2 + [vmem((1024, 512), BF16)] * 2 + [vmem((512, 512), BF16)] * 2
-        + [vmem((1024, 256), f32), vmem((2, 1024, 128), f32), vmem((128, 128), f32)],
+        + [vmem((1024, 256), F32), vmem((2, 1024, 128), F32), vmem((128, 128), F32)]
+        + [vmem((2, 1024, 256), BF16), sems((2, 4))],
         cost=4 * 10**9, grant=24,
     )
-    got = lax.ppermute(send, "core", [(0, 1), (1, 0)])
-    pieces = lax.all_to_all(keep + got, ("x", "z"), 0, 0, tiled=True)
-    return jnp.sum(pieces, axis=0, keepdims=True) * (1.0 / 31.0)
+    got = lax.ppermute(give, "core", [(0, 1), (1, 0)])
+    ring = lambda d: [(i, (i + d) % 4) for i in range(4)]
+    piece = [keep[4 * d : 4 * d + 4] + got[4 * d : 4 * d + 4] for d in range(4)]
+    x2, x1, x3 = (lax.ppermute(piece[d], "x", ring(d)) for d in (2, 1, 3))
+    cell = [(piece[0][e : e + 1] + x2[e : e + 1]) + (x1[e : e + 1] + x3[e : e + 1]) for e in range(4)]
+    z2, z1, z3 = (lax.ppermute(cell[e], "z", ring(e)) for e in (2, 1, 3))
+    return ((cell[0] + z2) + (z1 + z3)) * (1.0 / 31.0)
 
 
 def solution(mesh):
     grid = Mesh(mesh.devices.reshape(4, 4, 2, 4, 2), ("x", "z", "core", "gx", "gy"))
     mem = ("x", "z", "core")
     placed = (P(mem, None, "gx", "gy"), P(None, "gx", "gy"))
-    return jax.shard_map(
-        body, mesh=grid, in_specs=placed, out_specs=P(mem, "gx", "gy"), check_vma=False
-    )
+    return jax.shard_map(body, mesh=grid, in_specs=placed, out_specs=P(mem, "gx", "gy"), check_vma=False)

time: 60.6 us -> 57.3 us (0.946)
  blocking collectives: 28.8 us -> 0 us
  starting transfers between devices: 14.9 us -> 30 us
  waiting for transfers between devices: 6.53 us -> 18.1 us
  local copies, waits for them, and re-layouts: 4.05 us -> 0.09 us
  Pallas kernels: 4.91 us -> 8.11 us
    all_to_all x1 -> x0, blocking collectives: 28.8 us -> none  [body(): pieces = lax.all_to_all(keep + got, ('x', 'z'), 0, 0, tiled=True)]
    ppermute x3 -> x8, starting transfers between devices: 2.29 us -> 17.4 us  [the longest x3 10.2 us: body(): z2, z1, z3 = (lax.ppermute(cell[e], 'z', ring(e)) for e in (2, 1, 3))]
    ppermute x3 -> x8, waiting for transfers between devices: 2.85 us -> 13.2 us  [the longest x3 6.99 us: body(): x2, x1, x3 = (lax.ppermute(piece[d], 'x', ring(d)) for d in (2, 1, 3))]
    unnamed x12 -> x4, local copies, waits for them, and re-layouts: 4.05 us -> 0.01 us
    pallas_call x2, Pallas kernels: 4.91 us -> 8.11 us  [call(): pl.pallas_call(kernel, out_shape=[jax.ShapeDtypeStruct(s, F32) for s in o...]
    ppermute x1, waiting for transfers between devices: 0.82 us -> 1.77 us  [body(): below = lax.ppermute(top, 'gx', up)]
  transfers between devices with their start and end apart: 7 -> 12, of which waited for: 4 -> 8; matrix products, arithmetic and copies ran while one was open for 0% -> 0% of each run, Pallas kernels for 0% -> 0%
where the time goes in v2:
time: 57.3 us; the launch traced here: 57.1 us
  starting transfers between devices  30 us (52%)
  waiting for transfers between devices  18.1 us (32%)
  Pallas kernels  8.11 us (14%)
  other arithmetic  0.73 us (1%)
    ppermute x3, starting transfers between devices, body(): z2, z1, z3 = (lax.ppermute(cell[e], 'z', ring(e)) for e in (2, 1, 3))  10.2 us
    pallas_call x2, Pallas kernels, call(): pl.pallas_call(kernel, out_shape=[jax.ShapeDtypeStruct(s, F32) for s in o...  8.11 us
    ppermute x3, waiting for transfers between devices, body(): x2, x1, x3 = (lax.ppermute(piece[d], 'x', ring(d)) for d in (2, 1, 3))  6.99 us
    ppermute x3, starting transfers between devices, body(): x2, x1, x3 = (lax.ppermute(piece[d], 'x', ring(d)) for d in (2, 1, 3))  5.13 us
    ppermute x3, waiting for transfers between devices, body(): z2, z1, z3 = (lax.ppermute(cell[e], 'z', ring(e)) for e in (2, 1, 3))  4.36 us
    ppermute x1, starting transfers between devices, body(): side_below = lax.ppermute(edge_top, ('gx', 'gy'), cross(up))  3.74 us
    ppermute x1, starting transfers between devices, body(): above = lax.ppermute(bottom, 'gx', down)  3.48 us
    ppermute x1, waiting for transfers between devices, body(): side_below = lax.ppermute(edge_top, ('gx', 'gy'), cross(up))  3.01 us
  transfers between devices with their start and end apart: 12, of which 8 were waited for; matrix products, arithmetic and copies ran while one was open for 0% of the time, Pallas kernels for 0%

profile of v2, /device:TPU:8, one launch (start us, length us, event | category | flops | bytes accessed | tf_op | source)
XLA Modules:
  0.0 57.1 jit_solution(8687404113056314831)
XLA Ops:
  0.0 0.0 copy-start.1
  0.0 0.0 copy-start
  0.0 0.1 stack.23.where
  0.1 2.9 %shard_map.55 = (f32[32,16,256]{2,1,0:T(8,128)S(1)}, f32[32,16,256]{2,1,0:T(8,128)S(1)}, f32[4,32,128]{2,1,0:T(8,128)S(1)}, f32[4,16,128]{2,1,0:T(8,128)S(1)}, f...) custom-call(s32[5]{0:T(128)S(1)} %stack.23.where, f32[1,32,32,256]{3,2,1,0:T(8,128)} %p_hbm.1, f32[32,32,256]{2,1,0:T(8,128)} %c_hbm.1), custom_call_target="tpu_custom_call" | custom-call | bytes 1048576 | tf_op jit(solution)/shard_map/pallas_call | solution.py:187
  3.0 3.5 %collective-permute-start = (f32[32,16,256]{2,1,0:T(8,128)S(1)}, f32[32,16,256]{2,1,0:T(8,128)S(1)}, u32[]{:S(2)}, u32[]{:S(2)}) collective-permute-start(f32[32,16,256]{2,1,0:T(8,128)S(1)} %get-tuple-element.14.bottom_ref), channel_id=1, source_target_pairs={{0,2},{2,4},{4,6},{1,3},{3,5},{5,7},{8,10},{10,12},{12,14},{9,11},... | collective-permute-start | bytes 1572872 | tf_op jit(solution)/shard_map/ppermute | solution.py:216
  6.5 2.4 %collective-permute-start.1 = (f32[32,16,256]{2,1,0:T(8,128)S(1)}, f32[32,16,256]{2,1,0:T(8,128)S(1)}, u32[]{:S(2)}, u32[]{:S(2)}) collective-permute-start(f32[32,16,256]{2,1,0:T(8,128)S(1)} %get-tuple-element.15.top_ref), channel_id=1, source_target_pairs={{2,0},{4,2},{6,4},{3,1},{5,3},{7,5},{10,8},{12,10},{14,12},{11,9},... | collective-permute-start | bytes 1572872 | tf_op jit(solution)/shard_map/ppermute | solution.py:217
  8.9 2.0 %collective-permute-start.3 = (f32[4,32,128]{2,1,0:T(8,128)S(1)}, f32[4,32,128]{2,1,0:T(8,128)S(1)}, u32[]{:S(2)}, u32[]{:S(2)}) collective-permute-start(f32[4,32,128]{2,1,0:T(8,128)S(1)} %get-tuple-element.17), channel_id=1, source_target_pairs={{0,1},{1,0},{2,3},{3,2},{4,5},{5,4},{6,7},{7,6},{8,9},{9,8},{10,11... | collective-permute-start | bytes 196616 | tf_op jit(solution)/shard_map/ppermute | solution.py:213
  10.9 3.0 %collective-permute-start.2 = (f32[4,16,128]{2,1,0:T(8,128)S(1)}, f32[4,16,128]{2,1,0:T(8,128)S(1)}, u32[]{:S(2)}, u32[]{:S(2)}) collective-permute-start(f32[4,16,128]{2,1,0:T(8,128)S(1)} %get-tuple-element.16), channel_id=1, source_target_pairs={{0,3},{1,2},{2,5},{3,4},{4,7},{5,6},{8,11},{9,10},{10,13},{11,12},... | collective-permute-start | bytes 98312 | tf_op jit(solution)/shard_map/ppermute | solution.py:214
  13.9 3.7 %collective-permute-start.4 = (f32[4,16,128]{2,1,0:T(8,128)S(1)}, f32[4,16,128]{2,1,0:T(8,128)S(1)}, u32[]{:S(2)}, u32[]{:S(2)}) collective-permute-start(f32[4,16,128]{2,1,0:T(8,128)S(1)} %get-tuple-element.18), channel_id=1, source_target_pairs={{2,1},{3,0},{4,3},{5,2},{6,5},{7,4},{10,9},{11,8},{12,11},{13,10},... | collective-permute-start | bytes 98312 | tf_op jit(solution)/shard_map/ppermute | solution.py:215
  17.6 0.1 collective-permute-done.2.side_above_ref
  17.7 3.0 %collective-permute-done.4.side_below_ref = f32[4,16,128]{2,1,0:T(8,128)S(1)} collective-permute-done((f32[4,16,128]{2,1,0:T(8,128)S(1)}, f32[4,16,128]{2,1,0:T(8,128)S(1)}, u32[]{:S(2)}, u32[]{:S(2)}) %collective-permute-start.4) | collective-permute-done | bytes 32800 | tf_op jit(solution)/shard_map/ppermute | solution.py:215
  20.7 0.0 collective-permute-done.3.side_ref
  20.7 0.0 collective-permute-done.above_ref
  20.7 1.8 %collective-permute-done.1.below_ref = f32[32,16,256]{2,1,0:T(8,128)S(1)} collective-permute-done((f32[32,16,256]{2,1,0:T(8,128)S(1)}, f32[32,16,256]{2,1,0:T(8,128)S(1)}, u32[]{:S(2)}, u32[]{:S(2)}) %collective-permute-start.1) | collective-permute-done | bytes 524320 | tf_op jit(solution)/shard_map/ppermute | solution.py:217
  22.5 0.0 copy-done.1
  22.5 0.0 copy-done
  22.5 5.2 %shard_map.56 = (f32[16,32,256]{2,1,0:T(8,128)S(1)}, f32[16,32,256]{2,1,0:T(8,128)S(1)}) custom-call(s32[5]{0:T(128)S(1)} %stack.23.where, f32[32,32,256]{2,1,0:T(8,128)S(1)} %get-tuple-element.13.p_ref, f32[32,16,256]{2,1,0:T(8,128)S(1)} %collective-permute-done.above_ref, f32[32,16,256]{2,1,0:T(8,128)S(1)} %get-tuple-element.15.top_ref, ...), custom_call_target="tpu_custom_call" | custom-call | flops 4000000000 | bytes 1048576 | tf_op jit(solution)/shard_map/pallas_call | solution.py:187
  27.7 0.1 collective-permute-start.5
  27.8 1.9 %collective-permute-done.5 = f32[16,32,256]{2,1,0:T(8,128)S(1)} collective-permute-done((f32[16,32,256]{2,1,0:T(8,128)S(1)}, f32[16,32,256]{2,1,0:T(8,128)S(1)}, u32[]{:S(2)}, u32[]{:S(2)}) %collective-permute-start.5) | collective-permute-done | bytes 524320 | tf_op jit(solution)/shard_map/ppermute | solution.py:227
  29.7 0.1 slice_add_fusion.3
  29.8 2.8 %collective-permute-start.8 = (f32[4,32,256]{2,1,0:T(8,128)S(1)}, f32[4,32,256]{2,1,0:T(8,128)S(1)}, u32[]{:S(2)}, u32[]{:S(2)}) collective-permute-start(f32[4,32,256]{2,1,0:T(8,128)S(1)} %get-tuple-element.22), channel_id=1, source_target_pairs={{0,192},{64,0},{128,64},{192,128},{1,193},{65,1},{129,65},{193,129... | collective-permute-start | bytes 393224 | tf_op jit(solution)/shard_map/ppermute | solution.py:230
  32.6 0.0 collective-permute-start.7
  32.6 2.3 %collective-permute-start.6 = (f32[4,32,256]{2,1,0:T(8,128)S(1)}, f32[4,32,256]{2,1,0:T(8,128)S(1)}, u32[]{:S(2)}, u32[]{:S(2)}) collective-permute-start(f32[4,32,256]{2,1,0:T(8,128)S(1)} %get-tuple-element.24), channel_id=1, source_target_pairs={{0,128},{64,192},{128,0},{192,64},{1,129},{65,193},{129,1},{193,65... | collective-permute-start | bytes 393224 | tf_op jit(solution)/shard_map/ppermute | solution.py:230
  34.9 0.8 %collective-permute-done.8 = f32[4,32,256]{2,1,0:T(8,128)S(1)} collective-permute-done((f32[4,32,256]{2,1,0:T(8,128)S(1)}, f32[4,32,256]{2,1,0:T(8,128)S(1)}, u32[]{:S(2)}, u32[]{:S(2)}) %collective-permute-start.8) | collective-permute-done | bytes 131104 | tf_op jit(solution)/shard_map/ppermute | solution.py:230
  35.7 6.2 %collective-permute-done.7 = f32[4,32,256]{2,1,0:T(8,128)S(1)} collective-permute-done((f32[4,32,256]{2,1,0:T(8,128)S(1)}, f32[4,32,256]{2,1,0:T(8,128)S(1)}, u32[]{:S(2)}, u32[]{:S(2)}) %collective-permute-start.7) | collective-permute-done | bytes 131104 | tf_op jit(solution)/shard_map/ppermute | solution.py:230
  41.9 0.0 collective-permute-done.6
  41.9 6.4 %collective-permute-start.11 = (f32[1,32,256]{2,1,0:T(8,128)S(1)}, f32[1,32,256]{2,1,0:T(8,128)S(1)}, u32[]{:S(2)}, u32[]{:S(2)}) collective-permute-start(f32[1,32,256]{2,1,0:T(8,128)S(1)} %get-tuple-element.25), channel_id=1, source_target_pairs={{0,48},{16,0},{32,16},{48,32},{1,49},{17,1},{33,17},{49,33},{2,50}... | collective-permute-start | bytes 98312 | tf_op jit(solution)/shard_map/ppermute | solution.py:232
  48.3 0.0 collective-permute-start.10
  48.3 3.8 %collective-permute-start.9 = (f32[1,32,256]{2,1,0:T(8,128)S(1)}, f32[1,32,256]{2,1,0:T(8,128)S(1)}, u32[]{:S(2)}, u32[]{:S(2)}) collective-permute-start(f32[1,32,256]{2,1,0:T(8,128)S(1)} %get-tuple-element.27), channel_id=1, source_target_pairs={{0,32},{16,48},{32,0},{48,16},{1,33},{17,49},{33,1},{49,17},{2,34}... | collective-permute-start | bytes 98312 | tf_op jit(solution)/shard_map/ppermute | solution.py:232
  52.1 0.0 collective-permute-done.11
  52.1 2.2 %collective-permute-done.10 = f32[1,32,256]{2,1,0:T(8,128)S(1)} collective-permute-done((f32[1,32,256]{2,1,0:T(8,128)S(1)}, f32[1,32,256]{2,1,0:T(8,128)S(1)}, u32[]{:S(2)}, u32[]{:S(2)}) %collective-permute-start.10) | collective-permute-done | bytes 32800 | tf_op jit(solution)/shard_map/ppermute | solution.py:232
  54.3 2.2 %collective-permute-done.9 = f32[1,32,256]{2,1,0:T(8,128)S(1)} collective-permute-done((f32[1,32,256]{2,1,0:T(8,128)S(1)}, f32[1,32,256]{2,1,0:T(8,128)S(1)}, u32[]{:S(2)}, u32[]{:S(2)}) %collective-permute-start.9) | collective-permute-done | bytes 32800 | tf_op jit(solution)/shard_map/ppermute | solution.py:232
  56.5 0.6 %fusion.6 = f32[1,32,256]{2,1,0:T(8,128)} fusion(f32[1,32,256]{2,1,0:T(8,128)S(1)} %collective-permute-done.9, f32[4,32,256]{2,1,0:T(8,128)S(1)} %collective-permute-done.8, f32[4,32,256]{2,1,0:T(8,128)S(1)} %collective-permute-done.7, f32[4,32,256]{2,1,0:T(8,128)S(1)} %collective-permute-done.6, f32[4,32,256]{2,1,0:T(8,128)S(1)} %get-tuple-element.21, ...), kind=kLoop, calls=%fused_computation.17 | loop fusion | flops 57344 | bytes 262144 | tf_op jit(solution)/shard_map/mul | solution.py:233
  (1 shorter events, 0.0 us)
Async XLA Ops:
  0.0 22.5 %copy-start.1 = (bf16[2,2,64,128]{3,2,1,0:T(8,128)(2,1)S(1)}, bf16[2,2,64,128]{3,2,1,0:T(8,128)(2,1)}, u32[]{:S(2)}) copy-start(bf16[2,2,64,128]{3,2,1,0:T(8,128)(2,1)} %constant.29.clone.edge_ref) | copy-start | bytes 196612
  0.0 22.5 %copy-start = (bf16[4,2,96,256]{3,2,1,0:T(8,128)(2,1)S(1)}, bf16[4,2,96,256]{3,2,1,0:T(8,128)(2,1)}, u32[]{:S(2)}) copy-start(bf16[4,2,96,256]{3,2,1,0:T(8,128)(2,1)} %constant.27.clone.left_ref) | copy-start | bytes 1179652
  3.0 17.7 %collective-permute-start = (f32[32,16,256]{2,1,0:T(8,128)S(1)}, f32[32,16,256]{2,1,0:T(8,128)S(1)}, u32[]{:S(2)}, u32[]{:S(2)}) collective-permute-start(f32[32,16,256]{2,1,0:T(8,128)S(1)} %get-tuple-element.14.bottom_ref), channel_id=1, source_target_pairs={{0,2},{2,4},{4,6},{1,3},{3,5},{5,7},{8,10},{10,12},{12,14},{9,11},... | collective-permute-start | bytes 1572872 | tf_op jit(solution)/shard_map/ppermute | solution.py:216
  6.5 16.0 %collective-permute-start.1 = (f32[32,16,256]{2,1,0:T(8,128)S(1)}, f32[32,16,256]{2,1,0:T(8,128)S(1)}, u32[]{:S(2)}, u32[]{:S(2)}) collective-permute-start(f32[32,16,256]{2,1,0:T(8,128)S(1)} %get-tuple-element.15.top_ref), channel_id=1, source_target_pairs={{2,0},{4,2},{6,4},{3,1},{5,3},{7,5},{10,8},{12,10},{14,12},{11,9},... | collective-permute-start | bytes 1572872 | tf_op jit(solution)/shard_map/ppermute | solution.py:217
  8.9 11.8 %collective-permute-start.3 = (f32[4,32,128]{2,1,0:T(8,128)S(1)}, f32[4,32,128]{2,1,0:T(8,128)S(1)}, u32[]{:S(2)}, u32[]{:S(2)}) collective-permute-start(f32[4,32,128]{2,1,0:T(8,128)S(1)} %get-tuple-element.17), channel_id=1, source_target_pairs={{0,1},{1,0},{2,3},{3,2},{4,5},{5,4},{6,7},{7,6},{8,9},{9,8},{10,11... | collective-permute-start | bytes 196616 | tf_op jit(solution)/shard_map/ppermute | solution.py:213
  10.9 6.8 %collective-permute-start.2 = (f32[4,16,128]{2,1,0:T(8,128)S(1)}, f32[4,16,128]{2,1,0:T(8,128)S(1)}, u32[]{:S(2)}, u32[]{:S(2)}) collective-permute-start(f32[4,16,128]{2,1,0:T(8,128)S(1)} %get-tuple-element.16), channel_id=1, source_target_pairs={{0,3},{1,2},{2,5},{3,4},{4,7},{5,6},{8,11},{9,10},{10,13},{11,12},... | collective-permute-start | bytes 98312 | tf_op jit(solution)/shard_map/ppermute | solution.py:214
  13.9 6.8 %collective-permute-start.4 = (f32[4,16,128]{2,1,0:T(8,128)S(1)}, f32[4,16,128]{2,1,0:T(8,128)S(1)}, u32[]{:S(2)}, u32[]{:S(2)}) collective-permute-start(f32[4,16,128]{2,1,0:T(8,128)S(1)} %get-tuple-element.18), channel_id=1, source_target_pairs={{2,1},{3,0},{4,3},{5,2},{6,5},{7,4},{10,9},{11,8},{12,11},{13,10},... | collective-permute-start | bytes 98312 | tf_op jit(solution)/shard_map/ppermute | solution.py:215
  27.7 2.0 %collective-permute-start.5 = (f32[16,32,256]{2,1,0:T(8,128)S(1)}, f32[16,32,256]{2,1,0:T(8,128)S(1)}, u32[]{:S(2)}, u32[]{:S(2)}) collective-permute-start(f32[16,32,256]{2,1,0:T(8,128)S(1)} %get-tuple-element.20), channel_id=1, source_target_pairs={{0,8},{8,0},{1,9},{9,1},{2,10},{10,2},{3,11},{11,3},{4,12},{12,4},... | collective-permute-start | bytes 1572872 | tf_op jit(solution)/shard_map/ppermute | solution.py:227
  29.8 5.9 %collective-permute-start.8 = (f32[4,32,256]{2,1,0:T(8,128)S(1)}, f32[4,32,256]{2,1,0:T(8,128)S(1)}, u32[]{:S(2)}, u32[]{:S(2)}) collective-permute-start(f32[4,32,256]{2,1,0:T(8,128)S(1)} %get-tuple-element.22), channel_id=1, source_target_pairs={{0,192},{64,0},{128,64},{192,128},{1,193},{65,1},{129,65},{193,129... | collective-permute-start | bytes 393224 | tf_op jit(solution)/shard_map/ppermute | solution.py:230
  32.6 9.3 %collective-permute-start.7 = (f32[4,32,256]{2,1,0:T(8,128)S(1)}, f32[4,32,256]{2,1,0:T(8,128)S(1)}, u32[]{:S(2)}, u32[]{:S(2)}) collective-permute-start(f32[4,32,256]{2,1,0:T(8,128)S(1)} %get-tuple-element.23), channel_id=1, source_target_pairs={{0,64},{64,128},{128,192},{192,0},{1,65},{65,129},{129,193},{193,1... | collective-permute-start | bytes 393224 | tf_op jit(solution)/shard_map/ppermute | solution.py:230
  32.6 9.3 %collective-permute-start.6 = (f32[4,32,256]{2,1,0:T(8,128)S(1)}, f32[4,32,256]{2,1,0:T(8,128)S(1)}, u32[]{:S(2)}, u32[]{:S(2)}) collective-permute-start(f32[4,32,256]{2,1,0:T(8,128)S(1)} %get-tuple-element.24), channel_id=1, source_target_pairs={{0,128},{64,192},{128,0},{192,64},{1,129},{65,193},{129,1},{193,65... | collective-permute-start | bytes 393224 | tf_op jit(solution)/shard_map/ppermute | solution.py:230
  41.9 10.2 %collective-permute-start.11 = (f32[1,32,256]{2,1,0:T(8,128)S(1)}, f32[1,32,256]{2,1,0:T(8,128)S(1)}, u32[]{:S(2)}, u32[]{:S(2)}) collective-permute-start(f32[1,32,256]{2,1,0:T(8,128)S(1)} %get-tuple-element.25), channel_id=1, source_target_pairs={{0,48},{16,0},{32,16},{48,32},{1,49},{17,1},{33,17},{49,33},{2,50}... | collective-permute-start | bytes 98312 | tf_op jit(solution)/shard_map/ppermute | solution.py:232
  48.3 6.0 %collective-permute-start.10 = (f32[1,32,256]{2,1,0:T(8,128)S(1)}, f32[1,32,256]{2,1,0:T(8,128)S(1)}, u32[]{:S(2)}, u32[]{:S(2)}) collective-permute-start(f32[1,32,256]{2,1,0:T(8,128)S(1)} %get-tuple-element.26), channel_id=1, source_target_pairs={{0,16},{16,32},{32,48},{48,0},{1,17},{17,33},{33,49},{49,1},{2,18}... | collective-permute-start | bytes 98312 | tf_op jit(solution)/shard_map/ppermute | solution.py:232
  48.3 8.2 %collective-permute-start.9 = (f32[1,32,256]{2,1,0:T(8,128)S(1)}, f32[1,32,256]{2,1,0:T(8,128)S(1)}, u32[]{:S(2)}, u32[]{:S(2)}) collective-permute-start(f32[1,32,256]{2,1,0:T(8,128)S(1)} %get-tuple-element.27), channel_id=1, source_target_pairs={{0,32},{16,48},{32,0},{48,16},{1,33},{17,49},{33,1},{49,17},{2,34}... | collective-permute-start | bytes 98312 | tf_op jit(solution)/shard_map/ppermute | solution.py:232

commit v3 on v2

--- a/solution.py
+++ b/solution.py
@@ -74,74 +74,104 @@
     return dot(lh, rh) + (dot(lh, rl) + dot(ll, rh))
 
 
-def product_kernel(where, p_hbm, c_hbm, top_ref, bottom_ref, edge_ref, edge_top_ref, edge_bottom_ref, p_ref, c_ref, sems):
-    gy = where[2]
+def load_half(p_hbm, c_hbm, p_ref, c_ref, sems, half):
     copies = []
-    for g in range(8):
-        at = pl.ds(4 * g, 4)
-        copies.append(pltpu.make_async_copy(p_hbm.at[0, at], p_ref.at[at], sems.at[0, g]))
-        copies.append(pltpu.make_async_copy(c_hbm.at[at], c_ref.at[at], sems.at[1, g]))
+    lanes = pl.ds(pl.multiple_of(128 * half, 128), 128)
+    for g in range(4):
+        at = pl.ds(8 * g, 8)
+        copies.append(pltpu.make_async_copy(p_hbm.at[0, at, :, lanes], p_ref.at[at], sems.at[0, g]))
+        copies.append(pltpu.make_async_copy(c_hbm.at[at, :, lanes], c_ref.at[at], sems.at[1, g]))
     for copy in copies:
         copy.start()
+    return copies
+
+
+def edge_kernel(where, p_hbm, c_hbm, v_ref, edge_ref, p_ref, c_ref, sems):
+    gy = where[2]
+    copies = load_half(p_hbm, c_hbm, p_ref, c_ref, sems, 1 - gy)
     lane = lax.broadcasted_iota(jnp.int32, (1, 1, 128), 2)
     edges = jnp.zeros((4, 32, 128), F32)
     for g in range(8):
-        copies[2 * g].wait()
-        copies[2 * g + 1].wait()
-        v = p_ref[4 * g : 4 * g + 4] * c_ref[4 * g : 4 * g + 4]
-        top_ref[4 * g : 4 * g + 4] = v[:, :HALO]
-        bottom_ref[4 * g : 4 * g + 4] = v[:, HALO:]
-        last = v[:, :, 128:].reshape(128, 128)
-        first = v[:, :, :128].reshape(128, 128)
-        edge = jnp.where(gy == 0, pltpu.roll(last, 16, 1), first)
+        if g % 2 == 0:
+            copies[g].wait()
+            copies[g + 1].wait()
+        at = slice(4 * g, 4 * g + 4)
+        v = p_ref[at] * c_ref[at]
+        v_ref[at] = v
+        v = v.reshape(128, 128)
+        v = jnp.where(gy == 0, pltpu.roll(v, 16, 1), v)
         if g:
-            edge = pltpu.roll(edge, 16 * g, 1)
-        edges = jnp.where(lane // 16 == g, edge.reshape(4, 32, 128), edges)
-    edge_ref[...] = edges
-    edge_top_ref[...] = edges[:, :HALO]
-    edge_bottom_ref[...] = edges[:, HALO:]
-
-
-def filter_kernel(
-    where, p_ref, above_ref, top_ref, bottom_ref, below_ref,
-    side_above_ref, side_ref, side_below_ref, left_ref, edge_ref, right_hbm, keep_ref, send_ref,
-    xh_ref, xl_ref, fh_ref, fl_ref, ch_ref, cl_ref, alpha_ref, pairs_ref, near_ref, right_ref, sems,
+            v = pltpu.roll(v, 16 * g, 1)
+        edges = jnp.where(lane // 16 == g, v.reshape(4, 32, 128), edges)
+    for f in range(4):
+        edge_ref[f // 2, :, 128 * (f % 2) : 128 * (f % 2) + 128] = edges[f]
+
+
+def product_kernel(where, p_hbm, c_hbm, near_ref, top_ref, bottom_ref, p_ref, c_ref, sems):
+    gy = where[2]
+    copies = load_half(p_hbm, c_hbm, p_ref, c_ref, sems, gy)
+    for g in range(8):
+        if g % 2 == 0:
+            copies[g].wait()
+            copies[g + 1].wait()
+        at = slice(4 * g, 4 * g + 4)
+        far, near = p_ref[at] * c_ref[at], near_ref[at]
+        v = jnp.concatenate([jnp.where(gy == 0, far, near), jnp.where(gy == 0, near, far)], axis=2)
+        top_ref[at] = v[:, :HALO]
+        bottom_ref[at] = v[:, HALO:]
+
+
+def table_kernel(
+    where, left_ref, edge_ref, right_hbm, p_hbm, xh_ref, xl_ref, eh_ref, el_ref, right_ref, p_ref, sems
 ):
-    core, gx, gy = where[0], where[1], where[2]
+    gx, gy = where[1], where[2]
     copies = []
     for h in range(2):
         for k in range(4):
             at = pl.ds(256 * k, 256)
             copies.append(pltpu.make_async_copy(right_hbm.at[gy, h, at], right_ref.at[h, at], sems.at[h, k]))
+            at = pl.ds(16 * h + 4 * k, 4)
+            copies.append(pltpu.make_async_copy(p_hbm.at[0, at], p_ref.at[at], sems.at[2 + h, k]))
     for copy in copies:
         copy.start()
     lane = lax.broadcasted_iota(jnp.int32, (1, 256), 1)
-    row, start = 0, 0
-    for count in (32, 32, 16, 16):
-        for f in range(4):
-            mine = (lane // 16) % 4 == f
-            rows, at = slice(start, start + count), slice(row, row + count)
-            zero = jnp.zeros((count, 256), F32)
-            xh_ref[at] = jnp.where(mine, left_ref[gx, 0, rows].astype(F32), zero).astype(BF16)
-            xl_ref[at] = jnp.where(mine, left_ref[gx, 1, rows].astype(F32), zero).astype(BF16)
-            row += count
-        start += count
+    narrow = lax.broadcasted_iota(jnp.int32, (1, 128), 1)
+    for h, x_ref, e_ref in ((0, xh_ref, eh_ref), (1, xl_ref, el_ref)):
+        row, start = 0, 0
+        for count in (32, 32, 16, 16):
+            rows = left_ref[gx, h, start : start + count].astype(F32)
+            for f in range(4):
+                mine = (lane // 16) % 4 == f
+                x_ref[row : row + count] = jnp.where(mine, rows, jnp.zeros_like(rows)).astype(BF16)
+                row += count
+            start += count
+        for t in range(4):
+            rows = edge_ref[gy, h, 16 * t : 16 * t + 16].astype(F32)
+            for g in range(8):
+                at = 128 * t + 16 * g
+                e_ref[at : at + 16] = jnp.where(narrow // 16 == g, rows, jnp.zeros_like(rows)).astype(BF16)
+    for copy in copies:
+        copy.wait()
+
+
+def filter_kernel(
+    where, p_ref, above_ref, top_ref, bottom_ref, below_ref, side_ref,
+    xh_ref, xl_ref, eh_ref, el_ref, right_ref, keep_ref, send_ref,
+    fh_ref, fl_ref, ch_ref, cl_ref, alpha_ref, pairs_ref, near_ref,
+):
+    core, gy = where[0], where[2]
 
     def by_rows(parts):
         return dot3((xh_ref[...], xl_ref[...]), split(jnp.concatenate(parts)))
 
-    sides = (side_above_ref[...], side_ref[:, :HALO], side_ref[:, HALO:], side_below_ref[...])
-    side = by_rows([s.reshape(64, 128) for s in sides])
+    sides = (above_ref[32:], side_ref[:, :HALO], side_ref[:, HALO:], below_ref[32:])
+    lanes = (slice(0, 128), slice(128, 256))
+    side = by_rows([s[f // 2, :, lanes[f % 2]] for s in sides for f in range(4)])
     fine = split(jnp.concatenate([side[:128], side[128:256]], axis=1))
     pair = split(jnp.concatenate([side[256:320], side[320:]], axis=1))
     narrow = lax.broadcasted_iota(jnp.int32, (1, 128), 1)
-
-    def edge(h, t):
-        rows = edge_ref[gy, h, 16 * t : 16 * t + 16].astype(F32)
-        return [jnp.where(narrow // 16 == g, rows, jnp.zeros_like(rows)).astype(BF16) for g in range(8)]
-
-    near = dot3(fine, [jnp.concatenate(edge(h, 0) + edge(h, 1)) for h in range(2)])
-    near_pairs = dot3(pair, [jnp.concatenate(edge(h, 2) + edge(h, 3)) for h in range(2)])
+    near = dot3(fine, (eh_ref[:256], el_ref[:256]))
+    near_pairs = dot3(pair, (eh_ref[256:], el_ref[256:]))
     near_ref[pl.ds(0, 64, stride=2), :] = near_pairs
     near_ref[pl.ds(1, 64, stride=2), :] = near_pairs
     near = near + near_ref[...]
@@ -157,8 +187,6 @@
             at = slice(64 * g, 64 * g + 64)
             ch_ref[at, lanes], cl_ref[at, lanes] = split(u[256 + 64 * t : 320 + 64 * t])
 
-    for copy in copies:
-        copy.wait()
     alpha_ref[...] = dot3((fh_ref[...], fl_ref[...]), (right_ref[0, :512], right_ref[1, :512]))
     pairs = dot3((ch_ref[...], cl_ref[...]), (right_ref[0, 512:], right_ref[1, 512:]))
     for h in range(2):
@@ -186,7 +214,7 @@
     ]
     return pl.pallas_call(
         kernel,
-        out_shape=[jax.ShapeDtypeStruct(s, F32) for s in outs],
+        out_shape=[o if isinstance(o, jax.ShapeDtypeStruct) else jax.ShapeDtypeStruct(o, F32) for o in outs],
         in_specs=specs,
         out_specs=[VMEM] * len(outs),
         scratch_shapes=scratch,
@@ -202,30 +230,33 @@
     right, edge = (jnp.asarray(halves(t)) for t in right_tables(512, 2))
     vmem, sems = pltpu.VMEM, pltpu.SemaphoreType.DMA
 
-    top, bottom, edges, edge_top, edge_bottom, near_p = call(
-        product_kernel, [(32, 16, 256)] * 2 + [(4, 32, 128)] + [(4, 16, 128)] * 2 + [(32, 32, 256)],
-        where, perturbations, control, hbm=(1, 2), scratch=[vmem((32, 32, 256), F32), sems((2, 8))],
-    )
-    down = [(i, i + 1) for i in range(3)]
-    up = [(i + 1, i) for i in range(3)]
-    cross = lambda pairs: [(2 * a + s, 2 * b + 1 - s) for a, b in pairs for s in range(2)]
-
+    half = [vmem((32, 32, 128), F32)] * 2 + [sems((2, 4))]
+    near, edges = call(
+        edge_kernel, [(32, 32, 128), (2, 32, 256)], where, perturbations, control, hbm=(1, 2), scratch=half
+    )
+
+    ring = lambda d: [(i, (i + d) % 4) for i in range(4)]
     side = lax.ppermute(edges, "gy", [(0, 1), (1, 0)])
-    side_above = lax.ppermute(edge_bottom, ("gx", "gy"), cross(down))
-    side_below = lax.ppermute(edge_top, ("gx", "gy"), cross(up))
-    above = lax.ppermute(bottom, "gx", down)
-    below = lax.ppermute(top, "gx", up)
-
+    top, bottom = call(
+        product_kernel, [(34, 16, 256)] * 2, where, perturbations, control, near, hbm=(1, 2), scratch=half
+    )
+    top = top.at[32:].set(side[:, :HALO])
+    bottom = bottom.at[32:].set(side[:, HALO:])
+    above = lax.ppermute(bottom, "gx", ring(1))
+    below = lax.ppermute(top, "gx", ring(3))
+    *tables, near_p = call(
+        table_kernel,
+        [jax.ShapeDtypeStruct(s, BF16) for s in [(384, 256)] * 2 + [(512, 128)] * 2 + [(2, 1024, 256)]]
+        + [(32, 32, 256)],
+        where, left, edge, right, perturbations, hbm=(3, 4), scratch=[sems((4, 4))],
+    )
     keep, give = call(
-        filter_kernel, [(16, 32, 256)] * 2, where, near_p, above, top, bottom, below,
-        side_above, side, side_below, left, edge, right, hbm=(11,),
-        scratch=[vmem((384, 256), BF16)] * 2 + [vmem((1024, 512), BF16)] * 2 + [vmem((512, 512), BF16)] * 2
-        + [vmem((1024, 256), F32), vmem((2, 1024, 128), F32), vmem((128, 128), F32)]
-        + [vmem((2, 1024, 256), BF16), sems((2, 4))],
+        filter_kernel, [(16, 32, 256)] * 2, where, near_p, above, top, bottom, below, side, *tables,
+        scratch=[vmem((1024, 512), BF16)] * 2 + [vmem((512, 512), BF16)] * 2
+        + [vmem((1024, 256), F32), vmem((2, 1024, 128), F32), vmem((128, 128), F32)],
         cost=4 * 10**9, grant=24,
     )
     got = lax.ppermute(give, "core", [(0, 1), (1, 0)])
-    ring = lambda d: [(i, (i + d) % 4) for i in range(4)]
     piece = [keep[4 * d : 4 * d + 4] + got[4 * d : 4 * d + 4] for d in range(4)]
     x2, x1, x3 = (lax.ppermute(piece[d], "x", ring(d)) for d in (2, 1, 3))
     cell = [(piece[0][e : e + 1] + x2[e : e + 1]) + (x1[e : e + 1] + x3[e : e + 1]) for e in range(4)]

time: 57.3 us -> 56 us (0.977)
  the two profiles are of different devices: /device:TPU:8 before, /device:TPU:32 now
where the time goes in v3:
time: 56 us; the launch traced here: 55.9 us
  waiting for transfers between devices  25.3 us (45%)
  starting transfers between devices  19.4 us (35%)
  Pallas kernels  10.3 us (18%)
  other arithmetic  0.73 us (1%)
    pallas_call x4, Pallas kernels, call(): pl.pallas_call(kernel, out_shape=[o if isinstance(o, jax.ShapeDtypeStruct...  10.3 us
    ppermute x3, starting transfers between devices, body(): z2, z1, z3 = (lax.ppermute(cell[e], 'z', ring(e)) for e in (2, 1, 3))  9.29 us
    ppermute x1, waiting for transfers between devices, body(): below = lax.ppermute(top, 'gx', ring(3))  8.43 us
    ppermute x3, waiting for transfers between devices, body(): x2, x1, x3 = (lax.ppermute(piece[d], 'x', ring(d)) for d in (2, 1, 3))  6.99 us
    ppermute x3, starting transfers between devices, body(): x2, x1, x3 = (lax.ppermute(piece[d], 'x', ring(d)) for d in (2, 1, 3))  5.13 us
    ppermute x3, waiting for transfers between devices, body(): z2, z1, z3 = (lax.ppermute(cell[e], 'z', ring(e)) for e in (2, 1, 3))  4.01 us
    ppermute x1, waiting for transfers between devices, body(): above = lax.ppermute(bottom, 'gx', ring(1))  3.41 us
    ppermute x1, starting transfers between devices, body(): below = lax.ppermute(top, 'gx', ring(3))  3.01 us
  transfers between devices with their start and end apart: 10, of which 8 were waited for; matrix products, arithmetic and copies ran while one was open for 0% of the time, Pallas kernels for 8%

profile of v3, /device:TPU:32, one launch (start us, length us, event | category | flops | bytes accessed | tf_op | source)
XLA Modules:
  0.0 55.9 jit_solution(7200333864961917729)
XLA Ops:
  0.0 0.1 stack.23.where
  0.1 0.0 copy-start
  0.1 0.0 copy-start.1
  0.1 2.3 %shard_map.56 = (f32[32,32,128]{2,1,0:T(8,128)S(1)}, f32[2,32,256]{2,1,0:T(8,128)S(1)}) custom-call(s32[5]{0:T(128)S(1)} %stack.23.where, f32[1,32,32,256]{3,2,1,0:T(8,128)} %p_hbm.5, f32[32,32,256]{2,1,0:T(8,128)} %c_hbm.3), custom_call_target="tpu_custom_call" | custom-call | bytes 1048576 | tf_op jit(solution)/shard_map/pallas_call | solution.py:215
  2.4 1.9 %collective-permute-start = (f32[2,32,256]{2,1,0:T(8,128)S(1)}, f32[2,32,256]{2,1,0:T(8,128)S(1)}, u32[]{:S(2)}, u32[]{:S(2)}) collective-permute-start(f32[2,32,256]{2,1,0:T(8,128)S(1)} %get-tuple-element.44), channel_id=1, source_target_pairs={{0,1},{1,0},{2,3},{3,2},{4,5},{5,4},{6,7},{7,6},{8,9},{9,8},{10,11... | collective-permute-start | bytes 196616 | tf_op jit(solution)/shard_map/ppermute | solution.py:239
  4.3 1.9 %shard_map.57 = (f32[34,16,256]{2,1,0:T(8,128)S(1)}, f32[34,16,256]{2,1,0:T(8,128)S(1)}) custom-call(s32[5]{0:T(128)S(1)} %stack.23.where, f32[1,32,32,256]{3,2,1,0:T(8,128)} %p_hbm.5, f32[32,32,256]{2,1,0:T(8,128)} %c_hbm.3, f32[32,32,128]{2,1,0:T(8,128)S(1)} %get-tuple-element.42.near_ref), custom_call_target="tpu_custom_call" | custom-call | bytes 1048576 | tf_op jit(solution)/shard_map/pallas_call | solution.py:215
  6.2 0.5 collective-permute-done.side_ref
  6.7 3.0 %collective-permute-start.2 = (f32[34,16,256]{2,1,0:T(8,128)S(1)}, f32[34,16,256]{2,1,0:T(8,128)S(1)}, u32[]{:S(2)}, u32[]{:S(2)}) collective-permute-start(f32[34,16,256]{2,1,0:T(8,128)S(1)} %get-tuple-element.60.top_ref), channel_id=1, source_target_pairs={{0,6},{2,0},{4,2},{6,4},{1,7},{3,1},{5,3},{7,5},{8,14},{10,8},{12,... | collective-permute-start | bytes 1671176 | tf_op jit(solution)/shard_map/ppermute | solution.py:246
  9.7 0.0 collective-permute-start.1
  9.7 0.0 copy-done
  9.7 0.0 copy-done.1
  9.7 2.3 %shard_map.55 = (bf16[384,256]{1,0:T(8,128)(2,1)S(1)}, bf16[384,256]{1,0:T(8,128)(2,1)S(1)}, bf16[512,128]{1,0:T(8,128)(2,1)S(1)}, bf16[512,128]{1,0:T(8,128)(2,...) custom-call(s32[5]{0:T(128)S(1)} %stack.23.where, bf16[4,2,96,256]{3,2,1,0:T(8,128)(2,1)S(1)} %copy-done, ...), custom_call_target="tpu_custom_call" | custom-call | bytes 1048576 | tf_op jit(solution)/shard_map/pallas_call | solution.py:215
  12.0 8.4 %collective-permute-done.2.below_ref = f32[34,16,256]{2,1,0:T(8,128)S(1)} collective-permute-done((f32[34,16,256]{2,1,0:T(8,128)S(1)}, f32[34,16,256]{2,1,0:T(8,128)S(1)}, u32[]{:S(2)}, u32[]{:S(2)}) %collective-permute-start.2) | collective-permute-done | bytes 557088 | tf_op jit(solution)/shard_map/ppermute | solution.py:246
  20.5 3.4 %collective-permute-done.1.above_ref = f32[34,16,256]{2,1,0:T(8,128)S(1)} collective-permute-done((f32[34,16,256]{2,1,0:T(8,128)S(1)}, f32[34,16,256]{2,1,0:T(8,128)S(1)}, u32[]{:S(2)}, u32[]{:S(2)}) %collective-permute-start.1) | collective-permute-done | bytes 557088 | tf_op jit(solution)/shard_map/ppermute | solution.py:245
  23.9 3.8 %shard_map.58 = (f32[16,32,256]{2,1,0:T(8,128)S(1)}, f32[16,32,256]{2,1,0:T(8,128)S(1)}) custom-call(s32[5]{0:T(128)S(1)} %stack.23.where, f32[32,32,256]{2,1,0:T(8,128)S(1)} %get-tuple-element.41.p_ref, f32[34,16,256]{2,1,0:T(8,128)S(1)} %collective-permute-done.1.above_ref, f32[34,16,256]{2,1,0:T(8,128)S(1)} %get-tuple-element.60.top_ref, ...), custom_call_target="tpu_custom_call" | custom-call | flops 4000000000 | bytes 1048576 | tf_op jit(solution)/shard_map/pallas_call | solution.py:215
  27.7 0.1 collective-permute-start.3
  27.8 1.9 %collective-permute-done.3 = f32[16,32,256]{2,1,0:T(8,128)S(1)} collective-permute-done((f32[16,32,256]{2,1,0:T(8,128)S(1)}, f32[16,32,256]{2,1,0:T(8,128)S(1)}, u32[]{:S(2)}, u32[]{:S(2)}) %collective-permute-start.3) | collective-permute-done | bytes 524320 | tf_op jit(solution)/shard_map/ppermute | solution.py:259
  29.7 0.1 slice_add_fusion.3
  29.8 2.8 %collective-permute-start.6 = (f32[4,32,256]{2,1,0:T(8,128)S(1)}, f32[4,32,256]{2,1,0:T(8,128)S(1)}, u32[]{:S(2)}, u32[]{:S(2)}) collective-permute-start(f32[4,32,256]{2,1,0:T(8,128)S(1)} %get-tuple-element.54), channel_id=1, source_target_pairs={{0,192},{64,0},{128,64},{192,128},{1,193},{65,1},{129,65},{193,129... | collective-permute-start | bytes 393224 | tf_op jit(solution)/shard_map/ppermute | solution.py:261
  32.6 0.0 collective-permute-start.5
  32.6 2.3 %collective-permute-start.4 = (f32[4,32,256]{2,1,0:T(8,128)S(1)}, f32[4,32,256]{2,1,0:T(8,128)S(1)}, u32[]{:S(2)}, u32[]{:S(2)}) collective-permute-start(f32[4,32,256]{2,1,0:T(8,128)S(1)} %get-tuple-element.56), channel_id=1, source_target_pairs={{0,128},{64,192},{128,0},{192,64},{1,129},{65,193},{129,1},{193,65... | collective-permute-start | bytes 393224 | tf_op jit(solution)/shard_map/ppermute | solution.py:261
  34.9 0.8 %collective-permute-done.6 = f32[4,32,256]{2,1,0:T(8,128)S(1)} collective-permute-done((f32[4,32,256]{2,1,0:T(8,128)S(1)}, f32[4,32,256]{2,1,0:T(8,128)S(1)}, u32[]{:S(2)}, u32[]{:S(2)}) %collective-permute-start.6) | collective-permute-done | bytes 131104 | tf_op jit(solution)/shard_map/ppermute | solution.py:261
  35.7 6.2 %collective-permute-done.5 = f32[4,32,256]{2,1,0:T(8,128)S(1)} collective-permute-done((f32[4,32,256]{2,1,0:T(8,128)S(1)}, f32[4,32,256]{2,1,0:T(8,128)S(1)}, u32[]{:S(2)}, u32[]{:S(2)}) %collective-permute-start.5) | collective-permute-done | bytes 131104 | tf_op jit(solution)/shard_map/ppermute | solution.py:261
  41.9 0.0 collective-permute-done.4
  42.0 5.5 %collective-permute-start.9 = (f32[1,32,256]{2,1,0:T(8,128)S(1)}, f32[1,32,256]{2,1,0:T(8,128)S(1)}, u32[]{:S(2)}, u32[]{:S(2)}) collective-permute-start(f32[1,32,256]{2,1,0:T(8,128)S(1)} %get-tuple-element.57), channel_id=1, source_target_pairs={{0,48},{16,0},{32,16},{48,32},{1,49},{17,1},{33,17},{49,33},{2,50}... | collective-permute-start | bytes 98312 | tf_op jit(solution)/shard_map/ppermute | solution.py:263
  47.4 0.0 collective-permute-start.8
  47.4 3.8 %collective-permute-start.7 = (f32[1,32,256]{2,1,0:T(8,128)S(1)}, f32[1,32,256]{2,1,0:T(8,128)S(1)}, u32[]{:S(2)}, u32[]{:S(2)}) collective-permute-start(f32[1,32,256]{2,1,0:T(8,128)S(1)} %get-tuple-element.59), channel_id=1, source_target_pairs={{0,32},{16,48},{32,0},{48,16},{1,33},{17,49},{33,1},{49,17},{2,34}... | collective-permute-start | bytes 98312 | tf_op jit(solution)/shard_map/ppermute | solution.py:263
  51.2 0.0 collective-permute-done.9
  51.2 2.2 %collective-permute-done.8 = f32[1,32,256]{2,1,0:T(8,128)S(1)} collective-permute-done((f32[1,32,256]{2,1,0:T(8,128)S(1)}, f32[1,32,256]{2,1,0:T(8,128)S(1)}, u32[]{:S(2)}, u32[]{:S(2)}) %collective-permute-start.8) | collective-permute-done | bytes 32800 | tf_op jit(solution)/shard_map/ppermute | solution.py:263
  53.5 1.8 %collective-permute-done.7 = f32[1,32,256]{2,1,0:T(8,128)S(1)} collective-permute-done((f32[1,32,256]{2,1,0:T(8,128)S(1)}, f32[1,32,256]{2,1,0:T(8,128)S(1)}, u32[]{:S(2)}, u32[]{:S(2)}) %collective-permute-start.7) | collective-permute-done | bytes 32800 | tf_op jit(solution)/shard_map/ppermute | solution.py:263
  55.3 0.6 %fusion.6 = f32[1,32,256]{2,1,0:T(8,128)} fusion(f32[1,32,256]{2,1,0:T(8,128)S(1)} %collective-permute-done.7, f32[4,32,256]{2,1,0:T(8,128)S(1)} %collective-permute-done.6, f32[4,32,256]{2,1,0:T(8,128)S(1)} %collective-permute-done.5, f32[4,32,256]{2,1,0:T(8,128)S(1)} %collective-permute-done.4, f32[4,32,256]{2,1,0:T(8,128)S(1)} %get-tuple-element.53, ...), kind=kLoop, calls=%fused_computation.17 | loop fusion | flops 57344 | bytes 262144 | tf_op jit(solution)/shard_map/mul | solution.py:264
  (2 shorter events, 0.0 us)
Async XLA Ops:
  0.1 9.7 %copy-start = (bf16[4,2,96,256]{3,2,1,0:T(8,128)(2,1)S(1)}, bf16[4,2,96,256]{3,2,1,0:T(8,128)(2,1)}, u32[]{:S(2)}) copy-start(bf16[4,2,96,256]{3,2,1,0:T(8,128)(2,1)} %constant.76.clone.left_ref) | copy-start | bytes 1179652
  0.1 9.7 %copy-start.1 = (bf16[2,2,64,128]{3,2,1,0:T(8,128)(2,1)S(1)}, bf16[2,2,64,128]{3,2,1,0:T(8,128)(2,1)}, u32[]{:S(2)}) copy-start(bf16[2,2,64,128]{3,2,1,0:T(8,128)(2,1)} %constant.78.clone.edge_ref) | copy-start | bytes 196612
  2.4 4.4 %collective-permute-start = (f32[2,32,256]{2,1,0:T(8,128)S(1)}, f32[2,32,256]{2,1,0:T(8,128)S(1)}, u32[]{:S(2)}, u32[]{:S(2)}) collective-permute-start(f32[2,32,256]{2,1,0:T(8,128)S(1)} %get-tuple-element.44), channel_id=1, source_target_pairs={{0,1},{1,0},{2,3},{3,2},{4,5},{5,4},{6,7},{7,6},{8,9},{9,8},{10,11... | collective-permute-start | bytes 196616 | tf_op jit(solution)/shard_map/ppermute | solution.py:239
  6.7 13.7 %collective-permute-start.2 = (f32[34,16,256]{2,1,0:T(8,128)S(1)}, f32[34,16,256]{2,1,0:T(8,128)S(1)}, u32[]{:S(2)}, u32[]{:S(2)}) collective-permute-start(f32[34,16,256]{2,1,0:T(8,128)S(1)} %get-tuple-element.60.top_ref), channel_id=1, source_target_pairs={{0,6},{2,0},{4,2},{6,4},{1,7},{3,1},{5,3},{7,5},{8,14},{10,8},{12,... | collective-permute-start | bytes 1671176 | tf_op jit(solution)/shard_map/ppermute | solution.py:246
  9.7 14.1 %collective-permute-start.1 = (f32[34,16,256]{2,1,0:T(8,128)S(1)}, f32[34,16,256]{2,1,0:T(8,128)S(1)}, u32[]{:S(2)}, u32[]{:S(2)}) collective-permute-start(f32[34,16,256]{2,1,0:T(8,128)S(1)} %get-tuple-element.61.bottom_ref), channel_id=1, source_target_pairs={{0,2},{2,4},{4,6},{6,0},{1,3},{3,5},{5,7},{7,1},{8,10},{10,12},{12... | collective-permute-start | bytes 1671176 | tf_op jit(solution)/shard_map/ppermute | solution.py:245
  27.7 2.0 %collective-permute-start.3 = (f32[16,32,256]{2,1,0:T(8,128)S(1)}, f32[16,32,256]{2,1,0:T(8,128)S(1)}, u32[]{:S(2)}, u32[]{:S(2)}) collective-permute-start(f32[16,32,256]{2,1,0:T(8,128)S(1)} %get-tuple-element.52), channel_id=1, source_target_pairs={{0,8},{8,0},{1,9},{9,1},{2,10},{10,2},{3,11},{11,3},{4,12},{12,4},... | collective-permute-start | bytes 1572872 | tf_op jit(solution)/shard_map/ppermute | solution.py:259
  29.8 5.9 %collective-permute-start.6 = (f32[4,32,256]{2,1,0:T(8,128)S(1)}, f32[4,32,256]{2,1,0:T(8,128)S(1)}, u32[]{:S(2)}, u32[]{:S(2)}) collective-permute-start(f32[4,32,256]{2,1,0:T(8,128)S(1)} %get-tuple-element.54), channel_id=1, source_target_pairs={{0,192},{64,0},{128,64},{192,128},{1,193},{65,1},{129,65},{193,129... | collective-permute-start | bytes 393224 | tf_op jit(solution)/shard_map/ppermute | solution.py:261
  32.6 9.3 %collective-permute-start.5 = (f32[4,32,256]{2,1,0:T(8,128)S(1)}, f32[4,32,256]{2,1,0:T(8,128)S(1)}, u32[]{:S(2)}, u32[]{:S(2)}) collective-permute-start(f32[4,32,256]{2,1,0:T(8,128)S(1)} %get-tuple-element.55), channel_id=1, source_target_pairs={{0,64},{64,128},{128,192},{192,0},{1,65},{65,129},{129,193},{193,1... | collective-permute-start | bytes 393224 | tf_op jit(solution)/shard_map/ppermute | solution.py:261
  32.6 9.3 %collective-permute-start.4 = (f32[4,32,256]{2,1,0:T(8,128)S(1)}, f32[4,32,256]{2,1,0:T(8,128)S(1)}, u32[]{:S(2)}, u32[]{:S(2)}) collective-permute-start(f32[4,32,256]{2,1,0:T(8,128)S(1)} %get-tuple-element.56), channel_id=1, source_target_pairs={{0,128},{64,192},{128,0},{192,64},{1,129},{65,193},{129,1},{193,65... | collective-permute-start | bytes 393224 | tf_op jit(solution)/shard_map/ppermute | solution.py:261
  42.0 9.3 %collective-permute-start.9 = (f32[1,32,256]{2,1,0:T(8,128)S(1)}, f32[1,32,256]{2,1,0:T(8,128)S(1)}, u32[]{:S(2)}, u32[]{:S(2)}) collective-permute-start(f32[1,32,256]{2,1,0:T(8,128)S(1)} %get-tuple-element.57), channel_id=1, source_target_pairs={{0,48},{16,0},{32,16},{48,32},{1,49},{17,1},{33,17},{49,33},{2,50}... | collective-permute-start | bytes 98312 | tf_op jit(solution)/shard_map/ppermute | solution.py:263
  47.4 6.0 %collective-permute-start.8 = (f32[1,32,256]{2,1,0:T(8,128)S(1)}, f32[1,32,256]{2,1,0:T(8,128)S(1)}, u32[]{:S(2)}, u32[]{:S(2)}) collective-permute-start(f32[1,32,256]{2,1,0:T(8,128)S(1)} %get-tuple-element.58), channel_id=1, source_target_pairs={{0,16},{16,32},{32,48},{48,0},{1,17},{17,33},{33,49},{49,1},{2,18}... | collective-permute-start | bytes 98312 | tf_op jit(solution)/shard_map/ppermute | solution.py:263
  47.4 7.8 %collective-permute-start.7 = (f32[1,32,256]{2,1,0:T(8,128)S(1)}, f32[1,32,256]{2,1,0:T(8,128)S(1)}, u32[]{:S(2)}, u32[]{:S(2)}) collective-permute-start(f32[1,32,256]{2,1,0:T(8,128)S(1)} %get-tuple-element.59), channel_id=1, source_target_pairs={{0,32},{16,48},{32,0},{48,16},{1,33},{17,49},{33,1},{49,17},{2,34}... | collective-permute-start | bytes 98312 | tf_op jit(solution)/shard_map/ppermute | solution.py:263

commit v4 on v3

v4 whole, which is shorter than its diff:
```python
import functools

import jax
import jax.numpy as jnp
import numpy as np
from jax import lax
from jax.experimental import pallas as pl
from jax.experimental.pallas import tpu as pltpu
from jax.sharding import Mesh, PartitionSpec as P

F32, BF16 = jnp.float32, jnp.bfloat16
HALO = 16
VMEM = pl.BlockSpec(memory_space=pltpu.VMEM)


def line_terms(size):
    offsets = np.arange(-4, 5)
    taps = np.exp(-offsets * offsets / 18.0)
    taps = taps / np.sqrt(np.sum(taps * taps))

    def banded(count):
        return sum(t * np.eye(count, k=o) for t, o in zip(taps, offsets))

    pairs = np.repeat(np.eye(size // 2), 2, axis=1) * np.sqrt(0.5)
    coarse = np.sqrt(0.5) * banded(size // 2) @ pairs
    return banded(size), np.repeat(coarse, 2, axis=0), coarse


def split(values):
    high = values.astype(BF16)
    return high, (values - high.astype(values.dtype)).astype(BF16)


def left_table(size, parts):
    fine, pair, coarse = line_terms(size)
    rows = size // parts
    tables = []
    for part in range(parts):
        terms = []
        for term in (fine @ fine, fine @ pair, coarse @ fine, coarse @ pair):
            count = term.shape[0] // parts
            wide = np.zeros((count, rows + 2 * HALO))
            for e in range(rows + 2 * HALO):
                source = part * rows - HALO + e
                if 0 <= source < size:
                    wide[:, e] = term[part * count : (part + 1) * count, source]
            segments = wide.reshape(count, 4, 1, HALO)
            terms.append(np.broadcast_to(segments, (count, 4, 4, HALO)).reshape(count, 256))
        tables.append(np.concatenate(terms))
    return np.stack(tables)


def right_tables(size, parts):
    fine, pair, _ = line_terms(size)
    columns = size // parts
    owns, sides = [], []
    for part in range(parts):
        own = slice(part * columns, (part + 1) * columns)
        edge = slice(columns, columns + HALO) if part == 0 else slice(columns - HALO, columns)
        near = slice(columns - HALO, columns) if part == 0 else slice(columns, columns + HALO)
        terms = (fine @ fine, pair @ fine, fine @ pair, pair @ pair)
        owns.append(np.concatenate([term[own, own] for term in terms]))
        sides.append(np.concatenate([np.tile(term[edge, near], (1, 8)) for term in terms]))
    return np.stack(owns), np.stack(sides)


def halves(table):
    high = table.astype(np.float32).astype(BF16)
    low = (table - high.astype(np.float64)).astype(np.float32).astype(BF16)
    return np.stack([high, low], axis=1)


def dot3(left, right):
    (lh, ll), (rh, rl) = left, right
    dot = lambda a, b: jnp.dot(a, b, preferred_element_type=F32)
    return dot(lh, rh) + (dot(lh, rl) + dot(ll, rh))


def block_of(where, k):
    return lax.rem(where[3] + (2, 1, 3, 0)[k], 4)


def edge_kernel(where, p_hbm, c_hbm, p_ref, c_ref, edge_ref, sems):
    gy = where[2]
    copies = []
    for k in range(4):
        for h in range(2):
            source, at = pl.ds(8 * block_of(where, k) + 4 * h, 4), pl.ds(8 * k + 4 * h, 4)
            copies.append(pltpu.make_async_copy(p_hbm.at[0, source], p_ref.at[at], sems.at[0, 2 * k + h]))
            copies.append(pltpu.make_async_copy(c_hbm.at[source], c_ref.at[at], sems.at[1, 2 * k + h]))
    for copy in copies:
        copy.start()
    lane = lax.broadcasted_iota(jnp.int32, (1, 1, 128), 2)
    edges = jnp.zeros((4, 32, 128), F32)
    for g in range(8):
        copies[2 * g].wait()
        copies[2 * g + 1].wait()
        at = slice(4 * g, 4 * g + 4)
        last = (p_ref[at, :, 128:] * c_ref[at, :, 128:]).reshape(128, 128)
        first = (p_ref[at, :, :128] * c_ref[at, :, :128]).reshape(128, 128)
        v = jnp.where(gy == 0, pltpu.roll(last, 16, 1), first)
        if g:
            v = pltpu.roll(v, 16 * g, 1)
        edges = jnp.where(lane // 16 == g, v.reshape(4, 32, 128), edges)
    for f in range(4):
        edge_ref[f // 2, :, 128 * (f % 2) : 128 * (f % 2) + 128] = edges[f]


def product_kernel(where, p_ref, c_ref, *out_refs):
    for g in range(8):
        v = p_ref[4 * g : 4 * g + 4] * c_ref[4 * g : 4 * g + 4]
        top_ref, bottom_ref = out_refs[:2] if g < 4 else out_refs[2:]
        at = slice(4 * (g % 4), 4 * (g % 4) + 4)
        top_ref[at] = v[:, :HALO]
        bottom_ref[at] = v[:, HALO:]


def table_kernel(
    where, left_ref, edge_ref, right_hbm, xh_ref, xl_ref, eh_ref, el_ref, right_ref, sems
):
    gx, gy = where[1], where[2]
    copies = []
    for h in range(2):
        for k in range(4):
            at = pl.ds(256 * k, 256)
            copies.append(pltpu.make_async_copy(right_hbm.at[gy, h, at], right_ref.at[h, at], sems.at[h, k]))
    for copy in copies:
        copy.start()
    lane = lax.broadcasted_iota(jnp.int32, (1, 256), 1)
    narrow = lax.broadcasted_iota(jnp.int32, (1, 128), 1)
    for h, x_ref, e_ref in ((0, xh_ref, eh_ref), (1, xl_ref, el_ref)):
        row, start = 0, 0
        for count in (32, 32, 16, 16):
            rows = left_ref[gx, h, start : start + count].astype(F32)
            for f in range(4):
                mine = (lane // 16) % 4 == f
                x_ref[row : row + count] = jnp.where(mine, rows, jnp.zeros_like(rows)).astype(BF16)
                row += count
            start += count
        for t in range(4):
            rows = edge_ref[gy, h, 16 * t : 16 * t + 16].astype(F32)
            for g in range(8):
                at = 128 * t + 16 * g
                e_ref[at : at + 16] = jnp.where(narrow // 16 == g, rows, jnp.zeros_like(rows)).astype(BF16)
    for copy in copies:
        copy.wait()


def filter_kernel(
    part, where, p_ref, above_ref, top_ref, bottom_ref, below_ref, xh_ref, xl_ref, right_ref, *refs
):
    core, gy, z = where[0], where[2], where[4]
    dot_rows = lambda parts: dot3((xh_ref[...], xl_ref[...]), split(jnp.concatenate(parts)))
    narrow = lax.broadcasted_iota(jnp.int32, (1, 128), 1)
    if part == 0:
        side_ref, eh_ref, el_ref, keep_ref, send_ref, near_ref, *scratch = refs
        lanes = (slice(0, 128), slice(128, 256))
        sides = (above_ref[16:], side_ref[:, :HALO], side_ref[:, HALO:], below_ref[16:])
        side = dot_rows([s[f // 2, :, lanes[f % 2]] for s in sides for f in range(4)])
        fine = split(jnp.concatenate([side[:128], side[128:256]], axis=1))
        pair = split(jnp.concatenate([side[256:320], side[320:]], axis=1))
        near = dot3(fine, (eh_ref[:256], el_ref[:256]))
        near_pairs = dot3(pair, (eh_ref[256:], el_ref[256:]))
        near_ref[pl.ds(0, 64, stride=2), :] = near_pairs
        near_ref[pl.ds(1, 64, stride=2), :] = near_pairs
        near = near + near_ref[...]
        near = jnp.where(gy == 0, pltpu.roll(near, 112, 1), near)
        near_ref[...] = near
    else:
        near_ref, keep_ref, send_ref, *scratch = refs
        near = near_ref[...]
    fh_ref, fl_ref, ch_ref, cl_ref, alpha_ref, pairs_ref = scratch
    on_left = (narrow < HALO) & (gy == 1)
    on_right = (narrow >= 128 - HALO) & (gy == 0)

    for g in range(4):
        u = dot_rows([r[4 * g : 4 * g + 4].reshape(64, 256) for r in (above_ref, top_ref, bottom_ref, below_ref)])
        for t in range(2):
            at, lanes = slice(128 * g, 128 * g + 128), slice(256 * t, 256 * t + 256)
            fh_ref[at, lanes], fl_ref[at, lanes] = split(u[128 * t : 128 * t + 128])
            at = slice(64 * g, 64 * g + 64)
            ch_ref[at, lanes], cl_ref[at, lanes] = split(u[256 + 64 * t : 320 + 64 * t])

    alpha_ref[...] = dot3((fh_ref[...], fl_ref[...]), (right_ref[0, :512], right_ref[1, :512]))
    pairs = dot3((ch_ref[...], cl_ref[...]), (right_ref[0, 512:], right_ref[1, 512:]))
    for h in range(2):
        for s in range(2):
            pairs_ref[h, pl.ds(s, 256, stride=2), :] = pairs[:, 128 * h : 128 * h + 128]

    for g in range(4):
        at = slice(128 * g, 128 * g + 128)
        shift = (128 - 16 * (4 * part + g)) % 128
        moved = pltpu.roll(near, shift, 1) if shift else near
        zero = jnp.zeros_like(moved)
        low = pairs_ref[0, at] + jnp.where(on_left, moved, zero)
        high = pairs_ref[1, at] + jnp.where(on_right, moved, zero)
        alpha = alpha_ref[at] + jnp.concatenate([low, high], axis=1)
        first = 16 * part + 4 * g
        q = p_ref[first : first + 4] * alpha.reshape(4, 32, 256)
        for j in range(2):
            to = 4 * (g // 2) + lax.rem(2 * (g % 2) + j + 4 - z, 4)
            keep_ref[to] = jnp.where(core == 0, q[2 * j], q[2 * j + 1])
            send_ref[to] = jnp.where(core == 0, q[2 * j + 1], q[2 * j])


def call(kernel, outs, *args, hbm=(), scratch=(), cost=0, grant=16):
    args = [pltpu.with_memory_space_constraint(a, pltpu.HBM) if i in hbm else a for i, a in enumerate(args)]
    specs = [pl.BlockSpec(memory_space=pltpu.SMEM)] + [
        pl.BlockSpec(memory_space=pltpu.HBM) if i in hbm else VMEM for i in range(1, len(args))
    ]
    return pl.pallas_call(
        kernel,
        out_shape=[o if isinstance(o, jax.ShapeDtypeStruct) else jax.ShapeDtypeStruct(o, F32) for o in outs],
        in_specs=specs,
        out_specs=[VMEM] * len(outs),
        scratch_shapes=scratch,
        cost_estimate=pl.CostEstimate(flops=cost, bytes_accessed=1 << 20, transcendentals=0),
        compiler_params=pltpu.CompilerParams(vmem_limit_bytes=grant << 20),
    )(*args)


def body(perturbations, control):
    x, z, core, gx, gy = (lax.axis_index(a) for a in ("x", "z", "core", "gx", "gy"))
    where = jnp.stack([core, gx, gy, x, z]).astype(jnp.int32)
    left = jnp.asarray(halves(left_table(128, 4)))
    right, edge = (jnp.asarray(halves(t)) for t in right_tables(512, 2))
    vmem, sems = pltpu.VMEM, pltpu.SemaphoreType.DMA

    ring = lambda d: [(i, (i + d) % 4) for i in range(4)]
    swap = [(0, 1), (1, 0)]
    near_p, near_c, edges = call(
        edge_kernel, [(32, 32, 256)] * 2 + [(2, 32, 256)], where, perturbations, control, hbm=(1, 2),
        scratch=[sems((2, 8))],
    )
    side = lax.ppermute(edges, "gy", swap)
    tops, bottoms = [None] * 2, [None] * 2
    tops[0], bottoms[0], tops[1], bottoms[1] = call(
        product_kernel, [(18, 16, 256)] * 2 + [(16, 16, 256)] * 2, where, near_p, near_c
    )
    tops[0] = tops[0].at[16:].set(side[:, :HALO])
    bottoms[0] = bottoms[0].at[16:].set(side[:, HALO:])
    aboves, belows = [None] * 2, [None] * 2
    for part in range(2):
        aboves[part] = lax.ppermute(bottoms[part], "gx", ring(1))
        belows[part] = lax.ppermute(tops[part], "gx", ring(3))
    xh, xl, eh, el, right = call(
        table_kernel,
        [jax.ShapeDtypeStruct(s, BF16) for s in [(384, 256)] * 2 + [(512, 128)] * 2 + [(2, 1024, 256)]],
        where, left, edge, right, hbm=(3,), scratch=[sems((2, 4))],
    )
    piece = {}
    for part in range(2):
        extra = (side, eh, el) if part == 0 else (near,)
        keep, give, *rest = call(
            functools.partial(filter_kernel, part), [(8, 32, 256)] * 2 + [(128, 128)] * (part == 0),
            where, near_p, aboves[part], tops[part], bottoms[part], belows[part], xh, xl, right, *extra,
            scratch=[vmem((512, 512), BF16)] * 2 + [vmem((256, 512), BF16)] * 2
            + [vmem((512, 256), F32), vmem((2, 512, 128), F32)],
            cost=2 * 10**9,
        )
        near = rest[0] if rest else None
        got = lax.ppermute(give, "core", swap)
        for i in range(2):
            piece[((2, 1), (3, 0))[part][i]] = keep[4 * i : 4 * i + 4] + got[4 * i : 4 * i + 4]
        if part == 0:
            x2, x1 = (lax.ppermute(piece[d], "x", ring(d)) for d in (2, 1))
    x3 = lax.ppermute(piece[3], "x", ring(3))
    cell = [(piece[0][e : e + 1] + x2[e : e + 1]) + (x1[e : e + 1] + x3[e : e + 1]) for e in range(4)]
    z2, z1, z3 = (lax.ppermute(cell[e], "z", ring(e)) for e in (2, 1, 3))
    return ((cell[0] + z2) + (z1 + z3)) * (1.0 / 31.0)


def solution(mesh):
    grid = Mesh(mesh.devices.reshape(4, 4, 2, 4, 2), ("x", "z", "core", "gx", "gy"))
    mem = ("x", "z", "core")
    placed = (P(mem, None, "gx", "gy"), P(None, "gx", "gy"))
    return jax.shard_map(body, mesh=grid, in_specs=placed, out_specs=P(mem, "gx", "gy"), check_vma=False)
```

time: 56 us -> 49 us (0.88)
  the two profiles are of different devices: /device:TPU:32 before, /device:TPU:8 now
where the time goes in v4:
time: 49 us; the launch traced here: 48.7 us
  starting transfers between devices  25.3 us (52%)
  waiting for transfers between devices  12.5 us (26%)
  Pallas kernels  10.1 us (21%)
  other arithmetic  0.73 us (1%)
    ppermute x3, starting transfers between devices, body(): z2, z1, z3 = (lax.ppermute(cell[e], 'z', ring(e)) for e in (2, 1, 3))  11.3 us
    pallas_call x5, Pallas kernels, call(): pl.pallas_call(kernel, out_shape=[o if isinstance(o, jax.ShapeDtypeStruct...  10.1 us
    ppermute x2, waiting for transfers between devices, body(): x2, x1 = (lax.ppermute(piece[d], 'x', ring(d)) for d in (2, 1))  3.88 us
    ppermute x2, starting transfers between devices, body(): x2, x1 = (lax.ppermute(piece[d], 'x', ring(d)) for d in (2, 1))  3.7 us
    ppermute x2, starting transfers between devices, body(): aboves[part] = lax.ppermute(bottoms[part], 'gx', ring(1))  2.94 us
    ppermute x1, starting transfers between devices, body(): x3 = lax.ppermute(piece[3], 'x', ring(3))  2.72 us
    ppermute x2, waiting for transfers between devices, body(): aboves[part] = lax.ppermute(bottoms[part], 'gx', ring(1))  2.71 us
    ppermute x2, starting transfers between devices, body(): belows[part] = lax.ppermute(tops[part], 'gx', ring(3))  2.46 us
  transfers between devices with their start and end apart: 13, of which 8 were waited for; matrix products, arithmetic and copies ran while one was open for 0% of the time, Pallas kernels for 15%

profile of v4, /device:TPU:8, one launch (start us, length us, event | category | flops | bytes accessed | tf_op | source)
XLA Modules:
  0.0 48.7 jit_solution(8900444934284218984)
XLA Ops:
  0.0 0.1 stack.23.where
  0.1 0.0 copy-start
  0.1 0.0 copy-start.1
  0.1 2.9 %shard_map.55 = (f32[32,32,256]{2,1,0:T(8,128)S(1)}, f32[32,32,256]{2,1,0:T(8,128)S(1)}, f32[2,32,256]{2,1,0:T(8,128)S(1)}) custom-call(s32[5]{0:T(128)S(1)} %stack.23.where, f32[1,32,32,256]{3,2,1,0:T(8,128)} %p_hbm.1, f32[32,32,256]{2,1,0:T(8,128)} %c_hbm.1), custom_call_target="tpu_custom_call" | custom-call | bytes 1048576 | tf_op jit(solution)/shard_map/pallas_call | solution.py:211
  3.0 2.0 %collective-permute-start.2 = (f32[2,32,256]{2,1,0:T(8,128)S(1)}, f32[2,32,256]{2,1,0:T(8,128)S(1)}, u32[]{:S(2)}, u32[]{:S(2)}) collective-permute-start(f32[2,32,256]{2,1,0:T(8,128)S(1)} %get-tuple-element.54), channel_id=1, source_target_pairs={{0,1},{1,0},{2,3},{3,2},{4,5},{5,4},{6,7},{7,6},{8,9},{9,8},{10,11... | collective-permute-start | bytes 196616 | tf_op jit(solution)/shard_map/ppermute | solution.py:235
  5.0 0.6 %shard_map.56 = (f32[18,16,256]{2,1,0:T(8,128)S(1)}, f32[18,16,256]{2,1,0:T(8,128)S(1)}, f32[16,16,256]{2,1,0:T(8,128)S(1)}, f32[16,16,256]{2,1,0:T(8,128)S(1)}) custom-call(s32[5]{0:T(128)S(1)} %stack.23.where, f32[32,32,256]{2,1,0:T(8,128)S(1)} %get-tuple-element.46.p_ref, f32[32,32,256]{2,1,0:T(8,128)S(1)} %get-tuple-element.47.c_ref), custom_call_target="tpu_custom_call" | custom-call | bytes 1048576 | tf_op jit(solution)/shard_map/pallas_call | solution.py:211
  5.6 1.7 %collective-permute-done.2.refs_0_ = f32[2,32,256]{2,1,0:T(8,128)S(1)} collective-permute-done((f32[2,32,256]{2,1,0:T(8,128)S(1)}, f32[2,32,256]{2,1,0:T(8,128)S(1)}, u32[]{:S(2)}, u32[]{:S(2)}) %collective-permute-start.2) | collective-permute-done | bytes 65568 | tf_op jit(solution)/shard_map/ppermute | solution.py:235
  7.3 1.6 %collective-permute-start.3 = (f32[18,16,256]{2,1,0:T(8,128)S(1)}, f32[18,16,256]{2,1,0:T(8,128)S(1)}, u32[]{:S(2)}, u32[]{:S(2)}) collective-permute-start(f32[18,16,256]{2,1,0:T(8,128)S(1)} %get-tuple-element.71.bottom_ref), channel_id=1, source_target_pairs={{0,2},{2,4},{4,6},{6,0},{1,3},{3,5},{5,7},{7,1},{8,10},{10,12},{12... | collective-permute-start | bytes 884744 | tf_op jit(solution)/shard_map/ppermute | solution.py:244
  8.9 0.7 %collective-permute-start.4 = (f32[18,16,256]{2,1,0:T(8,128)S(1)}, f32[18,16,256]{2,1,0:T(8,128)S(1)}, u32[]{:S(2)}, u32[]{:S(2)}) collective-permute-start(f32[18,16,256]{2,1,0:T(8,128)S(1)} %get-tuple-element.70.top_ref), channel_id=1, source_target_pairs={{0,6},{2,0},{4,2},{6,4},{1,7},{3,1},{5,3},{7,5},{8,14},{10,8},{12,... | collective-permute-start | bytes 884744 | tf_op jit(solution)/shard_map/ppermute | solution.py:245
  9.6 1.4 %collective-permute-start = (f32[16,16,256]{2,1,0:T(8,128)S(1)}, f32[16,16,256]{2,1,0:T(8,128)S(1)}, u32[]{:S(2)}, u32[]{:S(2)}) collective-permute-start(f32[16,16,256]{2,1,0:T(8,128)S(1)} %get-tuple-element.48.bottom_ref), channel_id=1, source_target_pairs={{0,2},{2,4},{4,6},{6,0},{1,3},{3,5},{5,7},{7,1},{8,10},{10,12},{12... | collective-permute-start | bytes 786440 | tf_op jit(solution)/shard_map/ppermute | solution.py:244
  10.9 1.8 %collective-permute-start.1 = (f32[16,16,256]{2,1,0:T(8,128)S(1)}, f32[16,16,256]{2,1,0:T(8,128)S(1)}, u32[]{:S(2)}, u32[]{:S(2)}) collective-permute-start(f32[16,16,256]{2,1,0:T(8,128)S(1)} %get-tuple-element.49.top_ref), channel_id=1, source_target_pairs={{0,6},{2,0},{4,2},{6,4},{1,7},{3,1},{5,3},{7,5},{8,14},{10,8},{12,... | collective-permute-start | bytes 786440 | tf_op jit(solution)/shard_map/ppermute | solution.py:245
  12.7 0.0 copy-done
  12.7 0.0 copy-done.1
  12.7 1.9 %shard_map.57 = (bf16[384,256]{1,0:T(8,128)(2,1)S(1)}, bf16[384,256]{1,0:T(8,128)(2,1)S(1)}, bf16[512,128]{1,0:T(8,128)(2,1)S(1)}, bf16[512,128]{1,0:T(8,128)(2,1)S(1)}, bf16[2,1024,256]{2,1,0:T(8,128)(2,1)S(1)}) custom-call(s32[5]{0:T(128)S(1)} %stack.23.where, bf16[4,2,96,256]{3,2,1,0:T(8,128)(2,1)S(1)} %copy-done, bf16[2,2,64,128]{3,2,1,0:T(8,128)(2,1)S(1)} %copy-done.1, ...), custom_call_target="tpu_custom_call" | custom-call | bytes 1048576 | tf_op jit(solution)/shard_map/pallas_call | solution.py:211
  14.6 2.7 %collective-permute-done.3.above_ref = f32[18,16,256]{2,1,0:T(8,128)S(1)} collective-permute-done((f32[18,16,256]{2,1,0:T(8,128)S(1)}, f32[18,16,256]{2,1,0:T(8,128)S(1)}, u32[]{:S(2)}, u32[]{:S(2)}) %collective-permute-start.3) | collective-permute-done | bytes 294944 | tf_op jit(solution)/shard_map/ppermute | solution.py:244
  17.4 1.4 %collective-permute-done.4.below_ref = f32[18,16,256]{2,1,0:T(8,128)S(1)} collective-permute-done((f32[18,16,256]{2,1,0:T(8,128)S(1)}, f32[18,16,256]{2,1,0:T(8,128)S(1)}, u32[]{:S(2)}, u32[]{:S(2)}) %collective-permute-start.4) | collective-permute-done | bytes 294944 | tf_op jit(solution)/shard_map/ppermute | solution.py:245
  18.8 2.6 %shard_map.58 = (f32[8,32,256]{2,1,0:T(8,128)S(1)}, f32[8,32,256]{2,1,0:T(8,128)S(1)}, f32[128,128]{1,0:T(8,128)S(1)}) custom-call(s32[5]{0:T(128)S(1)} %stack.23.where, f32[32,32,256]{2,1,0:T(8,128)S(1)} %get-tuple-element.46.p_ref, f32[18,16,256]{2,1,0:T(8,128)S(1)} %collective-permute-done.3.above_ref, f32[18,16,256]{2,1,0:T(8,128)S(1)} %get-tuple-element.70.top_ref, ...), custom_call_target="tpu_custom_call" | custom-call | flops 2000000000 | bytes 1048576 | tf_op jit(solution)/shard_map/pallas_call | solution.py:211
  21.4 0.1 collective-permute-start.6
  21.5 0.0 collective-permute-done.above_ref
  21.5 0.6 %collective-permute-done.1.below_ref = f32[16,16,256]{2,1,0:T(8,128)S(1)} collective-permute-done((f32[16,16,256]{2,1,0:T(8,128)S(1)}, f32[16,16,256]{2,1,0:T(8,128)S(1)}, u32[]{:S(2)}, u32[]{:S(2)}) %collective-permute-start.1) | collective-permute-done | bytes 262176 | tf_op jit(solution)/shard_map/ppermute | solution.py:245
  22.0 2.1 %shard_map.59 = (f32[8,32,256]{2,1,0:T(8,128)S(1)}, f32[8,32,256]{2,1,0:T(8,128)S(1)}) custom-call(s32[5]{0:T(128)S(1)} %stack.23.where, f32[32,32,256]{2,1,0:T(8,128)S(1)} %get-tuple-element.46.p_ref, f32[16,16,256]{2,1,0:T(8,128)S(1)} %collective-permute-done.above_ref, f32[16,16,256]{2,1,0:T(8,128)S(1)} %get-tuple-element.49.top_ref, ...), custom_call_target="tpu_custom_call" | custom-call | flops 2000000000 | bytes 1048576 | tf_op jit(solution)/shard_map/pallas_call | solution.py:211
  24.1 0.1 collective-permute-start.5
  24.2 0.0 collective-permute-done.6
  24.3 3.1 %collective-permute-start.7 = (f32[4,32,256]{2,1,0:T(8,128)S(1)}, f32[4,32,256]{2,1,0:T(8,128)S(1)}, u32[]{:S(2)}, u32[]{:S(2)}) collective-permute-start(f32[4,32,256]{2,1,0:T(8,128)S(1)} %get-tuple-element.68), channel_id=1, source_target_pairs={{0,128},{64,192},{128,0},{192,64},{1,129},{65,193},{129,1},{193,65... | collective-permute-start | bytes 393224 | tf_op jit(solution)/shard_map/ppermute | solution.py:266
  27.4 0.6 %collective-permute-start.8 = (f32[4,32,256]{2,1,0:T(8,128)S(1)}, f32[4,32,256]{2,1,0:T(8,128)S(1)}, u32[]{:S(2)}, u32[]{:S(2)}) collective-permute-start(f32[4,32,256]{2,1,0:T(8,128)S(1)} %get-tuple-element.69), channel_id=1, source_target_pairs={{0,64},{64,128},{128,192},{192,0},{1,65},{65,129},{129,193},{193,1... | collective-permute-start | bytes 393224 | tf_op jit(solution)/shard_map/ppermute | solution.py:266
  28.0 0.0 collective-permute-done.5
  28.0 2.7 %collective-permute-start.9 = (f32[4,32,256]{2,1,0:T(8,128)S(1)}, f32[4,32,256]{2,1,0:T(8,128)S(1)}, u32[]{:S(2)}, u32[]{:S(2)}) collective-permute-start(f32[4,32,256]{2,1,0:T(8,128)S(1)} %get-tuple-element.67), channel_id=1, source_target_pairs={{0,192},{64,0},{128,64},{192,128},{1,193},{65,1},{129,65},{193,129... | collective-permute-start | bytes 393224 | tf_op jit(solution)/shard_map/ppermute | solution.py:267
  30.7 1.5 %collective-permute-done.7 = f32[4,32,256]{2,1,0:T(8,128)S(1)} collective-permute-done((f32[4,32,256]{2,1,0:T(8,128)S(1)}, f32[4,32,256]{2,1,0:T(8,128)S(1)}, u32[]{:S(2)}, u32[]{:S(2)}) %collective-permute-start.7) | collective-permute-done | bytes 131104 | tf_op jit(solution)/shard_map/ppermute | solution.py:266
  32.2 2.4 %collective-permute-done.8 = f32[4,32,256]{2,1,0:T(8,128)S(1)} collective-permute-done((f32[4,32,256]{2,1,0:T(8,128)S(1)}, f32[4,32,256]{2,1,0:T(8,128)S(1)}, u32[]{:S(2)}, u32[]{:S(2)}) %collective-permute-start.8) | collective-permute-done | bytes 131104 | tf_op jit(solution)/shard_map/ppermute | solution.py:266
  34.6 0.0 collective-permute-done.9
  34.7 7.1 %collective-permute-start.10 = (f32[1,32,256]{2,1,0:T(8,128)S(1)}, f32[1,32,256]{2,1,0:T(8,128)S(1)}, u32[]{:S(2)}, u32[]{:S(2)}) collective-permute-start(f32[1,32,256]{2,1,0:T(8,128)S(1)} %get-tuple-element.65), channel_id=1, source_target_pairs={{0,32},{16,48},{32,0},{48,16},{1,33},{17,49},{33,1},{49,17},{2,34}... | collective-permute-start | bytes 98312 | tf_op jit(solution)/shard_map/ppermute | solution.py:269
  41.8 1.5 %collective-permute-start.11 = (f32[1,32,256]{2,1,0:T(8,128)S(1)}, f32[1,32,256]{2,1,0:T(8,128)S(1)}, u32[]{:S(2)}, u32[]{:S(2)}) collective-permute-start(f32[1,32,256]{2,1,0:T(8,128)S(1)} %get-tuple-element.64), channel_id=1, source_target_pairs={{0,16},{16,32},{32,48},{48,0},{1,17},{17,33},{33,49},{49,1},{2,18}... | collective-permute-start | bytes 98312 | tf_op jit(solution)/shard_map/ppermute | solution.py:269
  43.3 2.7 %collective-permute-start.12 = (f32[1,32,256]{2,1,0:T(8,128)S(1)}, f32[1,32,256]{2,1,0:T(8,128)S(1)}, u32[]{:S(2)}, u32[]{:S(2)}) collective-permute-start(f32[1,32,256]{2,1,0:T(8,128)S(1)} %get-tuple-element.63), channel_id=1, source_target_pairs={{0,48},{16,0},{32,16},{48,32},{1,49},{17,1},{33,17},{49,33},{2,50}... | collective-permute-start | bytes 98312 | tf_op jit(solution)/shard_map/ppermute | solution.py:269
  45.9 0.0 collective-permute-done.10
  45.9 1.9 %collective-permute-done.11 = f32[1,32,256]{2,1,0:T(8,128)S(1)} collective-permute-done((f32[1,32,256]{2,1,0:T(8,128)S(1)}, f32[1,32,256]{2,1,0:T(8,128)S(1)}, u32[]{:S(2)}, u32[]{:S(2)}) %collective-permute-start.11) | collective-permute-done | bytes 32800 | tf_op jit(solution)/shard_map/ppermute | solution.py:269
  47.8 0.3 collective-permute-done.12
  48.1 0.6 %fusion.6 = f32[1,32,256]{2,1,0:T(8,128)} fusion(f32[1,32,256]{2,1,0:T(8,128)S(1)} %collective-permute-done.10, f32[4,32,256]{2,1,0:T(8,128)S(1)} %collective-permute-done.9, f32[4,32,256]{2,1,0:T(8,128)S(1)} %collective-permute-done.8, f32[4,32,256]{2,1,0:T(8,128)S(1)} %collective-permute-done.7, f32[4,32,256]{2,1,0:T(8,128)S(1)} %get-tuple-element.66, ...), kind=kLoop, calls=%fused_computation.17 | loop fusion | flops 57344 | bytes 262144 | tf_op jit(solution)/shard_map/mul | solution.py:270
  (4 shorter events, 0.1 us)
Async XLA Ops:
  0.1 12.7 %copy-start = (bf16[4,2,96,256]{3,2,1,0:T(8,128)(2,1)S(1)}, bf16[4,2,96,256]{3,2,1,0:T(8,128)(2,1)}, u32[]{:S(2)}) copy-start(bf16[4,2,96,256]{3,2,1,0:T(8,128)(2,1)} %constant.76.clone.left_ref) | copy-start | bytes 1179652
  0.1 12.7 %copy-start.1 = (bf16[2,2,64,128]{3,2,1,0:T(8,128)(2,1)S(1)}, bf16[2,2,64,128]{3,2,1,0:T(8,128)(2,1)}, u32[]{:S(2)}) copy-start(bf16[2,2,64,128]{3,2,1,0:T(8,128)(2,1)} %constant.78.clone.edge_ref) | copy-start | bytes 196612
  3.0 4.4 %collective-permute-start.2 = (f32[2,32,256]{2,1,0:T(8,128)S(1)}, f32[2,32,256]{2,1,0:T(8,128)S(1)}, u32[]{:S(2)}, u32[]{:S(2)}) collective-permute-start(f32[2,32,256]{2,1,0:T(8,128)S(1)} %get-tuple-element.54), channel_id=1, source_target_pairs={{0,1},{1,0},{2,3},{3,2},{4,5},{5,4},{6,7},{7,6},{8,9},{9,8},{10,11... | collective-permute-start | bytes 196616 | tf_op jit(solution)/shard_map/ppermute | solution.py:235
  7.3 10.0 %collective-permute-start.3 = (f32[18,16,256]{2,1,0:T(8,128)S(1)}, f32[18,16,256]{2,1,0:T(8,128)S(1)}, u32[]{:S(2)}, u32[]{:S(2)}) collective-permute-start(f32[18,16,256]{2,1,0:T(8,128)S(1)} %get-tuple-element.71.bottom_ref), channel_id=1, source_target_pairs={{0,2},{2,4},{4,6},{6,0},{1,3},{3,5},{5,7},{7,1},{8,10},{10,12},{12... | collective-permute-start | bytes 884744 | tf_op jit(solution)/shard_map/ppermute | solution.py:244
  8.9 9.9 %collective-permute-start.4 = (f32[18,16,256]{2,1,0:T(8,128)S(1)}, f32[18,16,256]{2,1,0:T(8,128)S(1)}, u32[]{:S(2)}, u32[]{:S(2)}) collective-permute-start(f32[18,16,256]{2,1,0:T(8,128)S(1)} %get-tuple-element.70.top_ref), channel_id=1, source_target_pairs={{0,6},{2,0},{4,2},{6,4},{1,7},{3,1},{5,3},{7,5},{8,14},{10,8},{12,... | collective-permute-start | bytes 884744 | tf_op jit(solution)/shard_map/ppermute | solution.py:245
  9.6 11.9 %collective-permute-start = (f32[16,16,256]{2,1,0:T(8,128)S(1)}, f32[16,16,256]{2,1,0:T(8,128)S(1)}, u32[]{:S(2)}, u32[]{:S(2)}) collective-permute-start(f32[16,16,256]{2,1,0:T(8,128)S(1)} %get-tuple-element.48.bottom_ref), channel_id=1, source_target_pairs={{0,2},{2,4},{4,6},{6,0},{1,3},{3,5},{5,7},{7,1},{8,10},{10,12},{12... | collective-permute-start | bytes 786440 | tf_op jit(solution)/shard_map/ppermute | solution.py:244
  10.9 11.1 %collective-permute-start.1 = (f32[16,16,256]{2,1,0:T(8,128)S(1)}, f32[16,16,256]{2,1,0:T(8,128)S(1)}, u32[]{:S(2)}, u32[]{:S(2)}) collective-permute-start(f32[16,16,256]{2,1,0:T(8,128)S(1)} %get-tuple-element.49.top_ref), channel_id=1, source_target_pairs={{0,6},{2,0},{4,2},{6,4},{1,7},{3,1},{5,3},{7,5},{8,14},{10,8},{12,... | collective-permute-start | bytes 786440 | tf_op jit(solution)/shard_map/ppermute | solution.py:245
  21.4 2.9 %collective-permute-start.6 = (f32[8,32,256]{2,1,0:T(8,128)S(1)}, f32[8,32,256]{2,1,0:T(8,128)S(1)}, u32[]{:S(2)}, u32[]{:S(2)}) collective-permute-start(f32[8,32,256]{2,1,0:T(8,128)S(1)} %get-tuple-element.62), channel_id=1, source_target_pairs={{0,8},{8,0},{1,9},{9,1},{2,10},{10,2},{3,11},{11,3},{4,12},{12,4},... | collective-permute-start | bytes 786440 | tf_op jit(solution)/shard_map/ppermute | solution.py:262
  24.1 3.9 %collective-permute-start.5 = (f32[8,32,256]{2,1,0:T(8,128)S(1)}, f32[8,32,256]{2,1,0:T(8,128)S(1)}, u32[]{:S(2)}, u32[]{:S(2)}) collective-permute-start(f32[8,32,256]{2,1,0:T(8,128)S(1)} %get-tuple-element.60), channel_id=1, source_target_pairs={{0,8},{8,0},{1,9},{9,1},{2,10},{10,2},{3,11},{11,3},{4,12},{12,4},... | collective-permute-start | bytes 786440 | tf_op jit(solution)/shard_map/ppermute | solution.py:262
  24.3 8.0 %collective-permute-start.7 = (f32[4,32,256]{2,1,0:T(8,128)S(1)}, f32[4,32,256]{2,1,0:T(8,128)S(1)}, u32[]{:S(2)}, u32[]{:S(2)}) collective-permute-start(f32[4,32,256]{2,1,0:T(8,128)S(1)} %get-tuple-element.68), channel_id=1, source_target_pairs={{0,128},{64,192},{128,0},{192,64},{1,129},{65,193},{129,1},{193,65... | collective-permute-start | bytes 393224 | tf_op jit(solution)/shard_map/ppermute | solution.py:266
  27.4 7.2 %collective-permute-start.8 = (f32[4,32,256]{2,1,0:T(8,128)S(1)}, f32[4,32,256]{2,1,0:T(8,128)S(1)}, u32[]{:S(2)}, u32[]{:S(2)}) collective-permute-start(f32[4,32,256]{2,1,0:T(8,128)S(1)} %get-tuple-element.69), channel_id=1, source_target_pairs={{0,64},{64,128},{128,192},{192,0},{1,65},{65,129},{129,193},{193,1... | collective-permute-start | bytes 393224 | tf_op jit(solution)/shard_map/ppermute | solution.py:266
  28.0 6.6 %collective-permute-start.9 = (f32[4,32,256]{2,1,0:T(8,128)S(1)}, f32[4,32,256]{2,1,0:T(8,128)S(1)}, u32[]{:S(2)}, u32[]{:S(2)}) collective-permute-start(f32[4,32,256]{2,1,0:T(8,128)S(1)} %get-tuple-element.67), channel_id=1, source_target_pairs={{0,192},{64,0},{128,64},{192,128},{1,193},{65,1},{129,65},{193,129... | collective-permute-start | bytes 393224 | tf_op jit(solution)/shard_map/ppermute | solution.py:267
  34.7 11.3 %collective-permute-start.10 = (f32[1,32,256]{2,1,0:T(8,128)S(1)}, f32[1,32,256]{2,1,0:T(8,128)S(1)}, u32[]{:S(2)}, u32[]{:S(2)}) collective-permute-start(f32[1,32,256]{2,1,0:T(8,128)S(1)} %get-tuple-element.65), channel_id=1, source_target_pairs={{0,32},{16,48},{32,0},{48,16},{1,33},{17,49},{33,1},{49,17},{2,34}... | collective-permute-start | bytes 98312 | tf_op jit(solution)/shard_map/ppermute | solution.py:269
  41.8 6.0 %collective-permute-start.11 = (f32[1,32,256]{2,1,0:T(8,128)S(1)}, f32[1,32,256]{2,1,0:T(8,128)S(1)}, u32[]{:S(2)}, u32[]{:S(2)}) collective-permute-start(f32[1,32,256]{2,1,0:T(8,128)S(1)} %get-tuple-element.64), channel_id=1, source_target_pairs={{0,16},{16,32},{32,48},{48,0},{1,17},{17,33},{33,49},{49,1},{2,18}... | collective-permute-start | bytes 98312 | tf_op jit(solution)/shard_map/ppermute | solution.py:269
  43.3 4.8 %collective-permute-start.12 = (f32[1,32,256]{2,1,0:T(8,128)S(1)}, f32[1,32,256]{2,1,0:T(8,128)S(1)}, u32[]{:S(2)}, u32[]{:S(2)}) collective-permute-start(f32[1,32,256]{2,1,0:T(8,128)S(1)} %get-tuple-element.63), channel_id=1, source_target_pairs={{0,48},{16,0},{32,16},{48,32},{1,49},{17,1},{33,17},{49,33},{2,50}... | collective-permute-start | bytes 98312 | tf_op jit(solution)/shard_map/ppermute | solution.py:269

commit v5 on v4

--- a/solution.py
+++ b/solution.py
@@ -80,8 +80,7 @@
     return lax.rem(where[3] + (2, 1, 3, 0)[k], 4)
 
 
-def edge_kernel(where, p_hbm, c_hbm, p_ref, c_ref, edge_ref, sems):
-    gy = where[2]
+def product_kernel(where, p_hbm, c_hbm, p_ref, top_ref, bottom_ref, c_ref, sems):
     copies = []
     for k in range(4):
         for h in range(2):
@@ -90,29 +89,30 @@
             copies.append(pltpu.make_async_copy(c_hbm.at[source], c_ref.at[at], sems.at[1, 2 * k + h]))
     for copy in copies:
         copy.start()
-    lane = lax.broadcasted_iota(jnp.int32, (1, 1, 128), 2)
-    edges = jnp.zeros((4, 32, 128), F32)
     for g in range(8):
         copies[2 * g].wait()
         copies[2 * g + 1].wait()
         at = slice(4 * g, 4 * g + 4)
-        last = (p_ref[at, :, 128:] * c_ref[at, :, 128:]).reshape(128, 128)
-        first = (p_ref[at, :, :128] * c_ref[at, :, :128]).reshape(128, 128)
-        v = jnp.where(gy == 0, pltpu.roll(last, 16, 1), first)
-        if g:
-            v = pltpu.roll(v, 16 * g, 1)
-        edges = jnp.where(lane // 16 == g, v.reshape(4, 32, 128), edges)
-    for f in range(4):
-        edge_ref[f // 2, :, 128 * (f % 2) : 128 * (f % 2) + 128] = edges[f]
-
-
-def product_kernel(where, p_ref, c_ref, *out_refs):
-    for g in range(8):
-        v = p_ref[4 * g : 4 * g + 4] * c_ref[4 * g : 4 * g + 4]
-        top_ref, bottom_ref = out_refs[:2] if g < 4 else out_refs[2:]
-        at = slice(4 * (g % 4), 4 * (g % 4) + 4)
+        v = p_ref[at] * c_ref[at]
         top_ref[at] = v[:, :HALO]
         bottom_ref[at] = v[:, HALO:]
+
+
+def edge_kernel(where, top_ref, bottom_ref, edge_ref):
+    gy = where[2]
+    lane = lax.broadcasted_iota(jnp.int32, (1, 1, 128), 2)
+    for r_ref, rows in ((top_ref, slice(0, HALO)), (bottom_ref, slice(HALO, 2 * HALO))):
+        edges = jnp.zeros((4, HALO, 128), F32)
+        for g in range(8):
+            at = slice(4 * g, 4 * g + 4)
+            last = r_ref[at, :, 128:].reshape(64, 128)
+            first = r_ref[at, :, :128].reshape(64, 128)
+            v = jnp.where(gy == 0, pltpu.roll(last, 16, 1), first)
+            if g:
+                v = pltpu.roll(v, 16 * g, 1)
+            edges = jnp.where(lane // 16 == g, v.reshape(4, HALO, 128), edges)
+        for f in range(4):
+            edge_ref[f // 2, rows, 128 * (f % 2) : 128 * (f % 2) + 128] = edges[f]
 
 
 def table_kernel(
@@ -153,9 +153,9 @@
     dot_rows = lambda parts: dot3((xh_ref[...], xl_ref[...]), split(jnp.concatenate(parts)))
     narrow = lax.broadcasted_iota(jnp.int32, (1, 128), 1)
     if part == 0:
-        side_ref, eh_ref, el_ref, keep_ref, send_ref, near_ref, *scratch = refs
+        side_above_ref, side_ref, side_below_ref, eh_ref, el_ref, keep_ref, send_ref, near_ref, *scratch = refs
         lanes = (slice(0, 128), slice(128, 256))
-        sides = (above_ref[16:], side_ref[:, :HALO], side_ref[:, HALO:], below_ref[16:])
+        sides = (side_above_ref, side_ref.at[:, :HALO], side_ref.at[:, HALO:], side_below_ref)
         side = dot_rows([s[f // 2, :, lanes[f % 2]] for s in sides for f in range(4)])
         fine = split(jnp.concatenate([side[:128], side[128:256]], axis=1))
         pair = split(jnp.concatenate([side[256:320], side[320:]], axis=1))
@@ -174,7 +174,8 @@
     on_right = (narrow >= 128 - HALO) & (gy == 0)
 
     for g in range(4):
-        u = dot_rows([r[4 * g : 4 * g + 4].reshape(64, 256) for r in (above_ref, top_ref, bottom_ref, below_ref)])
+        fields = slice(16 * part + 4 * g, 16 * part + 4 * g + 4)
+        u = dot_rows([r[fields].reshape(64, 256) for r in (above_ref, top_ref, bottom_ref, below_ref)])
         for t in range(2):
             at, lanes = slice(128 * g, 128 * g + 128), slice(256 * t, 256 * t + 256)
             fh_ref[at, lanes], fl_ref[at, lanes] = split(u[128 * t : 128 * t + 128])
@@ -228,21 +229,16 @@
 
     ring = lambda d: [(i, (i + d) % 4) for i in range(4)]
     swap = [(0, 1), (1, 0)]
-    near_p, near_c, edges = call(
-        edge_kernel, [(32, 32, 256)] * 2 + [(2, 32, 256)], where, perturbations, control, hbm=(1, 2),
-        scratch=[sems((2, 8))],
+    near_p, top, bottom = call(
+        product_kernel, [(32, 32, 256)] + [(32, 16, 256)] * 2, where, perturbations, control, hbm=(1, 2),
+        scratch=[vmem((32, 32, 256), F32), sems((2, 8))],
     )
+    above = lax.ppermute(bottom, "gx", ring(1))
+    below = lax.ppermute(top, "gx", ring(3))
+    edges = call(edge_kernel, [(2, 32, 256)], where, top, bottom)[0]
     side = lax.ppermute(edges, "gy", swap)
-    tops, bottoms = [None] * 2, [None] * 2
-    tops[0], bottoms[0], tops[1], bottoms[1] = call(
-        product_kernel, [(18, 16, 256)] * 2 + [(16, 16, 256)] * 2, where, near_p, near_c
-    )
-    tops[0] = tops[0].at[16:].set(side[:, :HALO])
-    bottoms[0] = bottoms[0].at[16:].set(side[:, HALO:])
-    aboves, belows = [None] * 2, [None] * 2
-    for part in range(2):
-        aboves[part] = lax.ppermute(bottoms[part], "gx", ring(1))
-        belows[part] = lax.ppermute(tops[part], "gx", ring(3))
+    side_above = lax.ppermute(side[:, HALO:], "gx", ring(1))
+    side_below = lax.ppermute(side[:, :HALO], "gx", ring(3))
     xh, xl, eh, el, right = call(
         table_kernel,
         [jax.ShapeDtypeStruct(s, BF16) for s in [(384, 256)] * 2 + [(512, 128)] * 2 + [(2, 1024, 256)]],
@@ -250,10 +246,10 @@
     )
     piece = {}
     for part in range(2):
-        extra = (side, eh, el) if part == 0 else (near,)
+        extra = (side_above, side, side_below, eh, el) if part == 0 else (near,)
         keep, give, *rest = call(
             functools.partial(filter_kernel, part), [(8, 32, 256)] * 2 + [(128, 128)] * (part == 0),
-            where, near_p, aboves[part], tops[part], bottoms[part], belows[part], xh, xl, right, *extra,
+            where, near_p, above, top, bottom, below, xh, xl, right, *extra,
             scratch=[vmem((512, 512), BF16)] * 2 + [vmem((256, 512), BF16)] * 2
             + [vmem((512, 256), F32), vmem((2, 512, 128), F32)],
             cost=2 * 10**9,
@@ -262,9 +258,7 @@
         got = lax.ppermute(give, "core", swap)
         for i in range(2):
             piece[((2, 1), (3, 0))[part][i]] = keep[4 * i : 4 * i + 4] + got[4 * i : 4 * i + 4]
-        if part == 0:
-            x2, x1 = (lax.ppermute(piece[d], "x", ring(d)) for d in (2, 1))
-    x3 = lax.ppermute(piece[3], "x", ring(3))
+    x2, x1, x3 = (lax.ppermute(piece[d], "x", ring(d)) for d in (2, 1, 3))
     cell = [(piece[0][e : e + 1] + x2[e : e + 1]) + (x1[e : e + 1] + x3[e : e + 1]) for e in range(4)]
     z2, z1, z3 = (lax.ppermute(cell[e], "z", ring(e)) for e in (2, 1, 3))
     return ((cell[0] + z2) + (z1 + z3)) * (1.0 / 31.0)

time: 49 us -> 48.2 us (0.984)
  waiting for transfers between devices: 12.5 us -> 11 us
  starting transfers between devices: 25.3 us -> 25.8 us
    ppermute x7, waiting for transfers between devices: 8.62 us -> 6.29 us  [the longest x3 3.66 us: body(): x2, x1, x3 = (lax.ppermute(piece[d], 'x', ring(d)) for d in (2, 1, 3))]
    ppermute x1, waiting for transfers between devices: 1.69 us -> 2.57 us  [body(): side = lax.ppermute(edges, 'gy', swap)]
  transfers between devices with their start and end apart: 13 -> 13, of which waited for: 8 -> 7; matrix products, arithmetic and copies ran while one was open for 0% -> 0% of each run, Pallas kernels for 15% -> 11%
where the time goes in v5:
time: 48.2 us; the launch traced here: 47.9 us
  starting transfers between devices  25.8 us (54%)
  waiting for transfers between devices  11 us (23%)
  Pallas kernels  10.1 us (21%)
  other arithmetic  0.73 us (2%)
    ppermute x3, starting transfers between devices, body(): z2, z1, z3 = (lax.ppermute(cell[e], 'z', ring(e)) for e in (2, 1, 3))  11.4 us
    pallas_call x5, Pallas kernels, call(): pl.pallas_call(kernel, out_shape=[o if isinstance(o, jax.ShapeDtypeStruct...  10.1 us
    ppermute x3, starting transfers between devices, body(): x2, x1, x3 = (lax.ppermute(piece[d], 'x', ring(d)) for d in (2, 1, 3))  6.43 us
    ppermute x3, waiting for transfers between devices, body(): x2, x1, x3 = (lax.ppermute(piece[d], 'x', ring(d)) for d in (2, 1, 3))  3.66 us
    ppermute x1, waiting for transfers between devices, body(): side = lax.ppermute(edges, 'gy', swap)  2.57 us
    ppermute x3, waiting for transfers between devices, body(): z2, z1, z3 = (lax.ppermute(cell[e], 'z', ring(e)) for e in (2, 1, 3))  2.15 us
    ppermute x1, starting transfers between devices, body(): side_below = lax.ppermute(side[:, :HALO], 'gx', ring(3))  1.88 us
    ppermute x1, starting transfers between devices, body(): side = lax.ppermute(edges, 'gy', swap)  1.78 us
  transfers between devices with their start and end apart: 13, of which 7 were waited for; matrix products, arithmetic and copies ran while one was open for 0% of the time, Pallas kernels for 11%

profile of v5, /device:TPU:8, one launch (start us, length us, event | category | flops | bytes accessed | tf_op | source)
XLA Modules:
  0.0 47.9 jit_solution(15253519735016227395)
XLA Ops:
  0.0 0.0 copy-start
  0.0 0.0 copy-start.1
  0.0 0.1 stack.23.where
  0.1 2.3 %shard_map.55 = (f32[32,32,256]{2,1,0:T(8,128)S(1)}, f32[32,16,256]{2,1,0:T(8,128)S(1)}, f32[32,16,256]{2,1,0:T(8,128)S(1)}) custom-call(s32[5]{0:T(128)S(1)} %stack.23.where, f32[1,32,32,256]{3,2,1,0:T(8,128)} %p_hbm.1, f32[32,32,256]{2,1,0:T(8,128)} %c_hbm.1), custom_call_target="tpu_custom_call" | custom-call | bytes 1048576 | tf_op jit(solution)/shard_map/pallas_call | solution.py:212
  2.4 1.7 %collective-permute-start = (f32[32,16,256]{2,1,0:T(8,128)S(1)}, f32[32,16,256]{2,1,0:T(8,128)S(1)}, u32[]{:S(2)}, u32[]{:S(2)}) collective-permute-start(f32[32,16,256]{2,1,0:T(8,128)S(1)} %get-tuple-element.19.bottom_ref), channel_id=1, source_target_pairs={{0,2},{2,4},{4,6},{6,0},{1,3},{3,5},{5,7},{7,1},{8,10},{10,12},{12... | collective-permute-start | bytes 1572872 | tf_op jit(solution)/shard_map/ppermute | solution.py:236
  4.0 0.7 %collective-permute-start.1 = (f32[32,16,256]{2,1,0:T(8,128)S(1)}, f32[32,16,256]{2,1,0:T(8,128)S(1)}, u32[]{:S(2)}, u32[]{:S(2)}) collective-permute-start(f32[32,16,256]{2,1,0:T(8,128)S(1)} %get-tuple-element.20.top_ref), channel_id=1, source_target_pairs={{0,6},{2,0},{4,2},{6,4},{1,7},{3,1},{5,3},{7,5},{8,14},{10,8},{12,... | collective-permute-start | bytes 1572872 | tf_op jit(solution)/shard_map/ppermute | solution.py:237
  4.7 1.3 %shard_map.57 = f32[2,32,256]{2,1,0:T(8,128)S(1)} custom-call(s32[5]{0:T(128)S(1)} %stack.23.where, f32[32,16,256]{2,1,0:T(8,128)S(1)} %get-tuple-element.20.top_ref, f32[32,16,256]{2,1,0:T(8,128)S(1)} %get-tuple-element.19.bottom_ref), custom_call_target="tpu_custom_call" | custom-call | bytes 1048576 | tf_op jit(solution)/shard_map/pallas_call | solution.py:212
  6.0 1.8 %collective-permute-start.2 = (f32[2,32,256]{2,1,0:T(8,128)S(1)}, f32[2,32,256]{2,1,0:T(8,128)S(1)}, u32[]{:S(2)}, u32[]{:S(2)}) collective-permute-start(f32[2,32,256]{2,1,0:T(8,128)S(1)} %shard_map.57), channel_id=1, source_target_pairs={{0,1},{1,0},{2,3},{3,2},{4,5},{5,4},{6,7},{7,6},{8,9},{9,8},{10,11... | collective-permute-start | bytes 196616 | tf_op jit(solution)/shard_map/ppermute | solution.py:239
  7.8 2.6 %collective-permute-done.2.refs_1_ = f32[2,32,256]{2,1,0:T(8,128)S(1)} collective-permute-done((f32[2,32,256]{2,1,0:T(8,128)S(1)}, f32[2,32,256]{2,1,0:T(8,128)S(1)}, u32[]{:S(2)}, u32[]{:S(2)}) %collective-permute-start.2) | collective-permute-done | bytes 65568 | tf_op jit(solution)/shard_map/ppermute | solution.py:239
  10.4 1.4 %collective-permute-start.3 = (f32[2,16,256]{2,1,0:T(8,128)S(1)}, f32[2,16,256]{2,1,0:T(8,128)S(1)}, u32[]{:S(2)}, u32[]{:S(2)}) collective-permute-start(f32[2,16,256]{2,1,0:T(8,128)S(1)} %get-tuple-element.39), channel_id=1, source_target_pairs={{0,2},{2,4},{4,6},{6,0},{1,3},{3,5},{5,7},{7,1},{8,10},{10,12},{12... | collective-permute-start | bytes 98312 | tf_op jit(solution)/shard_map/ppermute | solution.py:240
  11.7 1.9 %collective-permute-start.4 = (f32[2,16,256]{2,1,0:T(8,128)S(1)}, f32[2,16,256]{2,1,0:T(8,128)S(1)}, u32[]{:S(2)}, u32[]{:S(2)}) collective-permute-start(f32[2,16,256]{2,1,0:T(8,128)S(1)} %get-tuple-element.38), channel_id=1, source_target_pairs={{0,6},{2,0},{4,2},{6,4},{1,7},{3,1},{5,3},{7,5},{8,14},{10,8},{12,... | collective-permute-start | bytes 98312 | tf_op jit(solution)/shard_map/ppermute | solution.py:241
  13.6 0.0 copy-done
  13.6 0.0 copy-done.1
  13.6 1.9 %shard_map.56 = (bf16[384,256]{1,0:T(8,128)(2,1)S(1)}, bf16[384,256]{1,0:T(8,128)(2,1)S(1)}, bf16[512,128]{1,0:T(8,128)(2,1)S(1)}, bf16[512,128]{1,0:T(8,128)(2,1)S(1)}, bf16[2,1024,256]{2,1,0:T(8,128)(2,1)S(1)}) custom-call(s32[5]{0:T(128)S(1)} %stack.23.where, bf16[4,2,96,256]{3,2,1,0:T(8,128)(2,1)S(1)} %copy-done, bf16[2,2,64,128]{3,2,1,0:T(8,128)(2,1)S(1)} %copy-done.1, ...), custom_call_target="tpu_custom_call" | custom-call | bytes 1048576 | tf_op jit(solution)/shard_map/pallas_call | solution.py:212
  15.5 1.3 %collective-permute-done.3.refs_0_ = f32[2,16,256]{2,1,0:T(8,128)S(1)} collective-permute-done((f32[2,16,256]{2,1,0:T(8,128)S(1)}, f32[2,16,256]{2,1,0:T(8,128)S(1)}, u32[]{:S(2)}, u32[]{:S(2)}) %collective-permute-start.3) | collective-permute-done | bytes 32800 | tf_op jit(solution)/shard_map/ppermute | solution.py:240
  16.8 1.3 %collective-permute-done.4.refs_2_ = f32[2,16,256]{2,1,0:T(8,128)S(1)} collective-permute-done((f32[2,16,256]{2,1,0:T(8,128)S(1)}, f32[2,16,256]{2,1,0:T(8,128)S(1)}, u32[]{:S(2)}, u32[]{:S(2)}) %collective-permute-start.4) | collective-permute-done | bytes 32800 | tf_op jit(solution)/shard_map/ppermute | solution.py:241
  18.1 0.0 collective-permute-done.above_ref
  18.1 0.0 collective-permute-done.1.below_ref
  18.1 2.6 %shard_map.58 = (f32[8,32,256]{2,1,0:T(8,128)S(1)}, f32[8,32,256]{2,1,0:T(8,128)S(1)}, f32[128,128]{1,0:T(8,128)S(1)}) custom-call(s32[5]{0:T(128)S(1)} %stack.23.where, f32[32,32,256]{2,1,0:T(8,128)S(1)} %get-tuple-element.18.p_ref, f32[32,16,256]{2,1,0:T(8,128)S(1)} %collective-permute-done.above_ref, f32[32,16,256]{2,1,0:T(8,128)S(1)} %get-tuple-element.20.top_ref, ...), custom_call_target="tpu_custom_call" | custom-call | flops 2000000000 | bytes 1048576 | tf_op jit(solution)/shard_map/pallas_call | solution.py:212
  20.7 0.1 collective-permute-start.6
  20.8 2.1 %shard_map.59 = (f32[8,32,256]{2,1,0:T(8,128)S(1)}, f32[8,32,256]{2,1,0:T(8,128)S(1)}) custom-call(s32[5]{0:T(128)S(1)} %stack.23.where, f32[32,32,256]{2,1,0:T(8,128)S(1)} %get-tuple-element.18.p_ref, f32[32,16,256]{2,1,0:T(8,128)S(1)} %collective-permute-done.above_ref, f32[32,16,256]{2,1,0:T(8,128)S(1)} %get-tuple-element.20.top_ref, ...), custom_call_target="tpu_custom_call" | custom-call | flops 2000000000 | bytes 1048576 | tf_op jit(solution)/shard_map/pallas_call | solution.py:212
  22.9 0.6 %collective-permute-start.5 = (f32[8,32,256]{2,1,0:T(8,128)S(1)}, f32[8,32,256]{2,1,0:T(8,128)S(1)}, u32[]{:S(2)}, u32[]{:S(2)}) collective-permute-start(f32[8,32,256]{2,1,0:T(8,128)S(1)} %get-tuple-element.28), channel_id=1, source_target_pairs={{0,8},{8,0},{1,9},{9,1},{2,10},{10,2},{3,11},{11,3},{4,12},{12,4},... | collective-permute-start | bytes 786440 | tf_op jit(solution)/shard_map/ppermute | solution.py:258
  23.5 0.0 collective-permute-done.6
  23.5 3.1 %collective-permute-start.7 = (f32[4,32,256]{2,1,0:T(8,128)S(1)}, f32[4,32,256]{2,1,0:T(8,128)S(1)}, u32[]{:S(2)}, u32[]{:S(2)}) collective-permute-start(f32[4,32,256]{2,1,0:T(8,128)S(1)} %get-tuple-element.36), channel_id=1, source_target_pairs={{0,128},{64,192},{128,0},{192,64},{1,129},{65,193},{129,1},{193,65... | collective-permute-start | bytes 393224 | tf_op jit(solution)/shard_map/ppermute | solution.py:261
  26.6 0.6 %collective-permute-start.8 = (f32[4,32,256]{2,1,0:T(8,128)S(1)}, f32[4,32,256]{2,1,0:T(8,128)S(1)}, u32[]{:S(2)}, u32[]{:S(2)}) collective-permute-start(f32[4,32,256]{2,1,0:T(8,128)S(1)} %get-tuple-element.37), channel_id=1, source_target_pairs={{0,64},{64,128},{128,192},{192,0},{1,65},{65,129},{129,193},{193,1... | collective-permute-start | bytes 393224 | tf_op jit(solution)/shard_map/ppermute | solution.py:261
  27.2 0.0 collective-permute-done.5
  27.3 2.7 %collective-permute-start.9 = (f32[4,32,256]{2,1,0:T(8,128)S(1)}, f32[4,32,256]{2,1,0:T(8,128)S(1)}, u32[]{:S(2)}, u32[]{:S(2)}) collective-permute-start(f32[4,32,256]{2,1,0:T(8,128)S(1)} %get-tuple-element.35), channel_id=1, source_target_pairs={{0,192},{64,0},{128,64},{192,128},{1,193},{65,1},{129,65},{193,129... | collective-permute-start | bytes 393224 | tf_op jit(solution)/shard_map/ppermute | solution.py:261
  30.0 1.5 %collective-permute-done.7 = f32[4,32,256]{2,1,0:T(8,128)S(1)} collective-permute-done((f32[4,32,256]{2,1,0:T(8,128)S(1)}, f32[4,32,256]{2,1,0:T(8,128)S(1)}, u32[]{:S(2)}, u32[]{:S(2)}) %collective-permute-start.7) | collective-permute-done | bytes 131104 | tf_op jit(solution)/shard_map/ppermute | solution.py:261
  31.5 2.2 %collective-permute-done.8 = f32[4,32,256]{2,1,0:T(8,128)S(1)} collective-permute-done((f32[4,32,256]{2,1,0:T(8,128)S(1)}, f32[4,32,256]{2,1,0:T(8,128)S(1)}, u32[]{:S(2)}, u32[]{:S(2)}) %collective-permute-start.8) | collective-permute-done | bytes 131104 | tf_op jit(solution)/shard_map/ppermute | solution.py:261
  33.6 0.0 collective-permute-done.9
  33.7 7.3 %collective-permute-start.10 = (f32[1,32,256]{2,1,0:T(8,128)S(1)}, f32[1,32,256]{2,1,0:T(8,128)S(1)}, u32[]{:S(2)}, u32[]{:S(2)}) collective-permute-start(f32[1,32,256]{2,1,0:T(8,128)S(1)} %get-tuple-element.33), channel_id=1, source_target_pairs={{0,32},{16,48},{32,0},{48,16},{1,33},{17,49},{33,1},{49,17},{2,34}... | collective-permute-start | bytes 98312 | tf_op jit(solution)/shard_map/ppermute | solution.py:263
  41.0 1.5 %collective-permute-start.11 = (f32[1,32,256]{2,1,0:T(8,128)S(1)}, f32[1,32,256]{2,1,0:T(8,128)S(1)}, u32[]{:S(2)}, u32[]{:S(2)}) collective-permute-start(f32[1,32,256]{2,1,0:T(8,128)S(1)} %get-tuple-element.32), channel_id=1, source_target_pairs={{0,16},{16,32},{32,48},{48,0},{1,17},{17,33},{33,49},{49,1},{2,18}... | collective-permute-start | bytes 98312 | tf_op jit(solution)/shard_map/ppermute | solution.py:263
  42.4 2.7 %collective-permute-start.12 = (f32[1,32,256]{2,1,0:T(8,128)S(1)}, f32[1,32,256]{2,1,0:T(8,128)S(1)}, u32[]{:S(2)}, u32[]{:S(2)}) collective-permute-start(f32[1,32,256]{2,1,0:T(8,128)S(1)} %get-tuple-element.31), channel_id=1, source_target_pairs={{0,48},{16,0},{32,16},{48,32},{1,49},{17,1},{33,17},{49,33},{2,50}... | collective-permute-start | bytes 98312 | tf_op jit(solution)/shard_map/ppermute | solution.py:263
  45.1 0.0 collective-permute-done.10
  45.1 1.9 %collective-permute-done.11 = f32[1,32,256]{2,1,0:T(8,128)S(1)} collective-permute-done((f32[1,32,256]{2,1,0:T(8,128)S(1)}, f32[1,32,256]{2,1,0:T(8,128)S(1)}, u32[]{:S(2)}, u32[]{:S(2)}) %collective-permute-start.11) | collective-permute-done | bytes 32800 | tf_op jit(solution)/shard_map/ppermute | solution.py:263
  47.0 0.3 collective-permute-done.12
  47.2 0.6 %fusion.6 = f32[1,32,256]{2,1,0:T(8,128)} fusion(f32[1,32,256]{2,1,0:T(8,128)S(1)} %collective-permute-done.10, f32[4,32,256]{2,1,0:T(8,128)S(1)} %collective-permute-done.9, f32[4,32,256]{2,1,0:T(8,128)S(1)} %collective-permute-done.8, f32[4,32,256]{2,1,0:T(8,128)S(1)} %collective-permute-done.7, f32[4,32,256]{2,1,0:T(8,128)S(1)} %get-tuple-element.34, ...), kind=kLoop, calls=%fused_computation.17 | loop fusion | flops 57344 | bytes 262144 | tf_op jit(solution)/shard_map/mul | solution.py:264
  (4 shorter events, 0.1 us)
Async XLA Ops:
  0.0 13.6 %copy-start = (bf16[4,2,96,256]{3,2,1,0:T(8,128)(2,1)S(1)}, bf16[4,2,96,256]{3,2,1,0:T(8,128)(2,1)}, u32[]{:S(2)}) copy-start(bf16[4,2,96,256]{3,2,1,0:T(8,128)(2,1)} %constant.27.clone.left_ref) | copy-start | bytes 1179652
  0.0 13.6 %copy-start.1 = (bf16[2,2,64,128]{3,2,1,0:T(8,128)(2,1)S(1)}, bf16[2,2,64,128]{3,2,1,0:T(8,128)(2,1)}, u32[]{:S(2)}) copy-start(bf16[2,2,64,128]{3,2,1,0:T(8,128)(2,1)} %constant.29.clone.edge_ref) | copy-start | bytes 196612
  2.4 15.7 %collective-permute-start = (f32[32,16,256]{2,1,0:T(8,128)S(1)}, f32[32,16,256]{2,1,0:T(8,128)S(1)}, u32[]{:S(2)}, u32[]{:S(2)}) collective-permute-start(f32[32,16,256]{2,1,0:T(8,128)S(1)} %get-tuple-element.19.bottom_ref), channel_id=1, source_target_pairs={{0,2},{2,4},{4,6},{6,0},{1,3},{3,5},{5,7},{7,1},{8,10},{10,12},{12... | collective-permute-start | bytes 1572872 | tf_op jit(solution)/shard_map/ppermute | solution.py:236
  4.0 14.1 %collective-permute-start.1 = (f32[32,16,256]{2,1,0:T(8,128)S(1)}, f32[32,16,256]{2,1,0:T(8,128)S(1)}, u32[]{:S(2)}, u32[]{:S(2)}) collective-permute-start(f32[32,16,256]{2,1,0:T(8,128)S(1)} %get-tuple-element.20.top_ref), channel_id=1, source_target_pairs={{0,6},{2,0},{4,2},{6,4},{1,7},{3,1},{5,3},{7,5},{8,14},{10,8},{12,... | collective-permute-start | bytes 1572872 | tf_op jit(solution)/shard_map/ppermute | solution.py:237
  6.0 4.4 %collective-permute-start.2 = (f32[2,32,256]{2,1,0:T(8,128)S(1)}, f32[2,32,256]{2,1,0:T(8,128)S(1)}, u32[]{:S(2)}, u32[]{:S(2)}) collective-permute-start(f32[2,32,256]{2,1,0:T(8,128)S(1)} %shard_map.57), channel_id=1, source_target_pairs={{0,1},{1,0},{2,3},{3,2},{4,5},{5,4},{6,7},{7,6},{8,9},{9,8},{10,11... | collective-permute-start | bytes 196616 | tf_op jit(solution)/shard_map/ppermute | solution.py:239
  10.4 6.5 %collective-permute-start.3 = (f32[2,16,256]{2,1,0:T(8,128)S(1)}, f32[2,16,256]{2,1,0:T(8,128)S(1)}, u32[]{:S(2)}, u32[]{:S(2)}) collective-permute-start(f32[2,16,256]{2,1,0:T(8,128)S(1)} %get-tuple-element.39), channel_id=1, source_target_pairs={{0,2},{2,4},{4,6},{6,0},{1,3},{3,5},{5,7},{7,1},{8,10},{10,12},{12... | collective-permute-start | bytes 98312 | tf_op jit(solution)/shard_map/ppermute | solution.py:240
  11.7 6.4 %collective-permute-start.4 = (f32[2,16,256]{2,1,0:T(8,128)S(1)}, f32[2,16,256]{2,1,0:T(8,128)S(1)}, u32[]{:S(2)}, u32[]{:S(2)}) collective-permute-start(f32[2,16,256]{2,1,0:T(8,128)S(1)} %get-tuple-element.38), channel_id=1, source_target_pairs={{0,6},{2,0},{4,2},{6,4},{1,7},{3,1},{5,3},{7,5},{8,14},{10,8},{12,... | collective-permute-start | bytes 98312 | tf_op jit(solution)/shard_map/ppermute | solution.py:241
  20.7 2.8 %collective-permute-start.6 = (f32[8,32,256]{2,1,0:T(8,128)S(1)}, f32[8,32,256]{2,1,0:T(8,128)S(1)}, u32[]{:S(2)}, u32[]{:S(2)}) collective-permute-start(f32[8,32,256]{2,1,0:T(8,128)S(1)} %get-tuple-element.30), channel_id=1, source_target_pairs={{0,8},{8,0},{1,9},{9,1},{2,10},{10,2},{3,11},{11,3},{4,12},{12,4},... | collective-permute-start | bytes 786440 | tf_op jit(solution)/shard_map/ppermute | solution.py:258
  22.9 4.3 %collective-permute-start.5 = (f32[8,32,256]{2,1,0:T(8,128)S(1)}, f32[8,32,256]{2,1,0:T(8,128)S(1)}, u32[]{:S(2)}, u32[]{:S(2)}) collective-permute-start(f32[8,32,256]{2,1,0:T(8,128)S(1)} %get-tuple-element.28), channel_id=1, source_target_pairs={{0,8},{8,0},{1,9},{9,1},{2,10},{10,2},{3,11},{11,3},{4,12},{12,4},... | collective-permute-start | bytes 786440 | tf_op jit(solution)/shard_map/ppermute | solution.py:258
  23.5 8.0 %collective-permute-start.7 = (f32[4,32,256]{2,1,0:T(8,128)S(1)}, f32[4,32,256]{2,1,0:T(8,128)S(1)}, u32[]{:S(2)}, u32[]{:S(2)}) collective-permute-start(f32[4,32,256]{2,1,0:T(8,128)S(1)} %get-tuple-element.36), channel_id=1, source_target_pairs={{0,128},{64,192},{128,0},{192,64},{1,129},{65,193},{129,1},{193,65... | collective-permute-start | bytes 393224 | tf_op jit(solution)/shard_map/ppermute | solution.py:261
  26.6 7.0 %collective-permute-start.8 = (f32[4,32,256]{2,1,0:T(8,128)S(1)}, f32[4,32,256]{2,1,0:T(8,128)S(1)}, u32[]{:S(2)}, u32[]{:S(2)}) collective-permute-start(f32[4,32,256]{2,1,0:T(8,128)S(1)} %get-tuple-element.37), channel_id=1, source_target_pairs={{0,64},{64,128},{128,192},{192,0},{1,65},{65,129},{129,193},{193,1... | collective-permute-start | bytes 393224 | tf_op jit(solution)/shard_map/ppermute | solution.py:261
  27.3 6.4 %collective-permute-start.9 = (f32[4,32,256]{2,1,0:T(8,128)S(1)}, f32[4,32,256]{2,1,0:T(8,128)S(1)}, u32[]{:S(2)}, u32[]{:S(2)}) collective-permute-start(f32[4,32,256]{2,1,0:T(8,128)S(1)} %get-tuple-element.35), channel_id=1, source_target_pairs={{0,192},{64,0},{128,64},{192,128},{1,193},{65,1},{129,65},{193,129... | collective-permute-start | bytes 393224 | tf_op jit(solution)/shard_map/ppermute | solution.py:261
  33.7 11.4 %collective-permute-start.10 = (f32[1,32,256]{2,1,0:T(8,128)S(1)}, f32[1,32,256]{2,1,0:T(8,128)S(1)}, u32[]{:S(2)}, u32[]{:S(2)}) collective-permute-start(f32[1,32,256]{2,1,0:T(8,128)S(1)} %get-tuple-element.33), channel_id=1, source_target_pairs={{0,32},{16,48},{32,0},{48,16},{1,33},{17,49},{33,1},{49,17},{2,34}... | collective-permute-start | bytes 98312 | tf_op jit(solution)/shard_map/ppermute | solution.py:263
  41.0 6.0 %collective-permute-start.11 = (f32[1,32,256]{2,1,0:T(8,128)S(1)}, f32[1,32,256]{2,1,0:T(8,128)S(1)}, u32[]{:S(2)}, u32[]{:S(2)}) collective-permute-start(f32[1,32,256]{2,1,0:T(8,128)S(1)} %get-tuple-element.32), channel_id=1, source_target_pairs={{0,16},{16,32},{32,48},{48,0},{1,17},{17,33},{33,49},{49,1},{2,18}... | collective-permute-start | bytes 98312 | tf_op jit(solution)/shard_map/ppermute | solution.py:263
  42.4 4.8 %collective-permute-start.12 = (f32[1,32,256]{2,1,0:T(8,128)S(1)}, f32[1,32,256]{2,1,0:T(8,128)S(1)}, u32[]{:S(2)}, u32[]{:S(2)}) collective-permute-start(f32[1,32,256]{2,1,0:T(8,128)S(1)} %get-tuple-element.31), channel_id=1, source_target_pairs={{0,48},{16,0},{32,16},{48,32},{1,49},{17,1},{33,17},{49,33},{2,50}... | collective-permute-start | bytes 98312 | tf_op jit(solution)/shard_map/ppermute | solution.py:263

commit v6 on v5

--- a/solution.py
+++ b/solution.py
@@ -7,6 +7,7 @@
 from jax.experimental import pallas as pl
 from jax.experimental.pallas import tpu as pltpu
 from jax.sharding import Mesh, PartitionSpec as P
+
 
 F32, BF16 = jnp.float32, jnp.bfloat16
 HALO = 16
@@ -116,14 +117,14 @@
 
 
 def table_kernel(
-    where, left_ref, edge_ref, right_hbm, xh_ref, xl_ref, eh_ref, el_ref, right_ref, sems
+    where, left_ref, edge_ref, patch_ref, right_hbm, xh_ref, xl_ref, eh_ref, el_ref, right_ref, sems
 ):
     gx, gy = where[1], where[2]
     copies = []
     for h in range(2):
         for k in range(4):
             at = pl.ds(256 * k, 256)
-            copies.append(pltpu.make_async_copy(right_hbm.at[gy, h, at], right_ref.at[h, at], sems.at[h, k]))
+            copies.append(pltpu.make_async_copy(right_hbm.at[h, at], right_ref.at[h, at], sems.at[h, k]))
     for copy in copies:
         copy.start()
     lane = lax.broadcasted_iota(jnp.int32, (1, 256), 1)
@@ -144,6 +145,13 @@
                 e_ref[at : at + 16] = jnp.where(narrow // 16 == g, rows, jnp.zeros_like(rows)).astype(BF16)
     for copy in copies:
         copy.wait()
+
+    @pl.when(gy == 1)
+    def _():
+        for h in range(2):
+            for t in range(4):
+                right_ref[h, 256 * t : 256 * t + 32, :128] = patch_ref[h, 0, t]
+                right_ref[h, 256 * t + 224 : 256 * t + 256, 128:] = patch_ref[h, 1, t]
 
 
 def filter_kernel(
@@ -199,7 +207,7 @@
         first = 16 * part + 4 * g
         q = p_ref[first : first + 4] * alpha.reshape(4, 32, 256)
         for j in range(2):
-            to = 4 * (g // 2) + lax.rem(2 * (g % 2) + j + 4 - z, 4)
+            to = 4 * (g // 2) + lax.rem(6 + z - (2 * (g % 2) + j), 4)
             keep_ref[to] = jnp.where(core == 0, q[2 * j], q[2 * j + 1])
             send_ref[to] = jnp.where(core == 0, q[2 * j + 1], q[2 * j])
 
@@ -224,7 +232,10 @@
     x, z, core, gx, gy = (lax.axis_index(a) for a in ("x", "z", "core", "gx", "gy"))
     where = jnp.stack([core, gx, gy, x, z]).astype(jnp.int32)
     left = jnp.asarray(halves(left_table(128, 4)))
-    right, edge = (jnp.asarray(halves(t)) for t in right_tables(512, 2))
+    right, edge = (halves(t) for t in right_tables(512, 2))
+    blocks = right[1].reshape(2, 4, 256, 256)
+    patch = jnp.asarray(np.stack([blocks[:, :, :32, :128], blocks[:, :, 224:, 128:]], axis=1))
+    right, edge = jnp.asarray(right[0]), jnp.asarray(edge)
     vmem, sems = pltpu.VMEM, pltpu.SemaphoreType.DMA
 
     ring = lambda d: [(i, (i + d) % 4) for i in range(4)]
@@ -242,7 +253,7 @@
     xh, xl, eh, el, right = call(
         table_kernel,
         [jax.ShapeDtypeStruct(s, BF16) for s in [(384, 256)] * 2 + [(512, 128)] * 2 + [(2, 1024, 256)]],
-        where, left, edge, right, hbm=(3,), scratch=[sems((2, 4))],
+        where, left, edge, patch, right, hbm=(4,), scratch=[sems((2, 4))],
     )
     piece = {}
     for part in range(2):
@@ -257,11 +268,16 @@
         near = rest[0] if rest else None
         got = lax.ppermute(give, "core", swap)
         for i in range(2):
-            piece[((2, 1), (3, 0))[part][i]] = keep[4 * i : 4 * i + 4] + got[4 * i : 4 * i + 4]
-    x2, x1, x3 = (lax.ppermute(piece[d], "x", ring(d)) for d in (2, 1, 3))
-    cell = [(piece[0][e : e + 1] + x2[e : e + 1]) + (x1[e : e + 1] + x3[e : e + 1]) for e in range(4)]
-    z2, z1, z3 = (lax.ppermute(cell[e], "z", ring(e)) for e in (2, 1, 3))
-    return ((cell[0] + z2) + (z1 + z3)) * (1.0 / 31.0)
+            for wave in range(2):
+                at = slice(4 * i + 2 * wave, 4 * i + 2 * wave + 2)
+                piece[((2, 1), (3, 0))[part][i], wave] = keep[at] + got[at]
+    waves = []
+    for wave in range(2):
+        x2, x1, x3 = (lax.ppermute(piece[d, wave], "x", ring(d)) for d in (2, 1, 3))
+        waves.append([(piece[0, wave][i : i + 1] + x2[i : i + 1]) + (x1[i : i + 1] + x3[i : i + 1]) for i in range(2)])
+    (far, next_), (own, last) = waves
+    z2, z1, z3 = (lax.ppermute(cell, "z", ring(e)) for e, cell in ((2, far), (1, next_), (3, last)))
+    return ((own + z2) + (z1 + z3)) * (1.0 / 31.0)
 
 
 def solution(mesh):

time: 48.2 us -> 50.3 us (1.044)
  starting transfers between devices: 25.8 us -> 29.3 us
  waiting for transfers between devices: 11 us -> 9.77 us
    ppermute x6 -> x9, starting transfers between devices: 17.8 us -> 21.3 us  [the longest x3 11.7 us: body(): lax.ppermute(cell, 'z', ring(e))]
    ppermute x6 -> x9, waiting for transfers between devices: 5.8 us -> 4.56 us  [the longest x3 4.55 us: body(): lax.ppermute(cell, 'z', ring(e))]
  transfers between devices with their start and end apart: 13 -> 16, of which waited for: 7 -> 5; matrix products, arithmetic and copies ran while one was open for 0% -> 0% of each run, Pallas kernels for 11% -> 10%
where the time goes in v6:
time: 50.3 us; the launch traced here: 50.1 us
  starting transfers between devices  29.3 us (58%)
  Pallas kernels  10.1 us (20%)
  waiting for transfers between devices  9.77 us (19%)
  other arithmetic  0.73 us (1%)
    ppermute x3, starting transfers between devices, body(): lax.ppermute(cell, 'z', ring(e))  11.7 us
    pallas_call x5, Pallas kernels, call(): pl.pallas_call(kernel, out_shape=[o if isinstance(o, jax.ShapeDtypeStruct...  10.1 us
    ppermute x6, starting transfers between devices, body(): x2, x1, x3 = (lax.ppermute(piece[d, wave], 'x', ring(d)) for d in (2, 1, 3))  9.66 us
    ppermute x3, waiting for transfers between devices, body(): lax.ppermute(cell, 'z', ring(e))  4.55 us
    ppermute x1, waiting for transfers between devices, body(): side = lax.ppermute(edges, 'gy', swap)  2.58 us
    ppermute x1, starting transfers between devices, body(): side_below = lax.ppermute(side[:, :HALO], 'gx', ring(3))  1.88 us
    ppermute x1, starting transfers between devices, body(): side = lax.ppermute(edges, 'gy', swap)  1.77 us
    ppermute x1, starting transfers between devices, body(): above = lax.ppermute(bottom, 'gx', ring(1))  1.65 us
  transfers between devices with their start and end apart: 16, of which 5 were waited for; matrix products, arithmetic and copies ran while one was open for 0% of the time, Pallas kernels for 10%

profile of v6, /device:TPU:8, one launch (start us, length us, event | category | flops | bytes accessed | tf_op | source)
XLA Modules:
  0.0 50.1 jit_solution(14543627223019520841)
XLA Ops:
  0.0 0.1 stack.23.where
  0.1 2.3 %shard_map.64 = (f32[32,32,256]{2,1,0:T(8,128)S(1)}, f32[32,16,256]{2,1,0:T(8,128)S(1)}, f32[32,16,256]{2,1,0:T(8,128)S(1)}) custom-call(s32[5]{0:T(128)S(1)} %stack.23.where, f32[1,32,32,256]{3,2,1,0:T(8,128)} %p_hbm.1, f32[32,32,256]{2,1,0:T(8,128)} %c_hbm.1), custom_call_target="tpu_custom_call" | custom-call | bytes 1048576 | tf_op jit(solution)/shard_map/pallas_call | solution.py:220
  2.4 1.7 %collective-permute-start = (f32[32,16,256]{2,1,0:T(8,128)S(1)}, f32[32,16,256]{2,1,0:T(8,128)S(1)}, u32[]{:S(2)}, u32[]{:S(2)}) collective-permute-start(f32[32,16,256]{2,1,0:T(8,128)S(1)} %get-tuple-element.19.bottom_ref), channel_id=1, source_target_pairs={{0,2},{2,4},{4,6},{6,0},{1,3},{3,5},{5,7},{7,1},{8,10},{10,12},{12... | collective-permute-start | bytes 1572872 | tf_op jit(solution)/shard_map/ppermute | solution.py:247
  4.0 0.0 copy-start
  4.0 0.7 %collective-permute-start.1 = (f32[32,16,256]{2,1,0:T(8,128)S(1)}, f32[32,16,256]{2,1,0:T(8,128)S(1)}, u32[]{:S(2)}, u32[]{:S(2)}) collective-permute-start(f32[32,16,256]{2,1,0:T(8,128)S(1)} %get-tuple-element.20.top_ref), channel_id=1, source_target_pairs={{0,6},{2,0},{4,2},{6,4},{1,7},{3,1},{5,3},{7,5},{8,14},{10,8},{12,... | collective-permute-start | bytes 1572872 | tf_op jit(solution)/shard_map/ppermute | solution.py:248
  4.7 0.0 copy-start.2
  4.7 1.3 %shard_map.66 = f32[2,32,256]{2,1,0:T(8,128)S(1)} custom-call(s32[5]{0:T(128)S(1)} %stack.23.where, f32[32,16,256]{2,1,0:T(8,128)S(1)} %get-tuple-element.20.top_ref, f32[32,16,256]{2,1,0:T(8,128)S(1)} %get-tuple-element.19.bottom_ref), custom_call_target="tpu_custom_call" | custom-call | bytes 1048576 | tf_op jit(solution)/shard_map/pallas_call | solution.py:220
  6.0 0.0 copy-start.1
  6.0 1.8 %collective-permute-start.2 = (f32[2,32,256]{2,1,0:T(8,128)S(1)}, f32[2,32,256]{2,1,0:T(8,128)S(1)}, u32[]{:S(2)}, u32[]{:S(2)}) collective-permute-start(f32[2,32,256]{2,1,0:T(8,128)S(1)} %shard_map.66), channel_id=1, source_target_pairs={{0,1},{1,0},{2,3},{3,2},{4,5},{5,4},{6,7},{7,6},{8,9},{9,8},{10,11... | collective-permute-start | bytes 196616 | tf_op jit(solution)/shard_map/ppermute | solution.py:250
  7.8 2.6 %collective-permute-done.2.refs_1_ = f32[2,32,256]{2,1,0:T(8,128)S(1)} collective-permute-done((f32[2,32,256]{2,1,0:T(8,128)S(1)}, f32[2,32,256]{2,1,0:T(8,128)S(1)}, u32[]{:S(2)}, u32[]{:S(2)}) %collective-permute-start.2) | collective-permute-done | bytes 65568 | tf_op jit(solution)/shard_map/ppermute | solution.py:250
  10.4 1.3 %collective-permute-start.3 = (f32[2,16,256]{2,1,0:T(8,128)S(1)}, f32[2,16,256]{2,1,0:T(8,128)S(1)}, u32[]{:S(2)}, u32[]{:S(2)}) collective-permute-start(f32[2,16,256]{2,1,0:T(8,128)S(1)} %get-tuple-element.42), channel_id=1, source_target_pairs={{0,2},{2,4},{4,6},{6,0},{1,3},{3,5},{5,7},{7,1},{8,10},{10,12},{12... | collective-permute-start | bytes 98312 | tf_op jit(solution)/shard_map/ppermute | solution.py:251
  11.7 1.9 %collective-permute-start.4 = (f32[2,16,256]{2,1,0:T(8,128)S(1)}, f32[2,16,256]{2,1,0:T(8,128)S(1)}, u32[]{:S(2)}, u32[]{:S(2)}) collective-permute-start(f32[2,16,256]{2,1,0:T(8,128)S(1)} %get-tuple-element.41), channel_id=1, source_target_pairs={{0,6},{2,0},{4,2},{6,4},{1,7},{3,1},{5,3},{7,5},{8,14},{10,8},{12,... | collective-permute-start | bytes 98312 | tf_op jit(solution)/shard_map/ppermute | solution.py:252
  13.6 0.0 copy-done
  13.6 0.0 copy-done.2
  13.6 0.0 copy-done.1
  13.6 1.9 %shard_map.65 = (bf16[384,256]{1,0:T(8,128)(2,1)S(1)}, bf16[384,256]{1,0:T(8,128)(2,1)S(1)}, bf16[512,128]{1,0:T(8,128)(2,1)S(1)}, bf16[512,128]{1,0:T(8,128)(2,1)S(1)}, bf16[2,1024,256]{2,1,0:T(8,128)(2,1)S(1)}) custom-call(s32[5]{0:T(128)S(1)} %stack.23.where, bf16[4,2,96,256]{3,2,1,0:T(8,128)(2,1)S(1)} %copy-done, bf16[2,2,64,128]{3,2,1,0:T(8,128)(2,1)S(1)} %copy-done.2, ...), custom_call_target="tpu_custom_call" | custom-call | bytes 1048576 | tf_op jit(solution)/shard_map/pallas_call | solution.py:220
  15.5 1.3 %collective-permute-done.3.refs_0_ = f32[2,16,256]{2,1,0:T(8,128)S(1)} collective-permute-done((f32[2,16,256]{2,1,0:T(8,128)S(1)}, f32[2,16,256]{2,1,0:T(8,128)S(1)}, u32[]{:S(2)}, u32[]{:S(2)}) %collective-permute-start.3) | collective-permute-done | bytes 32800 | tf_op jit(solution)/shard_map/ppermute | solution.py:251
  16.8 1.3 %collective-permute-done.4.refs_2_ = f32[2,16,256]{2,1,0:T(8,128)S(1)} collective-permute-done((f32[2,16,256]{2,1,0:T(8,128)S(1)}, f32[2,16,256]{2,1,0:T(8,128)S(1)}, u32[]{:S(2)}, u32[]{:S(2)}) %collective-permute-start.4) | collective-permute-done | bytes 32800 | tf_op jit(solution)/shard_map/ppermute | solution.py:252
  18.1 0.0 collective-permute-done.above_ref
  18.1 0.0 collective-permute-done.1.below_ref
  18.1 2.6 %shard_map.67 = (f32[8,32,256]{2,1,0:T(8,128)S(1)}, f32[8,32,256]{2,1,0:T(8,128)S(1)}, f32[128,128]{1,0:T(8,128)S(1)}) custom-call(s32[5]{0:T(128)S(1)} %stack.23.where, f32[32,32,256]{2,1,0:T(8,128)S(1)} %get-tuple-element.18.p_ref, f32[32,16,256]{2,1,0:T(8,128)S(1)} %collective-permute-done.above_ref, f32[32,16,256]{2,1,0:T(8,128)S(1)} %get-tuple-element.20.top_ref, ...), custom_call_target="tpu_custom_call" | custom-call | flops 2000000000 | bytes 1048576 | tf_op jit(solution)/shard_map/pallas_call | solution.py:220
  20.7 0.1 collective-permute-start.6
  20.8 2.1 %shard_map.68 = (f32[8,32,256]{2,1,0:T(8,128)S(1)}, f32[8,32,256]{2,1,0:T(8,128)S(1)}) custom-call(s32[5]{0:T(128)S(1)} %stack.23.where, f32[32,32,256]{2,1,0:T(8,128)S(1)} %get-tuple-element.18.p_ref, f32[32,16,256]{2,1,0:T(8,128)S(1)} %collective-permute-done.above_ref, f32[32,16,256]{2,1,0:T(8,128)S(1)} %get-tuple-element.20.top_ref, ...), custom_call_target="tpu_custom_call" | custom-call | flops 2000000000 | bytes 1048576 | tf_op jit(solution)/shard_map/pallas_call | solution.py:220
  22.9 0.6 %collective-permute-start.5 = (f32[8,32,256]{2,1,0:T(8,128)S(1)}, f32[8,32,256]{2,1,0:T(8,128)S(1)}, u32[]{:S(2)}, u32[]{:S(2)}) collective-permute-start(f32[8,32,256]{2,1,0:T(8,128)S(1)} %get-tuple-element.28), channel_id=1, source_target_pairs={{0,8},{8,0},{1,9},{9,1},{2,10},{10,2},{3,11},{11,3},{4,12},{12,4},... | collective-permute-start | bytes 786440 | tf_op jit(solution)/shard_map/ppermute | solution.py:269
  23.5 0.0 collective-permute-done.6
  23.5 3.1 %collective-permute-start.7 = (f32[2,32,256]{2,1,0:T(8,128)S(1)}, f32[2,32,256]{2,1,0:T(8,128)S(1)}, u32[]{:S(2)}, u32[]{:S(2)}) collective-permute-start(f32[2,32,256]{2,1,0:T(8,128)S(1)} %get-tuple-element.35), channel_id=1, source_target_pairs={{0,128},{64,192},{128,0},{192,64},{1,129},{65,193},{129,1},{193,65... | collective-permute-start | bytes 196616 | tf_op jit(solution)/shard_map/ppermute | solution.py:276
  26.6 0.6 %collective-permute-start.8 = (f32[2,32,256]{2,1,0:T(8,128)S(1)}, f32[2,32,256]{2,1,0:T(8,128)S(1)}, u32[]{:S(2)}, u32[]{:S(2)}) collective-permute-start(f32[2,32,256]{2,1,0:T(8,128)S(1)} %get-tuple-element.38), channel_id=1, source_target_pairs={{0,64},{64,128},{128,192},{192,0},{1,65},{65,129},{129,193},{193,1... | collective-permute-start | bytes 196616 | tf_op jit(solution)/shard_map/ppermute | solution.py:276
  27.2 0.0 collective-permute-done.5
  27.3 2.7 %collective-permute-start.9 = (f32[2,32,256]{2,1,0:T(8,128)S(1)}, f32[2,32,256]{2,1,0:T(8,128)S(1)}, u32[]{:S(2)}, u32[]{:S(2)}) collective-permute-start(f32[2,32,256]{2,1,0:T(8,128)S(1)} %get-tuple-element.34), channel_id=1, source_target_pairs={{0,192},{64,0},{128,64},{192,128},{1,193},{65,1},{129,65},{193,129... | collective-permute-start | bytes 196616 | tf_op jit(solution)/shard_map/ppermute | solution.py:276
  30.0 0.0 collective-permute-start.10
  30.0 1.0 %collective-permute-start.11 = (f32[2,32,256]{2,1,0:T(8,128)S(1)}, f32[2,32,256]{2,1,0:T(8,128)S(1)}, u32[]{:S(2)}, u32[]{:S(2)}) collective-permute-start(f32[2,32,256]{2,1,0:T(8,128)S(1)} %get-tuple-element.36), channel_id=1, source_target_pairs={{0,64},{64,128},{128,192},{192,0},{1,65},{65,129},{129,193},{193,1... | collective-permute-start | bytes 196616 | tf_op jit(solution)/shard_map/ppermute | solution.py:276
  30.9 0.0 collective-permute-done.7
  30.9 2.3 %collective-permute-start.12 = (f32[2,32,256]{2,1,0:T(8,128)S(1)}, f32[2,32,256]{2,1,0:T(8,128)S(1)}, u32[]{:S(2)}, u32[]{:S(2)}) collective-permute-start(f32[2,32,256]{2,1,0:T(8,128)S(1)} %get-tuple-element.32), channel_id=1, source_target_pairs={{0,192},{64,0},{128,64},{192,128},{1,193},{65,1},{129,65},{193,129... | collective-permute-start | bytes 196616 | tf_op jit(solution)/shard_map/ppermute | solution.py:276
  33.2 0.0 collective-permute-done.8
  33.2 0.0 collective-permute-done.9
  33.2 6.4 %collective-permute-start.15 = (f32[1,32,256]{2,1,0:T(8,128)S(1)}, f32[1,32,256]{2,1,0:T(8,128)S(1)}, u32[]{:S(2)}, u32[]{:S(2)}) collective-permute-start(f32[1,32,256]{2,1,0:T(8,128)S(1)} %fusion), channel_id=1, source_target_pairs={{0,48},{16,0},{32,16},{48,32},{1,49},{17,1},{33,17},{49,33},{2,50}... | collective-permute-start | bytes 98312 | tf_op jit(solution)/shard_map/ppermute | solution.py:279
  39.6 0.0 collective-permute-done.10
  39.6 0.0 collective-permute-done.11
  39.6 0.0 collective-permute-done.12
  39.7 3.8 %collective-permute-start.13 = (f32[1,32,256]{2,1,0:T(8,128)S(1)}, f32[1,32,256]{2,1,0:T(8,128)S(1)}, u32[]{:S(2)}, u32[]{:S(2)}) collective-permute-start(f32[1,32,256]{2,1,0:T(8,128)S(1)} %get-tuple-element.40), channel_id=1, source_target_pairs={{0,32},{16,48},{32,0},{48,16},{1,33},{17,49},{33,1},{49,17},{2,34}... | collective-permute-start | bytes 98312 | tf_op jit(solution)/shard_map/ppermute | solution.py:279
  43.5 1.5 %collective-permute-start.14 = (f32[1,32,256]{2,1,0:T(8,128)S(1)}, f32[1,32,256]{2,1,0:T(8,128)S(1)}, u32[]{:S(2)}, u32[]{:S(2)}) collective-permute-start(f32[1,32,256]{2,1,0:T(8,128)S(1)} %get-tuple-element.39), channel_id=1, source_target_pairs={{0,16},{16,32},{32,48},{48,0},{1,17},{17,33},{33,49},{49,1},{2,18}... | collective-permute-start | bytes 98312 | tf_op jit(solution)/shard_map/ppermute | solution.py:279
  44.9 0.0 collective-permute-done.15
  44.9 2.6 %collective-permute-done.13 = f32[1,32,256]{2,1,0:T(8,128)S(1)} collective-permute-done((f32[1,32,256]{2,1,0:T(8,128)S(1)}, f32[1,32,256]{2,1,0:T(8,128)S(1)}, u32[]{:S(2)}, u32[]{:S(2)}) %collective-permute-start.13) | collective-permute-done | bytes 32800 | tf_op jit(solution)/shard_map/ppermute | solution.py:279
  47.6 1.9 %collective-permute-done.14 = f32[1,32,256]{2,1,0:T(8,128)S(1)} collective-permute-done((f32[1,32,256]{2,1,0:T(8,128)S(1)}, f32[1,32,256]{2,1,0:T(8,128)S(1)}, u32[]{:S(2)}, u32[]{:S(2)}) %collective-permute-start.14) | collective-permute-done | bytes 32800 | tf_op jit(solution)/shard_map/ppermute | solution.py:279
  49.5 0.6 %fusion.6 = f32[1,32,256]{2,1,0:T(8,128)} fusion(f32[1,32,256]{2,1,0:T(8,128)S(1)} %collective-permute-done.13, f32[2,32,256]{2,1,0:T(8,128)S(1)} %collective-permute-done.9, f32[2,32,256]{2,1,0:T(8,128)S(1)} %collective-permute-done.8, f32[2,32,256]{2,1,0:T(8,128)S(1)} %collective-permute-done.7, f32[2,32,256]{2,1,0:T(8,128)S(1)} %get-tuple-element.31, ...), kind=kLoop, calls=%fused_computation.21 | loop fusion | flops 57344 | bytes 262144 | tf_op jit(solution)/shard_map/mul | solution.py:280
  (5 shorter events, 0.1 us)
Async XLA Ops:
  2.4 15.7 %collective-permute-start = (f32[32,16,256]{2,1,0:T(8,128)S(1)}, f32[32,16,256]{2,1,0:T(8,128)S(1)}, u32[]{:S(2)}, u32[]{:S(2)}) collective-permute-start(f32[32,16,256]{2,1,0:T(8,128)S(1)} %get-tuple-element.19.bottom_ref), channel_id=1, source_target_pairs={{0,2},{2,4},{4,6},{6,0},{1,3},{3,5},{5,7},{7,1},{8,10},{10,12},{12... | collective-permute-start | bytes 1572872 | tf_op jit(solution)/shard_map/ppermute | solution.py:247
  4.0 9.6 %copy-start = (bf16[4,2,96,256]{3,2,1,0:T(8,128)(2,1)S(1)}, bf16[4,2,96,256]{3,2,1,0:T(8,128)(2,1)}, u32[]{:S(2)}) copy-start(bf16[4,2,96,256]{3,2,1,0:T(8,128)(2,1)} %constant.29.clone.left_ref) | copy-start | bytes 1179652
  4.0 14.1 %collective-permute-start.1 = (f32[32,16,256]{2,1,0:T(8,128)S(1)}, f32[32,16,256]{2,1,0:T(8,128)S(1)}, u32[]{:S(2)}, u32[]{:S(2)}) collective-permute-start(f32[32,16,256]{2,1,0:T(8,128)S(1)} %get-tuple-element.20.top_ref), channel_id=1, source_target_pairs={{0,6},{2,0},{4,2},{6,4},{1,7},{3,1},{5,3},{7,5},{8,14},{10,8},{12,... | collective-permute-start | bytes 1572872 | tf_op jit(solution)/shard_map/ppermute | solution.py:248
  4.7 8.9 %copy-start.2 = (bf16[2,2,64,128]{3,2,1,0:T(8,128)(2,1)S(1)}, bf16[2,2,64,128]{3,2,1,0:T(8,128)(2,1)}, u32[]{:S(2)}) copy-start(bf16[2,2,64,128]{3,2,1,0:T(8,128)(2,1)} %constant.32.clone.edge_ref) | copy-start | bytes 196612
  6.0 7.6 %copy-start.1 = (bf16[2,2,4,32,128]{4,3,2,1,0:T(8,128)(2,1)S(1)}, bf16[2,2,4,32,128]{4,3,2,1,0:T(8,128)(2,1)}, u32[]{:S(2)}) copy-start(bf16[2,2,4,32,128]{4,3,2,1,0:T(8,128)(2,1)} %constant.30.clone.patch_ref) | copy-start | bytes 393220
  6.0 4.4 %collective-permute-start.2 = (f32[2,32,256]{2,1,0:T(8,128)S(1)}, f32[2,32,256]{2,1,0:T(8,128)S(1)}, u32[]{:S(2)}, u32[]{:S(2)}) collective-permute-start(f32[2,32,256]{2,1,0:T(8,128)S(1)} %shard_map.66), channel_id=1, source_target_pairs={{0,1},{1,0},{2,3},{3,2},{4,5},{5,4},{6,7},{7,6},{8,9},{9,8},{10,11... | collective-permute-start | bytes 196616 | tf_op jit(solution)/shard_map/ppermute | solution.py:250
  10.4 6.4 %collective-permute-start.3 = (f32[2,16,256]{2,1,0:T(8,128)S(1)}, f32[2,16,256]{2,1,0:T(8,128)S(1)}, u32[]{:S(2)}, u32[]{:S(2)}) collective-permute-start(f32[2,16,256]{2,1,0:T(8,128)S(1)} %get-tuple-element.42), channel_id=1, source_target_pairs={{0,2},{2,4},{4,6},{6,0},{1,3},{3,5},{5,7},{7,1},{8,10},{10,12},{12... | collective-permute-start | bytes 98312 | tf_op jit(solution)/shard_map/ppermute | solution.py:251
  11.7 6.4 %collective-permute-start.4 = (f32[2,16,256]{2,1,0:T(8,128)S(1)}, f32[2,16,256]{2,1,0:T(8,128)S(1)}, u32[]{:S(2)}, u32[]{:S(2)}) collective-permute-start(f32[2,16,256]{2,1,0:T(8,128)S(1)} %get-tuple-element.41), channel_id=1, source_target_pairs={{0,6},{2,0},{4,2},{6,4},{1,7},{3,1},{5,3},{7,5},{8,14},{10,8},{12,... | collective-permute-start | bytes 98312 | tf_op jit(solution)/shard_map/ppermute | solution.py:252
  20.7 2.8 %collective-permute-start.6 = (f32[8,32,256]{2,1,0:T(8,128)S(1)}, f32[8,32,256]{2,1,0:T(8,128)S(1)}, u32[]{:S(2)}, u32[]{:S(2)}) collective-permute-start(f32[8,32,256]{2,1,0:T(8,128)S(1)} %get-tuple-element.30), channel_id=1, source_target_pairs={{0,8},{8,0},{1,9},{9,1},{2,10},{10,2},{3,11},{11,3},{4,12},{12,4},... | collective-permute-start | bytes 786440 | tf_op jit(solution)/shard_map/ppermute | solution.py:269
  22.9 4.3 %collective-permute-start.5 = (f32[8,32,256]{2,1,0:T(8,128)S(1)}, f32[8,32,256]{2,1,0:T(8,128)S(1)}, u32[]{:S(2)}, u32[]{:S(2)}) collective-permute-start(f32[8,32,256]{2,1,0:T(8,128)S(1)} %get-tuple-element.28), channel_id=1, source_target_pairs={{0,8},{8,0},{1,9},{9,1},{2,10},{10,2},{3,11},{11,3},{4,12},{12,4},... | collective-permute-start | bytes 786440 | tf_op jit(solution)/shard_map/ppermute | solution.py:269
  23.5 7.4 %collective-permute-start.7 = (f32[2,32,256]{2,1,0:T(8,128)S(1)}, f32[2,32,256]{2,1,0:T(8,128)S(1)}, u32[]{:S(2)}, u32[]{:S(2)}) collective-permute-start(f32[2,32,256]{2,1,0:T(8,128)S(1)} %get-tuple-element.35), channel_id=1, source_target_pairs={{0,128},{64,192},{128,0},{192,64},{1,129},{65,193},{129,1},{193,65... | collective-permute-start | bytes 196616 | tf_op jit(solution)/shard_map/ppermute | solution.py:276
  26.6 6.6 %collective-permute-start.8 = (f32[2,32,256]{2,1,0:T(8,128)S(1)}, f32[2,32,256]{2,1,0:T(8,128)S(1)}, u32[]{:S(2)}, u32[]{:S(2)}) collective-permute-start(f32[2,32,256]{2,1,0:T(8,128)S(1)} %get-tuple-element.38), channel_id=1, source_target_pairs={{0,64},{64,128},{128,192},{192,0},{1,65},{65,129},{129,193},{193,1... | collective-permute-start | bytes 196616 | tf_op jit(solution)/shard_map/ppermute | solution.py:276
  27.3 6.0 %collective-permute-start.9 = (f32[2,32,256]{2,1,0:T(8,128)S(1)}, f32[2,32,256]{2,1,0:T(8,128)S(1)}, u32[]{:S(2)}, u32[]{:S(2)}) collective-permute-start(f32[2,32,256]{2,1,0:T(8,128)S(1)} %get-tuple-element.34), channel_id=1, source_target_pairs={{0,192},{64,0},{128,64},{192,128},{1,193},{65,1},{129,65},{193,129... | collective-permute-start | bytes 196616 | tf_op jit(solution)/shard_map/ppermute | solution.py:276
  30.0 9.6 %collective-permute-start.10 = (f32[2,32,256]{2,1,0:T(8,128)S(1)}, f32[2,32,256]{2,1,0:T(8,128)S(1)}, u32[]{:S(2)}, u32[]{:S(2)}) collective-permute-start(f32[2,32,256]{2,1,0:T(8,128)S(1)} %get-tuple-element.37), channel_id=1, source_target_pairs={{0,128},{64,192},{128,0},{192,64},{1,129},{65,193},{129,1},{193,65... | collective-permute-start | bytes 196616 | tf_op jit(solution)/shard_map/ppermute | solution.py:276
  30.0 9.6 %collective-permute-start.11 = (f32[2,32,256]{2,1,0:T(8,128)S(1)}, f32[2,32,256]{2,1,0:T(8,128)S(1)}, u32[]{:S(2)}, u32[]{:S(2)}) collective-permute-start(f32[2,32,256]{2,1,0:T(8,128)S(1)} %get-tuple-element.36), channel_id=1, source_target_pairs={{0,64},{64,128},{128,192},{192,0},{1,65},{65,129},{129,193},{193,1... | collective-permute-start | bytes 196616 | tf_op jit(solution)/shard_map/ppermute | solution.py:276
  30.9 8.7 %collective-permute-start.12 = (f32[2,32,256]{2,1,0:T(8,128)S(1)}, f32[2,32,256]{2,1,0:T(8,128)S(1)}, u32[]{:S(2)}, u32[]{:S(2)}) collective-permute-start(f32[2,32,256]{2,1,0:T(8,128)S(1)} %get-tuple-element.32), channel_id=1, source_target_pairs={{0,192},{64,0},{128,64},{192,128},{1,193},{65,1},{129,65},{193,129... | collective-permute-start | bytes 196616 | tf_op jit(solution)/shard_map/ppermute | solution.py:276
  33.2 11.7 %collective-permute-start.15 = (f32[1,32,256]{2,1,0:T(8,128)S(1)}, f32[1,32,256]{2,1,0:T(8,128)S(1)}, u32[]{:S(2)}, u32[]{:S(2)}) collective-permute-start(f32[1,32,256]{2,1,0:T(8,128)S(1)} %fusion), channel_id=1, source_target_pairs={{0,48},{16,0},{32,16},{48,32},{1,49},{17,1},{33,17},{49,33},{2,50}... | collective-permute-start | bytes 98312 | tf_op jit(solution)/shard_map/ppermute | solution.py:279
  39.7 7.9 %collective-permute-start.13 = (f32[1,32,256]{2,1,0:T(8,128)S(1)}, f32[1,32,256]{2,1,0:T(8,128)S(1)}, u32[]{:S(2)}, u32[]{:S(2)}) collective-permute-start(f32[1,32,256]{2,1,0:T(8,128)S(1)} %get-tuple-element.40), channel_id=1, source_target_pairs={{0,32},{16,48},{32,0},{48,16},{1,33},{17,49},{33,1},{49,17},{2,34}... | collective-permute-start | bytes 98312 | tf_op jit(solution)/shard_map/ppermute | solution.py:279
  43.5 6.0 %collective-permute-start.14 = (f32[1,32,256]{2,1,0:T(8,128)S(1)}, f32[1,32,256]{2,1,0:T(8,128)S(1)}, u32[]{:S(2)}, u32[]{:S(2)}) collective-permute-start(f32[1,32,256]{2,1,0:T(8,128)S(1)} %get-tuple-element.39), channel_id=1, source_target_pairs={{0,16},{16,32},{32,48},{48,0},{1,17},{17,33},{33,49},{49,1},{2,18}... | collective-permute-start | bytes 98312 | tf_op jit(solution)/shard_map/ppermute | solution.py:279

commit v7 on v6

--- a/solution.py
+++ b/solution.py
@@ -81,16 +81,16 @@
     return lax.rem(where[3] + (2, 1, 3, 0)[k], 4)
 
 
-def product_kernel(where, p_hbm, c_hbm, p_ref, top_ref, bottom_ref, c_ref, sems):
+def product_kernel(part, where, p_hbm, c_hbm, p_ref, top_ref, bottom_ref, c_ref, sems):
     copies = []
-    for k in range(4):
+    for k in range(2):
         for h in range(2):
-            source, at = pl.ds(8 * block_of(where, k) + 4 * h, 4), pl.ds(8 * k + 4 * h, 4)
+            source, at = pl.ds(8 * block_of(where, 2 * part + k) + 4 * h, 4), pl.ds(8 * k + 4 * h, 4)
             copies.append(pltpu.make_async_copy(p_hbm.at[0, source], p_ref.at[at], sems.at[0, 2 * k + h]))
             copies.append(pltpu.make_async_copy(c_hbm.at[source], c_ref.at[at], sems.at[1, 2 * k + h]))
     for copy in copies:
         copy.start()
-    for g in range(8):
+    for g in range(4):
         copies[2 * g].wait()
         copies[2 * g + 1].wait()
         at = slice(4 * g, 4 * g + 4)
@@ -99,21 +99,20 @@
         bottom_ref[at] = v[:, HALO:]
 
 
-def edge_kernel(where, top_ref, bottom_ref, edge_ref):
+def edge_kernel(where, top0_ref, bottom0_ref, top1_ref, bottom1_ref, edge_ref):
     gy = where[2]
-    lane = lax.broadcasted_iota(jnp.int32, (1, 1, 128), 2)
-    for r_ref, rows in ((top_ref, slice(0, HALO)), (bottom_ref, slice(HALO, 2 * HALO))):
-        edges = jnp.zeros((4, HALO, 128), F32)
+    lane = lax.broadcasted_iota(jnp.int32, (1, 128), 1)
+    near = pl.ds(pl.multiple_of(128 * (1 - gy), 128), 128)
+    for refs, rows in (((top0_ref, top1_ref), slice(0, HALO)), ((bottom0_ref, bottom1_ref), slice(HALO, 2 * HALO))):
+        edges = jnp.zeros((64, 128), F32)
         for g in range(8):
-            at = slice(4 * g, 4 * g + 4)
-            last = r_ref[at, :, 128:].reshape(64, 128)
-            first = r_ref[at, :, :128].reshape(64, 128)
-            v = jnp.where(gy == 0, pltpu.roll(last, 16, 1), first)
+            at = slice(4 * (g % 4), 4 * (g % 4) + 4)
+            v = refs[g // 4][at, :, near].reshape(64, 128)
             if g:
                 v = pltpu.roll(v, 16 * g, 1)
-            edges = jnp.where(lane // 16 == g, v.reshape(4, HALO, 128), edges)
+            edges = jnp.where(lane // 16 == lax.rem(g + 7 * (1 - gy), 8), v, edges)
         for f in range(4):
-            edge_ref[f // 2, rows, 128 * (f % 2) : 128 * (f % 2) + 128] = edges[f]
+            edge_ref[f // 2, rows, 128 * (f % 2) : 128 * (f % 2) + 128] = edges[16 * f : 16 * f + 16]
 
 
 def table_kernel(
@@ -172,7 +171,7 @@
         near_ref[pl.ds(0, 64, stride=2), :] = near_pairs
         near_ref[pl.ds(1, 64, stride=2), :] = near_pairs
         near = near + near_ref[...]
-        near = jnp.where(gy == 0, pltpu.roll(near, 112, 1), near)
+        near = jnp.where(gy == 0, pltpu.roll(near, 112, 1), pltpu.roll(near, 16, 1))
         near_ref[...] = near
     else:
         near_ref, keep_ref, send_ref, *scratch = refs
@@ -182,7 +181,7 @@
     on_right = (narrow >= 128 - HALO) & (gy == 0)
 
     for g in range(4):
-        fields = slice(16 * part + 4 * g, 16 * part + 4 * g + 4)
+        fields = slice(4 * g, 4 * g + 4)
         u = dot_rows([r[fields].reshape(64, 256) for r in (above_ref, top_ref, bottom_ref, below_ref)])
         for t in range(2):
             at, lanes = slice(128 * g, 128 * g + 128), slice(256 * t, 256 * t + 256)
@@ -204,8 +203,7 @@
         low = pairs_ref[0, at] + jnp.where(on_left, moved, zero)
         high = pairs_ref[1, at] + jnp.where(on_right, moved, zero)
         alpha = alpha_ref[at] + jnp.concatenate([low, high], axis=1)
-        first = 16 * part + 4 * g
-        q = p_ref[first : first + 4] * alpha.reshape(4, 32, 256)
+        q = p_ref[4 * g : 4 * g + 4] * alpha.reshape(4, 32, 256)
         for j in range(2):
             to = 4 * (g // 2) + lax.rem(6 + z - (2 * (g % 2) + j), 4)
             keep_ref[to] = jnp.where(core == 0, q[2 * j], q[2 * j + 1])
@@ -240,13 +238,18 @@
 
     ring = lambda d: [(i, (i + d) % 4) for i in range(4)]
     swap = [(0, 1), (1, 0)]
-    near_p, top, bottom = call(
-        product_kernel, [(32, 32, 256)] + [(32, 16, 256)] * 2, where, perturbations, control, hbm=(1, 2),
-        scratch=[vmem((32, 32, 256), F32), sems((2, 8))],
-    )
-    above = lax.ppermute(bottom, "gx", ring(1))
-    below = lax.ppermute(top, "gx", ring(3))
-    edges = call(edge_kernel, [(2, 32, 256)], where, top, bottom)[0]
+    ps, tops, bottoms, aboves, belows = [], [], [], [], []
+    for part in range(2):
+        p, top, bottom = call(
+            functools.partial(product_kernel, part), [(16, 32, 256)] + [(16, 16, 256)] * 2,
+            where, perturbations, control, hbm=(1, 2), scratch=[vmem((16, 32, 256), F32), sems((2, 4))],
+        )
+        ps.append(p)
+        tops.append(top)
+        bottoms.append(bottom)
+        aboves.append(lax.ppermute(bottom, "gx", ring(1)))
+        belows.append(lax.ppermute(top, "gx", ring(3)))
+    edges = call(edge_kernel, [(2, 32, 256)], where, tops[0], bottoms[0], tops[1], bottoms[1])[0]
     side = lax.ppermute(edges, "gy", swap)
     side_above = lax.ppermute(side[:, HALO:], "gx", ring(1))
     side_below = lax.ppermute(side[:, :HALO], "gx", ring(3))
@@ -260,7 +263,7 @@
         extra = (side_above, side, side_below, eh, el) if part == 0 else (near,)
         keep, give, *rest = call(
             functools.partial(filter_kernel, part), [(8, 32, 256)] * 2 + [(128, 128)] * (part == 0),
-            where, near_p, above, top, bottom, below, xh, xl, right, *extra,
+            where, ps[part], aboves[part], tops[part], bottoms[part], belows[part], xh, xl, right, *extra,
             scratch=[vmem((512, 512), BF16)] * 2 + [vmem((256, 512), BF16)] * 2
             + [vmem((512, 256), F32), vmem((2, 512, 128), F32)],
             cost=2 * 10**9,

time: 50.3 us -> 52.4 us (1.042)
  the two profiles are of different devices: /device:TPU:8 before, /device:TPU:6 now
where the time goes in v7:
time: 52.4 us; the launch traced here: 52.3 us
  starting transfers between devices  31.4 us (60%)
  Pallas kernels  11.1 us (21%)
  waiting for transfers between devices  8.8 us (17%)
  other arithmetic  0.73 us (1%)
    ppermute x3, starting transfers between devices, body(): lax.ppermute(cell, 'z', ring(e))  11.6 us
    pallas_call x6, Pallas kernels, call(): pl.pallas_call(kernel, out_shape=[o if isinstance(o, jax.ShapeDtypeStruct...  11.1 us
    ppermute x6, starting transfers between devices, body(): x2, x1, x3 = (lax.ppermute(piece[d, wave], 'x', ring(d)) for d in (2, 1, 3))  8.34 us
    ppermute x3, waiting for transfers between devices, body(): lax.ppermute(cell, 'z', ring(e))  4.55 us
    ppermute x1, waiting for transfers between devices, body(): side_above = lax.ppermute(side[:, HALO:], 'gx', ring(1))  4.04 us
    ppermute x2, starting transfers between devices, body(): belows.append(lax.ppermute(top, 'gx', ring(3)))  3.94 us
    ppermute x1, starting transfers between devices, body(): side_below = lax.ppermute(side[:, :HALO], 'gx', ring(3))  2.63 us
    ppermute x1, starting transfers between devices, body(): side = lax.ppermute(edges, 'gy', swap)  2 us
  transfers between devices with their start and end apart: 18, of which 4 were waited for; matrix products, arithmetic and copies ran while one was open for 0% of the time, Pallas kernels for 12%

profile of v7, /device:TPU:6, one launch (start us, length us, event | category | flops | bytes accessed | tf_op | source)
XLA Modules:
  0.0 52.3 jit_solution(17782147127448284126)
XLA Ops:
  0.0 0.1 stack.23.where
  0.1 1.9 %shard_map.64 = (f32[16,32,256]{2,1,0:T(8,128)S(1)}, f32[16,16,256]{2,1,0:T(8,128)S(1)}, f32[16,16,256]{2,1,0:T(8,128)S(1)}) custom-call(s32[5]{0:T(128)S(1)} %stack.23.where, f32[1,32,32,256]{3,2,1,0:T(8,128)} %p_hbm.3, f32[32,32,256]{2,1,0:T(8,128)} %c_hbm.3), custom_call_target="tpu_custom_call" | custom-call | bytes 1048576 | tf_op jit(solution)/shard_map/pallas_call | solution.py:218
  2.0 1.9 %shard_map.66 = (f32[16,32,256]{2,1,0:T(8,128)S(1)}, f32[16,16,256]{2,1,0:T(8,128)S(1)}, f32[16,16,256]{2,1,0:T(8,128)S(1)}) custom-call(s32[5]{0:T(128)S(1)} %stack.23.where, f32[1,32,32,256]{3,2,1,0:T(8,128)} %p_hbm.3, f32[32,32,256]{2,1,0:T(8,128)} %c_hbm.3), custom_call_target="tpu_custom_call" | custom-call | bytes 1048576 | tf_op jit(solution)/shard_map/pallas_call | solution.py:218
  3.9 0.0 copy-start
  3.9 0.0 copy-start.2
  4.0 0.7 %shard_map.67 = f32[2,32,256]{2,1,0:T(8,128)S(1)} custom-call(s32[5]{0:T(128)S(1)} %stack.23.where, f32[16,16,256]{2,1,0:T(8,128)S(1)} %get-tuple-element.29.top0_ref.top_ref, f32[16,16,256]{2,1,0:T(8,128)S(1)} %get-tuple-element.28.bottom0_ref.bottom_ref, f32[16,16,256]{2,1,0:T(8,128)S(1)} %get-tuple-element.23.top1_ref.top_ref, ...), custom_call_target="tpu_custom_call" | custom-call | bytes 1048576 | tf_op jit(solution)/shard_map/pallas_call | solution.py:218
  4.7 0.0 copy-start.1
  4.7 2.0 %collective-permute-start.4 = (f32[2,32,256]{2,1,0:T(8,128)S(1)}, f32[2,32,256]{2,1,0:T(8,128)S(1)}, u32[]{:S(2)}, u32[]{:S(2)}) collective-permute-start(f32[2,32,256]{2,1,0:T(8,128)S(1)} %shard_map.67), channel_id=1, source_target_pairs={{0,1},{1,0},{2,3},{3,2},{4,5},{5,4},{6,7},{7,6},{8,9},{9,8},{10,11... | collective-permute-start | bytes 196616 | tf_op jit(solution)/shard_map/ppermute | solution.py:253
  6.7 1.6 %collective-permute-start.2 = (f32[16,16,256]{2,1,0:T(8,128)S(1)}, f32[16,16,256]{2,1,0:T(8,128)S(1)}, u32[]{:S(2)}, u32[]{:S(2)}) collective-permute-start(f32[16,16,256]{2,1,0:T(8,128)S(1)} %get-tuple-element.28.bottom0_ref.bottom_ref), channel_id=1, source_target_pairs={{0,2},{2,4},{4,6},{6,0},{1,3},{3,5},{5,7},{7,1},{8,10},{10,12},{12... | collective-permute-start | bytes 786440 | tf_op jit(solution)/shard_map/ppermute | solution.py:250
  8.3 1.7 %collective-permute-start.3 = (f32[16,16,256]{2,1,0:T(8,128)S(1)}, f32[16,16,256]{2,1,0:T(8,128)S(1)}, u32[]{:S(2)}, u32[]{:S(2)}) collective-permute-start(f32[16,16,256]{2,1,0:T(8,128)S(1)} %get-tuple-element.29.top0_ref.top_ref), channel_id=1, source_target_pairs={{0,6},{2,0},{4,2},{6,4},{1,7},{3,1},{5,3},{7,5},{8,14},{10,8},{12,... | collective-permute-start | bytes 786440 | tf_op jit(solution)/shard_map/ppermute | solution.py:251
  9.9 0.0 collective-permute-done.4.refs_1_
  10.0 0.7 %collective-permute-start.5 = (f32[2,16,256]{2,1,0:T(8,128)S(1)}, f32[2,16,256]{2,1,0:T(8,128)S(1)}, u32[]{:S(2)}, u32[]{:S(2)}) collective-permute-start(f32[2,16,256]{2,1,0:T(8,128)S(1)} %get-tuple-element.48), channel_id=1, source_target_pairs={{0,2},{2,4},{4,6},{6,0},{1,3},{3,5},{5,7},{7,1},{8,10},{10,12},{12... | collective-permute-start | bytes 98312 | tf_op jit(solution)/shard_map/ppermute | solution.py:254
  10.6 2.6 %collective-permute-start.6 = (f32[2,16,256]{2,1,0:T(8,128)S(1)}, f32[2,16,256]{2,1,0:T(8,128)S(1)}, u32[]{:S(2)}, u32[]{:S(2)}) collective-permute-start(f32[2,16,256]{2,1,0:T(8,128)S(1)} %get-tuple-element.47), channel_id=1, source_target_pairs={{0,6},{2,0},{4,2},{6,4},{1,7},{3,1},{5,3},{7,5},{8,14},{10,8},{12,... | collective-permute-start | bytes 98312 | tf_op jit(solution)/shard_map/ppermute | solution.py:255
  13.3 0.0 collective-permute-start
  13.3 4.0 %collective-permute-done.5.refs_0_ = f32[2,16,256]{2,1,0:T(8,128)S(1)} collective-permute-done((f32[2,16,256]{2,1,0:T(8,128)S(1)}, f32[2,16,256]{2,1,0:T(8,128)S(1)}, u32[]{:S(2)}, u32[]{:S(2)}) %collective-permute-start.5) | collective-permute-done | bytes 32800 | tf_op jit(solution)/shard_map/ppermute | solution.py:254
  17.3 2.3 %collective-permute-start.1 = (f32[16,16,256]{2,1,0:T(8,128)S(1)}, f32[16,16,256]{2,1,0:T(8,128)S(1)}, u32[]{:S(2)}, u32[]{:S(2)}) collective-permute-start(f32[16,16,256]{2,1,0:T(8,128)S(1)} %get-tuple-element.23.top1_ref.top_ref), channel_id=1, source_target_pairs={{0,6},{2,0},{4,2},{6,4},{1,7},{3,1},{5,3},{7,5},{8,14},{10,8},{12,... | collective-permute-start | bytes 786440 | tf_op jit(solution)/shard_map/ppermute | solution.py:251
  19.6 0.0 copy-done
  19.6 1.9 %shard_map.65 = (bf16[384,256]{1,0:T(8,128)(2,1)S(1)}, bf16[384,256]{1,0:T(8,128)(2,1)S(1)}, bf16[512,128]{1,0:T(8,128)(2,1)S(1)}, bf16[512,128]{1,0:T(8,128)(2,1)S(1)}, bf16[2,1024,256]{2,1,0:T(8,128)(2,1)S(1)}) custom-call(s32[5]{0:T(128)S(1)} %stack.23.where, bf16[4,2,96,256]{3,2,1,0:T(8,128)(2,1)S(1)} %copy-done, bf16[2,2,64,128]{3,2,1,0:T(8,128)(2,1)S(1)} %copy-done.2, ...), custom_call_target="tpu_custom_call" | custom-call | bytes 1048576 | tf_op jit(solution)/shard_map/pallas_call | solution.py:218
  21.5 0.0 collective-permute-done.6.refs_2_
  21.5 0.0 collective-permute-done.2.above_ref
  21.5 0.0 collective-permute-done.3.below_ref
  21.5 2.6 %shard_map.68 = (f32[8,32,256]{2,1,0:T(8,128)S(1)}, f32[8,32,256]{2,1,0:T(8,128)S(1)}, f32[128,128]{1,0:T(8,128)S(1)}) custom-call(s32[5]{0:T(128)S(1)} %stack.23.where, f32[16,32,256]{2,1,0:T(8,128)S(1)} %get-tuple-element.27.p_ref, f32[16,16,256]{2,1,0:T(8,128)S(1)} %collective-permute-done.2.above_ref, ...), custom_call_target="tpu_custom_call" | custom-call | flops 2000000000 | bytes 1048576 | tf_op jit(solution)/shard_map/pallas_call | solution.py:218
  24.1 0.1 collective-permute-start.8
  24.2 0.0 collective-permute-done.above_ref
  24.2 0.0 collective-permute-done.1.below_ref
  24.2 2.1 %shard_map.69 = (f32[8,32,256]{2,1,0:T(8,128)S(1)}, f32[8,32,256]{2,1,0:T(8,128)S(1)}) custom-call(s32[5]{0:T(128)S(1)} %stack.23.where, f32[16,32,256]{2,1,0:T(8,128)S(1)} %get-tuple-element.21.p_ref, f32[16,16,256]{2,1,0:T(8,128)S(1)} %collective-permute-done.above_ref, f32[16,16,256]{2,1,0:T(8,128)S(1)} %get-tuple-element.23.top1_ref.top_ref, ...), custom_call_target="tpu_custom_call" | custom-call | flops 2000000000 | bytes 1048576 | tf_op jit(solution)/shard_map/pallas_call | solution.py:218
  26.3 0.6 %collective-permute-start.7 = (f32[8,32,256]{2,1,0:T(8,128)S(1)}, f32[8,32,256]{2,1,0:T(8,128)S(1)}, u32[]{:S(2)}, u32[]{:S(2)}) collective-permute-start(f32[8,32,256]{2,1,0:T(8,128)S(1)} %get-tuple-element.34), channel_id=1, source_target_pairs={{0,8},{8,0},{1,9},{9,1},{2,10},{10,2},{3,11},{11,3},{4,12},{12,4},... | collective-permute-start | bytes 786440 | tf_op jit(solution)/shard_map/ppermute | solution.py:272
  26.9 0.0 collective-permute-done.8
  26.9 0.6 %collective-permute-start.10 = (f32[2,32,256]{2,1,0:T(8,128)S(1)}, f32[2,32,256]{2,1,0:T(8,128)S(1)}, u32[]{:S(2)}, u32[]{:S(2)}) collective-permute-start(f32[2,32,256]{2,1,0:T(8,128)S(1)} %get-tuple-element.44), channel_id=1, source_target_pairs={{0,64},{64,128},{128,192},{192,0},{1,65},{65,129},{129,193},{193,1... | collective-permute-start | bytes 196616 | tf_op jit(solution)/shard_map/ppermute | solution.py:279
  27.5 2.4 %collective-permute-start.9 = (f32[2,32,256]{2,1,0:T(8,128)S(1)}, f32[2,32,256]{2,1,0:T(8,128)S(1)}, u32[]{:S(2)}, u32[]{:S(2)}) collective-permute-start(f32[2,32,256]{2,1,0:T(8,128)S(1)} %get-tuple-element.41), channel_id=1, source_target_pairs={{0,128},{64,192},{128,0},{192,64},{1,129},{65,193},{129,1},{193,65... | collective-permute-start | bytes 196616 | tf_op jit(solution)/shard_map/ppermute | solution.py:279
  29.9 0.0 collective-permute-done.7
  29.9 0.1 collective-permute-start.11
  30.0 3.3 %collective-permute-start.12 = (f32[2,32,256]{2,1,0:T(8,128)S(1)}, f32[2,32,256]{2,1,0:T(8,128)S(1)}, u32[]{:S(2)}, u32[]{:S(2)}) collective-permute-start(f32[2,32,256]{2,1,0:T(8,128)S(1)} %get-tuple-element.43), channel_id=1, source_target_pairs={{0,128},{64,192},{128,0},{192,64},{1,129},{65,193},{129,1},{193,65... | collective-permute-start | bytes 196616 | tf_op jit(solution)/shard_map/ppermute | solution.py:279
  33.3 0.5 collective-permute-start.13
  33.8 0.0 collective-permute-done.10
  33.8 1.5 %collective-permute-start.14 = (f32[2,32,256]{2,1,0:T(8,128)S(1)}, f32[2,32,256]{2,1,0:T(8,128)S(1)}, u32[]{:S(2)}, u32[]{:S(2)}) collective-permute-start(f32[2,32,256]{2,1,0:T(8,128)S(1)} %get-tuple-element.38), channel_id=1, source_target_pairs={{0,192},{64,0},{128,64},{192,128},{1,193},{65,1},{129,65},{193,129... | collective-permute-start | bytes 196616 | tf_op jit(solution)/shard_map/ppermute | solution.py:279
  35.3 0.0 collective-permute-done.9
  35.3 0.2 collective-permute-done.11
  35.5 5.5 %collective-permute-start.17 = (f32[1,32,256]{2,1,0:T(8,128)S(1)}, f32[1,32,256]{2,1,0:T(8,128)S(1)}, u32[]{:S(2)}, u32[]{:S(2)}) collective-permute-start(f32[1,32,256]{2,1,0:T(8,128)S(1)} %fusion), channel_id=1, source_target_pairs={{0,48},{16,0},{32,16},{48,32},{1,49},{17,1},{33,17},{49,33},{2,50}... | collective-permute-start | bytes 98312 | tf_op jit(solution)/shard_map/ppermute | solution.py:282
  41.0 0.0 collective-permute-done.12
  41.0 0.0 collective-permute-done.13
  41.0 0.0 collective-permute-done.14
  41.0 4.6 %collective-permute-start.15 = (f32[1,32,256]{2,1,0:T(8,128)S(1)}, f32[1,32,256]{2,1,0:T(8,128)S(1)}, u32[]{:S(2)}, u32[]{:S(2)}) collective-permute-start(f32[1,32,256]{2,1,0:T(8,128)S(1)} %get-tuple-element.46), channel_id=1, source_target_pairs={{0,32},{16,48},{32,0},{48,16},{1,33},{17,49},{33,1},{49,17},{2,34}... | collective-permute-start | bytes 98312 | tf_op jit(solution)/shard_map/ppermute | solution.py:282
  45.6 1.5 %collective-permute-start.16 = (f32[1,32,256]{2,1,0:T(8,128)S(1)}, f32[1,32,256]{2,1,0:T(8,128)S(1)}, u32[]{:S(2)}, u32[]{:S(2)}) collective-permute-start(f32[1,32,256]{2,1,0:T(8,128)S(1)} %get-tuple-element.45), channel_id=1, source_target_pairs={{0,16},{16,32},{32,48},{48,0},{1,17},{17,33},{33,49},{49,1},{2,18}... | collective-permute-start | bytes 98312 | tf_op jit(solution)/shard_map/ppermute | solution.py:282
  47.1 0.0 collective-permute-done.17
  47.1 2.2 %collective-permute-done.15 = f32[1,32,256]{2,1,0:T(8,128)S(1)} collective-permute-done((f32[1,32,256]{2,1,0:T(8,128)S(1)}, f32[1,32,256]{2,1,0:T(8,128)S(1)}, u32[]{:S(2)}, u32[]{:S(2)}) %collective-permute-start.15) | collective-permute-done | bytes 32800 | tf_op jit(solution)/shard_map/ppermute | solution.py:282
  49.3 2.4 %collective-permute-done.16 = f32[1,32,256]{2,1,0:T(8,128)S(1)} collective-permute-done((f32[1,32,256]{2,1,0:T(8,128)S(1)}, f32[1,32,256]{2,1,0:T(8,128)S(1)}, u32[]{:S(2)}, u32[]{:S(2)}) %collective-permute-start.16) | collective-permute-done | bytes 32800 | tf_op jit(solution)/shard_map/ppermute | solution.py:282
  51.7 0.6 %fusion.6 = f32[1,32,256]{2,1,0:T(8,128)} fusion(f32[1,32,256]{2,1,0:T(8,128)S(1)} %collective-permute-done.15, f32[2,32,256]{2,1,0:T(8,128)S(1)} %collective-permute-done.11, f32[2,32,256]{2,1,0:T(8,128)S(1)} %collective-permute-done.10, f32[2,32,256]{2,1,0:T(8,128)S(1)} %collective-permute-done.9, f32[2,32,256]{2,1,0:T(8,128)S(1)} %get-tuple-element.37, ...), kind=kLoop, calls=%fused_computation.21 | loop fusion | flops 57344 | bytes 262144 | tf_op jit(solution)/shard_map/mul | solution.py:283
  (7 shorter events, 0.1 us)
Async XLA Ops:
  3.9 15.7 %copy-start = (bf16[4,2,96,256]{3,2,1,0:T(8,128)(2,1)S(1)}, bf16[4,2,96,256]{3,2,1,0:T(8,128)(2,1)}, u32[]{:S(2)}) copy-start(bf16[4,2,96,256]{3,2,1,0:T(8,128)(2,1)} %constant.29.clone.left_ref) | copy-start | bytes 1179652
  3.9 15.7 %copy-start.2 = (bf16[2,2,64,128]{3,2,1,0:T(8,128)(2,1)S(1)}, bf16[2,2,64,128]{3,2,1,0:T(8,128)(2,1)}, u32[]{:S(2)}) copy-start(bf16[2,2,64,128]{3,2,1,0:T(8,128)(2,1)} %constant.32.clone.edge_ref) | copy-start | bytes 196612
  4.7 14.9 %copy-start.1 = (bf16[2,2,4,32,128]{4,3,2,1,0:T(8,128)(2,1)S(1)}, bf16[2,2,4,32,128]{4,3,2,1,0:T(8,128)(2,1)}, u32[]{:S(2)}) copy-start(bf16[2,2,4,32,128]{4,3,2,1,0:T(8,128)(2,1)} %constant.30.clone.patch_ref) | copy-start | bytes 393220
  4.7 5.2 %collective-permute-start.4 = (f32[2,32,256]{2,1,0:T(8,128)S(1)}, f32[2,32,256]{2,1,0:T(8,128)S(1)}, u32[]{:S(2)}, u32[]{:S(2)}) collective-permute-start(f32[2,32,256]{2,1,0:T(8,128)S(1)} %shard_map.67), channel_id=1, source_target_pairs={{0,1},{1,0},{2,3},{3,2},{4,5},{5,4},{6,7},{7,6},{8,9},{9,8},{10,11... | collective-permute-start | bytes 196616 | tf_op jit(solution)/shard_map/ppermute | solution.py:253
  6.7 14.8 %collective-permute-start.2 = (f32[16,16,256]{2,1,0:T(8,128)S(1)}, f32[16,16,256]{2,1,0:T(8,128)S(1)}, u32[]{:S(2)}, u32[]{:S(2)}) collective-permute-start(f32[16,16,256]{2,1,0:T(8,128)S(1)} %get-tuple-element.28.bottom0_ref.bottom_ref), channel_id=1, source_target_pairs={{0,2},{2,4},{4,6},{6,0},{1,3},{3,5},{5,7},{7,1},{8,10},{10,12},{12... | collective-permute-start | bytes 786440 | tf_op jit(solution)/shard_map/ppermute | solution.py:250
  8.3 13.2 %collective-permute-start.3 = (f32[16,16,256]{2,1,0:T(8,128)S(1)}, f32[16,16,256]{2,1,0:T(8,128)S(1)}, u32[]{:S(2)}, u32[]{:S(2)}) collective-permute-start(f32[16,16,256]{2,1,0:T(8,128)S(1)} %get-tuple-element.29.top0_ref.top_ref), channel_id=1, source_target_pairs={{0,6},{2,0},{4,2},{6,4},{1,7},{3,1},{5,3},{7,5},{8,14},{10,8},{12,... | collective-permute-start | bytes 786440 | tf_op jit(solution)/shard_map/ppermute | solution.py:251
  10.0 7.4 %collective-permute-start.5 = (f32[2,16,256]{2,1,0:T(8,128)S(1)}, f32[2,16,256]{2,1,0:T(8,128)S(1)}, u32[]{:S(2)}, u32[]{:S(2)}) collective-permute-start(f32[2,16,256]{2,1,0:T(8,128)S(1)} %get-tuple-element.48), channel_id=1, source_target_pairs={{0,2},{2,4},{4,6},{6,0},{1,3},{3,5},{5,7},{7,1},{8,10},{10,12},{12... | collective-permute-start | bytes 98312 | tf_op jit(solution)/shard_map/ppermute | solution.py:254
  10.6 10.9 %collective-permute-start.6 = (f32[2,16,256]{2,1,0:T(8,128)S(1)}, f32[2,16,256]{2,1,0:T(8,128)S(1)}, u32[]{:S(2)}, u32[]{:S(2)}) collective-permute-start(f32[2,16,256]{2,1,0:T(8,128)S(1)} %get-tuple-element.47), channel_id=1, source_target_pairs={{0,6},{2,0},{4,2},{6,4},{1,7},{3,1},{5,3},{7,5},{8,14},{10,8},{12,... | collective-permute-start | bytes 98312 | tf_op jit(solution)/shard_map/ppermute | solution.py:255
  13.3 10.9 %collective-permute-start = (f32[16,16,256]{2,1,0:T(8,128)S(1)}, f32[16,16,256]{2,1,0:T(8,128)S(1)}, u32[]{:S(2)}, u32[]{:S(2)}) collective-permute-start(f32[16,16,256]{2,1,0:T(8,128)S(1)} %get-tuple-element.22.bottom1_ref.bottom_ref), channel_id=1, source_target_pairs={{0,2},{2,4},{4,6},{6,0},{1,3},{3,5},{5,7},{7,1},{8,10},{10,12},{12... | collective-permute-start | bytes 786440 | tf_op jit(solution)/shard_map/ppermute | solution.py:250
  17.3 6.9 %collective-permute-start.1 = (f32[16,16,256]{2,1,0:T(8,128)S(1)}, f32[16,16,256]{2,1,0:T(8,128)S(1)}, u32[]{:S(2)}, u32[]{:S(2)}) collective-permute-start(f32[16,16,256]{2,1,0:T(8,128)S(1)} %get-tuple-element.23.top1_ref.top_ref), channel_id=1, source_target_pairs={{0,6},{2,0},{4,2},{6,4},{1,7},{3,1},{5,3},{7,5},{8,14},{10,8},{12,... | collective-permute-start | bytes 786440 | tf_op jit(solution)/shard_map/ppermute | solution.py:251
  24.1 2.8 %collective-permute-start.8 = (f32[8,32,256]{2,1,0:T(8,128)S(1)}, f32[8,32,256]{2,1,0:T(8,128)S(1)}, u32[]{:S(2)}, u32[]{:S(2)}) collective-permute-start(f32[8,32,256]{2,1,0:T(8,128)S(1)} %get-tuple-element.36), channel_id=1, source_target_pairs={{0,8},{8,0},{1,9},{9,1},{2,10},{10,2},{3,11},{11,3},{4,12},{12,4},... | collective-permute-start | bytes 786440 | tf_op jit(solution)/shard_map/ppermute | solution.py:272
  26.3 3.6 %collective-permute-start.7 = (f32[8,32,256]{2,1,0:T(8,128)S(1)}, f32[8,32,256]{2,1,0:T(8,128)S(1)}, u32[]{:S(2)}, u32[]{:S(2)}) collective-permute-start(f32[8,32,256]{2,1,0:T(8,128)S(1)} %get-tuple-element.34), channel_id=1, source_target_pairs={{0,8},{8,0},{1,9},{9,1},{2,10},{10,2},{3,11},{11,3},{4,12},{12,4},... | collective-permute-start | bytes 786440 | tf_op jit(solution)/shard_map/ppermute | solution.py:272
  26.9 6.8 %collective-permute-start.10 = (f32[2,32,256]{2,1,0:T(8,128)S(1)}, f32[2,32,256]{2,1,0:T(8,128)S(1)}, u32[]{:S(2)}, u32[]{:S(2)}) collective-permute-start(f32[2,32,256]{2,1,0:T(8,128)S(1)} %get-tuple-element.44), channel_id=1, source_target_pairs={{0,64},{64,128},{128,192},{192,0},{1,65},{65,129},{129,193},{193,1... | collective-permute-start | bytes 196616 | tf_op jit(solution)/shard_map/ppermute | solution.py:279
  27.5 7.8 %collective-permute-start.9 = (f32[2,32,256]{2,1,0:T(8,128)S(1)}, f32[2,32,256]{2,1,0:T(8,128)S(1)}, u32[]{:S(2)}, u32[]{:S(2)}) collective-permute-start(f32[2,32,256]{2,1,0:T(8,128)S(1)} %get-tuple-element.41), channel_id=1, source_target_pairs={{0,128},{64,192},{128,0},{192,64},{1,129},{65,193},{129,1},{193,65... | collective-permute-start | bytes 196616 | tf_op jit(solution)/shard_map/ppermute | solution.py:279
  29.9 5.6 %collective-permute-start.11 = (f32[2,32,256]{2,1,0:T(8,128)S(1)}, f32[2,32,256]{2,1,0:T(8,128)S(1)}, u32[]{:S(2)}, u32[]{:S(2)}) collective-permute-start(f32[2,32,256]{2,1,0:T(8,128)S(1)} %get-tuple-element.40), channel_id=1, source_target_pairs={{0,192},{64,0},{128,64},{192,128},{1,193},{65,1},{129,65},{193,129... | collective-permute-start | bytes 196616 | tf_op jit(solution)/shard_map/ppermute | solution.py:279
  30.0 11.0 %collective-permute-start.12 = (f32[2,32,256]{2,1,0:T(8,128)S(1)}, f32[2,32,256]{2,1,0:T(8,128)S(1)}, u32[]{:S(2)}, u32[]{:S(2)}) collective-permute-start(f32[2,32,256]{2,1,0:T(8,128)S(1)} %get-tuple-element.43), channel_id=1, source_target_pairs={{0,128},{64,192},{128,0},{192,64},{1,129},{65,193},{129,1},{193,65... | collective-permute-start | bytes 196616 | tf_op jit(solution)/shard_map/ppermute | solution.py:279
  33.3 7.7 %collective-permute-start.13 = (f32[2,32,256]{2,1,0:T(8,128)S(1)}, f32[2,32,256]{2,1,0:T(8,128)S(1)}, u32[]{:S(2)}, u32[]{:S(2)}) collective-permute-start(f32[2,32,256]{2,1,0:T(8,128)S(1)} %get-tuple-element.42), channel_id=1, source_target_pairs={{0,64},{64,128},{128,192},{192,0},{1,65},{65,129},{129,193},{193,1... | collective-permute-start | bytes 196616 | tf_op jit(solution)/shard_map/ppermute | solution.py:279
  33.8 7.2 %collective-permute-start.14 = (f32[2,32,256]{2,1,0:T(8,128)S(1)}, f32[2,32,256]{2,1,0:T(8,128)S(1)}, u32[]{:S(2)}, u32[]{:S(2)}) collective-permute-start(f32[2,32,256]{2,1,0:T(8,128)S(1)} %get-tuple-element.38), channel_id=1, source_target_pairs={{0,192},{64,0},{128,64},{192,128},{1,193},{65,1},{129,65},{193,129... | collective-permute-start | bytes 196616 | tf_op jit(solution)/shard_map/ppermute | solution.py:279
  35.5 11.6 %collective-permute-start.17 = (f32[1,32,256]{2,1,0:T(8,128)S(1)}, f32[1,32,256]{2,1,0:T(8,128)S(1)}, u32[]{:S(2)}, u32[]{:S(2)}) collective-permute-start(f32[1,32,256]{2,1,0:T(8,128)S(1)} %fusion), channel_id=1, source_target_pairs={{0,48},{16,0},{32,16},{48,32},{1,49},{17,1},{33,17},{49,33},{2,50}... | collective-permute-start | bytes 98312 | tf_op jit(solution)/shard_map/ppermute | solution.py:282
  41.0 8.3 %collective-permute-start.15 = (f32[1,32,256]{2,1,0:T(8,128)S(1)}, f32[1,32,256]{2,1,0:T(8,128)S(1)}, u32[]{:S(2)}, u32[]{:S(2)}) collective-permute-start(f32[1,32,256]{2,1,0:T(8,128)S(1)} %get-tuple-element.46), channel_id=1, source_target_pairs={{0,32},{16,48},{32,0},{48,16},{1,33},{17,49},{33,1},{49,17},{2,34}... | collective-permute-start | bytes 98312 | tf_op jit(solution)/shard_map/ppermute | solution.py:282
  45.6 6.0 %collective-permute-start.16 = (f32[1,32,256]{2,1,0:T(8,128)S(1)}, f32[1,32,256]{2,1,0:T(8,128)S(1)}, u32[]{:S(2)}, u32[]{:S(2)}) collective-permute-start(f32[1,32,256]{2,1,0:T(8,128)S(1)} %get-tuple-element.45), channel_id=1, source_target_pairs={{0,16},{16,32},{32,48},{48,0},{1,17},{17,33},{33,49},{49,1},{2,18}... | collective-permute-start | bytes 98312 | tf_op jit(solution)/shard_map/ppermute | solution.py:282

commit v8 on v6

--- a/solution.py
+++ b/solution.py
@@ -45,8 +45,7 @@
                 source = part * rows - HALO + e
                 if 0 <= source < size:
                     wide[:, e] = term[part * count : (part + 1) * count, source]
-            segments = wide.reshape(count, 4, 1, HALO)
-            terms.append(np.broadcast_to(segments, (count, 4, 4, HALO)).reshape(count, 256))
+            terms.append(wide)
         tables.append(np.concatenate(terms))
     return np.stack(tables)
 
@@ -101,25 +100,23 @@
 
 def edge_kernel(where, top_ref, bottom_ref, edge_ref):
     gy = where[2]
-    lane = lax.broadcasted_iota(jnp.int32, (1, 1, 128), 2)
+    lane = lax.broadcasted_iota(jnp.int32, (1, 128), 1)
+    near = pl.ds(pl.multiple_of(128 * (1 - gy), 128), 128)
     for r_ref, rows in ((top_ref, slice(0, HALO)), (bottom_ref, slice(HALO, 2 * HALO))):
-        edges = jnp.zeros((4, HALO, 128), F32)
+        edges = jnp.zeros((64, 128), F32)
         for g in range(8):
-            at = slice(4 * g, 4 * g + 4)
-            last = r_ref[at, :, 128:].reshape(64, 128)
-            first = r_ref[at, :, :128].reshape(64, 128)
-            v = jnp.where(gy == 0, pltpu.roll(last, 16, 1), first)
+            v = r_ref[4 * g : 4 * g + 4, :, near].reshape(64, 128)
             if g:
                 v = pltpu.roll(v, 16 * g, 1)
-            edges = jnp.where(lane // 16 == g, v.reshape(4, HALO, 128), edges)
+            edges = jnp.where(lane // 16 == lax.rem(g + 7 * (1 - gy), 8), v, edges)
         for f in range(4):
-            edge_ref[f // 2, rows, 128 * (f % 2) : 128 * (f % 2) + 128] = edges[f]
+            edge_ref[f // 2, rows, 128 * (f % 2) : 128 * (f % 2) + 128] = edges[16 * f : 16 * f + 16]
 
 
 def table_kernel(
-    where, left_ref, edge_ref, patch_ref, right_hbm, xh_ref, xl_ref, eh_ref, el_ref, right_ref, sems
+    where, edge_ref, patch_ref, right_hbm, eh_ref, el_ref, right_ref, sems
 ):
-    gx, gy = where[1], where[2]
+    gy = where[2]
     copies = []
     for h in range(2):
         for k in range(4):
@@ -127,17 +124,8 @@
             copies.append(pltpu.make_async_copy(right_hbm.at[h, at], right_ref.at[h, at], sems.at[h, k]))
     for copy in copies:
         copy.start()
-    lane = lax.broadcasted_iota(jnp.int32, (1, 256), 1)
     narrow = lax.broadcasted_iota(jnp.int32, (1, 128), 1)
-    for h, x_ref, e_ref in ((0, xh_ref, eh_ref), (1, xl_ref, el_ref)):
-        row, start = 0, 0
-        for count in (32, 32, 16, 16):
-            rows = left_ref[gx, h, start : start + count].astype(F32)
-            for f in range(4):
-                mine = (lane // 16) % 4 == f
-                x_ref[row : row + count] = jnp.where(mine, rows, jnp.zeros_like(rows)).astype(BF16)
-                row += count
-            start += count
+    for h, e_ref in ((0, eh_ref), (1, el_ref)):
         for t in range(4):
             rows = edge_ref[gy, h, 16 * t : 16 * t + 16].astype(F32)
             for g in range(8):
@@ -155,24 +143,29 @@
 
 
 def filter_kernel(
-    part, where, p_ref, above_ref, top_ref, bottom_ref, below_ref, xh_ref, xl_ref, right_ref, *refs
+    part, where, p_ref, above_ref, top_ref, bottom_ref, below_ref, left_ref, right_ref, *refs
 ):
     core, gy, z = where[0], where[2], where[4]
-    dot_rows = lambda parts: dot3((xh_ref[...], xl_ref[...]), split(jnp.concatenate(parts)))
+    left = left_ref[where[1]]
+
+    def dot_rows(parts):
+        high, low = split(jnp.concatenate(parts))
+        return jnp.dot(left, jnp.concatenate([high, high, low]), preferred_element_type=F32)
+
     narrow = lax.broadcasted_iota(jnp.int32, (1, 128), 1)
     if part == 0:
         side_above_ref, side_ref, side_below_ref, eh_ref, el_ref, keep_ref, send_ref, near_ref, *scratch = refs
         lanes = (slice(0, 128), slice(128, 256))
         sides = (side_above_ref, side_ref.at[:, :HALO], side_ref.at[:, HALO:], side_below_ref)
-        side = dot_rows([s[f // 2, :, lanes[f % 2]] for s in sides for f in range(4)])
-        fine = split(jnp.concatenate([side[:128], side[128:256]], axis=1))
-        pair = split(jnp.concatenate([side[256:320], side[320:]], axis=1))
+        side = [dot_rows([s[f // 2, :, lanes[f % 2]] for s in sides]) for f in range(4)]
+        fine = split(jnp.concatenate([jnp.concatenate([u[:32], u[32:64]], axis=1) for u in side]))
+        pair = split(jnp.concatenate([jnp.concatenate([u[64:80], u[80:]], axis=1) for u in side]))
         near = dot3(fine, (eh_ref[:256], el_ref[:256]))
         near_pairs = dot3(pair, (eh_ref[256:], el_ref[256:]))
         near_ref[pl.ds(0, 64, stride=2), :] = near_pairs
         near_ref[pl.ds(1, 64, stride=2), :] = near_pairs
         near = near + near_ref[...]
-        near = jnp.where(gy == 0, pltpu.roll(near, 112, 1), near)
+        near = jnp.where(gy == 0, pltpu.roll(near, 112, 1), pltpu.roll(near, 16, 1))
         near_ref[...] = near
     else:
         near_ref, keep_ref, send_ref, *scratch = refs
@@ -181,14 +174,13 @@
     on_left = (narrow < HALO) & (gy == 1)
     on_right = (narrow >= 128 - HALO) & (gy == 0)
 
-    for g in range(4):
-        fields = slice(16 * part + 4 * g, 16 * part + 4 * g + 4)
-        u = dot_rows([r[fields].reshape(64, 256) for r in (above_ref, top_ref, bottom_ref, below_ref)])
+    for f in range(16):
+        u = dot_rows([r[16 * part + f] for r in (above_ref, top_ref, bottom_ref, below_ref)])
         for t in range(2):
-            at, lanes = slice(128 * g, 128 * g + 128), slice(256 * t, 256 * t + 256)
-            fh_ref[at, lanes], fl_ref[at, lanes] = split(u[128 * t : 128 * t + 128])
-            at = slice(64 * g, 64 * g + 64)
-            ch_ref[at, lanes], cl_ref[at, lanes] = split(u[256 + 64 * t : 320 + 64 * t])
+            at, lanes = slice(32 * f, 32 * f + 32), slice(256 * t, 256 * t + 256)
+            fh_ref[at, lanes], fl_ref[at, lanes] = split(u[32 * t : 32 * t + 32])
+            at = slice(16 * f, 16 * f + 16)
+            ch_ref[at, lanes], cl_ref[at, lanes] = split(u[64 + 16 * t : 80 + 16 * t])
 
     alpha_ref[...] = dot3((fh_ref[...], fl_ref[...]), (right_ref[0, :512], right_ref[1, :512]))
     pairs = dot3((ch_ref[...], cl_ref[...]), (right_ref[0, 512:], right_ref[1, 512:]))
@@ -231,7 +223,8 @@
 def body(perturbations, control):
     x, z, core, gx, gy = (lax.axis_index(a) for a in ("x", "z", "core", "gx", "gy"))
     where = jnp.stack([core, gx, gy, x, z]).astype(jnp.int32)
-    left = jnp.asarray(halves(left_table(128, 4)))
+    high, low = np.moveaxis(halves(left_table(128, 4)), 1, 0)
+    left = jnp.asarray(np.concatenate([high, low, high], axis=2))
     right, edge = (halves(t) for t in right_tables(512, 2))
     blocks = right[1].reshape(2, 4, 256, 256)
     patch = jnp.asarray(np.stack([blocks[:, :, :32, :128], blocks[:, :, 224:, 128:]], axis=1))
@@ -250,17 +243,16 @@
     side = lax.ppermute(edges, "gy", swap)
     side_above = lax.ppermute(side[:, HALO:], "gx", ring(1))
     side_below = lax.ppermute(side[:, :HALO], "gx", ring(3))
-    xh, xl, eh, el, right = call(
-        table_kernel,
-        [jax.ShapeDtypeStruct(s, BF16) for s in [(384, 256)] * 2 + [(512, 128)] * 2 + [(2, 1024, 256)]],
-        where, left, edge, patch, right, hbm=(4,), scratch=[sems((2, 4))],
+    eh, el, right = call(
+        table_kernel, [jax.ShapeDtypeStruct(s, BF16) for s in [(512, 128)] * 2 + [(2, 1024, 256)]],
+        where, edge, patch, right, hbm=(3,), scratch=[sems((2, 4))],
     )
     piece = {}
     for part in range(2):
         extra = (side_above, side, side_below, eh, el) if part == 0 else (near,)
         keep, give, *rest = call(
             functools.partial(filter_kernel, part), [(8, 32, 256)] * 2 + [(128, 128)] * (part == 0),
-            where, near_p, above, top, bottom, below, xh, xl, right, *extra,
+            where, near_p, above, top, bottom, below, left, right, *extra,
             scratch=[vmem((512, 512), BF16)] * 2 + [vmem((256, 512), BF16)] * 2
             + [vmem((512, 256), F32), vmem((2, 512, 128), F32)],
             cost=2 * 10**9,

time: 50.3 us -> 49.3 us (0.980)
  Pallas kernels: 10.1 us -> 8.48 us
  waiting for transfers between devices: 9.77 us -> 10.3 us
    pallas_call x5, Pallas kernels: 10.1 us -> 8.48 us  [call(): pl.pallas_call(kernel, out_shape=[o if isinstance(o, jax.ShapeDtypeStruct...]
    ppermute x1, waiting for transfers between devices: 1.32 us -> 1.86 us  [body(): side_above = lax.ppermute(side[:, HALO:], 'gx', ring(1))]
  transfers between devices with their start and end apart: 16 -> 16, of which waited for: 5 -> 5; matrix products, arithmetic and copies ran while one was open for 0% -> 0% of each run, Pallas kernels for 10% -> 9%
where the time goes in v8:
time: 49.3 us; the launch traced here: 49.1 us
  starting transfers between devices  29.3 us (59%)
  waiting for transfers between devices  10.3 us (21%)
  Pallas kernels  8.48 us (17%)
  other arithmetic  0.73 us (1%)
    ppermute x3, starting transfers between devices, body(): lax.ppermute(cell, 'z', ring(e))  11.7 us
    ppermute x6, starting transfers between devices, body(): x2, x1, x3 = (lax.ppermute(piece[d, wave], 'x', ring(d)) for d in (2, 1, 3))  9.67 us
    pallas_call x5, Pallas kernels, call(): pl.pallas_call(kernel, out_shape=[o if isinstance(o, jax.ShapeDtypeStruct...  8.48 us
    ppermute x3, waiting for transfers between devices, body(): lax.ppermute(cell, 'z', ring(e))  4.54 us
    ppermute x1, waiting for transfers between devices, body(): side = lax.ppermute(edges, 'gy', swap)  2.57 us
    ppermute x1, starting transfers between devices, body(): side_below = lax.ppermute(side[:, :HALO], 'gx', ring(3))  1.89 us
    ppermute x1, waiting for transfers between devices, body(): side_above = lax.ppermute(side[:, HALO:], 'gx', ring(1))  1.86 us
    ppermute x1, starting transfers between devices, body(): side = lax.ppermute(edges, 'gy', swap)  1.78 us
  transfers between devices with their start and end apart: 16, of which 5 were waited for; matrix products, arithmetic and copies ran while one was open for 0% of the time, Pallas kernels for 9%

profile of v8, /device:TPU:8, one launch (start us, length us, event | category | flops | bytes accessed | tf_op | source)
XLA Modules:
  0.0 49.1 jit_solution(8924898381595529793)
XLA Ops:
  0.0 0.1 stack.23.where
  0.1 2.3 %shard_map.64 = (f32[32,32,256]{2,1,0:T(8,128)S(1)}, f32[32,16,256]{2,1,0:T(8,128)S(1)}, f32[32,16,256]{2,1,0:T(8,128)S(1)}) custom-call(s32[5]{0:T(128)S(1)} %stack.23.where, f32[1,32,32,256]{3,2,1,0:T(8,128)} %p_hbm.1, f32[32,32,256]{2,1,0:T(8,128)} %c_hbm.1), custom_call_target="tpu_custom_call" | custom-call | bytes 1048576 | tf_op jit(solution)/shard_map/pallas_call | solution.py:212
  2.4 1.7 %collective-permute-start = (f32[32,16,256]{2,1,0:T(8,128)S(1)}, f32[32,16,256]{2,1,0:T(8,128)S(1)}, u32[]{:S(2)}, u32[]{:S(2)}) collective-permute-start(f32[32,16,256]{2,1,0:T(8,128)S(1)} %get-tuple-element.17.bottom_ref), channel_id=1, source_target_pairs={{0,2},{2,4},{4,6},{6,0},{1,3},{3,5},{5,7},{7,1},{8,10},{10,12},{12... | collective-permute-start | bytes 1572872 | tf_op jit(solution)/shard_map/ppermute | solution.py:240
  4.0 0.7 %collective-permute-start.1 = (f32[32,16,256]{2,1,0:T(8,128)S(1)}, f32[32,16,256]{2,1,0:T(8,128)S(1)}, u32[]{:S(2)}, u32[]{:S(2)}) collective-permute-start(f32[32,16,256]{2,1,0:T(8,128)S(1)} %get-tuple-element.18.top_ref), channel_id=1, source_target_pairs={{0,6},{2,0},{4,2},{6,4},{1,7},{3,1},{5,3},{7,5},{8,14},{10,8},{12,... | collective-permute-start | bytes 1572872 | tf_op jit(solution)/shard_map/ppermute | solution.py:241
  4.7 0.0 copy-start.1
  4.7 0.7 %shard_map.66 = f32[2,32,256]{2,1,0:T(8,128)S(1)} custom-call(s32[5]{0:T(128)S(1)} %stack.23.where, f32[32,16,256]{2,1,0:T(8,128)S(1)} %get-tuple-element.18.top_ref, f32[32,16,256]{2,1,0:T(8,128)S(1)} %get-tuple-element.17.bottom_ref), custom_call_target="tpu_custom_call" | custom-call | bytes 1048576 | tf_op jit(solution)/shard_map/pallas_call | solution.py:212
  5.5 0.0 copy-start
  5.5 1.8 %collective-permute-start.2 = (f32[2,32,256]{2,1,0:T(8,128)S(1)}, f32[2,32,256]{2,1,0:T(8,128)S(1)}, u32[]{:S(2)}, u32[]{:S(2)}) collective-permute-start(f32[2,32,256]{2,1,0:T(8,128)S(1)} %shard_map.66), channel_id=1, source_target_pairs={{0,1},{1,0},{2,3},{3,2},{4,5},{5,4},{6,7},{7,6},{8,9},{9,8},{10,11... | collective-permute-start | bytes 196616 | tf_op jit(solution)/shard_map/ppermute | solution.py:243
  7.2 2.6 %collective-permute-done.2.refs_1_ = f32[2,32,256]{2,1,0:T(8,128)S(1)} collective-permute-done((f32[2,32,256]{2,1,0:T(8,128)S(1)}, f32[2,32,256]{2,1,0:T(8,128)S(1)}, u32[]{:S(2)}, u32[]{:S(2)}) %collective-permute-start.2) | collective-permute-done | bytes 65568 | tf_op jit(solution)/shard_map/ppermute | solution.py:243
  9.8 1.4 %collective-permute-start.3 = (f32[2,16,256]{2,1,0:T(8,128)S(1)}, f32[2,16,256]{2,1,0:T(8,128)S(1)}, u32[]{:S(2)}, u32[]{:S(2)}) collective-permute-start(f32[2,16,256]{2,1,0:T(8,128)S(1)} %get-tuple-element.38), channel_id=1, source_target_pairs={{0,2},{2,4},{4,6},{6,0},{1,3},{3,5},{5,7},{7,1},{8,10},{10,12},{12... | collective-permute-start | bytes 98312 | tf_op jit(solution)/shard_map/ppermute | solution.py:244
  11.2 0.0 copy-start.2
  11.2 1.9 %collective-permute-start.4 = (f32[2,16,256]{2,1,0:T(8,128)S(1)}, f32[2,16,256]{2,1,0:T(8,128)S(1)}, u32[]{:S(2)}, u32[]{:S(2)}) collective-permute-start(f32[2,16,256]{2,1,0:T(8,128)S(1)} %get-tuple-element.37), channel_id=1, source_target_pairs={{0,6},{2,0},{4,2},{6,4},{1,7},{3,1},{5,3},{7,5},{8,14},{10,8},{12,... | collective-permute-start | bytes 98312 | tf_op jit(solution)/shard_map/ppermute | solution.py:245
  13.1 0.0 copy-done.1
  13.1 0.0 copy-done
  13.1 1.9 %shard_map.65 = (bf16[512,128]{1,0:T(8,128)(2,1)S(1)}, bf16[512,128]{1,0:T(8,128)(2,1)S(1)}, bf16[2,1024,256]{2,1,0:T(8,128)(2,1)S(1)}) custom-call(s32[5]{0:T(128)S(1)} %stack.23.where, bf16[2,2,64,128]{3,2,1,0:T(8,128)(2,1)S(1)} %copy-done.1, bf16[2,2,4,32,128]{4,3,2,1,0:T(8,128)(2,1)S(1)} %copy-done, bf16[2,1024,256]{2,1,0:T(8,128)(2,1)} %constant.31.clone.right_hbm), custom_call_target="tpu_custom_call" | custom-call | bytes 1048576 | tf_op jit(solution)/shard_map/pallas_call | solution.py:212
  15.0 1.9 %collective-permute-done.3.refs_0_ = f32[2,16,256]{2,1,0:T(8,128)S(1)} collective-permute-done((f32[2,16,256]{2,1,0:T(8,128)S(1)}, f32[2,16,256]{2,1,0:T(8,128)S(1)}, u32[]{:S(2)}, u32[]{:S(2)}) %collective-permute-start.3) | collective-permute-done | bytes 32800 | tf_op jit(solution)/shard_map/ppermute | solution.py:244
  16.8 1.3 %collective-permute-done.4.refs_2_ = f32[2,16,256]{2,1,0:T(8,128)S(1)} collective-permute-done((f32[2,16,256]{2,1,0:T(8,128)S(1)}, f32[2,16,256]{2,1,0:T(8,128)S(1)}, u32[]{:S(2)}, u32[]{:S(2)}) %collective-permute-start.4) | collective-permute-done | bytes 32800 | tf_op jit(solution)/shard_map/ppermute | solution.py:245
  18.1 0.0 collective-permute-done.above_ref
  18.1 0.0 collective-permute-done.1.below_ref
  18.1 0.0 copy-done.2
  18.1 1.9 %shard_map.67 = (f32[8,32,256]{2,1,0:T(8,128)S(1)}, f32[8,32,256]{2,1,0:T(8,128)S(1)}, f32[128,128]{1,0:T(8,128)S(1)}) custom-call(s32[5]{0:T(128)S(1)} %stack.23.where, f32[32,32,256]{2,1,0:T(8,128)S(1)} %get-tuple-element.16.p_ref, f32[32,16,256]{2,1,0:T(8,128)S(1)} %collective-permute-done.above_ref, f32[32,16,256]{2,1,0:T(8,128)S(1)} %get-tuple-element.18.top_ref, ...), custom_call_target="tpu_custom_call" | custom-call | flops 2000000000 | bytes 1048576 | tf_op jit(solution)/shard_map/pallas_call | solution.py:212
  20.0 0.1 collective-permute-start.6
  20.1 1.7 %shard_map.68 = (f32[8,32,256]{2,1,0:T(8,128)S(1)}, f32[8,32,256]{2,1,0:T(8,128)S(1)}) custom-call(s32[5]{0:T(128)S(1)} %stack.23.where, f32[32,32,256]{2,1,0:T(8,128)S(1)} %get-tuple-element.16.p_ref, f32[32,16,256]{2,1,0:T(8,128)S(1)} %collective-permute-done.above_ref, f32[32,16,256]{2,1,0:T(8,128)S(1)} %get-tuple-element.18.top_ref, ...), custom_call_target="tpu_custom_call" | custom-call | flops 2000000000 | bytes 1048576 | tf_op jit(solution)/shard_map/pallas_call | solution.py:212
  21.8 0.6 %collective-permute-start.5 = (f32[8,32,256]{2,1,0:T(8,128)S(1)}, f32[8,32,256]{2,1,0:T(8,128)S(1)}, u32[]{:S(2)}, u32[]{:S(2)}) collective-permute-start(f32[8,32,256]{2,1,0:T(8,128)S(1)} %get-tuple-element.24), channel_id=1, source_target_pairs={{0,8},{8,0},{1,9},{9,1},{2,10},{10,2},{3,11},{11,3},{4,12},{12,4},... | collective-permute-start | bytes 786440 | tf_op jit(solution)/shard_map/ppermute | solution.py:261
  22.4 0.0 collective-permute-done.6
  22.4 3.1 %collective-permute-start.7 = (f32[2,32,256]{2,1,0:T(8,128)S(1)}, f32[2,32,256]{2,1,0:T(8,128)S(1)}, u32[]{:S(2)}, u32[]{:S(2)}) collective-permute-start(f32[2,32,256]{2,1,0:T(8,128)S(1)} %get-tuple-element.31), channel_id=1, source_target_pairs={{0,128},{64,192},{128,0},{192,64},{1,129},{65,193},{129,1},{193,65... | collective-permute-start | bytes 196616 | tf_op jit(solution)/shard_map/ppermute | solution.py:268
  25.6 0.6 %collective-permute-start.8 = (f32[2,32,256]{2,1,0:T(8,128)S(1)}, f32[2,32,256]{2,1,0:T(8,128)S(1)}, u32[]{:S(2)}, u32[]{:S(2)}) collective-permute-start(f32[2,32,256]{2,1,0:T(8,128)S(1)} %get-tuple-element.34), channel_id=1, source_target_pairs={{0,64},{64,128},{128,192},{192,0},{1,65},{65,129},{129,193},{193,1... | collective-permute-start | bytes 196616 | tf_op jit(solution)/shard_map/ppermute | solution.py:268
  26.2 0.0 collective-permute-done.5
  26.2 2.7 %collective-permute-start.9 = (f32[2,32,256]{2,1,0:T(8,128)S(1)}, f32[2,32,256]{2,1,0:T(8,128)S(1)}, u32[]{:S(2)}, u32[]{:S(2)}) collective-permute-start(f32[2,32,256]{2,1,0:T(8,128)S(1)} %get-tuple-element.30), channel_id=1, source_target_pairs={{0,192},{64,0},{128,64},{192,128},{1,193},{65,1},{129,65},{193,129... | collective-permute-start | bytes 196616 | tf_op jit(solution)/shard_map/ppermute | solution.py:268
  28.9 0.0 collective-permute-start.10
  28.9 1.0 %collective-permute-start.11 = (f32[2,32,256]{2,1,0:T(8,128)S(1)}, f32[2,32,256]{2,1,0:T(8,128)S(1)}, u32[]{:S(2)}, u32[]{:S(2)}) collective-permute-start(f32[2,32,256]{2,1,0:T(8,128)S(1)} %get-tuple-element.32), channel_id=1, source_target_pairs={{0,64},{64,128},{128,192},{192,0},{1,65},{65,129},{129,193},{193,1... | collective-permute-start | bytes 196616 | tf_op jit(solution)/shard_map/ppermute | solution.py:268
  29.9 0.0 collective-permute-done.7
  29.9 2.3 %collective-permute-start.12 = (f32[2,32,256]{2,1,0:T(8,128)S(1)}, f32[2,32,256]{2,1,0:T(8,128)S(1)}, u32[]{:S(2)}, u32[]{:S(2)}) collective-permute-start(f32[2,32,256]{2,1,0:T(8,128)S(1)} %get-tuple-element.28), channel_id=1, source_target_pairs={{0,192},{64,0},{128,64},{192,128},{1,193},{65,1},{129,65},{193,129... | collective-permute-start | bytes 196616 | tf_op jit(solution)/shard_map/ppermute | solution.py:268
  32.2 0.0 collective-permute-done.8
  32.2 0.0 collective-permute-done.9
  32.2 6.4 %collective-permute-start.15 = (f32[1,32,256]{2,1,0:T(8,128)S(1)}, f32[1,32,256]{2,1,0:T(8,128)S(1)}, u32[]{:S(2)}, u32[]{:S(2)}) collective-permute-start(f32[1,32,256]{2,1,0:T(8,128)S(1)} %fusion), channel_id=1, source_target_pairs={{0,48},{16,0},{32,16},{48,32},{1,49},{17,1},{33,17},{49,33},{2,50}... | collective-permute-start | bytes 98312 | tf_op jit(solution)/shard_map/ppermute | solution.py:271
  38.6 0.0 collective-permute-done.10
  38.6 0.0 collective-permute-done.11
  38.6 0.0 collective-permute-done.12
  38.6 3.8 %collective-permute-start.13 = (f32[1,32,256]{2,1,0:T(8,128)S(1)}, f32[1,32,256]{2,1,0:T(8,128)S(1)}, u32[]{:S(2)}, u32[]{:S(2)}) collective-permute-start(f32[1,32,256]{2,1,0:T(8,128)S(1)} %get-tuple-element.36), channel_id=1, source_target_pairs={{0,32},{16,48},{32,0},{48,16},{1,33},{17,49},{33,1},{49,17},{2,34}... | collective-permute-start | bytes 98312 | tf_op jit(solution)/shard_map/ppermute | solution.py:271
  42.4 1.5 %collective-permute-start.14 = (f32[1,32,256]{2,1,0:T(8,128)S(1)}, f32[1,32,256]{2,1,0:T(8,128)S(1)}, u32[]{:S(2)}, u32[]{:S(2)}) collective-permute-start(f32[1,32,256]{2,1,0:T(8,128)S(1)} %get-tuple-element.35), channel_id=1, source_target_pairs={{0,16},{16,32},{32,48},{48,0},{1,17},{17,33},{33,49},{49,1},{2,18}... | collective-permute-start | bytes 98312 | tf_op jit(solution)/shard_map/ppermute | solution.py:271
  43.9 0.0 collective-permute-done.15
  43.9 2.6 %collective-permute-done.13 = f32[1,32,256]{2,1,0:T(8,128)S(1)} collective-permute-done((f32[1,32,256]{2,1,0:T(8,128)S(1)}, f32[1,32,256]{2,1,0:T(8,128)S(1)}, u32[]{:S(2)}, u32[]{:S(2)}) %collective-permute-start.13) | collective-permute-done | bytes 32800 | tf_op jit(solution)/shard_map/ppermute | solution.py:271
  46.5 1.9 %collective-permute-done.14 = f32[1,32,256]{2,1,0:T(8,128)S(1)} collective-permute-done((f32[1,32,256]{2,1,0:T(8,128)S(1)}, f32[1,32,256]{2,1,0:T(8,128)S(1)}, u32[]{:S(2)}, u32[]{:S(2)}) %collective-permute-start.14) | collective-permute-done | bytes 32800 | tf_op jit(solution)/shard_map/ppermute | solution.py:271
  48.4 0.6 %fusion.6 = f32[1,32,256]{2,1,0:T(8,128)} fusion(f32[1,32,256]{2,1,0:T(8,128)S(1)} %collective-permute-done.13, f32[2,32,256]{2,1,0:T(8,128)S(1)} %collective-permute-done.9, f32[2,32,256]{2,1,0:T(8,128)S(1)} %collective-permute-done.8, f32[2,32,256]{2,1,0:T(8,128)S(1)} %collective-permute-done.7, f32[2,32,256]{2,1,0:T(8,128)S(1)} %get-tuple-element.27, ...), kind=kLoop, calls=%fused_computation.21 | loop fusion | flops 57344 | bytes 262144 | tf_op jit(solution)/shard_map/mul | solution.py:272
  (5 shorter events, 0.1 us)
Async XLA Ops:
  2.4 15.7 %collective-permute-start = (f32[32,16,256]{2,1,0:T(8,128)S(1)}, f32[32,16,256]{2,1,0:T(8,128)S(1)}, u32[]{:S(2)}, u32[]{:S(2)}) collective-permute-start(f32[32,16,256]{2,1,0:T(8,128)S(1)} %get-tuple-element.17.bottom_ref), channel_id=1, source_target_pairs={{0,2},{2,4},{4,6},{6,0},{1,3},{3,5},{5,7},{7,1},{8,10},{10,12},{12... | collective-permute-start | bytes 1572872 | tf_op jit(solution)/shard_map/ppermute | solution.py:240
  4.0 14.1 %collective-permute-start.1 = (f32[32,16,256]{2,1,0:T(8,128)S(1)}, f32[32,16,256]{2,1,0:T(8,128)S(1)}, u32[]{:S(2)}, u32[]{:S(2)}) collective-permute-start(f32[32,16,256]{2,1,0:T(8,128)S(1)} %get-tuple-element.18.top_ref), channel_id=1, source_target_pairs={{0,6},{2,0},{4,2},{6,4},{1,7},{3,1},{5,3},{7,5},{8,14},{10,8},{12,... | collective-permute-start | bytes 1572872 | tf_op jit(solution)/shard_map/ppermute | solution.py:241
  4.7 8.4 %copy-start.1 = (bf16[2,2,64,128]{3,2,1,0:T(8,128)(2,1)S(1)}, bf16[2,2,64,128]{3,2,1,0:T(8,128)(2,1)}, u32[]{:S(2)}) copy-start(bf16[2,2,64,128]{3,2,1,0:T(8,128)(2,1)} %constant.32.clone.edge_ref) | copy-start | bytes 196612
  5.5 7.6 %copy-start = (bf16[2,2,4,32,128]{4,3,2,1,0:T(8,128)(2,1)S(1)}, bf16[2,2,4,32,128]{4,3,2,1,0:T(8,128)(2,1)}, u32[]{:S(2)}) copy-start(bf16[2,2,4,32,128]{4,3,2,1,0:T(8,128)(2,1)} %constant.30.clone.patch_ref) | copy-start | bytes 393220
  5.5 4.4 %collective-permute-start.2 = (f32[2,32,256]{2,1,0:T(8,128)S(1)}, f32[2,32,256]{2,1,0:T(8,128)S(1)}, u32[]{:S(2)}, u32[]{:S(2)}) collective-permute-start(f32[2,32,256]{2,1,0:T(8,128)S(1)} %shard_map.66), channel_id=1, source_target_pairs={{0,1},{1,0},{2,3},{3,2},{4,5},{5,4},{6,7},{7,6},{8,9},{9,8},{10,11... | collective-permute-start | bytes 196616 | tf_op jit(solution)/shard_map/ppermute | solution.py:243
  9.8 7.0 %collective-permute-start.3 = (f32[2,16,256]{2,1,0:T(8,128)S(1)}, f32[2,16,256]{2,1,0:T(8,128)S(1)}, u32[]{:S(2)}, u32[]{:S(2)}) collective-permute-start(f32[2,16,256]{2,1,0:T(8,128)S(1)} %get-tuple-element.38), channel_id=1, source_target_pairs={{0,2},{2,4},{4,6},{6,0},{1,3},{3,5},{5,7},{7,1},{8,10},{10,12},{12... | collective-permute-start | bytes 98312 | tf_op jit(solution)/shard_map/ppermute | solution.py:244
  11.2 7.0 %copy-start.2 = (bf16[4,96,192]{2,1,0:T(8,128)(2,1)S(1)}, bf16[4,96,192]{2,1,0:T(8,128)(2,1)}, u32[]{:S(2)}) copy-start(bf16[4,96,192]{2,1,0:T(8,128)(2,1)} %constant.29.clone.left_ref) | copy-start | bytes 442372
  11.2 6.9 %collective-permute-start.4 = (f32[2,16,256]{2,1,0:T(8,128)S(1)}, f32[2,16,256]{2,1,0:T(8,128)S(1)}, u32[]{:S(2)}, u32[]{:S(2)}) collective-permute-start(f32[2,16,256]{2,1,0:T(8,128)S(1)} %get-tuple-element.37), channel_id=1, source_target_pairs={{0,6},{2,0},{4,2},{6,4},{1,7},{3,1},{5,3},{7,5},{8,14},{10,8},{12,... | collective-permute-start | bytes 98312 | tf_op jit(solution)/shard_map/ppermute | solution.py:245
  20.0 2.4 %collective-permute-start.6 = (f32[8,32,256]{2,1,0:T(8,128)S(1)}, f32[8,32,256]{2,1,0:T(8,128)S(1)}, u32[]{:S(2)}, u32[]{:S(2)}) collective-permute-start(f32[8,32,256]{2,1,0:T(8,128)S(1)} %get-tuple-element.26), channel_id=1, source_target_pairs={{0,8},{8,0},{1,9},{9,1},{2,10},{10,2},{3,11},{11,3},{4,12},{12,4},... | collective-permute-start | bytes 786440 | tf_op jit(solution)/shard_map/ppermute | solution.py:261
  21.8 4.3 %collective-permute-start.5 = (f32[8,32,256]{2,1,0:T(8,128)S(1)}, f32[8,32,256]{2,1,0:T(8,128)S(1)}, u32[]{:S(2)}, u32[]{:S(2)}) collective-permute-start(f32[8,32,256]{2,1,0:T(8,128)S(1)} %get-tuple-element.24), channel_id=1, source_target_pairs={{0,8},{8,0},{1,9},{9,1},{2,10},{10,2},{3,11},{11,3},{4,12},{12,4},... | collective-permute-start | bytes 786440 | tf_op jit(solution)/shard_map/ppermute | solution.py:261
  22.4 7.4 %collective-permute-start.7 = (f32[2,32,256]{2,1,0:T(8,128)S(1)}, f32[2,32,256]{2,1,0:T(8,128)S(1)}, u32[]{:S(2)}, u32[]{:S(2)}) collective-permute-start(f32[2,32,256]{2,1,0:T(8,128)S(1)} %get-tuple-element.31), channel_id=1, source_target_pairs={{0,128},{64,192},{128,0},{192,64},{1,129},{65,193},{129,1},{193,65... | collective-permute-start | bytes 196616 | tf_op jit(solution)/shard_map/ppermute | solution.py:268
  25.6 6.6 %collective-permute-start.8 = (f32[2,32,256]{2,1,0:T(8,128)S(1)}, f32[2,32,256]{2,1,0:T(8,128)S(1)}, u32[]{:S(2)}, u32[]{:S(2)}) collective-permute-start(f32[2,32,256]{2,1,0:T(8,128)S(1)} %get-tuple-element.34), channel_id=1, source_target_pairs={{0,64},{64,128},{128,192},{192,0},{1,65},{65,129},{129,193},{193,1... | collective-permute-start | bytes 196616 | tf_op jit(solution)/shard_map/ppermute | solution.py:268
  26.2 6.0 %collective-permute-start.9 = (f32[2,32,256]{2,1,0:T(8,128)S(1)}, f32[2,32,256]{2,1,0:T(8,128)S(1)}, u32[]{:S(2)}, u32[]{:S(2)}) collective-permute-start(f32[2,32,256]{2,1,0:T(8,128)S(1)} %get-tuple-element.30), channel_id=1, source_target_pairs={{0,192},{64,0},{128,64},{192,128},{1,193},{65,1},{129,65},{193,129... | collective-permute-start | bytes 196616 | tf_op jit(solution)/shard_map/ppermute | solution.py:268
  28.9 9.6 %collective-permute-start.10 = (f32[2,32,256]{2,1,0:T(8,128)S(1)}, f32[2,32,256]{2,1,0:T(8,128)S(1)}, u32[]{:S(2)}, u32[]{:S(2)}) collective-permute-start(f32[2,32,256]{2,1,0:T(8,128)S(1)} %get-tuple-element.33), channel_id=1, source_target_pairs={{0,128},{64,192},{128,0},{192,64},{1,129},{65,193},{129,1},{193,65... | collective-permute-start | bytes 196616 | tf_op jit(solution)/shard_map/ppermute | solution.py:268
  28.9 9.6 %collective-permute-start.11 = (f32[2,32,256]{2,1,0:T(8,128)S(1)}, f32[2,32,256]{2,1,0:T(8,128)S(1)}, u32[]{:S(2)}, u32[]{:S(2)}) collective-permute-start(f32[2,32,256]{2,1,0:T(8,128)S(1)} %get-tuple-element.32), channel_id=1, source_target_pairs={{0,64},{64,128},{128,192},{192,0},{1,65},{65,129},{129,193},{193,1... | collective-permute-start | bytes 196616 | tf_op jit(solution)/shard_map/ppermute | solution.py:268
  29.9 8.7 %collective-permute-start.12 = (f32[2,32,256]{2,1,0:T(8,128)S(1)}, f32[2,32,256]{2,1,0:T(8,128)S(1)}, u32[]{:S(2)}, u32[]{:S(2)}) collective-permute-start(f32[2,32,256]{2,1,0:T(8,128)S(1)} %get-tuple-element.28), channel_id=1, source_target_pairs={{0,192},{64,0},{128,64},{192,128},{1,193},{65,1},{129,65},{193,129... | collective-permute-start | bytes 196616 | tf_op jit(solution)/shard_map/ppermute | solution.py:268
  32.2 11.7 %collective-permute-start.15 = (f32[1,32,256]{2,1,0:T(8,128)S(1)}, f32[1,32,256]{2,1,0:T(8,128)S(1)}, u32[]{:S(2)}, u32[]{:S(2)}) collective-permute-start(f32[1,32,256]{2,1,0:T(8,128)S(1)} %fusion), channel_id=1, source_target_pairs={{0,48},{16,0},{32,16},{48,32},{1,49},{17,1},{33,17},{49,33},{2,50}... | collective-permute-start | bytes 98312 | tf_op jit(solution)/shard_map/ppermute | solution.py:271
  38.6 7.9 %collective-permute-start.13 = (f32[1,32,256]{2,1,0:T(8,128)S(1)}, f32[1,32,256]{2,1,0:T(8,128)S(1)}, u32[]{:S(2)}, u32[]{:S(2)}) collective-permute-start(f32[1,32,256]{2,1,0:T(8,128)S(1)} %get-tuple-element.36), channel_id=1, source_target_pairs={{0,32},{16,48},{32,0},{48,16},{1,33},{17,49},{33,1},{49,17},{2,34}... | collective-permute-start | bytes 98312 | tf_op jit(solution)/shard_map/ppermute | solution.py:271
  42.4 6.0 %collective-permute-start.14 = (f32[1,32,256]{2,1,0:T(8,128)S(1)}, f32[1,32,256]{2,1,0:T(8,128)S(1)}, u32[]{:S(2)}, u32[]{:S(2)}) collective-permute-start(f32[1,32,256]{2,1,0:T(8,128)S(1)} %get-tuple-element.35), channel_id=1, source_target_pairs={{0,16},{16,32},{32,48},{48,0},{1,17},{17,33},{33,49},{49,1},{2,18}... | collective-permute-start | bytes 98312 | tf_op jit(solution)/shard_map/ppermute | solution.py:271

commit v9 on v8

--- a/solution.py
+++ b/solution.py
@@ -199,7 +199,9 @@
         first = 16 * part + 4 * g
         q = p_ref[first : first + 4] * alpha.reshape(4, 32, 256)
         for j in range(2):
-            to = 4 * (g // 2) + lax.rem(6 + z - (2 * (g % 2) + j), 4)
+            e = lax.rem(2 * (g % 2) + j + 4 - z, 4)
+            odd, half = lax.rem(e, 2), lax.div(e, 2)
+            to = 4 * (g // 2) + odd * half + (1 - odd) * (3 - half)
             keep_ref[to] = jnp.where(core == 0, q[2 * j], q[2 * j + 1])
             send_ref[to] = jnp.where(core == 0, q[2 * j + 1], q[2 * j])
 
@@ -259,16 +261,20 @@
         )
         near = rest[0] if rest else None
         got = lax.ppermute(give, "core", swap)
-        for i in range(2):
-            for wave in range(2):
-                at = slice(4 * i + 2 * wave, 4 * i + 2 * wave + 2)
-                piece[((2, 1), (3, 0))[part][i], wave] = keep[at] + got[at]
+        for i, d in enumerate(((2, 1), (3, 0))[part]):
+            for wave, at in enumerate((slice(0, 4),) if d == 2 else (slice(0, 2), slice(2, 4))):
+                piece[d, wave] = keep[4 * i : 4 * i + 4][at] + got[4 * i : 4 * i + 4][at]
+    x2 = lax.ppermute(piece[2, 0], "x", ring(2))
     waves = []
     for wave in range(2):
-        x2, x1, x3 = (lax.ppermute(piece[d, wave], "x", ring(d)) for d in (2, 1, 3))
-        waves.append([(piece[0, wave][i : i + 1] + x2[i : i + 1]) + (x1[i : i + 1] + x3[i : i + 1]) for i in range(2)])
-    (far, next_), (own, last) = waves
-    z2, z1, z3 = (lax.ppermute(cell, "z", ring(e)) for e, cell in ((2, far), (1, next_), (3, last)))
+        x1, x3 = (lax.ppermute(piece[d, wave], "x", ring(d)) for d in (1, 3))
+        waves.append([
+            (piece[0, wave][i : i + 1] + x2[2 * wave + i : 2 * wave + i + 1]) + (x1[i : i + 1] + x3[i : i + 1])
+            for i in range(2)
+        ])
+        x2, waves[wave] = lax.optimization_barrier((x2, waves[wave]))
+    (next_, last), (far, own) = waves
+    z1, z3, z2 = (lax.ppermute(cell, "z", ring(e)) for e, cell in ((1, next_), (3, last), (2, far)))
     return ((own + z2) + (z1 + z3)) * (1.0 / 31.0)
 
 

time: 49.3 us -> 50.3 us (1.020)
  waiting for transfers between devices: 10.3 us -> 14.4 us
  starting transfers between devices: 29.3 us -> 26.3 us
    ppermute x6 -> x5, waiting for transfers between devices: 0.02 us -> 5.44 us  [the longest x4 5.44 us: body(): x1, x3 = (lax.ppermute(piece[d, wave], 'x', ring(d)) for d in (1, 3))]
    ppermute x6 -> x5, starting transfers between devices: 9.67 us -> 7.04 us  [the longest x4 6.16 us: body(): x1, x3 = (lax.ppermute(piece[d, wave], 'x', ring(d)) for d in (1, 3))]
    ppermute x3, waiting for transfers between devices: 4.54 us -> 2.15 us  [body(): lax.ppermute(cell, 'z', ring(e))]
    ppermute x1, waiting for transfers between devices: 1.3 us -> 3.24 us  [body(): side_below = lax.ppermute(side[:, :HALO], 'gx', ring(3))]
    ppermute x1, waiting for transfers between devices: 1.86 us -> 0.01 us  [body(): side_above = lax.ppermute(side[:, HALO:], 'gx', ring(1))]
    ppermute x1, starting transfers between devices: 1.35 us -> 0.01 us  [body(): side_above = lax.ppermute(side[:, HALO:], 'gx', ring(1))]
    ppermute x1, starting transfers between devices: 1.89 us -> 3.15 us  [body(): side_below = lax.ppermute(side[:, :HALO], 'gx', ring(3))]
    ppermute x2, waiting for transfers between devices: 0.01 us -> 1.03 us  [body(): got = lax.ppermute(give, 'core', swap)]
  transfers between devices with their start and end apart: 16 -> 15, of which waited for: 5 -> 7; matrix products, arithmetic and copies ran while one was open for 0% -> 0% of each run, Pallas kernels for 9% -> 5%
where the time goes in v9:
time: 50.3 us; the launch traced here: 50.2 us
  starting transfers between devices  26.3 us (52%)
  waiting for transfers between devices  14.4 us (29%)
  Pallas kernels  8.48 us (17%)
  other arithmetic  0.73 us (1%)
    ppermute x3, starting transfers between devices, body(): lax.ppermute(cell, 'z', ring(e))  11.4 us
    pallas_call x5, Pallas kernels, call(): pl.pallas_call(kernel, out_shape=[o if isinstance(o, jax.ShapeDtypeStruct...  8.48 us
    ppermute x4, starting transfers between devices, body(): x1, x3 = (lax.ppermute(piece[d, wave], 'x', ring(d)) for d in (1, 3))  6.16 us
    ppermute x4, waiting for transfers between devices, body(): x1, x3 = (lax.ppermute(piece[d, wave], 'x', ring(d)) for d in (1, 3))  5.44 us
    ppermute x1, waiting for transfers between devices, body(): side_below = lax.ppermute(side[:, :HALO], 'gx', ring(3))  3.24 us
    ppermute x1, starting transfers between devices, body(): side_below = lax.ppermute(side[:, :HALO], 'gx', ring(3))  3.15 us
    ppermute x1, waiting for transfers between devices, body(): side = lax.ppermute(edges, 'gy', swap)  2.57 us
    ppermute x3, waiting for transfers between devices, body(): lax.ppermute(cell, 'z', ring(e))  2.15 us
  transfers between devices with their start and end apart: 15, of which 7 were waited for; matrix products, arithmetic and copies ran while one was open for 0% of the time, Pallas kernels for 5%

profile of v9, /device:TPU:8, one launch (start us, length us, event | category | flops | bytes accessed | tf_op | source)
XLA Modules:
  0.0 50.2 jit_solution(5887692065183503071)
XLA Ops:
  0.0 0.1 stack.23.where
  0.1 2.3 %shard_map.64 = (f32[32,32,256]{2,1,0:T(8,128)S(1)}, f32[32,16,256]{2,1,0:T(8,128)S(1)}, f32[32,16,256]{2,1,0:T(8,128)S(1)}) custom-call(s32[5]{0:T(128)S(1)} %stack.23.where, f32[1,32,32,256]{3,2,1,0:T(8,128)} %p_hbm.1, f32[32,32,256]{2,1,0:T(8,128)} %c_hbm.1), custom_call_target="tpu_custom_call" | custom-call | bytes 1048576 | tf_op jit(solution)/shard_map/pallas_call | solution.py:214
  2.4 1.7 %collective-permute-start = (f32[32,16,256]{2,1,0:T(8,128)S(1)}, f32[32,16,256]{2,1,0:T(8,128)S(1)}, u32[]{:S(2)}, u32[]{:S(2)}) collective-permute-start(f32[32,16,256]{2,1,0:T(8,128)S(1)} %get-tuple-element.22.bottom_ref), channel_id=1, source_target_pairs={{0,2},{2,4},{4,6},{6,0},{1,3},{3,5},{5,7},{7,1},{8,10},{10,12},{12... | collective-permute-start | bytes 1572872 | tf_op jit(solution)/shard_map/ppermute | solution.py:242
  4.0 0.7 %collective-permute-start.1 = (f32[32,16,256]{2,1,0:T(8,128)S(1)}, f32[32,16,256]{2,1,0:T(8,128)S(1)}, u32[]{:S(2)}, u32[]{:S(2)}) collective-permute-start(f32[32,16,256]{2,1,0:T(8,128)S(1)} %get-tuple-element.23.top_ref), channel_id=1, source_target_pairs={{0,6},{2,0},{4,2},{6,4},{1,7},{3,1},{5,3},{7,5},{8,14},{10,8},{12,... | collective-permute-start | bytes 1572872 | tf_op jit(solution)/shard_map/ppermute | solution.py:243
  4.7 0.0 copy-start.1
  4.7 0.7 %shard_map.66 = f32[2,32,256]{2,1,0:T(8,128)S(1)} custom-call(s32[5]{0:T(128)S(1)} %stack.23.where, f32[32,16,256]{2,1,0:T(8,128)S(1)} %get-tuple-element.23.top_ref, f32[32,16,256]{2,1,0:T(8,128)S(1)} %get-tuple-element.22.bottom_ref), custom_call_target="tpu_custom_call" | custom-call | bytes 1048576 | tf_op jit(solution)/shard_map/pallas_call | solution.py:214
  5.5 0.0 copy-start
  5.5 1.8 %collective-permute-start.2 = (f32[2,32,256]{2,1,0:T(8,128)S(1)}, f32[2,32,256]{2,1,0:T(8,128)S(1)}, u32[]{:S(2)}, u32[]{:S(2)}) collective-permute-start(f32[2,32,256]{2,1,0:T(8,128)S(1)} %shard_map.66), channel_id=1, source_target_pairs={{0,1},{1,0},{2,3},{3,2},{4,5},{5,4},{6,7},{7,6},{8,9},{9,8},{10,11... | collective-permute-start | bytes 196616 | tf_op jit(solution)/shard_map/ppermute | solution.py:245
  7.2 2.6 %collective-permute-done.2.refs_1_ = f32[2,32,256]{2,1,0:T(8,128)S(1)} collective-permute-done((f32[2,32,256]{2,1,0:T(8,128)S(1)}, f32[2,32,256]{2,1,0:T(8,128)S(1)}, u32[]{:S(2)}, u32[]{:S(2)}) %collective-permute-start.2) | collective-permute-done | bytes 65568 | tf_op jit(solution)/shard_map/ppermute | solution.py:245
  9.8 3.1 %collective-permute-start.4 = (f32[2,16,256]{2,1,0:T(8,128)S(1)}, f32[2,16,256]{2,1,0:T(8,128)S(1)}, u32[]{:S(2)}, u32[]{:S(2)}) collective-permute-start(f32[2,16,256]{2,1,0:T(8,128)S(1)} %get-tuple-element.47), channel_id=1, source_target_pairs={{0,6},{2,0},{4,2},{6,4},{1,7},{3,1},{5,3},{7,5},{8,14},{10,8},{12,... | collective-permute-start | bytes 98312 | tf_op jit(solution)/shard_map/ppermute | solution.py:247
  13.0 0.0 copy-start.2
  13.0 0.0 collective-permute-start.3
  13.0 0.0 copy-done.1
  13.0 0.0 copy-done
  13.0 1.9 %shard_map.65 = (bf16[512,128]{1,0:T(8,128)(2,1)S(1)}, bf16[512,128]{1,0:T(8,128)(2,1)S(1)}, bf16[2,1024,256]{2,1,0:T(8,128)(2,1)S(1)}) custom-call(s32[5]{0:T(128)S(1)} %stack.23.where, bf16[2,2,64,128]{3,2,1,0:T(8,128)(2,1)S(1)} %copy-done.1, bf16[2,2,4,32,128]{4,3,2,1,0:T(8,128)(2,1)S(1)} %copy-done, bf16[2,1024,256]{2,1,0:T(8,128)(2,1)} %constant.31.clone.right_hbm), custom_call_target="tpu_custom_call" | custom-call | bytes 1048576 | tf_op jit(solution)/shard_map/pallas_call | solution.py:214
  14.9 3.2 %collective-permute-done.4.refs_2_ = f32[2,16,256]{2,1,0:T(8,128)S(1)} collective-permute-done((f32[2,16,256]{2,1,0:T(8,128)S(1)}, f32[2,16,256]{2,1,0:T(8,128)S(1)}, u32[]{:S(2)}, u32[]{:S(2)}) %collective-permute-start.4) | collective-permute-done | bytes 32800 | tf_op jit(solution)/shard_map/ppermute | solution.py:247
  18.1 0.0 collective-permute-done.3.refs_0_
  18.1 0.0 collective-permute-done.above_ref
  18.1 0.0 collective-permute-done.1.below_ref
  18.1 0.0 copy-done.2
  18.2 1.9 %shard_map.67 = (f32[8,32,256]{2,1,0:T(8,128)S(1)}, f32[8,32,256]{2,1,0:T(8,128)S(1)}, f32[128,128]{1,0:T(8,128)S(1)}) custom-call(s32[5]{0:T(128)S(1)} %stack.23.where, f32[32,32,256]{2,1,0:T(8,128)S(1)} %get-tuple-element.21.p_ref, f32[32,16,256]{2,1,0:T(8,128)S(1)} %collective-permute-done.above_ref, f32[32,16,256]{2,1,0:T(8,128)S(1)} %get-tuple-element.23.top_ref, ...), custom_call_target="tpu_custom_call" | custom-call | flops 2000000000 | bytes 1048576 | tf_op jit(solution)/shard_map/pallas_call | solution.py:214
  20.0 1.7 %shard_map.68 = (f32[8,32,256]{2,1,0:T(8,128)S(1)}, f32[8,32,256]{2,1,0:T(8,128)S(1)}) custom-call(s32[5]{0:T(128)S(1)} %stack.23.where, f32[32,32,256]{2,1,0:T(8,128)S(1)} %get-tuple-element.21.p_ref, f32[32,16,256]{2,1,0:T(8,128)S(1)} %collective-permute-done.above_ref, f32[32,16,256]{2,1,0:T(8,128)S(1)} %get-tuple-element.23.top_ref, ...), custom_call_target="tpu_custom_call" | custom-call | flops 2000000000 | bytes 1048576 | tf_op jit(solution)/shard_map/pallas_call | solution.py:214
  21.7 0.1 collective-permute-start.7
  21.8 0.5 collective-permute-start.5
  22.3 1.0 %collective-permute-done.7 = f32[8,32,256]{2,1,0:T(8,128)S(1)} collective-permute-done((f32[8,32,256]{2,1,0:T(8,128)S(1)}, f32[8,32,256]{2,1,0:T(8,128)S(1)}, u32[]{:S(2)}, u32[]{:S(2)}) %collective-permute-start.7) | collective-permute-done | bytes 262176 | tf_op jit(solution)/shard_map/ppermute | solution.py:263
  23.4 2.8 %collective-permute-start.9 = (f32[2,32,256]{2,1,0:T(8,128)S(1)}, f32[2,32,256]{2,1,0:T(8,128)S(1)}, u32[]{:S(2)}, u32[]{:S(2)}) collective-permute-start(f32[2,32,256]{2,1,0:T(8,128)S(1)} %get-tuple-element.39), channel_id=1, source_target_pairs={{0,192},{64,0},{128,64},{192,128},{1,193},{65,1},{129,65},{193,129... | collective-permute-start | bytes 196616 | tf_op jit(solution)/shard_map/ppermute | solution.py:270
  26.2 0.0 collective-permute-done.5
  26.3 0.9 %collective-permute-start.6 = (f32[4,32,256]{2,1,0:T(8,128)S(1)}, f32[4,32,256]{2,1,0:T(8,128)S(1)}, u32[]{:S(2)}, u32[]{:S(2)}) collective-permute-start(f32[4,32,256]{2,1,0:T(8,128)S(1)} %slice_add_fusion), channel_id=1, source_target_pairs={{0,128},{64,192},{128,0},{192,64},{1,129},{65,193},{129,1},{193,65... | collective-permute-start | bytes 393224 | tf_op jit(solution)/shard_map/ppermute | solution.py:267
  27.2 1.0 %collective-permute-start.8 = (f32[2,32,256]{2,1,0:T(8,128)S(1)}, f32[2,32,256]{2,1,0:T(8,128)S(1)}, u32[]{:S(2)}, u32[]{:S(2)}) collective-permute-start(f32[2,32,256]{2,1,0:T(8,128)S(1)} %get-tuple-element.42), channel_id=1, source_target_pairs={{0,64},{64,128},{128,192},{192,0},{1,65},{65,129},{129,193},{193,1... | collective-permute-start | bytes 196616 | tf_op jit(solution)/shard_map/ppermute | solution.py:270
  28.1 2.4 %collective-permute-start.11 = (f32[2,32,256]{2,1,0:T(8,128)S(1)}, f32[2,32,256]{2,1,0:T(8,128)S(1)}, u32[]{:S(2)}, u32[]{:S(2)}) collective-permute-start(f32[2,32,256]{2,1,0:T(8,128)S(1)} %get-tuple-element.38), channel_id=1, source_target_pairs={{0,192},{64,0},{128,64},{192,128},{1,193},{65,1},{129,65},{193,129... | collective-permute-start | bytes 196616 | tf_op jit(solution)/shard_map/ppermute | solution.py:270
  30.5 0.0 collective-permute-start.10
  30.5 0.0 collective-permute-done.9
  30.5 4.1 %collective-permute-done.8 = f32[2,32,256]{2,1,0:T(8,128)S(1)} collective-permute-done((f32[2,32,256]{2,1,0:T(8,128)S(1)}, f32[2,32,256]{2,1,0:T(8,128)S(1)}, u32[]{:S(2)}, u32[]{:S(2)}) %collective-permute-start.8) | collective-permute-done | bytes 65568 | tf_op jit(solution)/shard_map/ppermute | solution.py:270
  34.6 0.0 collective-permute-done.6
  34.6 0.0 collective-permute-done.11
  34.6 1.3 %collective-permute-done.10 = f32[2,32,256]{2,1,0:T(8,128)S(1)} collective-permute-done((f32[2,32,256]{2,1,0:T(8,128)S(1)}, f32[2,32,256]{2,1,0:T(8,128)S(1)}, u32[]{:S(2)}, u32[]{:S(2)}) %collective-permute-start.10) | collective-permute-done | bytes 65568 | tf_op jit(solution)/shard_map/ppermute | solution.py:270
  36.0 7.3 %collective-permute-start.12 = (f32[1,32,256]{2,1,0:T(8,128)S(1)}, f32[1,32,256]{2,1,0:T(8,128)S(1)}, u32[]{:S(2)}, u32[]{:S(2)}) collective-permute-start(f32[1,32,256]{2,1,0:T(8,128)S(1)} %get-tuple-element.34), channel_id=1, source_target_pairs={{0,32},{16,48},{32,0},{48,16},{1,33},{17,49},{33,1},{49,17},{2,34}... | collective-permute-start | bytes 98312 | tf_op jit(solution)/shard_map/ppermute | solution.py:277
  43.3 1.5 %collective-permute-start.13 = (f32[1,32,256]{2,1,0:T(8,128)S(1)}, f32[1,32,256]{2,1,0:T(8,128)S(1)}, u32[]{:S(2)}, u32[]{:S(2)}) collective-permute-start(f32[1,32,256]{2,1,0:T(8,128)S(1)} %get-tuple-element.35), channel_id=1, source_target_pairs={{0,16},{16,32},{32,48},{48,0},{1,17},{17,33},{33,49},{49,1},{2,18}... | collective-permute-start | bytes 98312 | tf_op jit(solution)/shard_map/ppermute | solution.py:277
  44.7 2.7 %collective-permute-start.14 = (f32[1,32,256]{2,1,0:T(8,128)S(1)}, f32[1,32,256]{2,1,0:T(8,128)S(1)}, u32[]{:S(2)}, u32[]{:S(2)}) collective-permute-start(f32[1,32,256]{2,1,0:T(8,128)S(1)} %get-tuple-element.36), channel_id=1, source_target_pairs={{0,48},{16,0},{32,16},{48,32},{1,49},{17,1},{33,17},{49,33},{2,50}... | collective-permute-start | bytes 98312 | tf_op jit(solution)/shard_map/ppermute | solution.py:277
  47.4 0.0 collective-permute-done.12
  47.4 1.9 %collective-permute-done.13 = f32[1,32,256]{2,1,0:T(8,128)S(1)} collective-permute-done((f32[1,32,256]{2,1,0:T(8,128)S(1)}, f32[1,32,256]{2,1,0:T(8,128)S(1)}, u32[]{:S(2)}, u32[]{:S(2)}) %collective-permute-start.13) | collective-permute-done | bytes 32800 | tf_op jit(solution)/shard_map/ppermute | solution.py:277
  49.3 0.3 collective-permute-done.14
  49.5 0.6 %add_multiply_fusion = f32[1,32,256]{2,1,0:T(8,128)} fusion(f32[1,32,256]{2,1,0:T(8,128)S(1)} %collective-permute-done.13, f32[1,32,256]{2,1,0:T(8,128)S(1)} %collective-permute-done.14, f32[1,32,256]{2,1,0:T(8,128)S(1)} %get-tuple-element.33, f32[1,32,256]{2,1,0:T(8,128)S(1)} %collective-permute-done.12), kind=kLoop, calls=%fused_computation.19 | loop fusion | flops 32768 | bytes 163840 | tf_op jit(solution)/shard_map/mul | solution.py:278
  (6 shorter events, 0.1 us)
Async XLA Ops:
  2.4 15.7 %collective-permute-start = (f32[32,16,256]{2,1,0:T(8,128)S(1)}, f32[32,16,256]{2,1,0:T(8,128)S(1)}, u32[]{:S(2)}, u32[]{:S(2)}) collective-permute-start(f32[32,16,256]{2,1,0:T(8,128)S(1)} %get-tuple-element.22.bottom_ref), channel_id=1, source_target_pairs={{0,2},{2,4},{4,6},{6,0},{1,3},{3,5},{5,7},{7,1},{8,10},{10,12},{12... | collective-permute-start | bytes 1572872 | tf_op jit(solution)/shard_map/ppermute | solution.py:242
  4.0 14.1 %collective-permute-start.1 = (f32[32,16,256]{2,1,0:T(8,128)S(1)}, f32[32,16,256]{2,1,0:T(8,128)S(1)}, u32[]{:S(2)}, u32[]{:S(2)}) collective-permute-start(f32[32,16,256]{2,1,0:T(8,128)S(1)} %get-tuple-element.23.top_ref), channel_id=1, source_target_pairs={{0,6},{2,0},{4,2},{6,4},{1,7},{3,1},{5,3},{7,5},{8,14},{10,8},{12,... | collective-permute-start | bytes 1572872 | tf_op jit(solution)/shard_map/ppermute | solution.py:243
  4.7 8.3 %copy-start.1 = (bf16[2,2,64,128]{3,2,1,0:T(8,128)(2,1)S(1)}, bf16[2,2,64,128]{3,2,1,0:T(8,128)(2,1)}, u32[]{:S(2)}) copy-start(bf16[2,2,64,128]{3,2,1,0:T(8,128)(2,1)} %constant.32.clone.edge_ref) | copy-start | bytes 196612
  5.5 7.5 %copy-start = (bf16[2,2,4,32,128]{4,3,2,1,0:T(8,128)(2,1)S(1)}, bf16[2,2,4,32,128]{4,3,2,1,0:T(8,128)(2,1)}, u32[]{:S(2)}) copy-start(bf16[2,2,4,32,128]{4,3,2,1,0:T(8,128)(2,1)} %constant.30.clone.patch_ref) | copy-start | bytes 393220
  5.5 4.4 %collective-permute-start.2 = (f32[2,32,256]{2,1,0:T(8,128)S(1)}, f32[2,32,256]{2,1,0:T(8,128)S(1)}, u32[]{:S(2)}, u32[]{:S(2)}) collective-permute-start(f32[2,32,256]{2,1,0:T(8,128)S(1)} %shard_map.66), channel_id=1, source_target_pairs={{0,1},{1,0},{2,3},{3,2},{4,5},{5,4},{6,7},{7,6},{8,9},{9,8},{10,11... | collective-permute-start | bytes 196616 | tf_op jit(solution)/shard_map/ppermute | solution.py:245
  9.8 8.3 %collective-permute-start.4 = (f32[2,16,256]{2,1,0:T(8,128)S(1)}, f32[2,16,256]{2,1,0:T(8,128)S(1)}, u32[]{:S(2)}, u32[]{:S(2)}) collective-permute-start(f32[2,16,256]{2,1,0:T(8,128)S(1)} %get-tuple-element.47), channel_id=1, source_target_pairs={{0,6},{2,0},{4,2},{6,4},{1,7},{3,1},{5,3},{7,5},{8,14},{10,8},{12,... | collective-permute-start | bytes 98312 | tf_op jit(solution)/shard_map/ppermute | solution.py:247
  13.0 5.2 %copy-start.2 = (bf16[4,96,192]{2,1,0:T(8,128)(2,1)S(1)}, bf16[4,96,192]{2,1,0:T(8,128)(2,1)}, u32[]{:S(2)}) copy-start(bf16[4,96,192]{2,1,0:T(8,128)(2,1)} %constant.29.clone.left_ref) | copy-start | bytes 442372
  13.0 5.2 %collective-permute-start.3 = (f32[2,16,256]{2,1,0:T(8,128)S(1)}, f32[2,16,256]{2,1,0:T(8,128)S(1)}, u32[]{:S(2)}, u32[]{:S(2)}) collective-permute-start(f32[2,16,256]{2,1,0:T(8,128)S(1)} %get-tuple-element.48), channel_id=1, source_target_pairs={{0,2},{2,4},{4,6},{6,0},{1,3},{3,5},{5,7},{7,1},{8,10},{10,12},{12... | collective-permute-start | bytes 98312 | tf_op jit(solution)/shard_map/ppermute | solution.py:246
  21.7 1.6 %collective-permute-start.7 = (f32[8,32,256]{2,1,0:T(8,128)S(1)}, f32[8,32,256]{2,1,0:T(8,128)S(1)}, u32[]{:S(2)}, u32[]{:S(2)}) collective-permute-start(f32[8,32,256]{2,1,0:T(8,128)S(1)} %get-tuple-element.31), channel_id=1, source_target_pairs={{0,8},{8,0},{1,9},{9,1},{2,10},{10,2},{3,11},{11,3},{4,12},{12,4},... | collective-permute-start | bytes 786440 | tf_op jit(solution)/shard_map/ppermute | solution.py:263
  21.8 4.4 %collective-permute-start.5 = (f32[8,32,256]{2,1,0:T(8,128)S(1)}, f32[8,32,256]{2,1,0:T(8,128)S(1)}, u32[]{:S(2)}, u32[]{:S(2)}) collective-permute-start(f32[8,32,256]{2,1,0:T(8,128)S(1)} %get-tuple-element.28), channel_id=1, source_target_pairs={{0,8},{8,0},{1,9},{9,1},{2,10},{10,2},{3,11},{11,3},{4,12},{12,4},... | collective-permute-start | bytes 786440 | tf_op jit(solution)/shard_map/ppermute | solution.py:263
  23.4 7.1 %collective-permute-start.9 = (f32[2,32,256]{2,1,0:T(8,128)S(1)}, f32[2,32,256]{2,1,0:T(8,128)S(1)}, u32[]{:S(2)}, u32[]{:S(2)}) collective-permute-start(f32[2,32,256]{2,1,0:T(8,128)S(1)} %get-tuple-element.39), channel_id=1, source_target_pairs={{0,192},{64,0},{128,64},{192,128},{1,193},{65,1},{129,65},{193,129... | collective-permute-start | bytes 196616 | tf_op jit(solution)/shard_map/ppermute | solution.py:270
  26.3 8.4 %collective-permute-start.6 = (f32[4,32,256]{2,1,0:T(8,128)S(1)}, f32[4,32,256]{2,1,0:T(8,128)S(1)}, u32[]{:S(2)}, u32[]{:S(2)}) collective-permute-start(f32[4,32,256]{2,1,0:T(8,128)S(1)} %slice_add_fusion), channel_id=1, source_target_pairs={{0,128},{64,192},{128,0},{192,64},{1,129},{65,193},{129,1},{193,65... | collective-permute-start | bytes 393224 | tf_op jit(solution)/shard_map/ppermute | solution.py:267
  27.2 7.4 %collective-permute-start.8 = (f32[2,32,256]{2,1,0:T(8,128)S(1)}, f32[2,32,256]{2,1,0:T(8,128)S(1)}, u32[]{:S(2)}, u32[]{:S(2)}) collective-permute-start(f32[2,32,256]{2,1,0:T(8,128)S(1)} %get-tuple-element.42), channel_id=1, source_target_pairs={{0,64},{64,128},{128,192},{192,0},{1,65},{65,129},{129,193},{193,1... | collective-permute-start | bytes 196616 | tf_op jit(solution)/shard_map/ppermute | solution.py:270
  28.1 6.5 %collective-permute-start.11 = (f32[2,32,256]{2,1,0:T(8,128)S(1)}, f32[2,32,256]{2,1,0:T(8,128)S(1)}, u32[]{:S(2)}, u32[]{:S(2)}) collective-permute-start(f32[2,32,256]{2,1,0:T(8,128)S(1)} %get-tuple-element.38), channel_id=1, source_target_pairs={{0,192},{64,0},{128,64},{192,128},{1,193},{65,1},{129,65},{193,129... | collective-permute-start | bytes 196616 | tf_op jit(solution)/shard_map/ppermute | solution.py:270
  30.5 5.5 %collective-permute-start.10 = (f32[2,32,256]{2,1,0:T(8,128)S(1)}, f32[2,32,256]{2,1,0:T(8,128)S(1)}, u32[]{:S(2)}, u32[]{:S(2)}) collective-permute-start(f32[2,32,256]{2,1,0:T(8,128)S(1)} %get-tuple-element.41), channel_id=1, source_target_pairs={{0,64},{64,128},{128,192},{192,0},{1,65},{65,129},{129,193},{193,1... | collective-permute-start | bytes 196616 | tf_op jit(solution)/shard_map/ppermute | solution.py:270
  36.0 11.4 %collective-permute-start.12 = (f32[1,32,256]{2,1,0:T(8,128)S(1)}, f32[1,32,256]{2,1,0:T(8,128)S(1)}, u32[]{:S(2)}, u32[]{:S(2)}) collective-permute-start(f32[1,32,256]{2,1,0:T(8,128)S(1)} %get-tuple-element.34), channel_id=1, source_target_pairs={{0,32},{16,48},{32,0},{48,16},{1,33},{17,49},{33,1},{49,17},{2,34}... | collective-permute-start | bytes 98312 | tf_op jit(solution)/shard_map/ppermute | solution.py:277
  43.3 6.0 %collective-permute-start.13 = (f32[1,32,256]{2,1,0:T(8,128)S(1)}, f32[1,32,256]{2,1,0:T(8,128)S(1)}, u32[]{:S(2)}, u32[]{:S(2)}) collective-permute-start(f32[1,32,256]{2,1,0:T(8,128)S(1)} %get-tuple-element.35), channel_id=1, source_target_pairs={{0,16},{16,32},{32,48},{48,0},{1,17},{17,33},{33,49},{49,1},{2,18}... | collective-permute-start | bytes 98312 | tf_op jit(solution)/shard_map/ppermute | solution.py:277
  44.7 4.8 %collective-permute-start.14 = (f32[1,32,256]{2,1,0:T(8,128)S(1)}, f32[1,32,256]{2,1,0:T(8,128)S(1)}, u32[]{:S(2)}, u32[]{:S(2)}) collective-permute-start(f32[1,32,256]{2,1,0:T(8,128)S(1)} %get-tuple-element.36), channel_id=1, source_target_pairs={{0,48},{16,0},{32,16},{48,32},{1,49},{17,1},{33,17},{49,33},{2,50}... | collective-permute-start | bytes 98312 | tf_op jit(solution)/shard_map/ppermute | solution.py:277

commit v10 on v8

--- a/solution.py
+++ b/solution.py
@@ -98,11 +98,13 @@
         bottom_ref[at] = v[:, HALO:]
 
 
-def edge_kernel(where, top_ref, bottom_ref, edge_ref):
+def edge_kernel(where, top_ref, bottom_ref, edge_ref, edge_top_ref, edge_bottom_ref):
     gy = where[2]
     lane = lax.broadcasted_iota(jnp.int32, (1, 128), 1)
     near = pl.ds(pl.multiple_of(128 * (1 - gy), 128), 128)
-    for r_ref, rows in ((top_ref, slice(0, HALO)), (bottom_ref, slice(HALO, 2 * HALO))):
+    for r_ref, rows, half_ref in (
+        (top_ref, slice(0, HALO), edge_top_ref), (bottom_ref, slice(HALO, 2 * HALO), edge_bottom_ref)
+    ):
         edges = jnp.zeros((64, 128), F32)
         for g in range(8):
             v = r_ref[4 * g : 4 * g + 4, :, near].reshape(64, 128)
@@ -110,7 +112,9 @@
                 v = pltpu.roll(v, 16 * g, 1)
             edges = jnp.where(lane // 16 == lax.rem(g + 7 * (1 - gy), 8), v, edges)
         for f in range(4):
-            edge_ref[f // 2, rows, 128 * (f % 2) : 128 * (f % 2) + 128] = edges[16 * f : 16 * f + 16]
+            lanes = slice(128 * (f % 2), 128 * (f % 2) + 128)
+            edge_ref[f // 2, rows, lanes] = edges[16 * f : 16 * f + 16]
+            half_ref[f // 2, :, lanes] = edges[16 * f : 16 * f + 16]
 
 
 def table_kernel(
@@ -239,10 +243,13 @@
     )
     above = lax.ppermute(bottom, "gx", ring(1))
     below = lax.ppermute(top, "gx", ring(3))
-    edges = call(edge_kernel, [(2, 32, 256)], where, top, bottom)[0]
+    edges, edge_top, edge_bottom = call(
+        edge_kernel, [(2, 32, 256)] + [(2, 16, 256)] * 2, where, top, bottom
+    )
+    diagonal = lambda d: [(2 * a + b, 2 * ((a + d) % 4) + 1 - b) for a in range(4) for b in range(2)]
+    side_above = lax.ppermute(edge_bottom, ("gx", "gy"), diagonal(1))
+    side_below = lax.ppermute(edge_top, ("gx", "gy"), diagonal(3))
     side = lax.ppermute(edges, "gy", swap)
-    side_above = lax.ppermute(side[:, HALO:], "gx", ring(1))
-    side_below = lax.ppermute(side[:, :HALO], "gx", ring(3))
     eh, el, right = call(
         table_kernel, [jax.ShapeDtypeStruct(s, BF16) for s in [(512, 128)] * 2 + [(2, 1024, 256)]],
         where, edge, patch, right, hbm=(3,), scratch=[sems((2, 4))],

time: 49.3 us -> 49.3 us (level)
    ppermute x1, waiting for transfers between devices: 0.01 us -> 3.5 us  [body(): above = lax.ppermute(bottom, 'gx', ring(1))]
    ppermute x1, waiting for transfers between devices: 2.57 us -> 0.01 us  [body(): side = lax.ppermute(edges, 'gy', swap)]
    ppermute x2, waiting for transfers between devices: 3.16 us -> 1.26 us  [the longest x1 1.12 us: body(): side_above = lax.ppermute(edge_bottom, ('gx', 'gy'), diagonal(1))]
    ppermute x1, waiting for transfers between devices: 0.01 us -> 1.3 us  [body(): below = lax.ppermute(top, 'gx', ring(3))]
  transfers between devices with their start and end apart: 16 -> 16, of which waited for: 5 -> 6; matrix products, arithmetic and copies ran while one was open for 0% -> 0% of each run, Pallas kernels for 9% -> 9%
where the time goes in v10:
time: 49.3 us; the launch traced here: 49 us
  starting transfers between devices  29 us (59%)
  waiting for transfers between devices  10.6 us (22%)
  Pallas kernels  8.47 us (17%)
  other arithmetic  0.73 us (1%)
    ppermute x3, starting transfers between devices, body(): lax.ppermute(cell, 'z', ring(e))  11.6 us
    ppermute x6, starting transfers between devices, body(): x2, x1, x3 = (lax.ppermute(piece[d, wave], 'x', ring(d)) for d in (2, 1, 3))  9.67 us
    pallas_call x5, Pallas kernels, call(): pl.pallas_call(kernel, out_shape=[o if isinstance(o, jax.ShapeDtypeStruct...  8.47 us
    ppermute x3, waiting for transfers between devices, body(): lax.ppermute(cell, 'z', ring(e))  4.55 us
    ppermute x1, waiting for transfers between devices, body(): above = lax.ppermute(bottom, 'gx', ring(1))  3.5 us
    ppermute x1, starting transfers between devices, body(): side_below = lax.ppermute(edge_top, ('gx', 'gy'), diagonal(3))  1.8 us
    ppermute x1, starting transfers between devices, body(): side = lax.ppermute(edges, 'gy', swap)  1.76 us
    ppermute x1, starting transfers between devices, body(): above = lax.ppermute(bottom, 'gx', ring(1))  1.65 us
  transfers between devices with their start and end apart: 16, of which 6 were waited for; matrix products, arithmetic and copies ran while one was open for 0% of the time, Pallas kernels for 9%

profile of v10, /device:TPU:8, one launch (start us, length us, event | category | flops | bytes accessed | tf_op | source)
XLA Modules:
  0.0 49.0 jit_solution(5677905710676025100)
XLA Ops:
  0.0 0.1 stack.23.where
  0.1 2.3 %shard_map.64 = (f32[32,32,256]{2,1,0:T(8,128)S(1)}, f32[32,16,256]{2,1,0:T(8,128)S(1)}, f32[32,16,256]{2,1,0:T(8,128)S(1)}) custom-call(s32[5]{0:T(128)S(1)} %stack.23.where, f32[1,32,32,256]{3,2,1,0:T(8,128)} %p_hbm.1, f32[32,32,256]{2,1,0:T(8,128)} %c_hbm.1), custom_call_target="tpu_custom_call" | custom-call | bytes 1048576 | tf_op jit(solution)/shard_map/pallas_call | solution.py:216
  2.4 1.7 %collective-permute-start = (f32[32,16,256]{2,1,0:T(8,128)S(1)}, f32[32,16,256]{2,1,0:T(8,128)S(1)}, u32[]{:S(2)}, u32[]{:S(2)}) collective-permute-start(f32[32,16,256]{2,1,0:T(8,128)S(1)} %get-tuple-element.20.bottom_ref), channel_id=1, source_target_pairs={{0,2},{2,4},{4,6},{6,0},{1,3},{3,5},{5,7},{7,1},{8,10},{10,12},{12... | collective-permute-start | bytes 1572872 | tf_op jit(solution)/shard_map/ppermute | solution.py:244
  4.0 0.0 copy-start
  4.0 0.0 copy-start.1
  4.0 0.7 %collective-permute-start.1 = (f32[32,16,256]{2,1,0:T(8,128)S(1)}, f32[32,16,256]{2,1,0:T(8,128)S(1)}, u32[]{:S(2)}, u32[]{:S(2)}) collective-permute-start(f32[32,16,256]{2,1,0:T(8,128)S(1)} %get-tuple-element.21.top_ref), channel_id=1, source_target_pairs={{0,6},{2,0},{4,2},{6,4},{1,7},{3,1},{5,3},{7,5},{8,14},{10,8},{12,... | collective-permute-start | bytes 1572872 | tf_op jit(solution)/shard_map/ppermute | solution.py:245
  4.7 0.7 %shard_map.66 = (f32[2,32,256]{2,1,0:T(8,128)S(1)}, f32[2,16,256]{2,1,0:T(8,128)S(1)}, f32[2,16,256]{2,1,0:T(8,128)S(1)}) custom-call(s32[5]{0:T(128)S(1)} %stack.23.where, f32[32,16,256]{2,1,0:T(8,128)S(1)} %get-tuple-element.21.top_ref, f32[32,16,256]{2,1,0:T(8,128)S(1)} %get-tuple-element.20.bottom_ref), custom_call_target="tpu_custom_call" | custom-call | bytes 1048576 | tf_op jit(solution)/shard_map/pallas_call | solution.py:216
  5.5 1.8 %collective-permute-start.3 = (f32[2,32,256]{2,1,0:T(8,128)S(1)}, f32[2,32,256]{2,1,0:T(8,128)S(1)}, u32[]{:S(2)}, u32[]{:S(2)}) collective-permute-start(f32[2,32,256]{2,1,0:T(8,128)S(1)} %get-tuple-element.24), channel_id=1, source_target_pairs={{0,1},{1,0},{2,3},{3,2},{4,5},{5,4},{6,7},{7,6},{8,9},{9,8},{10,11... | collective-permute-start | bytes 196616 | tf_op jit(solution)/shard_map/ppermute | solution.py:252
  7.2 1.1 %collective-permute-start.2 = (f32[2,16,256]{2,1,0:T(8,128)S(1)}, f32[2,16,256]{2,1,0:T(8,128)S(1)}, u32[]{:S(2)}, u32[]{:S(2)}) collective-permute-start(f32[2,16,256]{2,1,0:T(8,128)S(1)} %get-tuple-element.23), channel_id=1, source_target_pairs={{0,3},{1,2},{2,5},{3,4},{4,7},{5,6},{6,1},{7,0},{8,11},{9,10},{10,... | collective-permute-start | bytes 98312 | tf_op jit(solution)/shard_map/ppermute | solution.py:250
  8.4 0.0 copy-start.2
  8.4 1.8 %collective-permute-start.4 = (f32[2,16,256]{2,1,0:T(8,128)S(1)}, f32[2,16,256]{2,1,0:T(8,128)S(1)}, u32[]{:S(2)}, u32[]{:S(2)}) collective-permute-start(f32[2,16,256]{2,1,0:T(8,128)S(1)} %get-tuple-element.25), channel_id=1, source_target_pairs={{0,7},{1,6},{2,1},{3,0},{4,3},{5,2},{6,5},{7,4},{8,15},{9,14},{10,... | collective-permute-start | bytes 98312 | tf_op jit(solution)/shard_map/ppermute | solution.py:251
  10.2 0.0 copy-done
  10.2 0.0 copy-done.1
  10.2 1.9 %shard_map.65 = (bf16[512,128]{1,0:T(8,128)(2,1)S(1)}, bf16[512,128]{1,0:T(8,128)(2,1)S(1)}, bf16[2,1024,256]{2,1,0:T(8,128)(2,1)S(1)}) custom-call(s32[5]{0:T(128)S(1)} %stack.23.where, bf16[2,2,64,128]{3,2,1,0:T(8,128)(2,1)S(1)} %copy-done.1, bf16[2,2,4,32,128]{4,3,2,1,0:T(8,128)(2,1)S(1)} %copy-done, bf16[2,1024,256]{2,1,0:T(8,128)(2,1)} %constant.31.clone.right_hbm), custom_call_target="tpu_custom_call" | custom-call | bytes 1048576 | tf_op jit(solution)/shard_map/pallas_call | solution.py:216
  12.1 1.1 %collective-permute-done.2.refs_0_ = f32[2,16,256]{2,1,0:T(8,128)S(1)} collective-permute-done((f32[2,16,256]{2,1,0:T(8,128)S(1)}, f32[2,16,256]{2,1,0:T(8,128)S(1)}, u32[]{:S(2)}, u32[]{:S(2)}) %collective-permute-start.2) | collective-permute-done | bytes 32800 | tf_op jit(solution)/shard_map/ppermute | solution.py:250
  13.2 0.1 collective-permute-done.4.refs_2_
  13.3 0.0 collective-permute-done.3.refs_1_
  13.3 3.5 %collective-permute-done.above_ref = f32[32,16,256]{2,1,0:T(8,128)S(1)} collective-permute-done((f32[32,16,256]{2,1,0:T(8,128)S(1)}, f32[32,16,256]{2,1,0:T(8,128)S(1)}, u32[]{:S(2)}, u32[]{:S(2)}) %collective-permute-start) | collective-permute-done | bytes 524320 | tf_op jit(solution)/shard_map/ppermute | solution.py:244
  16.8 1.3 %collective-permute-done.1.below_ref = f32[32,16,256]{2,1,0:T(8,128)S(1)} collective-permute-done((f32[32,16,256]{2,1,0:T(8,128)S(1)}, f32[32,16,256]{2,1,0:T(8,128)S(1)}, u32[]{:S(2)}, u32[]{:S(2)}) %collective-permute-start.1) | collective-permute-done | bytes 524320 | tf_op jit(solution)/shard_map/ppermute | solution.py:245
  18.1 0.0 copy-done.2
  18.1 1.9 %shard_map.67 = (f32[8,32,256]{2,1,0:T(8,128)S(1)}, f32[8,32,256]{2,1,0:T(8,128)S(1)}, f32[128,128]{1,0:T(8,128)S(1)}) custom-call(s32[5]{0:T(128)S(1)} %stack.23.where, f32[32,32,256]{2,1,0:T(8,128)S(1)} %get-tuple-element.19.p_ref, f32[32,16,256]{2,1,0:T(8,128)S(1)} %collective-permute-done.above_ref, f32[32,16,256]{2,1,0:T(8,128)S(1)} %get-tuple-element.21.top_ref, ...), custom_call_target="tpu_custom_call" | custom-call | flops 2000000000 | bytes 1048576 | tf_op jit(solution)/shard_map/pallas_call | solution.py:216
  20.0 0.1 collective-permute-start.6
  20.1 1.7 %shard_map.68 = (f32[8,32,256]{2,1,0:T(8,128)S(1)}, f32[8,32,256]{2,1,0:T(8,128)S(1)}) custom-call(s32[5]{0:T(128)S(1)} %stack.23.where, f32[32,32,256]{2,1,0:T(8,128)S(1)} %get-tuple-element.19.p_ref, f32[32,16,256]{2,1,0:T(8,128)S(1)} %collective-permute-done.above_ref, f32[32,16,256]{2,1,0:T(8,128)S(1)} %get-tuple-element.21.top_ref, ...), custom_call_target="tpu_custom_call" | custom-call | flops 2000000000 | bytes 1048576 | tf_op jit(solution)/shard_map/pallas_call | solution.py:216
  21.8 0.6 %collective-permute-start.5 = (f32[8,32,256]{2,1,0:T(8,128)S(1)}, f32[8,32,256]{2,1,0:T(8,128)S(1)}, u32[]{:S(2)}, u32[]{:S(2)}) collective-permute-start(f32[8,32,256]{2,1,0:T(8,128)S(1)} %get-tuple-element.30), channel_id=1, source_target_pairs={{0,8},{8,0},{1,9},{9,1},{2,10},{10,2},{3,11},{11,3},{4,12},{12,4},... | collective-permute-start | bytes 786440 | tf_op jit(solution)/shard_map/ppermute | solution.py:268
  22.4 0.0 collective-permute-done.6
  22.4 3.1 %collective-permute-start.7 = (f32[2,32,256]{2,1,0:T(8,128)S(1)}, f32[2,32,256]{2,1,0:T(8,128)S(1)}, u32[]{:S(2)}, u32[]{:S(2)}) collective-permute-start(f32[2,32,256]{2,1,0:T(8,128)S(1)} %get-tuple-element.37), channel_id=1, source_target_pairs={{0,128},{64,192},{128,0},{192,64},{1,129},{65,193},{129,1},{193,65... | collective-permute-start | bytes 196616 | tf_op jit(solution)/shard_map/ppermute | solution.py:275
  25.6 0.6 %collective-permute-start.8 = (f32[2,32,256]{2,1,0:T(8,128)S(1)}, f32[2,32,256]{2,1,0:T(8,128)S(1)}, u32[]{:S(2)}, u32[]{:S(2)}) collective-permute-start(f32[2,32,256]{2,1,0:T(8,128)S(1)} %get-tuple-element.40), channel_id=1, source_target_pairs={{0,64},{64,128},{128,192},{192,0},{1,65},{65,129},{129,193},{193,1... | collective-permute-start | bytes 196616 | tf_op jit(solution)/shard_map/ppermute | solution.py:275
  26.1 0.0 collective-permute-done.5
  26.2 2.7 %collective-permute-start.9 = (f32[2,32,256]{2,1,0:T(8,128)S(1)}, f32[2,32,256]{2,1,0:T(8,128)S(1)}, u32[]{:S(2)}, u32[]{:S(2)}) collective-permute-start(f32[2,32,256]{2,1,0:T(8,128)S(1)} %get-tuple-element.36), channel_id=1, source_target_pairs={{0,192},{64,0},{128,64},{192,128},{1,193},{65,1},{129,65},{193,129... | collective-permute-start | bytes 196616 | tf_op jit(solution)/shard_map/ppermute | solution.py:275
  28.9 0.0 collective-permute-start.10
  28.9 1.0 %collective-permute-start.11 = (f32[2,32,256]{2,1,0:T(8,128)S(1)}, f32[2,32,256]{2,1,0:T(8,128)S(1)}, u32[]{:S(2)}, u32[]{:S(2)}) collective-permute-start(f32[2,32,256]{2,1,0:T(8,128)S(1)} %get-tuple-element.38), channel_id=1, source_target_pairs={{0,64},{64,128},{128,192},{192,0},{1,65},{65,129},{129,193},{193,1... | collective-permute-start | bytes 196616 | tf_op jit(solution)/shard_map/ppermute | solution.py:275
  29.9 0.0 collective-permute-done.7
  29.9 2.3 %collective-permute-start.12 = (f32[2,32,256]{2,1,0:T(8,128)S(1)}, f32[2,32,256]{2,1,0:T(8,128)S(1)}, u32[]{:S(2)}, u32[]{:S(2)}) collective-permute-start(f32[2,32,256]{2,1,0:T(8,128)S(1)} %get-tuple-element.34), channel_id=1, source_target_pairs={{0,192},{64,0},{128,64},{192,128},{1,193},{65,1},{129,65},{193,129... | collective-permute-start | bytes 196616 | tf_op jit(solution)/shard_map/ppermute | solution.py:275
  32.2 0.0 collective-permute-done.8
  32.2 0.0 collective-permute-done.9
  32.2 6.4 %collective-permute-start.15 = (f32[1,32,256]{2,1,0:T(8,128)S(1)}, f32[1,32,256]{2,1,0:T(8,128)S(1)}, u32[]{:S(2)}, u32[]{:S(2)}) collective-permute-start(f32[1,32,256]{2,1,0:T(8,128)S(1)} %fusion), channel_id=1, source_target_pairs={{0,48},{16,0},{32,16},{48,32},{1,49},{17,1},{33,17},{49,33},{2,50}... | collective-permute-start | bytes 98312 | tf_op jit(solution)/shard_map/ppermute | solution.py:278
  38.5 0.0 collective-permute-done.10
  38.5 0.0 collective-permute-done.11
  38.6 0.0 collective-permute-done.12
  38.6 3.8 %collective-permute-start.13 = (f32[1,32,256]{2,1,0:T(8,128)S(1)}, f32[1,32,256]{2,1,0:T(8,128)S(1)}, u32[]{:S(2)}, u32[]{:S(2)}) collective-permute-start(f32[1,32,256]{2,1,0:T(8,128)S(1)} %get-tuple-element.42), channel_id=1, source_target_pairs={{0,32},{16,48},{32,0},{48,16},{1,33},{17,49},{33,1},{49,17},{2,34}... | collective-permute-start | bytes 98312 | tf_op jit(solution)/shard_map/ppermute | solution.py:278
  42.4 1.5 %collective-permute-start.14 = (f32[1,32,256]{2,1,0:T(8,128)S(1)}, f32[1,32,256]{2,1,0:T(8,128)S(1)}, u32[]{:S(2)}, u32[]{:S(2)}) collective-permute-start(f32[1,32,256]{2,1,0:T(8,128)S(1)} %get-tuple-element.41), channel_id=1, source_target_pairs={{0,16},{16,32},{32,48},{48,0},{1,17},{17,33},{33,49},{49,1},{2,18}... | collective-permute-start | bytes 98312 | tf_op jit(solution)/shard_map/ppermute | solution.py:278
  43.9 0.0 collective-permute-done.15
  43.9 2.6 %collective-permute-done.13 = f32[1,32,256]{2,1,0:T(8,128)S(1)} collective-permute-done((f32[1,32,256]{2,1,0:T(8,128)S(1)}, f32[1,32,256]{2,1,0:T(8,128)S(1)}, u32[]{:S(2)}, u32[]{:S(2)}) %collective-permute-start.13) | collective-permute-done | bytes 32800 | tf_op jit(solution)/shard_map/ppermute | solution.py:278
  46.5 1.9 %collective-permute-done.14 = f32[1,32,256]{2,1,0:T(8,128)S(1)} collective-permute-done((f32[1,32,256]{2,1,0:T(8,128)S(1)}, f32[1,32,256]{2,1,0:T(8,128)S(1)}, u32[]{:S(2)}, u32[]{:S(2)}) %collective-permute-start.14) | collective-permute-done | bytes 32800 | tf_op jit(solution)/shard_map/ppermute | solution.py:278
  48.4 0.6 %fusion.6 = f32[1,32,256]{2,1,0:T(8,128)} fusion(f32[1,32,256]{2,1,0:T(8,128)S(1)} %collective-permute-done.13, f32[2,32,256]{2,1,0:T(8,128)S(1)} %collective-permute-done.9, f32[2,32,256]{2,1,0:T(8,128)S(1)} %collective-permute-done.8, f32[2,32,256]{2,1,0:T(8,128)S(1)} %collective-permute-done.7, f32[2,32,256]{2,1,0:T(8,128)S(1)} %get-tuple-element.33, ...), kind=kLoop, calls=%fused_computation.21 | loop fusion | flops 57344 | bytes 262144 | tf_op jit(solution)/shard_map/mul | solution.py:279
  (4 shorter events, 0.1 us)
Async XLA Ops:
  2.4 14.4 %collective-permute-start = (f32[32,16,256]{2,1,0:T(8,128)S(1)}, f32[32,16,256]{2,1,0:T(8,128)S(1)}, u32[]{:S(2)}, u32[]{:S(2)}) collective-permute-start(f32[32,16,256]{2,1,0:T(8,128)S(1)} %get-tuple-element.20.bottom_ref), channel_id=1, source_target_pairs={{0,2},{2,4},{4,6},{6,0},{1,3},{3,5},{5,7},{7,1},{8,10},{10,12},{12... | collective-permute-start | bytes 1572872 | tf_op jit(solution)/shard_map/ppermute | solution.py:244
  4.0 6.1 %copy-start = (bf16[2,2,4,32,128]{4,3,2,1,0:T(8,128)(2,1)S(1)}, bf16[2,2,4,32,128]{4,3,2,1,0:T(8,128)(2,1)}, u32[]{:S(2)}) copy-start(bf16[2,2,4,32,128]{4,3,2,1,0:T(8,128)(2,1)} %constant.30.clone.patch_ref) | copy-start | bytes 393220
  4.0 6.1 %copy-start.1 = (bf16[2,2,64,128]{3,2,1,0:T(8,128)(2,1)S(1)}, bf16[2,2,64,128]{3,2,1,0:T(8,128)(2,1)}, u32[]{:S(2)}) copy-start(bf16[2,2,64,128]{3,2,1,0:T(8,128)(2,1)} %constant.32.clone.edge_ref) | copy-start | bytes 196612
  4.0 14.1 %collective-permute-start.1 = (f32[32,16,256]{2,1,0:T(8,128)S(1)}, f32[32,16,256]{2,1,0:T(8,128)S(1)}, u32[]{:S(2)}, u32[]{:S(2)}) collective-permute-start(f32[32,16,256]{2,1,0:T(8,128)S(1)} %get-tuple-element.21.top_ref), channel_id=1, source_target_pairs={{0,6},{2,0},{4,2},{6,4},{1,7},{3,1},{5,3},{7,5},{8,14},{10,8},{12,... | collective-permute-start | bytes 1572872 | tf_op jit(solution)/shard_map/ppermute | solution.py:245
  5.5 7.9 %collective-permute-start.3 = (f32[2,32,256]{2,1,0:T(8,128)S(1)}, f32[2,32,256]{2,1,0:T(8,128)S(1)}, u32[]{:S(2)}, u32[]{:S(2)}) collective-permute-start(f32[2,32,256]{2,1,0:T(8,128)S(1)} %get-tuple-element.24), channel_id=1, source_target_pairs={{0,1},{1,0},{2,3},{3,2},{4,5},{5,4},{6,7},{7,6},{8,9},{9,8},{10,11... | collective-permute-start | bytes 196616 | tf_op jit(solution)/shard_map/ppermute | solution.py:252
  7.2 6.0 %collective-permute-start.2 = (f32[2,16,256]{2,1,0:T(8,128)S(1)}, f32[2,16,256]{2,1,0:T(8,128)S(1)}, u32[]{:S(2)}, u32[]{:S(2)}) collective-permute-start(f32[2,16,256]{2,1,0:T(8,128)S(1)} %get-tuple-element.23), channel_id=1, source_target_pairs={{0,3},{1,2},{2,5},{3,4},{4,7},{5,6},{6,1},{7,0},{8,11},{9,10},{10,... | collective-permute-start | bytes 98312 | tf_op jit(solution)/shard_map/ppermute | solution.py:250
  8.4 9.8 %copy-start.2 = (bf16[4,96,192]{2,1,0:T(8,128)(2,1)S(1)}, bf16[4,96,192]{2,1,0:T(8,128)(2,1)}, u32[]{:S(2)}) copy-start(bf16[4,96,192]{2,1,0:T(8,128)(2,1)} %constant.29.clone.left_ref) | copy-start | bytes 442372
  8.4 5.0 %collective-permute-start.4 = (f32[2,16,256]{2,1,0:T(8,128)S(1)}, f32[2,16,256]{2,1,0:T(8,128)S(1)}, u32[]{:S(2)}, u32[]{:S(2)}) collective-permute-start(f32[2,16,256]{2,1,0:T(8,128)S(1)} %get-tuple-element.25), channel_id=1, source_target_pairs={{0,7},{1,6},{2,1},{3,0},{4,3},{5,2},{6,5},{7,4},{8,15},{9,14},{10,... | collective-permute-start | bytes 98312 | tf_op jit(solution)/shard_map/ppermute | solution.py:251
  20.0 2.4 %collective-permute-start.6 = (f32[8,32,256]{2,1,0:T(8,128)S(1)}, f32[8,32,256]{2,1,0:T(8,128)S(1)}, u32[]{:S(2)}, u32[]{:S(2)}) collective-permute-start(f32[8,32,256]{2,1,0:T(8,128)S(1)} %get-tuple-element.32), channel_id=1, source_target_pairs={{0,8},{8,0},{1,9},{9,1},{2,10},{10,2},{3,11},{11,3},{4,12},{12,4},... | collective-permute-start | bytes 786440 | tf_op jit(solution)/shard_map/ppermute | solution.py:268
  21.8 4.3 %collective-permute-start.5 = (f32[8,32,256]{2,1,0:T(8,128)S(1)}, f32[8,32,256]{2,1,0:T(8,128)S(1)}, u32[]{:S(2)}, u32[]{:S(2)}) collective-permute-start(f32[8,32,256]{2,1,0:T(8,128)S(1)} %get-tuple-element.30), channel_id=1, source_target_pairs={{0,8},{8,0},{1,9},{9,1},{2,10},{10,2},{3,11},{11,3},{4,12},{12,4},... | collective-permute-start | bytes 786440 | tf_op jit(solution)/shard_map/ppermute | solution.py:268
  22.4 7.4 %collective-permute-start.7 = (f32[2,32,256]{2,1,0:T(8,128)S(1)}, f32[2,32,256]{2,1,0:T(8,128)S(1)}, u32[]{:S(2)}, u32[]{:S(2)}) collective-permute-start(f32[2,32,256]{2,1,0:T(8,128)S(1)} %get-tuple-element.37), channel_id=1, source_target_pairs={{0,128},{64,192},{128,0},{192,64},{1,129},{65,193},{129,1},{193,65... | collective-permute-start | bytes 196616 | tf_op jit(solution)/shard_map/ppermute | solution.py:275
  25.6 6.6 %collective-permute-start.8 = (f32[2,32,256]{2,1,0:T(8,128)S(1)}, f32[2,32,256]{2,1,0:T(8,128)S(1)}, u32[]{:S(2)}, u32[]{:S(2)}) collective-permute-start(f32[2,32,256]{2,1,0:T(8,128)S(1)} %get-tuple-element.40), channel_id=1, source_target_pairs={{0,64},{64,128},{128,192},{192,0},{1,65},{65,129},{129,193},{193,1... | collective-permute-start | bytes 196616 | tf_op jit(solution)/shard_map/ppermute | solution.py:275
  26.2 6.0 %collective-permute-start.9 = (f32[2,32,256]{2,1,0:T(8,128)S(1)}, f32[2,32,256]{2,1,0:T(8,128)S(1)}, u32[]{:S(2)}, u32[]{:S(2)}) collective-permute-start(f32[2,32,256]{2,1,0:T(8,128)S(1)} %get-tuple-element.36), channel_id=1, source_target_pairs={{0,192},{64,0},{128,64},{192,128},{1,193},{65,1},{129,65},{193,129... | collective-permute-start | bytes 196616 | tf_op jit(solution)/shard_map/ppermute | solution.py:275
  28.9 9.6 %collective-permute-start.10 = (f32[2,32,256]{2,1,0:T(8,128)S(1)}, f32[2,32,256]{2,1,0:T(8,128)S(1)}, u32[]{:S(2)}, u32[]{:S(2)}) collective-permute-start(f32[2,32,256]{2,1,0:T(8,128)S(1)} %get-tuple-element.39), channel_id=1, source_target_pairs={{0,128},{64,192},{128,0},{192,64},{1,129},{65,193},{129,1},{193,65... | collective-permute-start | bytes 196616 | tf_op jit(solution)/shard_map/ppermute | solution.py:275
  28.9 9.6 %collective-permute-start.11 = (f32[2,32,256]{2,1,0:T(8,128)S(1)}, f32[2,32,256]{2,1,0:T(8,128)S(1)}, u32[]{:S(2)}, u32[]{:S(2)}) collective-permute-start(f32[2,32,256]{2,1,0:T(8,128)S(1)} %get-tuple-element.38), channel_id=1, source_target_pairs={{0,64},{64,128},{128,192},{192,0},{1,65},{65,129},{129,193},{193,1... | collective-permute-start | bytes 196616 | tf_op jit(solution)/shard_map/ppermute | solution.py:275
  29.9 8.7 %collective-permute-start.12 = (f32[2,32,256]{2,1,0:T(8,128)S(1)}, f32[2,32,256]{2,1,0:T(8,128)S(1)}, u32[]{:S(2)}, u32[]{:S(2)}) collective-permute-start(f32[2,32,256]{2,1,0:T(8,128)S(1)} %get-tuple-element.34), channel_id=1, source_target_pairs={{0,192},{64,0},{128,64},{192,128},{1,193},{65,1},{129,65},{193,129... | collective-permute-start | bytes 196616 | tf_op jit(solution)/shard_map/ppermute | solution.py:275
  32.2 11.7 %collective-permute-start.15 = (f32[1,32,256]{2,1,0:T(8,128)S(1)}, f32[1,32,256]{2,1,0:T(8,128)S(1)}, u32[]{:S(2)}, u32[]{:S(2)}) collective-permute-start(f32[1,32,256]{2,1,0:T(8,128)S(1)} %fusion), channel_id=1, source_target_pairs={{0,48},{16,0},{32,16},{48,32},{1,49},{17,1},{33,17},{49,33},{2,50}... | collective-permute-start | bytes 98312 | tf_op jit(solution)/shard_map/ppermute | solution.py:278
  38.6 7.9 %collective-permute-start.13 = (f32[1,32,256]{2,1,0:T(8,128)S(1)}, f32[1,32,256]{2,1,0:T(8,128)S(1)}, u32[]{:S(2)}, u32[]{:S(2)}) collective-permute-start(f32[1,32,256]{2,1,0:T(8,128)S(1)} %get-tuple-element.42), channel_id=1, source_target_pairs={{0,32},{16,48},{32,0},{48,16},{1,33},{17,49},{33,1},{49,17},{2,34}... | collective-permute-start | bytes 98312 | tf_op jit(solution)/shard_map/ppermute | solution.py:278
  42.4 6.0 %collective-permute-start.14 = (f32[1,32,256]{2,1,0:T(8,128)S(1)}, f32[1,32,256]{2,1,0:T(8,128)S(1)}, u32[]{:S(2)}, u32[]{:S(2)}) collective-permute-start(f32[1,32,256]{2,1,0:T(8,128)S(1)} %get-tuple-element.41), channel_id=1, source_target_pairs={{0,16},{16,32},{32,48},{48,0},{1,17},{17,33},{33,49},{49,1},{2,18}... | collective-permute-start | bytes 98312 | tf_op jit(solution)/shard_map/ppermute | solution.py:278

commit v11 on v10

--- a/solution.py
+++ b/solution.py
@@ -8,6 +8,8 @@
 from jax.experimental.pallas import tpu as pltpu
 from jax.sharding import Mesh, PartitionSpec as P
 
+
+PARTS = ((2,), (1,), (3, 0))
 
 F32, BF16 = jnp.float32, jnp.bfloat16
 HALO = 16
@@ -147,7 +149,7 @@
 
 
 def filter_kernel(
-    part, where, p_ref, above_ref, top_ref, bottom_ref, below_ref, left_ref, right_ref, *refs
+    block, count, where, p_ref, above_ref, top_ref, bottom_ref, below_ref, left_ref, right_ref, *refs
 ):
     core, gy, z = where[0], where[2], where[4]
     left = left_ref[where[1]]
@@ -157,7 +159,7 @@
         return jnp.dot(left, jnp.concatenate([high, high, low]), preferred_element_type=F32)
 
     narrow = lax.broadcasted_iota(jnp.int32, (1, 128), 1)
-    if part == 0:
+    if block == 0:
         side_above_ref, side_ref, side_below_ref, eh_ref, el_ref, keep_ref, send_ref, near_ref, *scratch = refs
         lanes = (slice(0, 128), slice(128, 256))
         sides = (side_above_ref, side_ref.at[:, :HALO], side_ref.at[:, HALO:], side_below_ref)
@@ -178,8 +180,8 @@
     on_left = (narrow < HALO) & (gy == 1)
     on_right = (narrow >= 128 - HALO) & (gy == 0)
 
-    for f in range(16):
-        u = dot_rows([r[16 * part + f] for r in (above_ref, top_ref, bottom_ref, below_ref)])
+    for f in range(8 * count):
+        u = dot_rows([r[8 * block + f] for r in (above_ref, top_ref, bottom_ref, below_ref)])
         for t in range(2):
             at, lanes = slice(32 * f, 32 * f + 32), slice(256 * t, 256 * t + 256)
             fh_ref[at, lanes], fl_ref[at, lanes] = split(u[32 * t : 32 * t + 32])
@@ -190,17 +192,17 @@
     pairs = dot3((ch_ref[...], cl_ref[...]), (right_ref[0, 512:], right_ref[1, 512:]))
     for h in range(2):
         for s in range(2):
-            pairs_ref[h, pl.ds(s, 256, stride=2), :] = pairs[:, 128 * h : 128 * h + 128]
-
-    for g in range(4):
+            pairs_ref[h, pl.ds(s, 128 * count, stride=2), :] = pairs[:, 128 * h : 128 * h + 128]
+
+    for g in range(2 * count):
         at = slice(128 * g, 128 * g + 128)
-        shift = (128 - 16 * (4 * part + g)) % 128
+        shift = (128 - 16 * (2 * block + g)) % 128
         moved = pltpu.roll(near, shift, 1) if shift else near
         zero = jnp.zeros_like(moved)
         low = pairs_ref[0, at] + jnp.where(on_left, moved, zero)
         high = pairs_ref[1, at] + jnp.where(on_right, moved, zero)
         alpha = alpha_ref[at] + jnp.concatenate([low, high], axis=1)
-        first = 16 * part + 4 * g
+        first = 8 * block + 4 * g
         q = p_ref[first : first + 4] * alpha.reshape(4, 32, 256)
         for j in range(2):
             to = 4 * (g // 2) + lax.rem(6 + z - (2 * (g % 2) + j), 4)
@@ -237,6 +239,7 @@
 
     ring = lambda d: [(i, (i + d) % 4) for i in range(4)]
     swap = [(0, 1), (1, 0)]
+    near = None
     near_p, top, bottom = call(
         product_kernel, [(32, 32, 256)] + [(32, 16, 256)] * 2, where, perturbations, control, hbm=(1, 2),
         scratch=[vmem((32, 32, 256), F32), sems((2, 8))],
@@ -254,26 +257,34 @@
         table_kernel, [jax.ShapeDtypeStruct(s, BF16) for s in [(512, 128)] * 2 + [(2, 1024, 256)]],
         where, edge, patch, right, hbm=(3,), scratch=[sems((2, 4))],
     )
-    piece = {}
-    for part in range(2):
+    piece, block = {}, 0
+    for part, distances in enumerate(PARTS):
+        count = len(distances)
         extra = (side_above, side, side_below, eh, el) if part == 0 else (near,)
         keep, give, *rest = call(
-            functools.partial(filter_kernel, part), [(8, 32, 256)] * 2 + [(128, 128)] * (part == 0),
+            functools.partial(filter_kernel, block, count),
+            [(4 * count, 32, 256)] * 2 + [(128, 128)] * (part == 0),
             where, near_p, above, top, bottom, below, left, right, *extra,
-            scratch=[vmem((512, 512), BF16)] * 2 + [vmem((256, 512), BF16)] * 2
-            + [vmem((512, 256), F32), vmem((2, 512, 128), F32)],
-            cost=2 * 10**9,
+            scratch=[vmem((256 * count, 512), BF16)] * 2 + [vmem((128 * count, 512), BF16)] * 2
+            + [vmem((256 * count, 256), F32), vmem((2, 256 * count, 128), F32)],
+            cost=10**9 * count,
         )
-        near = rest[0] if rest else None
+        near = rest[0] if rest else near
         got = lax.ppermute(give, "core", swap)
-        for i in range(2):
-            for wave in range(2):
-                at = slice(4 * i + 2 * wave, 4 * i + 2 * wave + 2)
-                piece[((2, 1), (3, 0))[part][i], wave] = keep[at] + got[at]
+        for i, d in enumerate(distances):
+            for wave, at in enumerate((slice(0, 4),) if d in (2, 1) else (slice(0, 2), slice(2, 4))):
+                piece[d, wave] = keep[4 * i : 4 * i + 4][at] + got[4 * i : 4 * i + 4][at]
+        block += count
+    x2, x1 = (lax.ppermute(piece[d, 0], "x", ring(d)) for d in (2, 1))
     waves = []
     for wave in range(2):
-        x2, x1, x3 = (lax.ppermute(piece[d, wave], "x", ring(d)) for d in (2, 1, 3))
-        waves.append([(piece[0, wave][i : i + 1] + x2[i : i + 1]) + (x1[i : i + 1] + x3[i : i + 1]) for i in range(2)])
+        x3 = lax.ppermute(piece[3, wave], "x", ring(3))
+        cells = [
+            (piece[0, wave][i : i + 1] + x2[j : j + 1]) + (x1[j : j + 1] + x3[i : i + 1])
+            for i, j in ((0, 2 * wave), (1, 2 * wave + 1))
+        ]
+        x2, x1, cells = lax.optimization_barrier((x2, x1, cells))
+        waves.append(cells)
     (far, next_), (own, last) = waves
     z2, z1, z3 = (lax.ppermute(cell, "z", ring(e)) for e, cell in ((2, far), (1, next_), (3, last)))
     return ((own + z2) + (z1 + z3)) * (1.0 / 31.0)

time: 49.3 us -> 49.6 us (level)
  starting transfers between devices: 29 us -> 25.9 us
  waiting for transfers between devices: 10.6 us -> 13.3 us
  Pallas kernels: 8.47 us -> 9.31 us
    ppermute x6 -> x4, waiting for transfers between devices: 0.02 us -> 3.7 us  [the longest x2 3.69 us: body(): x2, x1 = (lax.ppermute(piece[d, 0], 'x', ring(d)) for d in (2, 1))]
    ppermute x6 -> x4, starting transfers between devices: 9.67 us -> 6.6 us  [the longest x2 3.78 us: body(): x2, x1 = (lax.ppermute(piece[d, 0], 'x', ring(d)) for d in (2, 1))]
    ppermute x3, waiting for transfers between devices: 4.55 us -> 3.5 us  [body(): lax.ppermute(cell, 'z', ring(e))]
    pallas_call x5 -> x6, Pallas kernels: 8.47 us -> 9.31 us  [call(): pl.pallas_call(kernel, out_shape=[o if isinstance(o, jax.ShapeDtypeStruct...]
  transfers between devices with their start and end apart: 16 -> 15, of which waited for: 6 -> 7; matrix products, arithmetic and copies ran while one was open for 0% -> 0% of each run, Pallas kernels for 9% -> 8%
where the time goes in v11:
time: 49.6 us; the launch traced here: 49.4 us
  starting transfers between devices  25.9 us (52%)
  waiting for transfers between devices  13.3 us (27%)
  Pallas kernels  9.31 us (19%)
  other arithmetic  0.73 us (1%)
    ppermute x3, starting transfers between devices, body(): lax.ppermute(cell, 'z', ring(e))  11.5 us
    pallas_call x6, Pallas kernels, call(): pl.pallas_call(kernel, out_shape=[o if isinstance(o, jax.ShapeDtypeStruct...  9.31 us
    ppermute x2, starting transfers between devices, body(): x2, x1 = (lax.ppermute(piece[d, 0], 'x', ring(d)) for d in (2, 1))  3.78 us
    ppermute x2, waiting for transfers between devices, body(): x2, x1 = (lax.ppermute(piece[d, 0], 'x', ring(d)) for d in (2, 1))  3.69 us
    ppermute x3, waiting for transfers between devices, body(): lax.ppermute(cell, 'z', ring(e))  3.5 us
    ppermute x1, waiting for transfers between devices, body(): above = lax.ppermute(bottom, 'gx', ring(1))  3.5 us
    ppermute x2, starting transfers between devices, body(): x3 = lax.ppermute(piece[3, wave], 'x', ring(3))  2.82 us
    ppermute x1, starting transfers between devices, body(): side_below = lax.ppermute(edge_top, ('gx', 'gy'), diagonal(3))  1.8 us
  transfers between devices with their start and end apart: 15, of which 7 were waited for; matrix products, arithmetic and copies ran while one was open for 0% of the time, Pallas kernels for 8%

profile of v11, /device:TPU:8, one launch (start us, length us, event | category | flops | bytes accessed | tf_op | source)
XLA Modules:
  0.0 49.4 jit_solution(1570892586941512836)
XLA Ops:
  0.0 0.1 stack.23.where
  0.1 2.3 %shard_map.64 = (f32[32,32,256]{2,1,0:T(8,128)S(1)}, f32[32,16,256]{2,1,0:T(8,128)S(1)}, f32[32,16,256]{2,1,0:T(8,128)S(1)}) custom-call(s32[5]{0:T(128)S(1)} %stack.23.where, f32[1,32,32,256]{3,2,1,0:T(8,128)} %p_hbm.1, f32[32,32,256]{2,1,0:T(8,128)} %c_hbm.1), custom_call_target="tpu_custom_call" | custom-call | bytes 1048576 | tf_op jit(solution)/shard_map/pallas_call | solution.py:218
  2.4 1.7 %collective-permute-start = (f32[32,16,256]{2,1,0:T(8,128)S(1)}, f32[32,16,256]{2,1,0:T(8,128)S(1)}, u32[]{:S(2)}, u32[]{:S(2)}) collective-permute-start(f32[32,16,256]{2,1,0:T(8,128)S(1)} %get-tuple-element.28.bottom_ref), channel_id=1, source_target_pairs={{0,2},{2,4},{4,6},{6,0},{1,3},{3,5},{5,7},{7,1},{8,10},{10,12},{12... | collective-permute-start | bytes 1572872 | tf_op jit(solution)/shard_map/ppermute | solution.py:247
  4.0 0.0 copy-start.1
  4.0 0.0 copy-start.2
  4.0 0.7 %collective-permute-start.1 = (f32[32,16,256]{2,1,0:T(8,128)S(1)}, f32[32,16,256]{2,1,0:T(8,128)S(1)}, u32[]{:S(2)}, u32[]{:S(2)}) collective-permute-start(f32[32,16,256]{2,1,0:T(8,128)S(1)} %get-tuple-element.29.top_ref), channel_id=1, source_target_pairs={{0,6},{2,0},{4,2},{6,4},{1,7},{3,1},{5,3},{7,5},{8,14},{10,8},{12,... | collective-permute-start | bytes 1572872 | tf_op jit(solution)/shard_map/ppermute | solution.py:248
  4.7 0.7 %shard_map.66 = (f32[2,32,256]{2,1,0:T(8,128)S(1)}, f32[2,16,256]{2,1,0:T(8,128)S(1)}, f32[2,16,256]{2,1,0:T(8,128)S(1)}) custom-call(s32[5]{0:T(128)S(1)} %stack.23.where, f32[32,16,256]{2,1,0:T(8,128)S(1)} %get-tuple-element.29.top_ref, f32[32,16,256]{2,1,0:T(8,128)S(1)} %get-tuple-element.28.bottom_ref), custom_call_target="tpu_custom_call" | custom-call | bytes 1048576 | tf_op jit(solution)/shard_map/pallas_call | solution.py:218
  5.5 1.8 %collective-permute-start.3 = (f32[2,32,256]{2,1,0:T(8,128)S(1)}, f32[2,32,256]{2,1,0:T(8,128)S(1)}, u32[]{:S(2)}, u32[]{:S(2)}) collective-permute-start(f32[2,32,256]{2,1,0:T(8,128)S(1)} %get-tuple-element.32), channel_id=1, source_target_pairs={{0,1},{1,0},{2,3},{3,2},{4,5},{5,4},{6,7},{7,6},{8,9},{9,8},{10,11... | collective-permute-start | bytes 196616 | tf_op jit(solution)/shard_map/ppermute | solution.py:255
  7.2 1.1 %collective-permute-start.2 = (f32[2,16,256]{2,1,0:T(8,128)S(1)}, f32[2,16,256]{2,1,0:T(8,128)S(1)}, u32[]{:S(2)}, u32[]{:S(2)}) collective-permute-start(f32[2,16,256]{2,1,0:T(8,128)S(1)} %get-tuple-element.31), channel_id=1, source_target_pairs={{0,3},{1,2},{2,5},{3,4},{4,7},{5,6},{6,1},{7,0},{8,11},{9,10},{10,... | collective-permute-start | bytes 98312 | tf_op jit(solution)/shard_map/ppermute | solution.py:253
  8.4 0.0 copy-start
  8.4 1.8 %collective-permute-start.4 = (f32[2,16,256]{2,1,0:T(8,128)S(1)}, f32[2,16,256]{2,1,0:T(8,128)S(1)}, u32[]{:S(2)}, u32[]{:S(2)}) collective-permute-start(f32[2,16,256]{2,1,0:T(8,128)S(1)} %get-tuple-element.33), channel_id=1, source_target_pairs={{0,7},{1,6},{2,1},{3,0},{4,3},{5,2},{6,5},{7,4},{8,15},{9,14},{10,... | collective-permute-start | bytes 98312 | tf_op jit(solution)/shard_map/ppermute | solution.py:254
  10.2 0.0 copy-done.1
  10.2 0.0 copy-done.2
  10.2 1.9 %shard_map.65 = (bf16[512,128]{1,0:T(8,128)(2,1)S(1)}, bf16[512,128]{1,0:T(8,128)(2,1)S(1)}, bf16[2,1024,256]{2,1,0:T(8,128)(2,1)S(1)}) custom-call(s32[5]{0:T(128)S(1)} %stack.23.where, bf16[2,2,64,128]{3,2,1,0:T(8,128)(2,1)S(1)} %copy-done.2, bf16[2,2,4,32,128]{4,3,2,1,0:T(8,128)(2,1)S(1)} %copy-done.1, bf16[2,1024,256]{2,1,0:T(8,128)(2,1)} %constant.31.clone.right_hbm), custom_call_target="tpu_custom_call" | custom-call | bytes 1048576 | tf_op jit(solution)/shard_map/pallas_call | solution.py:218
  12.1 1.1 %collective-permute-done.2.refs_0_ = f32[2,16,256]{2,1,0:T(8,128)S(1)} collective-permute-done((f32[2,16,256]{2,1,0:T(8,128)S(1)}, f32[2,16,256]{2,1,0:T(8,128)S(1)}, u32[]{:S(2)}, u32[]{:S(2)}) %collective-permute-start.2) | collective-permute-done | bytes 32800 | tf_op jit(solution)/shard_map/ppermute | solution.py:253
  13.2 0.1 collective-permute-done.4.refs_2_
  13.3 0.0 collective-permute-done.3.refs_1_
  13.3 3.5 %collective-permute-done.above_ref = f32[32,16,256]{2,1,0:T(8,128)S(1)} collective-permute-done((f32[32,16,256]{2,1,0:T(8,128)S(1)}, f32[32,16,256]{2,1,0:T(8,128)S(1)}, u32[]{:S(2)}, u32[]{:S(2)}) %collective-permute-start) | collective-permute-done | bytes 524320 | tf_op jit(solution)/shard_map/ppermute | solution.py:247
  16.8 1.3 %collective-permute-done.1.below_ref = f32[32,16,256]{2,1,0:T(8,128)S(1)} collective-permute-done((f32[32,16,256]{2,1,0:T(8,128)S(1)}, f32[32,16,256]{2,1,0:T(8,128)S(1)}, u32[]{:S(2)}, u32[]{:S(2)}) %collective-permute-start.1) | collective-permute-done | bytes 524320 | tf_op jit(solution)/shard_map/ppermute | solution.py:248
  18.1 0.0 copy-done
  18.1 1.5 %shard_map.67 = (f32[4,32,256]{2,1,0:T(8,128)S(1)}, f32[4,32,256]{2,1,0:T(8,128)S(1)}, f32[128,128]{1,0:T(8,128)S(1)}) custom-call(s32[5]{0:T(128)S(1)} %stack.23.where, f32[32,32,256]{2,1,0:T(8,128)S(1)} %get-tuple-element.27.p_ref, f32[32,16,256]{2,1,0:T(8,128)S(1)} %collective-permute-done.above_ref, f32[32,16,256]{2,1,0:T(8,128)S(1)} %get-tuple-element.29.top_ref, ...), custom_call_target="tpu_custom_call" | custom-call | flops 1000000000 | bytes 1048576 | tf_op jit(solution)/shard_map/pallas_call | solution.py:218
  19.6 1.7 %shard_map.69 = (f32[8,32,256]{2,1,0:T(8,128)S(1)}, f32[8,32,256]{2,1,0:T(8,128)S(1)}) custom-call(s32[5]{0:T(128)S(1)} %stack.23.where, f32[32,32,256]{2,1,0:T(8,128)S(1)} %get-tuple-element.27.p_ref, f32[32,16,256]{2,1,0:T(8,128)S(1)} %collective-permute-done.above_ref, f32[32,16,256]{2,1,0:T(8,128)S(1)} %get-tuple-element.29.top_ref, ...), custom_call_target="tpu_custom_call" | custom-call | flops 2000000000 | bytes 1048576 | tf_op jit(solution)/shard_map/pallas_call | solution.py:218
  21.3 0.1 collective-permute-start.9
  21.4 0.5 %collective-permute-start.5 = (f32[4,32,256]{2,1,0:T(8,128)S(1)}, f32[4,32,256]{2,1,0:T(8,128)S(1)}, u32[]{:S(2)}, u32[]{:S(2)}) collective-permute-start(f32[4,32,256]{2,1,0:T(8,128)S(1)} %get-tuple-element.37), channel_id=1, source_target_pairs={{0,8},{8,0},{1,9},{9,1},{2,10},{10,2},{3,11},{11,3},{4,12},{12,4},... | collective-permute-start | bytes 393224 | tf_op jit(solution)/shard_map/ppermute | solution.py:273
  21.9 1.2 %shard_map.68 = (f32[4,32,256]{2,1,0:T(8,128)S(1)}, f32[4,32,256]{2,1,0:T(8,128)S(1)}) custom-call(s32[5]{0:T(128)S(1)} %stack.23.where, f32[32,32,256]{2,1,0:T(8,128)S(1)} %get-tuple-element.27.p_ref, f32[32,16,256]{2,1,0:T(8,128)S(1)} %collective-permute-done.above_ref, f32[32,16,256]{2,1,0:T(8,128)S(1)} %get-tuple-element.29.top_ref, ...), custom_call_target="tpu_custom_call" | custom-call | flops 1000000000 | bytes 1048576 | tf_op jit(solution)/shard_map/pallas_call | solution.py:218
  23.2 0.2 collective-permute-start.7
  23.3 0.0 collective-permute-done.5
  23.4 3.1 %collective-permute-start.6 = (f32[4,32,256]{2,1,0:T(8,128)S(1)}, f32[4,32,256]{2,1,0:T(8,128)S(1)}, u32[]{:S(2)}, u32[]{:S(2)}) collective-permute-start(f32[4,32,256]{2,1,0:T(8,128)S(1)} %add.63), channel_id=1, source_target_pairs={{0,128},{64,192},{128,0},{192,64},{1,129},{65,193},{129,1},{193,65... | collective-permute-start | bytes 393224 | tf_op jit(solution)/shard_map/ppermute | solution.py:278
  26.5 0.0 collective-permute-done.7
  26.5 0.7 %collective-permute-start.8 = (f32[4,32,256]{2,1,0:T(8,128)S(1)}, f32[4,32,256]{2,1,0:T(8,128)S(1)}, u32[]{:S(2)}, u32[]{:S(2)}) collective-permute-start(f32[4,32,256]{2,1,0:T(8,128)S(1)} %add.64), channel_id=1, source_target_pairs={{0,64},{64,128},{128,192},{192,0},{1,65},{65,129},{129,193},{193,1... | collective-permute-start | bytes 393224 | tf_op jit(solution)/shard_map/ppermute | solution.py:278
  27.2 0.0 collective-permute-done.9
  27.2 2.7 %collective-permute-start.10 = (f32[2,32,256]{2,1,0:T(8,128)S(1)}, f32[2,32,256]{2,1,0:T(8,128)S(1)}, u32[]{:S(2)}, u32[]{:S(2)}) collective-permute-start(f32[2,32,256]{2,1,0:T(8,128)S(1)} %get-tuple-element.51), channel_id=1, source_target_pairs={{0,192},{64,0},{128,64},{192,128},{1,193},{65,1},{129,65},{193,129... | collective-permute-start | bytes 196616 | tf_op jit(solution)/shard_map/ppermute | solution.py:281
  30.0 0.1 collective-permute-start.11
  30.0 1.3 %collective-permute-done.6 = f32[4,32,256]{2,1,0:T(8,128)S(1)} collective-permute-done((f32[4,32,256]{2,1,0:T(8,128)S(1)}, f32[4,32,256]{2,1,0:T(8,128)S(1)}, u32[]{:S(2)}, u32[]{:S(2)}) %collective-permute-start.6) | collective-permute-done | bytes 131104 | tf_op jit(solution)/shard_map/ppermute | solution.py:278
  31.3 2.4 %collective-permute-done.8 = f32[4,32,256]{2,1,0:T(8,128)S(1)} collective-permute-done((f32[4,32,256]{2,1,0:T(8,128)S(1)}, f32[4,32,256]{2,1,0:T(8,128)S(1)}, u32[]{:S(2)}, u32[]{:S(2)}) %collective-permute-start.8) | collective-permute-done | bytes 131104 | tf_op jit(solution)/shard_map/ppermute | solution.py:278
  33.7 0.0 collective-permute-done.10
  33.8 3.4 %collective-permute-start.13 = (f32[1,32,256]{2,1,0:T(8,128)S(1)}, f32[1,32,256]{2,1,0:T(8,128)S(1)}, u32[]{:S(2)}, u32[]{:S(2)}) collective-permute-start(f32[1,32,256]{2,1,0:T(8,128)S(1)} %get-tuple-element.47), channel_id=1, source_target_pairs={{0,16},{16,32},{32,48},{48,0},{1,17},{17,33},{33,49},{49,1},{2,18}... | collective-permute-start | bytes 98312 | tf_op jit(solution)/shard_map/ppermute | solution.py:289
  37.1 0.0 collective-permute-done.11
  37.1 3.5 %collective-permute-start.14 = (f32[1,32,256]{2,1,0:T(8,128)S(1)}, f32[1,32,256]{2,1,0:T(8,128)S(1)}, u32[]{:S(2)}, u32[]{:S(2)}) collective-permute-start(f32[1,32,256]{2,1,0:T(8,128)S(1)} %get-tuple-element.48), channel_id=1, source_target_pairs={{0,48},{16,0},{32,16},{48,32},{1,49},{17,1},{33,17},{49,33},{2,50}... | collective-permute-start | bytes 98312 | tf_op jit(solution)/shard_map/ppermute | solution.py:289
  40.6 4.7 %collective-permute-start.12 = (f32[1,32,256]{2,1,0:T(8,128)S(1)}, f32[1,32,256]{2,1,0:T(8,128)S(1)}, u32[]{:S(2)}, u32[]{:S(2)}) collective-permute-start(f32[1,32,256]{2,1,0:T(8,128)S(1)} %get-tuple-element.46), channel_id=1, source_target_pairs={{0,32},{16,48},{32,0},{48,16},{1,33},{17,49},{33,1},{49,17},{2,34}... | collective-permute-start | bytes 98312 | tf_op jit(solution)/shard_map/ppermute | solution.py:289
  45.3 0.0 collective-permute-done.13
  45.3 0.0 collective-permute-done.14
  45.3 3.5 %collective-permute-done.12 = f32[1,32,256]{2,1,0:T(8,128)S(1)} collective-permute-done((f32[1,32,256]{2,1,0:T(8,128)S(1)}, f32[1,32,256]{2,1,0:T(8,128)S(1)}, u32[]{:S(2)}, u32[]{:S(2)}) %collective-permute-start.12) | collective-permute-done | bytes 32800 | tf_op jit(solution)/shard_map/ppermute | solution.py:289
  48.8 0.6 %add_multiply_fusion = f32[1,32,256]{2,1,0:T(8,128)} fusion(f32[1,32,256]{2,1,0:T(8,128)S(1)} %collective-permute-done.13, f32[1,32,256]{2,1,0:T(8,128)S(1)} %collective-permute-done.14, f32[1,32,256]{2,1,0:T(8,128)S(1)} %get-tuple-element.45, f32[1,32,256]{2,1,0:T(8,128)S(1)} %collective-permute-done.12), kind=kLoop, calls=%fused_computation.16 | loop fusion | flops 32768 | bytes 163840 | tf_op jit(solution)/shard_map/mul | solution.py:290
  (5 shorter events, 0.1 us)
Async XLA Ops:
  2.4 14.4 %collective-permute-start = (f32[32,16,256]{2,1,0:T(8,128)S(1)}, f32[32,16,256]{2,1,0:T(8,128)S(1)}, u32[]{:S(2)}, u32[]{:S(2)}) collective-permute-start(f32[32,16,256]{2,1,0:T(8,128)S(1)} %get-tuple-element.28.bottom_ref), channel_id=1, source_target_pairs={{0,2},{2,4},{4,6},{6,0},{1,3},{3,5},{5,7},{7,1},{8,10},{10,12},{12... | collective-permute-start | bytes 1572872 | tf_op jit(solution)/shard_map/ppermute | solution.py:247
  4.0 6.1 %copy-start.1 = (bf16[2,2,4,32,128]{4,3,2,1,0:T(8,128)(2,1)S(1)}, bf16[2,2,4,32,128]{4,3,2,1,0:T(8,128)(2,1)}, u32[]{:S(2)}) copy-start(bf16[2,2,4,32,128]{4,3,2,1,0:T(8,128)(2,1)} %constant.30.clone.patch_ref) | copy-start | bytes 393220
  4.0 6.1 %copy-start.2 = (bf16[2,2,64,128]{3,2,1,0:T(8,128)(2,1)S(1)}, bf16[2,2,64,128]{3,2,1,0:T(8,128)(2,1)}, u32[]{:S(2)}) copy-start(bf16[2,2,64,128]{3,2,1,0:T(8,128)(2,1)} %constant.32.clone.edge_ref) | copy-start | bytes 196612
  4.0 14.1 %collective-permute-start.1 = (f32[32,16,256]{2,1,0:T(8,128)S(1)}, f32[32,16,256]{2,1,0:T(8,128)S(1)}, u32[]{:S(2)}, u32[]{:S(2)}) collective-permute-start(f32[32,16,256]{2,1,0:T(8,128)S(1)} %get-tuple-element.29.top_ref), channel_id=1, source_target_pairs={{0,6},{2,0},{4,2},{6,4},{1,7},{3,1},{5,3},{7,5},{8,14},{10,8},{12,... | collective-permute-start | bytes 1572872 | tf_op jit(solution)/shard_map/ppermute | solution.py:248
  5.5 7.9 %collective-permute-start.3 = (f32[2,32,256]{2,1,0:T(8,128)S(1)}, f32[2,32,256]{2,1,0:T(8,128)S(1)}, u32[]{:S(2)}, u32[]{:S(2)}) collective-permute-start(f32[2,32,256]{2,1,0:T(8,128)S(1)} %get-tuple-element.32), channel_id=1, source_target_pairs={{0,1},{1,0},{2,3},{3,2},{4,5},{5,4},{6,7},{7,6},{8,9},{9,8},{10,11... | collective-permute-start | bytes 196616 | tf_op jit(solution)/shard_map/ppermute | solution.py:255
  7.2 6.0 %collective-permute-start.2 = (f32[2,16,256]{2,1,0:T(8,128)S(1)}, f32[2,16,256]{2,1,0:T(8,128)S(1)}, u32[]{:S(2)}, u32[]{:S(2)}) collective-permute-start(f32[2,16,256]{2,1,0:T(8,128)S(1)} %get-tuple-element.31), channel_id=1, source_target_pairs={{0,3},{1,2},{2,5},{3,4},{4,7},{5,6},{6,1},{7,0},{8,11},{9,10},{10,... | collective-permute-start | bytes 98312 | tf_op jit(solution)/shard_map/ppermute | solution.py:253
  8.4 9.8 %copy-start = (bf16[4,96,192]{2,1,0:T(8,128)(2,1)S(1)}, bf16[4,96,192]{2,1,0:T(8,128)(2,1)}, u32[]{:S(2)}) copy-start(bf16[4,96,192]{2,1,0:T(8,128)(2,1)} %constant.29.clone.left_ref) | copy-start | bytes 442372
  8.4 5.0 %collective-permute-start.4 = (f32[2,16,256]{2,1,0:T(8,128)S(1)}, f32[2,16,256]{2,1,0:T(8,128)S(1)}, u32[]{:S(2)}, u32[]{:S(2)}) collective-permute-start(f32[2,16,256]{2,1,0:T(8,128)S(1)} %get-tuple-element.33), channel_id=1, source_target_pairs={{0,7},{1,6},{2,1},{3,0},{4,3},{5,2},{6,5},{7,4},{8,15},{9,14},{10,... | collective-permute-start | bytes 98312 | tf_op jit(solution)/shard_map/ppermute | solution.py:254
  21.3 5.9 %collective-permute-start.9 = (f32[8,32,256]{2,1,0:T(8,128)S(1)}, f32[8,32,256]{2,1,0:T(8,128)S(1)}, u32[]{:S(2)}, u32[]{:S(2)}) collective-permute-start(f32[8,32,256]{2,1,0:T(8,128)S(1)} %get-tuple-element.42), channel_id=1, source_target_pairs={{0,8},{8,0},{1,9},{9,1},{2,10},{10,2},{3,11},{11,3},{4,12},{12,4},... | collective-permute-start | bytes 786440 | tf_op jit(solution)/shard_map/ppermute | solution.py:273
  21.4 1.9 %collective-permute-start.5 = (f32[4,32,256]{2,1,0:T(8,128)S(1)}, f32[4,32,256]{2,1,0:T(8,128)S(1)}, u32[]{:S(2)}, u32[]{:S(2)}) collective-permute-start(f32[4,32,256]{2,1,0:T(8,128)S(1)} %get-tuple-element.37), channel_id=1, source_target_pairs={{0,8},{8,0},{1,9},{9,1},{2,10},{10,2},{3,11},{11,3},{4,12},{12,4},... | collective-permute-start | bytes 393224 | tf_op jit(solution)/shard_map/ppermute | solution.py:273
  23.2 3.3 %collective-permute-start.7 = (f32[4,32,256]{2,1,0:T(8,128)S(1)}, f32[4,32,256]{2,1,0:T(8,128)S(1)}, u32[]{:S(2)}, u32[]{:S(2)}) collective-permute-start(f32[4,32,256]{2,1,0:T(8,128)S(1)} %get-tuple-element.40), channel_id=1, source_target_pairs={{0,8},{8,0},{1,9},{9,1},{2,10},{10,2},{3,11},{11,3},{4,12},{12,4},... | collective-permute-start | bytes 393224 | tf_op jit(solution)/shard_map/ppermute | solution.py:273
  23.4 8.0 %collective-permute-start.6 = (f32[4,32,256]{2,1,0:T(8,128)S(1)}, f32[4,32,256]{2,1,0:T(8,128)S(1)}, u32[]{:S(2)}, u32[]{:S(2)}) collective-permute-start(f32[4,32,256]{2,1,0:T(8,128)S(1)} %add.63), channel_id=1, source_target_pairs={{0,128},{64,192},{128,0},{192,64},{1,129},{65,193},{129,1},{193,65... | collective-permute-start | bytes 393224 | tf_op jit(solution)/shard_map/ppermute | solution.py:278
  26.5 7.2 %collective-permute-start.8 = (f32[4,32,256]{2,1,0:T(8,128)S(1)}, f32[4,32,256]{2,1,0:T(8,128)S(1)}, u32[]{:S(2)}, u32[]{:S(2)}) collective-permute-start(f32[4,32,256]{2,1,0:T(8,128)S(1)} %add.64), channel_id=1, source_target_pairs={{0,64},{64,128},{128,192},{192,0},{1,65},{65,129},{129,193},{193,1... | collective-permute-start | bytes 393224 | tf_op jit(solution)/shard_map/ppermute | solution.py:278
  27.2 6.5 %collective-permute-start.10 = (f32[2,32,256]{2,1,0:T(8,128)S(1)}, f32[2,32,256]{2,1,0:T(8,128)S(1)}, u32[]{:S(2)}, u32[]{:S(2)}) collective-permute-start(f32[2,32,256]{2,1,0:T(8,128)S(1)} %get-tuple-element.51), channel_id=1, source_target_pairs={{0,192},{64,0},{128,64},{192,128},{1,193},{65,1},{129,65},{193,129... | collective-permute-start | bytes 196616 | tf_op jit(solution)/shard_map/ppermute | solution.py:281
  30.0 7.2 %collective-permute-start.11 = (f32[2,32,256]{2,1,0:T(8,128)S(1)}, f32[2,32,256]{2,1,0:T(8,128)S(1)}, u32[]{:S(2)}, u32[]{:S(2)}) collective-permute-start(f32[2,32,256]{2,1,0:T(8,128)S(1)} %get-tuple-element.50), channel_id=1, source_target_pairs={{0,192},{64,0},{128,64},{192,128},{1,193},{65,1},{129,65},{193,129... | collective-permute-start | bytes 196616 | tf_op jit(solution)/shard_map/ppermute | solution.py:281
  33.8 11.5 %collective-permute-start.13 = (f32[1,32,256]{2,1,0:T(8,128)S(1)}, f32[1,32,256]{2,1,0:T(8,128)S(1)}, u32[]{:S(2)}, u32[]{:S(2)}) collective-permute-start(f32[1,32,256]{2,1,0:T(8,128)S(1)} %get-tuple-element.47), channel_id=1, source_target_pairs={{0,16},{16,32},{32,48},{48,0},{1,17},{17,33},{33,49},{49,1},{2,18}... | collective-permute-start | bytes 98312 | tf_op jit(solution)/shard_map/ppermute | solution.py:289
  37.1 8.1 %collective-permute-start.14 = (f32[1,32,256]{2,1,0:T(8,128)S(1)}, f32[1,32,256]{2,1,0:T(8,128)S(1)}, u32[]{:S(2)}, u32[]{:S(2)}) collective-permute-start(f32[1,32,256]{2,1,0:T(8,128)S(1)} %get-tuple-element.48), channel_id=1, source_target_pairs={{0,48},{16,0},{32,16},{48,32},{1,49},{17,1},{33,17},{49,33},{2,50}... | collective-permute-start | bytes 98312 | tf_op jit(solution)/shard_map/ppermute | solution.py:289
  40.6 8.2 %collective-permute-start.12 = (f32[1,32,256]{2,1,0:T(8,128)S(1)}, f32[1,32,256]{2,1,0:T(8,128)S(1)}, u32[]{:S(2)}, u32[]{:S(2)}) collective-permute-start(f32[1,32,256]{2,1,0:T(8,128)S(1)} %get-tuple-element.46), channel_id=1, source_target_pairs={{0,32},{16,48},{32,0},{48,16},{1,33},{17,49},{33,1},{49,17},{2,34}... | collective-permute-start | bytes 98312 | tf_op jit(solution)/shard_map/ppermute | solution.py:289

commit v12 on v10

--- a/solution.py
+++ b/solution.py
@@ -146,47 +146,60 @@
                 right_ref[h, 256 * t + 224 : 256 * t + 256, 128:] = patch_ref[h, 1, t]
 
 
+def stack3(parts):
+    high, low = split(jnp.concatenate(parts))
+    return jnp.concatenate([high, high, low])
+
+
+def early_kernel(
+    where, top_ref, bottom_ref, side_above_ref, side_ref, side_below_ref, left_ref, inner_ref, eh_ref, el_ref, right_ref,
+    near_ref, own_ref, uh_ref, ul_ref, pairs_ref,
+):
+    gy = where[2]
+    left, inner = left_ref[where[1]], inner_ref[where[1]]
+    lanes = (slice(0, 128), slice(128, 256))
+    sides = (side_above_ref, side_ref.at[:, :HALO], side_ref.at[:, HALO:], side_below_ref)
+    side = [
+        jnp.dot(left, stack3([s[f // 2, :, lanes[f % 2]] for s in sides]), preferred_element_type=F32) for f in range(4)
+    ]
+    fine = split(jnp.concatenate([jnp.concatenate([u[:32], u[32:64]], axis=1) for u in side]))
+    pair = split(jnp.concatenate([jnp.concatenate([u[64:80], u[80:]], axis=1) for u in side]))
+    near = dot3(fine, (eh_ref[:256], el_ref[:256]))
+    near_pairs = dot3(pair, (eh_ref[256:], el_ref[256:]))
+    pairs_ref[pl.ds(0, 64, stride=2), :] = near_pairs
+    pairs_ref[pl.ds(1, 64, stride=2), :] = near_pairs
+    near = near + pairs_ref[...]
+    near_ref[...] = jnp.where(gy == 0, pltpu.roll(near, 112, 1), pltpu.roll(near, 16, 1))
+    for f in range(32):
+        at = slice(16 * f, 16 * f + 16)
+        u = jnp.dot(inner, stack3([top_ref[f], bottom_ref[f]]), preferred_element_type=F32)
+        uh_ref[at], ul_ref[at] = split(u)
+    own_ref[...] = dot3((uh_ref[...], ul_ref[...]), (right_ref[0, :256], right_ref[1, :256]))
+
+
 def filter_kernel(
-    part, where, p_ref, above_ref, top_ref, bottom_ref, below_ref, left_ref, right_ref, *refs
+    part, where, p_ref, above_ref, top_ref, bottom_ref, below_ref, left_ref, right_ref, near_ref, own_ref,
+    keep_ref, send_ref, fh_ref, fl_ref, mh_ref, ml_ref, ch_ref, cl_ref, outer_ref, middle_ref, pairs_ref,
 ):
     core, gy, z = where[0], where[2], where[4]
     left = left_ref[where[1]]
-
-    def dot_rows(parts):
-        high, low = split(jnp.concatenate(parts))
-        return jnp.dot(left, jnp.concatenate([high, high, low]), preferred_element_type=F32)
-
     narrow = lax.broadcasted_iota(jnp.int32, (1, 128), 1)
-    if part == 0:
-        side_above_ref, side_ref, side_below_ref, eh_ref, el_ref, keep_ref, send_ref, near_ref, *scratch = refs
-        lanes = (slice(0, 128), slice(128, 256))
-        sides = (side_above_ref, side_ref.at[:, :HALO], side_ref.at[:, HALO:], side_below_ref)
-        side = [dot_rows([s[f // 2, :, lanes[f % 2]] for s in sides]) for f in range(4)]
-        fine = split(jnp.concatenate([jnp.concatenate([u[:32], u[32:64]], axis=1) for u in side]))
-        pair = split(jnp.concatenate([jnp.concatenate([u[64:80], u[80:]], axis=1) for u in side]))
-        near = dot3(fine, (eh_ref[:256], el_ref[:256]))
-        near_pairs = dot3(pair, (eh_ref[256:], el_ref[256:]))
-        near_ref[pl.ds(0, 64, stride=2), :] = near_pairs
-        near_ref[pl.ds(1, 64, stride=2), :] = near_pairs
-        near = near + near_ref[...]
-        near = jnp.where(gy == 0, pltpu.roll(near, 112, 1), pltpu.roll(near, 16, 1))
-        near_ref[...] = near
-    else:
-        near_ref, keep_ref, send_ref, *scratch = refs
-        near = near_ref[...]
-    fh_ref, fl_ref, ch_ref, cl_ref, alpha_ref, pairs_ref = scratch
+    near = near_ref[...]
     on_left = (narrow < HALO) & (gy == 1)
     on_right = (narrow >= 128 - HALO) & (gy == 0)
 
     for f in range(16):
-        u = dot_rows([r[16 * part + f] for r in (above_ref, top_ref, bottom_ref, below_ref)])
-        for t in range(2):
-            at, lanes = slice(32 * f, 32 * f + 32), slice(256 * t, 256 * t + 256)
-            fh_ref[at, lanes], fl_ref[at, lanes] = split(u[32 * t : 32 * t + 32])
-            at = slice(16 * f, 16 * f + 16)
-            ch_ref[at, lanes], cl_ref[at, lanes] = split(u[64 + 16 * t : 80 + 16 * t])
-
-    alpha_ref[...] = dot3((fh_ref[...], fl_ref[...]), (right_ref[0, :512], right_ref[1, :512]))
+        v = stack3([r[16 * part + f] for r in (above_ref, top_ref, bottom_ref, below_ref)])
+        u = jnp.dot(left, v, preferred_element_type=F32)
+        at = slice(16 * f, 16 * f + 16)
+        fh_ref[at, :256], fl_ref[at, :256] = split(u[:16])
+        fh_ref[at, 256:], fl_ref[at, 256:] = split(u[16:32])
+        mh_ref[at], ml_ref[at] = split(u[32:48])
+        ch_ref[at, :256], cl_ref[at, :256] = split(u[48:64])
+        ch_ref[at, 256:], cl_ref[at, 256:] = split(u[64:])
+
+    outer_ref[...] = dot3((fh_ref[...], fl_ref[...]), (right_ref[0, :512], right_ref[1, :512]))
+    middle_ref[...] = dot3((mh_ref[...], ml_ref[...]), (right_ref[0, 256:512], right_ref[1, 256:512]))
     pairs = dot3((ch_ref[...], cl_ref[...]), (right_ref[0, 512:], right_ref[1, 512:]))
     for h in range(2):
         for s in range(2):
@@ -199,7 +212,12 @@
         zero = jnp.zeros_like(moved)
         low = pairs_ref[0, at] + jnp.where(on_left, moved, zero)
         high = pairs_ref[1, at] + jnp.where(on_right, moved, zero)
-        alpha = alpha_ref[at] + jnp.concatenate([low, high], axis=1)
+        rows = []
+        for f in range(4 * g, 4 * g + 4):
+            own = own_ref[16 * (16 * part + f) : 16 * (16 * part + f) + 16]
+            rows += [outer_ref[16 * f : 16 * f + 8], middle_ref[16 * f : 16 * f + 16] + own]
+            rows += [outer_ref[16 * f + 8 : 16 * f + 16]]
+        alpha = jnp.concatenate(rows) + jnp.concatenate([low, high], axis=1)
         first = 16 * part + 4 * g
         q = p_ref[first : first + 4] * alpha.reshape(4, 32, 256)
         for j in range(2):
@@ -228,7 +246,14 @@
     x, z, core, gx, gy = (lax.axis_index(a) for a in ("x", "z", "core", "gx", "gy"))
     where = jnp.stack([core, gx, gy, x, z]).astype(jnp.int32)
     high, low = np.moveaxis(halves(left_table(128, 4)), 1, 0)
-    left = jnp.asarray(np.concatenate([high, low, high], axis=2))
+    three = lambda rows, cells: jnp.asarray(
+        np.concatenate([t[:, rows, cells] for t in (high, low, high)], axis=2)
+    )
+    whole = slice(0, 64)
+    left = three(slice(0, 96), whole)
+    inner = three(slice(8, 24), slice(HALO, 48))
+    rows = np.r_[0:8, 24:32, 32:40, 56:64, 40:56, 64:96]
+    left_rest = three(rows, whole)
     right, edge = (halves(t) for t in right_tables(512, 2))
     blocks = right[1].reshape(2, 4, 256, 256)
     patch = jnp.asarray(np.stack([blocks[:, :, :32, :128], blocks[:, :, 224:, 128:]], axis=1))
@@ -254,17 +279,20 @@
         table_kernel, [jax.ShapeDtypeStruct(s, BF16) for s in [(512, 128)] * 2 + [(2, 1024, 256)]],
         where, edge, patch, right, hbm=(3,), scratch=[sems((2, 4))],
     )
+    near, own = call(
+        early_kernel, [(128, 128), (512, 256)], where, top, bottom, side_above, side, side_below,
+        left, inner, eh, el, right, scratch=[vmem((512, 256), BF16)] * 2 + [vmem((128, 128), F32)],
+        cost=10**9,
+    )
     piece = {}
     for part in range(2):
-        extra = (side_above, side, side_below, eh, el) if part == 0 else (near,)
-        keep, give, *rest = call(
-            functools.partial(filter_kernel, part), [(8, 32, 256)] * 2 + [(128, 128)] * (part == 0),
-            where, near_p, above, top, bottom, below, left, right, *extra,
-            scratch=[vmem((512, 512), BF16)] * 2 + [vmem((256, 512), BF16)] * 2
-            + [vmem((512, 256), F32), vmem((2, 512, 128), F32)],
+        keep, give = call(
+            functools.partial(filter_kernel, part), [(8, 32, 256)] * 2,
+            where, near_p, above, top, bottom, below, left_rest, right, near, own,
+            scratch=[vmem((256, 512), BF16)] * 2 + [vmem((256, 256), BF16)] * 2 + [vmem((256, 512), BF16)] * 2
+            + [vmem((256, 256), F32)] * 2 + [vmem((2, 512, 128), F32)],
             cost=2 * 10**9,
         )
-        near = rest[0] if rest else None
         got = lax.ppermute(give, "core", swap)
         for i in range(2):
             for wave in range(2):
@@ -274,9 +302,9 @@
     for wave in range(2):
         x2, x1, x3 = (lax.ppermute(piece[d, wave], "x", ring(d)) for d in (2, 1, 3))
         waves.append([(piece[0, wave][i : i + 1] + x2[i : i + 1]) + (x1[i : i + 1] + x3[i : i + 1]) for i in range(2)])
-    (far, next_), (own, last) = waves
+    (far, next_), (stay, last) = waves
     z2, z1, z3 = (lax.ppermute(cell, "z", ring(e)) for e, cell in ((2, far), (1, next_), (3, last)))
-    return ((own + z2) + (z1 + z3)) * (1.0 / 31.0)
+    return ((stay + z2) + (z1 + z3)) * (1.0 / 31.0)
 
 
 def solution(mesh):

time: 49.3 us -> 49 us (level)
  waiting for transfers between devices: 10.6 us -> 9.2 us
  Pallas kernels: 8.47 us -> 9.57 us
    ppermute x1, waiting for transfers between devices: 3.5 us -> 2.09 us  [body(): above = lax.ppermute(bottom, 'gx', ring(1))]
    pallas_call x5 -> x6, Pallas kernels: 8.47 us -> 9.57 us  [call(): pl.pallas_call(kernel, out_shape=[o if isinstance(o, jax.ShapeDtypeStruct...]
  transfers between devices with their start and end apart: 16 -> 16, of which waited for: 6 -> 6; matrix products, arithmetic and copies ran while one was open for 0% -> 0% of each run, Pallas kernels for 9% -> 12%
where the time goes in v12:
time: 49 us; the launch traced here: 48.7 us
  starting transfers between devices  29 us (59%)
  Pallas kernels  9.57 us (20%)
  waiting for transfers between devices  9.2 us (19%)
  other arithmetic  0.73 us (1%)
    ppermute x3, starting transfers between devices, body(): lax.ppermute(cell, 'z', ring(e))  11.6 us
    ppermute x6, starting transfers between devices, body(): x2, x1, x3 = (lax.ppermute(piece[d, wave], 'x', ring(d)) for d in (2, 1, 3))  9.71 us
    pallas_call x6, Pallas kernels, call(): pl.pallas_call(kernel, out_shape=[o if isinstance(o, jax.ShapeDtypeStruct...  9.57 us
    ppermute x3, waiting for transfers between devices, body(): lax.ppermute(cell, 'z', ring(e))  4.53 us
    ppermute x1, waiting for transfers between devices, body(): above = lax.ppermute(bottom, 'gx', ring(1))  2.09 us
    ppermute x1, starting transfers between devices, body(): side_below = lax.ppermute(edge_top, ('gx', 'gy'), diagonal(3))  1.8 us
    ppermute x1, starting transfers between devices, body(): side = lax.ppermute(edges, 'gy', swap)  1.76 us
    ppermute x1, starting transfers between devices, body(): above = lax.ppermute(bottom, 'gx', ring(1))  1.65 us
  transfers between devices with their start and end apart: 16, of which 6 were waited for; matrix products, arithmetic and copies ran while one was open for 0% of the time, Pallas kernels for 12%

profile of v12, /device:TPU:8, one launch (start us, length us, event | category | flops | bytes accessed | tf_op | source)
XLA Modules:
  0.0 48.7 jit_solution(6211926940952055497)
XLA Ops:
  0.0 0.1 stack.23.where
  0.1 2.3 %shard_map.82 = (f32[32,32,256]{2,1,0:T(8,128)S(1)}, f32[32,16,256]{2,1,0:T(8,128)S(1)}, f32[32,16,256]{2,1,0:T(8,128)S(1)}) custom-call(s32[5]{0:T(128)S(1)} %stack.23.where, f32[1,32,32,256]{3,2,1,0:T(8,128)} %p_hbm.1, f32[32,32,256]{2,1,0:T(8,128)} %c_hbm.1), custom_call_target="tpu_custom_call" | custom-call | bytes 1048576 | tf_op jit(solution)/shard_map/pallas_call | solution.py:234
  2.4 1.7 %collective-permute-start = (f32[32,16,256]{2,1,0:T(8,128)S(1)}, f32[32,16,256]{2,1,0:T(8,128)S(1)}, u32[]{:S(2)}, u32[]{:S(2)}) collective-permute-start(f32[32,16,256]{2,1,0:T(8,128)S(1)} %get-tuple-element.21.bottom_ref), channel_id=1, source_target_pairs={{0,2},{2,4},{4,6},{6,0},{1,3},{3,5},{5,7},{7,1},{8,10},{10,12},{12... | collective-permute-start | bytes 1572872 | tf_op jit(solution)/shard_map/ppermute | solution.py:269
  4.0 0.0 copy-start
  4.0 0.0 copy-start.1
  4.0 0.7 %collective-permute-start.1 = (f32[32,16,256]{2,1,0:T(8,128)S(1)}, f32[32,16,256]{2,1,0:T(8,128)S(1)}, u32[]{:S(2)}, u32[]{:S(2)}) collective-permute-start(f32[32,16,256]{2,1,0:T(8,128)S(1)} %get-tuple-element.22.top_ref), channel_id=1, source_target_pairs={{0,6},{2,0},{4,2},{6,4},{1,7},{3,1},{5,3},{7,5},{8,14},{10,8},{12,... | collective-permute-start | bytes 1572872 | tf_op jit(solution)/shard_map/ppermute | solution.py:270
  4.7 0.7 %shard_map.84 = (f32[2,32,256]{2,1,0:T(8,128)S(1)}, f32[2,16,256]{2,1,0:T(8,128)S(1)}, f32[2,16,256]{2,1,0:T(8,128)S(1)}) custom-call(s32[5]{0:T(128)S(1)} %stack.23.where, f32[32,16,256]{2,1,0:T(8,128)S(1)} %get-tuple-element.22.top_ref, f32[32,16,256]{2,1,0:T(8,128)S(1)} %get-tuple-element.21.bottom_ref), custom_call_target="tpu_custom_call" | custom-call | bytes 1048576 | tf_op jit(solution)/shard_map/pallas_call | solution.py:234
  5.5 1.8 %collective-permute-start.3 = (f32[2,32,256]{2,1,0:T(8,128)S(1)}, f32[2,32,256]{2,1,0:T(8,128)S(1)}, u32[]{:S(2)}, u32[]{:S(2)}) collective-permute-start(f32[2,32,256]{2,1,0:T(8,128)S(1)} %get-tuple-element.25), channel_id=1, source_target_pairs={{0,1},{1,0},{2,3},{3,2},{4,5},{5,4},{6,7},{7,6},{8,9},{9,8},{10,11... | collective-permute-start | bytes 196616 | tf_op jit(solution)/shard_map/ppermute | solution.py:277
  7.2 1.1 %collective-permute-start.2 = (f32[2,16,256]{2,1,0:T(8,128)S(1)}, f32[2,16,256]{2,1,0:T(8,128)S(1)}, u32[]{:S(2)}, u32[]{:S(2)}) collective-permute-start(f32[2,16,256]{2,1,0:T(8,128)S(1)} %get-tuple-element.24), channel_id=1, source_target_pairs={{0,3},{1,2},{2,5},{3,4},{4,7},{5,6},{6,1},{7,0},{8,11},{9,10},{10,... | collective-permute-start | bytes 98312 | tf_op jit(solution)/shard_map/ppermute | solution.py:275
  8.4 1.8 %collective-permute-start.4 = (f32[2,16,256]{2,1,0:T(8,128)S(1)}, f32[2,16,256]{2,1,0:T(8,128)S(1)}, u32[]{:S(2)}, u32[]{:S(2)}) collective-permute-start(f32[2,16,256]{2,1,0:T(8,128)S(1)} %get-tuple-element.26), channel_id=1, source_target_pairs={{0,7},{1,6},{2,1},{3,0},{4,3},{5,2},{6,5},{7,4},{8,15},{9,14},{10,... | collective-permute-start | bytes 98312 | tf_op jit(solution)/shard_map/ppermute | solution.py:276
  10.2 0.0 copy-done
  10.2 0.0 copy-done.1
  10.2 1.9 %shard_map.83 = (bf16[512,128]{1,0:T(8,128)(2,1)S(1)}, bf16[512,128]{1,0:T(8,128)(2,1)S(1)}, bf16[2,1024,256]{2,1,0:T(8,128)(2,1)S(1)}) custom-call(s32[5]{0:T(128)S(1)} %stack.23.where, bf16[2,2,64,128]{3,2,1,0:T(8,128)(2,1)S(1)} %copy-done.1, bf16[2,2,4,32,128]{4,3,2,1,0:T(8,128)(2,1)S(1)} %copy-done, bf16[2,1024,256]{2,1,0:T(8,128)(2,1)} %constant.37.clone.right_hbm), custom_call_target="tpu_custom_call" | custom-call | bytes 1048576 | tf_op jit(solution)/shard_map/pallas_call | solution.py:234
  12.1 1.1 %collective-permute-done.2.side_above_ref = f32[2,16,256]{2,1,0:T(8,128)S(1)} collective-permute-done((f32[2,16,256]{2,1,0:T(8,128)S(1)}, f32[2,16,256]{2,1,0:T(8,128)S(1)}, u32[]{:S(2)}, u32[]{:S(2)}) %collective-permute-start.2) | collective-permute-done | bytes 32800 | tf_op jit(solution)/shard_map/ppermute | solution.py:275
  13.2 0.1 collective-permute-done.4.side_below_ref
  13.3 0.0 collective-permute-done.3.side_ref
  13.3 0.0 copy-done.2
  13.3 0.0 copy-done.4
  13.3 0.0 copy-start.3
  13.4 1.4 %shard_map.85 = (f32[128,128]{1,0:T(8,128)S(1)}, f32[512,256]{1,0:T(8,128)S(1)}) custom-call(s32[5]{0:T(128)S(1)} %stack.23.where, f32[32,16,256]{2,1,0:T(8,128)S(1)} %get-tuple-element.22.top_ref, f32[32,16,256]{2,1,0:T(8,128)S(1)} %get-tuple-element.21.bottom_ref, f32[2,16,256]{2,1,0:T(8,128)S(1)} %collective-permute-done.2.side_above_ref, ...), custom_call_target="tpu_custom_call" | custom-call | flops 1000000000 | bytes 1048576 | tf_op jit(solution)/shard_map/pallas_call | solution.py:234
  14.7 2.1 %collective-permute-done.above_ref = f32[32,16,256]{2,1,0:T(8,128)S(1)} collective-permute-done((f32[32,16,256]{2,1,0:T(8,128)S(1)}, f32[32,16,256]{2,1,0:T(8,128)S(1)}, u32[]{:S(2)}, u32[]{:S(2)}) %collective-permute-start) | collective-permute-done | bytes 524320 | tf_op jit(solution)/shard_map/ppermute | solution.py:269
  16.8 1.3 %collective-permute-done.1.below_ref = f32[32,16,256]{2,1,0:T(8,128)S(1)} collective-permute-done((f32[32,16,256]{2,1,0:T(8,128)S(1)}, f32[32,16,256]{2,1,0:T(8,128)S(1)}, u32[]{:S(2)}, u32[]{:S(2)}) %collective-permute-start.1) | collective-permute-done | bytes 524320 | tf_op jit(solution)/shard_map/ppermute | solution.py:270
  18.1 0.0 copy-done.3
  18.1 1.6 %shard_map.87 = (f32[8,32,256]{2,1,0:T(8,128)S(1)}, f32[8,32,256]{2,1,0:T(8,128)S(1)}) custom-call(s32[5]{0:T(128)S(1)} %stack.23.where, f32[32,32,256]{2,1,0:T(8,128)S(1)} %get-tuple-element.20.p_ref, f32[32,16,256]{2,1,0:T(8,128)S(1)} %collective-permute-done.above_ref, f32[32,16,256]{2,1,0:T(8,128)S(1)} %get-tuple-element.22.top_ref, ...), custom_call_target="tpu_custom_call" | custom-call | flops 2000000000 | bytes 1048576 | tf_op jit(solution)/shard_map/pallas_call | solution.py:234
  19.8 0.1 collective-permute-start.6
  19.9 1.7 %shard_map.86 = (f32[8,32,256]{2,1,0:T(8,128)S(1)}, f32[8,32,256]{2,1,0:T(8,128)S(1)}) custom-call(s32[5]{0:T(128)S(1)} %stack.23.where, f32[32,32,256]{2,1,0:T(8,128)S(1)} %get-tuple-element.20.p_ref, f32[32,16,256]{2,1,0:T(8,128)S(1)} %collective-permute-done.above_ref, f32[32,16,256]{2,1,0:T(8,128)S(1)} %get-tuple-element.22.top_ref, ...), custom_call_target="tpu_custom_call" | custom-call | flops 2000000000 | bytes 1048576 | tf_op jit(solution)/shard_map/pallas_call | solution.py:234
  21.5 0.6 %collective-permute-start.5 = (f32[8,32,256]{2,1,0:T(8,128)S(1)}, f32[8,32,256]{2,1,0:T(8,128)S(1)}, u32[]{:S(2)}, u32[]{:S(2)}) collective-permute-start(f32[8,32,256]{2,1,0:T(8,128)S(1)} %get-tuple-element.32), channel_id=1, source_target_pairs={{0,8},{8,0},{1,9},{9,1},{2,10},{10,2},{3,11},{11,3},{4,12},{12,4},... | collective-permute-start | bytes 786440 | tf_op jit(solution)/shard_map/ppermute | solution.py:296
  22.1 0.0 collective-permute-done.6
  22.1 3.2 %collective-permute-start.7 = (f32[2,32,256]{2,1,0:T(8,128)S(1)}, f32[2,32,256]{2,1,0:T(8,128)S(1)}, u32[]{:S(2)}, u32[]{:S(2)}) collective-permute-start(f32[2,32,256]{2,1,0:T(8,128)S(1)} %get-tuple-element.39), channel_id=1, source_target_pairs={{0,128},{64,192},{128,0},{192,64},{1,129},{65,193},{129,1},{193,65... | collective-permute-start | bytes 196616 | tf_op jit(solution)/shard_map/ppermute | solution.py:303
  25.3 0.5 %collective-permute-start.8 = (f32[2,32,256]{2,1,0:T(8,128)S(1)}, f32[2,32,256]{2,1,0:T(8,128)S(1)}, u32[]{:S(2)}, u32[]{:S(2)}) collective-permute-start(f32[2,32,256]{2,1,0:T(8,128)S(1)} %get-tuple-element.42), channel_id=1, source_target_pairs={{0,64},{64,128},{128,192},{192,0},{1,65},{65,129},{129,193},{193,1... | collective-permute-start | bytes 196616 | tf_op jit(solution)/shard_map/ppermute | solution.py:303
  25.8 0.0 collective-permute-done.5
  25.9 2.8 %collective-permute-start.9 = (f32[2,32,256]{2,1,0:T(8,128)S(1)}, f32[2,32,256]{2,1,0:T(8,128)S(1)}, u32[]{:S(2)}, u32[]{:S(2)}) collective-permute-start(f32[2,32,256]{2,1,0:T(8,128)S(1)} %get-tuple-element.38), channel_id=1, source_target_pairs={{0,192},{64,0},{128,64},{192,128},{1,193},{65,1},{129,65},{193,129... | collective-permute-start | bytes 196616 | tf_op jit(solution)/shard_map/ppermute | solution.py:303
  28.6 0.0 collective-permute-start.10
  28.7 1.0 %collective-permute-start.11 = (f32[2,32,256]{2,1,0:T(8,128)S(1)}, f32[2,32,256]{2,1,0:T(8,128)S(1)}, u32[]{:S(2)}, u32[]{:S(2)}) collective-permute-start(f32[2,32,256]{2,1,0:T(8,128)S(1)} %get-tuple-element.40), channel_id=1, source_target_pairs={{0,64},{64,128},{128,192},{192,0},{1,65},{65,129},{129,193},{193,1... | collective-permute-start | bytes 196616 | tf_op jit(solution)/shard_map/ppermute | solution.py:303
  29.6 0.0 collective-permute-done.7
  29.6 2.3 %collective-permute-start.12 = (f32[2,32,256]{2,1,0:T(8,128)S(1)}, f32[2,32,256]{2,1,0:T(8,128)S(1)}, u32[]{:S(2)}, u32[]{:S(2)}) collective-permute-start(f32[2,32,256]{2,1,0:T(8,128)S(1)} %get-tuple-element.36), channel_id=1, source_target_pairs={{0,192},{64,0},{128,64},{192,128},{1,193},{65,1},{129,65},{193,129... | collective-permute-start | bytes 196616 | tf_op jit(solution)/shard_map/ppermute | solution.py:303
  31.9 0.0 collective-permute-done.8
  31.9 0.0 collective-permute-done.9
  31.9 6.3 %collective-permute-start.15 = (f32[1,32,256]{2,1,0:T(8,128)S(1)}, f32[1,32,256]{2,1,0:T(8,128)S(1)}, u32[]{:S(2)}, u32[]{:S(2)}) collective-permute-start(f32[1,32,256]{2,1,0:T(8,128)S(1)} %fusion), channel_id=1, source_target_pairs={{0,48},{16,0},{32,16},{48,32},{1,49},{17,1},{33,17},{49,33},{2,50}... | collective-permute-start | bytes 98312 | tf_op jit(solution)/shard_map/ppermute | solution.py:306
  38.3 0.0 collective-permute-done.10
  38.3 0.0 collective-permute-done.11
  38.3 0.0 collective-permute-done.12
  38.3 3.8 %collective-permute-start.13 = (f32[1,32,256]{2,1,0:T(8,128)S(1)}, f32[1,32,256]{2,1,0:T(8,128)S(1)}, u32[]{:S(2)}, u32[]{:S(2)}) collective-permute-start(f32[1,32,256]{2,1,0:T(8,128)S(1)} %get-tuple-element.44), channel_id=1, source_target_pairs={{0,32},{16,48},{32,0},{48,16},{1,33},{17,49},{33,1},{49,17},{2,34}... | collective-permute-start | bytes 98312 | tf_op jit(solution)/shard_map/ppermute | solution.py:306
  42.1 1.5 %collective-permute-start.14 = (f32[1,32,256]{2,1,0:T(8,128)S(1)}, f32[1,32,256]{2,1,0:T(8,128)S(1)}, u32[]{:S(2)}, u32[]{:S(2)}) collective-permute-start(f32[1,32,256]{2,1,0:T(8,128)S(1)} %get-tuple-element.43), channel_id=1, source_target_pairs={{0,16},{16,32},{32,48},{48,0},{1,17},{17,33},{33,49},{49,1},{2,18}... | collective-permute-start | bytes 98312 | tf_op jit(solution)/shard_map/ppermute | solution.py:306
  43.6 0.0 collective-permute-done.15
  43.6 2.6 %collective-permute-done.13 = f32[1,32,256]{2,1,0:T(8,128)S(1)} collective-permute-done((f32[1,32,256]{2,1,0:T(8,128)S(1)}, f32[1,32,256]{2,1,0:T(8,128)S(1)}, u32[]{:S(2)}, u32[]{:S(2)}) %collective-permute-start.13) | collective-permute-done | bytes 32800 | tf_op jit(solution)/shard_map/ppermute | solution.py:306
  46.2 1.9 %collective-permute-done.14 = f32[1,32,256]{2,1,0:T(8,128)S(1)} collective-permute-done((f32[1,32,256]{2,1,0:T(8,128)S(1)}, f32[1,32,256]{2,1,0:T(8,128)S(1)}, u32[]{:S(2)}, u32[]{:S(2)}) %collective-permute-start.14) | collective-permute-done | bytes 32800 | tf_op jit(solution)/shard_map/ppermute | solution.py:306
  48.1 0.6 %fusion.6 = f32[1,32,256]{2,1,0:T(8,128)} fusion(f32[1,32,256]{2,1,0:T(8,128)S(1)} %collective-permute-done.13, f32[2,32,256]{2,1,0:T(8,128)S(1)} %collective-permute-done.9, f32[2,32,256]{2,1,0:T(8,128)S(1)} %collective-permute-done.8, f32[2,32,256]{2,1,0:T(8,128)S(1)} %collective-permute-done.7, f32[2,32,256]{2,1,0:T(8,128)S(1)} %get-tuple-element.35, ...), kind=kLoop, calls=%fused_computation.21 | loop fusion | flops 57344 | bytes 262144 | tf_op jit(solution)/shard_map/mul | solution.py:307
  (6 shorter events, 0.1 us)
Async XLA Ops:
  2.4 14.4 %collective-permute-start = (f32[32,16,256]{2,1,0:T(8,128)S(1)}, f32[32,16,256]{2,1,0:T(8,128)S(1)}, u32[]{:S(2)}, u32[]{:S(2)}) collective-permute-start(f32[32,16,256]{2,1,0:T(8,128)S(1)} %get-tuple-element.21.bottom_ref), channel_id=1, source_target_pairs={{0,2},{2,4},{4,6},{6,0},{1,3},{3,5},{5,7},{7,1},{8,10},{10,12},{12... | collective-permute-start | bytes 1572872 | tf_op jit(solution)/shard_map/ppermute | solution.py:269
  4.0 6.1 %copy-start = (bf16[2,2,4,32,128]{4,3,2,1,0:T(8,128)(2,1)S(1)}, bf16[2,2,4,32,128]{4,3,2,1,0:T(8,128)(2,1)}, u32[]{:S(2)}) copy-start(bf16[2,2,4,32,128]{4,3,2,1,0:T(8,128)(2,1)} %constant.36.clone.patch_ref) | copy-start | bytes 393220
  4.0 6.1 %copy-start.1 = (bf16[2,2,64,128]{3,2,1,0:T(8,128)(2,1)S(1)}, bf16[2,2,64,128]{3,2,1,0:T(8,128)(2,1)}, u32[]{:S(2)}) copy-start(bf16[2,2,64,128]{3,2,1,0:T(8,128)(2,1)} %constant.38.clone.edge_ref) | copy-start | bytes 196612
  4.0 14.1 %collective-permute-start.1 = (f32[32,16,256]{2,1,0:T(8,128)S(1)}, f32[32,16,256]{2,1,0:T(8,128)S(1)}, u32[]{:S(2)}, u32[]{:S(2)}) collective-permute-start(f32[32,16,256]{2,1,0:T(8,128)S(1)} %get-tuple-element.22.top_ref), channel_id=1, source_target_pairs={{0,6},{2,0},{4,2},{6,4},{1,7},{3,1},{5,3},{7,5},{8,14},{10,8},{12,... | collective-permute-start | bytes 1572872 | tf_op jit(solution)/shard_map/ppermute | solution.py:270
  5.5 7.9 %collective-permute-start.3 = (f32[2,32,256]{2,1,0:T(8,128)S(1)}, f32[2,32,256]{2,1,0:T(8,128)S(1)}, u32[]{:S(2)}, u32[]{:S(2)}) collective-permute-start(f32[2,32,256]{2,1,0:T(8,128)S(1)} %get-tuple-element.25), channel_id=1, source_target_pairs={{0,1},{1,0},{2,3},{3,2},{4,5},{5,4},{6,7},{7,6},{8,9},{9,8},{10,11... | collective-permute-start | bytes 196616 | tf_op jit(solution)/shard_map/ppermute | solution.py:277
  7.2 6.0 %collective-permute-start.2 = (f32[2,16,256]{2,1,0:T(8,128)S(1)}, f32[2,16,256]{2,1,0:T(8,128)S(1)}, u32[]{:S(2)}, u32[]{:S(2)}) collective-permute-start(f32[2,16,256]{2,1,0:T(8,128)S(1)} %get-tuple-element.24), channel_id=1, source_target_pairs={{0,3},{1,2},{2,5},{3,4},{4,7},{5,6},{6,1},{7,0},{8,11},{9,10},{10,... | collective-permute-start | bytes 98312 | tf_op jit(solution)/shard_map/ppermute | solution.py:275
  8.4 5.0 %copy-start.2 = (bf16[4,96,192]{2,1,0:T(8,128)(2,1)S(1)}, bf16[4,96,192]{2,1,0:T(8,128)(2,1)}, u32[]{:S(2)}) copy-start(bf16[4,96,192]{2,1,0:T(8,128)(2,1)} %constant.33.clone.left_ref) | copy-start | bytes 442372
  8.4 5.0 %copy-start.4 = (bf16[4,16,96]{2,1,0:T(8,128)(2,1)S(1)}, bf16[4,16,96]{2,1,0:T(8,128)(2,1)}, u32[]{:S(2)}) copy-start(bf16[4,16,96]{2,1,0:T(8,128)(2,1)} %constant.34.clone.inner_ref) | copy-start | bytes 36868
  8.4 5.0 %collective-permute-start.4 = (f32[2,16,256]{2,1,0:T(8,128)S(1)}, f32[2,16,256]{2,1,0:T(8,128)S(1)}, u32[]{:S(2)}, u32[]{:S(2)}) collective-permute-start(f32[2,16,256]{2,1,0:T(8,128)S(1)} %get-tuple-element.26), channel_id=1, source_target_pairs={{0,7},{1,6},{2,1},{3,0},{4,3},{5,2},{6,5},{7,4},{8,15},{9,14},{10,... | collective-permute-start | bytes 98312 | tf_op jit(solution)/shard_map/ppermute | solution.py:276
  13.3 4.8 %copy-start.3 = (bf16[4,80,192]{2,1,0:T(8,128)(2,1)S(1)}, bf16[4,80,192]{2,1,0:T(8,128)(2,1)}, u32[]{:S(2)}) copy-start(bf16[4,80,192]{2,1,0:T(8,128)(2,1)} %constant.35.clone.left_ref) | copy-start | bytes 368644
  19.8 2.3 %collective-permute-start.6 = (f32[8,32,256]{2,1,0:T(8,128)S(1)}, f32[8,32,256]{2,1,0:T(8,128)S(1)}, u32[]{:S(2)}, u32[]{:S(2)}) collective-permute-start(f32[8,32,256]{2,1,0:T(8,128)S(1)} %get-tuple-element.34), channel_id=1, source_target_pairs={{0,8},{8,0},{1,9},{9,1},{2,10},{10,2},{3,11},{11,3},{4,12},{12,4},... | collective-permute-start | bytes 786440 | tf_op jit(solution)/shard_map/ppermute | solution.py:296
  21.5 4.3 %collective-permute-start.5 = (f32[8,32,256]{2,1,0:T(8,128)S(1)}, f32[8,32,256]{2,1,0:T(8,128)S(1)}, u32[]{:S(2)}, u32[]{:S(2)}) collective-permute-start(f32[8,32,256]{2,1,0:T(8,128)S(1)} %get-tuple-element.32), channel_id=1, source_target_pairs={{0,8},{8,0},{1,9},{9,1},{2,10},{10,2},{3,11},{11,3},{4,12},{12,4},... | collective-permute-start | bytes 786440 | tf_op jit(solution)/shard_map/ppermute | solution.py:296
  22.1 7.5 %collective-permute-start.7 = (f32[2,32,256]{2,1,0:T(8,128)S(1)}, f32[2,32,256]{2,1,0:T(8,128)S(1)}, u32[]{:S(2)}, u32[]{:S(2)}) collective-permute-start(f32[2,32,256]{2,1,0:T(8,128)S(1)} %get-tuple-element.39), channel_id=1, source_target_pairs={{0,128},{64,192},{128,0},{192,64},{1,129},{65,193},{129,1},{193,65... | collective-permute-start | bytes 196616 | tf_op jit(solution)/shard_map/ppermute | solution.py:303
  25.3 6.6 %collective-permute-start.8 = (f32[2,32,256]{2,1,0:T(8,128)S(1)}, f32[2,32,256]{2,1,0:T(8,128)S(1)}, u32[]{:S(2)}, u32[]{:S(2)}) collective-permute-start(f32[2,32,256]{2,1,0:T(8,128)S(1)} %get-tuple-element.42), channel_id=1, source_target_pairs={{0,64},{64,128},{128,192},{192,0},{1,65},{65,129},{129,193},{193,1... | collective-permute-start | bytes 196616 | tf_op jit(solution)/shard_map/ppermute | solution.py:303
  25.9 6.0 %collective-permute-start.9 = (f32[2,32,256]{2,1,0:T(8,128)S(1)}, f32[2,32,256]{2,1,0:T(8,128)S(1)}, u32[]{:S(2)}, u32[]{:S(2)}) collective-permute-start(f32[2,32,256]{2,1,0:T(8,128)S(1)} %get-tuple-element.38), channel_id=1, source_target_pairs={{0,192},{64,0},{128,64},{192,128},{1,193},{65,1},{129,65},{193,129... | collective-permute-start | bytes 196616 | tf_op jit(solution)/shard_map/ppermute | solution.py:303
  28.6 9.6 %collective-permute-start.10 = (f32[2,32,256]{2,1,0:T(8,128)S(1)}, f32[2,32,256]{2,1,0:T(8,128)S(1)}, u32[]{:S(2)}, u32[]{:S(2)}) collective-permute-start(f32[2,32,256]{2,1,0:T(8,128)S(1)} %get-tuple-element.41), channel_id=1, source_target_pairs={{0,128},{64,192},{128,0},{192,64},{1,129},{65,193},{129,1},{193,65... | collective-permute-start | bytes 196616 | tf_op jit(solution)/shard_map/ppermute | solution.py:303
  28.7 9.6 %collective-permute-start.11 = (f32[2,32,256]{2,1,0:T(8,128)S(1)}, f32[2,32,256]{2,1,0:T(8,128)S(1)}, u32[]{:S(2)}, u32[]{:S(2)}) collective-permute-start(f32[2,32,256]{2,1,0:T(8,128)S(1)} %get-tuple-element.40), channel_id=1, source_target_pairs={{0,64},{64,128},{128,192},{192,0},{1,65},{65,129},{129,193},{193,1... | collective-permute-start | bytes 196616 | tf_op jit(solution)/shard_map/ppermute | solution.py:303
  29.6 8.7 %collective-permute-start.12 = (f32[2,32,256]{2,1,0:T(8,128)S(1)}, f32[2,32,256]{2,1,0:T(8,128)S(1)}, u32[]{:S(2)}, u32[]{:S(2)}) collective-permute-start(f32[2,32,256]{2,1,0:T(8,128)S(1)} %get-tuple-element.36), channel_id=1, source_target_pairs={{0,192},{64,0},{128,64},{192,128},{1,193},{65,1},{129,65},{193,129... | collective-permute-start | bytes 196616 | tf_op jit(solution)/shard_map/ppermute | solution.py:303
  31.9 11.7 %collective-permute-start.15 = (f32[1,32,256]{2,1,0:T(8,128)S(1)}, f32[1,32,256]{2,1,0:T(8,128)S(1)}, u32[]{:S(2)}, u32[]{:S(2)}) collective-permute-start(f32[1,32,256]{2,1,0:T(8,128)S(1)} %fusion), channel_id=1, source_target_pairs={{0,48},{16,0},{32,16},{48,32},{1,49},{17,1},{33,17},{49,33},{2,50}... | collective-permute-start | bytes 98312 | tf_op jit(solution)/shard_map/ppermute | solution.py:306
  38.3 7.9 %collective-permute-start.13 = (f32[1,32,256]{2,1,0:T(8,128)S(1)}, f32[1,32,256]{2,1,0:T(8,128)S(1)}, u32[]{:S(2)}, u32[]{:S(2)}) collective-permute-start(f32[1,32,256]{2,1,0:T(8,128)S(1)} %get-tuple-element.44), channel_id=1, source_target_pairs={{0,32},{16,48},{32,0},{48,16},{1,33},{17,49},{33,1},{49,17},{2,34}... | collective-permute-start | bytes 98312 | tf_op jit(solution)/shard_map/ppermute | solution.py:306
  42.1 6.0 %collective-permute-start.14 = (f32[1,32,256]{2,1,0:T(8,128)S(1)}, f32[1,32,256]{2,1,0:T(8,128)S(1)}, u32[]{:S(2)}, u32[]{:S(2)}) collective-permute-start(f32[1,32,256]{2,1,0:T(8,128)S(1)} %get-tuple-element.43), channel_id=1, source_target_pairs={{0,16},{16,32},{32,48},{48,0},{1,17},{17,33},{33,49},{49,1},{2,18}... | collective-permute-start | bytes 98312 | tf_op jit(solution)/shard_map/ppermute | solution.py:306

commit v13 on v12

--- a/solution.py
+++ b/solution.py
@@ -83,19 +83,19 @@
 def product_kernel(where, p_hbm, c_hbm, p_ref, top_ref, bottom_ref, c_ref, sems):
     copies = []
     for k in range(4):
-        for h in range(2):
-            source, at = pl.ds(8 * block_of(where, k) + 4 * h, 4), pl.ds(8 * k + 4 * h, 4)
-            copies.append(pltpu.make_async_copy(p_hbm.at[0, source], p_ref.at[at], sems.at[0, 2 * k + h]))
-            copies.append(pltpu.make_async_copy(c_hbm.at[source], c_ref.at[at], sems.at[1, 2 * k + h]))
+        source, at = pl.ds(8 * block_of(where, k), 8), pl.ds(8 * k, 8)
+        copies.append(pltpu.make_async_copy(p_hbm.at[0, source], p_ref.at[at], sems.at[0, k]))
+        copies.append(pltpu.make_async_copy(c_hbm.at[source], c_ref.at[at], sems.at[1, k]))
     for copy in copies:
         copy.start()
-    for g in range(8):
-        copies[2 * g].wait()
-        copies[2 * g + 1].wait()
-        at = slice(4 * g, 4 * g + 4)
-        v = p_ref[at] * c_ref[at]
-        top_ref[at] = v[:, :HALO]
-        bottom_ref[at] = v[:, HALO:]
+    for k in range(4):
+        copies[2 * k].wait()
+        copies[2 * k + 1].wait()
+        for g in range(2 * k, 2 * k + 2):
+            at = slice(4 * g, 4 * g + 4)
+            v = p_ref[at] * c_ref[at]
+            top_ref[at] = v[:, :HALO]
+            bottom_ref[at] = v[:, HALO:]
 
 
 def edge_kernel(where, top_ref, bottom_ref, edge_ref, edge_top_ref, edge_bottom_ref):
@@ -264,7 +264,7 @@
     swap = [(0, 1), (1, 0)]
     near_p, top, bottom = call(
         product_kernel, [(32, 32, 256)] + [(32, 16, 256)] * 2, where, perturbations, control, hbm=(1, 2),
-        scratch=[vmem((32, 32, 256), F32), sems((2, 8))],
+        scratch=[vmem((32, 32, 256), F32), sems((2, 4))],
     )
     above = lax.ppermute(bottom, "gx", ring(1))
     below = lax.ppermute(top, "gx", ring(3))

time: 49 us -> 48.8 us (level)
  no operation moved by 1% of the time
where the time goes in v13:
time: 48.8 us; the launch traced here: 48.6 us
  starting transfers between devices  29 us (59%)
  Pallas kernels  9.42 us (19%)
  waiting for transfers between devices  9.22 us (19%)
  other arithmetic  0.73 us (1%)
    ppermute x3, starting transfers between devices, body(): lax.ppermute(cell, 'z', ring(e))  11.6 us
    ppermute x6, starting transfers between devices, body(): x2, x1, x3 = (lax.ppermute(piece[d, wave], 'x', ring(d)) for d in (2, 1, 3))  9.7 us
    pallas_call x6, Pallas kernels, call(): pl.pallas_call(kernel, out_shape=[o if isinstance(o, jax.ShapeDtypeStruct...  9.42 us
    ppermute x3, waiting for transfers between devices, body(): lax.ppermute(cell, 'z', ring(e))  4.55 us
    ppermute x1, waiting for transfers between devices, body(): above = lax.ppermute(bottom, 'gx', ring(1))  2.09 us
    ppermute x1, starting transfers between devices, body(): side_below = lax.ppermute(edge_top, ('gx', 'gy'), diagonal(3))  1.8 us
    ppermute x1, starting transfers between devices, body(): side = lax.ppermute(edges, 'gy', swap)  1.76 us
    ppermute x1, starting transfers between devices, body(): above = lax.ppermute(bottom, 'gx', ring(1))  1.65 us
  transfers between devices with their start and end apart: 16, of which 6 were waited for; matrix products, arithmetic and copies ran while one was open for 0% of the time, Pallas kernels for 12%

profile of v13, /device:TPU:8, one launch (start us, length us, event | category | flops | bytes accessed | tf_op | source)
XLA Modules:
  0.0 48.6 jit_solution(13471449422949687632)
XLA Ops:
  0.0 0.1 stack.23.where
  0.1 2.1 %shard_map.82 = (f32[32,32,256]{2,1,0:T(8,128)S(1)}, f32[32,16,256]{2,1,0:T(8,128)S(1)}, f32[32,16,256]{2,1,0:T(8,128)S(1)}) custom-call(s32[5]{0:T(128)S(1)} %stack.23.where, f32[1,32,32,256]{3,2,1,0:T(8,128)} %p_hbm.1, f32[32,32,256]{2,1,0:T(8,128)} %c_hbm.1), custom_call_target="tpu_custom_call" | custom-call | bytes 1048576 | tf_op jit(solution)/shard_map/pallas_call | solution.py:234
  2.2 1.7 %collective-permute-start = (f32[32,16,256]{2,1,0:T(8,128)S(1)}, f32[32,16,256]{2,1,0:T(8,128)S(1)}, u32[]{:S(2)}, u32[]{:S(2)}) collective-permute-start(f32[32,16,256]{2,1,0:T(8,128)S(1)} %get-tuple-element.21.bottom_ref), channel_id=1, source_target_pairs={{0,2},{2,4},{4,6},{6,0},{1,3},{3,5},{5,7},{7,1},{8,10},{10,12},{12... | collective-permute-start | bytes 1572872 | tf_op jit(solution)/shard_map/ppermute | solution.py:269
  3.9 0.0 copy-start
  3.9 0.0 copy-start.1
  3.9 0.7 %collective-permute-start.1 = (f32[32,16,256]{2,1,0:T(8,128)S(1)}, f32[32,16,256]{2,1,0:T(8,128)S(1)}, u32[]{:S(2)}, u32[]{:S(2)}) collective-permute-start(f32[32,16,256]{2,1,0:T(8,128)S(1)} %get-tuple-element.22.top_ref), channel_id=1, source_target_pairs={{0,6},{2,0},{4,2},{6,4},{1,7},{3,1},{5,3},{7,5},{8,14},{10,8},{12,... | collective-permute-start | bytes 1572872 | tf_op jit(solution)/shard_map/ppermute | solution.py:270
  4.6 0.7 %shard_map.84 = (f32[2,32,256]{2,1,0:T(8,128)S(1)}, f32[2,16,256]{2,1,0:T(8,128)S(1)}, f32[2,16,256]{2,1,0:T(8,128)S(1)}) custom-call(s32[5]{0:T(128)S(1)} %stack.23.where, f32[32,16,256]{2,1,0:T(8,128)S(1)} %get-tuple-element.22.top_ref, f32[32,16,256]{2,1,0:T(8,128)S(1)} %get-tuple-element.21.bottom_ref), custom_call_target="tpu_custom_call" | custom-call | bytes 1048576 | tf_op jit(solution)/shard_map/pallas_call | solution.py:234
  5.3 1.8 %collective-permute-start.3 = (f32[2,32,256]{2,1,0:T(8,128)S(1)}, f32[2,32,256]{2,1,0:T(8,128)S(1)}, u32[]{:S(2)}, u32[]{:S(2)}) collective-permute-start(f32[2,32,256]{2,1,0:T(8,128)S(1)} %get-tuple-element.25), channel_id=1, source_target_pairs={{0,1},{1,0},{2,3},{3,2},{4,5},{5,4},{6,7},{7,6},{8,9},{9,8},{10,11... | collective-permute-start | bytes 196616 | tf_op jit(solution)/shard_map/ppermute | solution.py:277
  7.1 1.1 %collective-permute-start.2 = (f32[2,16,256]{2,1,0:T(8,128)S(1)}, f32[2,16,256]{2,1,0:T(8,128)S(1)}, u32[]{:S(2)}, u32[]{:S(2)}) collective-permute-start(f32[2,16,256]{2,1,0:T(8,128)S(1)} %get-tuple-element.24), channel_id=1, source_target_pairs={{0,3},{1,2},{2,5},{3,4},{4,7},{5,6},{6,1},{7,0},{8,11},{9,10},{10,... | collective-permute-start | bytes 98312 | tf_op jit(solution)/shard_map/ppermute | solution.py:275
  8.2 1.8 %collective-permute-start.4 = (f32[2,16,256]{2,1,0:T(8,128)S(1)}, f32[2,16,256]{2,1,0:T(8,128)S(1)}, u32[]{:S(2)}, u32[]{:S(2)}) collective-permute-start(f32[2,16,256]{2,1,0:T(8,128)S(1)} %get-tuple-element.26), channel_id=1, source_target_pairs={{0,7},{1,6},{2,1},{3,0},{4,3},{5,2},{6,5},{7,4},{8,15},{9,14},{10,... | collective-permute-start | bytes 98312 | tf_op jit(solution)/shard_map/ppermute | solution.py:276
  10.0 0.0 copy-done
  10.0 0.0 copy-done.1
  10.0 1.9 %shard_map.83 = (bf16[512,128]{1,0:T(8,128)(2,1)S(1)}, bf16[512,128]{1,0:T(8,128)(2,1)S(1)}, bf16[2,1024,256]{2,1,0:T(8,128)(2,1)S(1)}) custom-call(s32[5]{0:T(128)S(1)} %stack.23.where, bf16[2,2,64,128]{3,2,1,0:T(8,128)(2,1)S(1)} %copy-done.1, bf16[2,2,4,32,128]{4,3,2,1,0:T(8,128)(2,1)S(1)} %copy-done, bf16[2,1024,256]{2,1,0:T(8,128)(2,1)} %constant.37.clone.right_hbm), custom_call_target="tpu_custom_call" | custom-call | bytes 1048576 | tf_op jit(solution)/shard_map/pallas_call | solution.py:234
  11.9 1.1 %collective-permute-done.2.side_above_ref = f32[2,16,256]{2,1,0:T(8,128)S(1)} collective-permute-done((f32[2,16,256]{2,1,0:T(8,128)S(1)}, f32[2,16,256]{2,1,0:T(8,128)S(1)}, u32[]{:S(2)}, u32[]{:S(2)}) %collective-permute-start.2) | collective-permute-done | bytes 32800 | tf_op jit(solution)/shard_map/ppermute | solution.py:275
  13.0 0.1 collective-permute-done.4.side_below_ref
  13.2 0.0 collective-permute-done.3.side_ref
  13.2 0.0 copy-done.2
  13.2 0.0 copy-done.4
  13.2 0.0 copy-start.3
  13.2 1.4 %shard_map.85 = (f32[128,128]{1,0:T(8,128)S(1)}, f32[512,256]{1,0:T(8,128)S(1)}) custom-call(s32[5]{0:T(128)S(1)} %stack.23.where, f32[32,16,256]{2,1,0:T(8,128)S(1)} %get-tuple-element.22.top_ref, f32[32,16,256]{2,1,0:T(8,128)S(1)} %get-tuple-element.21.bottom_ref, f32[2,16,256]{2,1,0:T(8,128)S(1)} %collective-permute-done.2.side_above_ref, ...), custom_call_target="tpu_custom_call" | custom-call | flops 1000000000 | bytes 1048576 | tf_op jit(solution)/shard_map/pallas_call | solution.py:234
  14.6 2.1 %collective-permute-done.above_ref = f32[32,16,256]{2,1,0:T(8,128)S(1)} collective-permute-done((f32[32,16,256]{2,1,0:T(8,128)S(1)}, f32[32,16,256]{2,1,0:T(8,128)S(1)}, u32[]{:S(2)}, u32[]{:S(2)}) %collective-permute-start) | collective-permute-done | bytes 524320 | tf_op jit(solution)/shard_map/ppermute | solution.py:269
  16.7 1.3 %collective-permute-done.1.below_ref = f32[32,16,256]{2,1,0:T(8,128)S(1)} collective-permute-done((f32[32,16,256]{2,1,0:T(8,128)S(1)}, f32[32,16,256]{2,1,0:T(8,128)S(1)}, u32[]{:S(2)}, u32[]{:S(2)}) %collective-permute-start.1) | collective-permute-done | bytes 524320 | tf_op jit(solution)/shard_map/ppermute | solution.py:270
  18.0 0.0 copy-done.3
  18.0 1.6 %shard_map.87 = (f32[8,32,256]{2,1,0:T(8,128)S(1)}, f32[8,32,256]{2,1,0:T(8,128)S(1)}) custom-call(s32[5]{0:T(128)S(1)} %stack.23.where, f32[32,32,256]{2,1,0:T(8,128)S(1)} %get-tuple-element.20.p_ref, f32[32,16,256]{2,1,0:T(8,128)S(1)} %collective-permute-done.above_ref, f32[32,16,256]{2,1,0:T(8,128)S(1)} %get-tuple-element.22.top_ref, ...), custom_call_target="tpu_custom_call" | custom-call | flops 2000000000 | bytes 1048576 | tf_op jit(solution)/shard_map/pallas_call | solution.py:234
  19.6 0.1 collective-permute-start.6
  19.7 1.7 %shard_map.86 = (f32[8,32,256]{2,1,0:T(8,128)S(1)}, f32[8,32,256]{2,1,0:T(8,128)S(1)}) custom-call(s32[5]{0:T(128)S(1)} %stack.23.where, f32[32,32,256]{2,1,0:T(8,128)S(1)} %get-tuple-element.20.p_ref, f32[32,16,256]{2,1,0:T(8,128)S(1)} %collective-permute-done.above_ref, f32[32,16,256]{2,1,0:T(8,128)S(1)} %get-tuple-element.22.top_ref, ...), custom_call_target="tpu_custom_call" | custom-call | flops 2000000000 | bytes 1048576 | tf_op jit(solution)/shard_map/pallas_call | solution.py:234
  21.4 0.6 %collective-permute-start.5 = (f32[8,32,256]{2,1,0:T(8,128)S(1)}, f32[8,32,256]{2,1,0:T(8,128)S(1)}, u32[]{:S(2)}, u32[]{:S(2)}) collective-permute-start(f32[8,32,256]{2,1,0:T(8,128)S(1)} %get-tuple-element.32), channel_id=1, source_target_pairs={{0,8},{8,0},{1,9},{9,1},{2,10},{10,2},{3,11},{11,3},{4,12},{12,4},... | collective-permute-start | bytes 786440 | tf_op jit(solution)/shard_map/ppermute | solution.py:296
  22.0 0.0 collective-permute-done.6
  22.0 3.1 %collective-permute-start.7 = (f32[2,32,256]{2,1,0:T(8,128)S(1)}, f32[2,32,256]{2,1,0:T(8,128)S(1)}, u32[]{:S(2)}, u32[]{:S(2)}) collective-permute-start(f32[2,32,256]{2,1,0:T(8,128)S(1)} %get-tuple-element.39), channel_id=1, source_target_pairs={{0,128},{64,192},{128,0},{192,64},{1,129},{65,193},{129,1},{193,65... | collective-permute-start | bytes 196616 | tf_op jit(solution)/shard_map/ppermute | solution.py:303
  25.1 0.5 %collective-permute-start.8 = (f32[2,32,256]{2,1,0:T(8,128)S(1)}, f32[2,32,256]{2,1,0:T(8,128)S(1)}, u32[]{:S(2)}, u32[]{:S(2)}) collective-permute-start(f32[2,32,256]{2,1,0:T(8,128)S(1)} %get-tuple-element.42), channel_id=1, source_target_pairs={{0,64},{64,128},{128,192},{192,0},{1,65},{65,129},{129,193},{193,1... | collective-permute-start | bytes 196616 | tf_op jit(solution)/shard_map/ppermute | solution.py:303
  25.7 0.0 collective-permute-done.5
  25.7 2.8 %collective-permute-start.9 = (f32[2,32,256]{2,1,0:T(8,128)S(1)}, f32[2,32,256]{2,1,0:T(8,128)S(1)}, u32[]{:S(2)}, u32[]{:S(2)}) collective-permute-start(f32[2,32,256]{2,1,0:T(8,128)S(1)} %get-tuple-element.38), channel_id=1, source_target_pairs={{0,192},{64,0},{128,64},{192,128},{1,193},{65,1},{129,65},{193,129... | collective-permute-start | bytes 196616 | tf_op jit(solution)/shard_map/ppermute | solution.py:303
  28.5 0.0 collective-permute-start.10
  28.5 1.0 %collective-permute-start.11 = (f32[2,32,256]{2,1,0:T(8,128)S(1)}, f32[2,32,256]{2,1,0:T(8,128)S(1)}, u32[]{:S(2)}, u32[]{:S(2)}) collective-permute-start(f32[2,32,256]{2,1,0:T(8,128)S(1)} %get-tuple-element.40), channel_id=1, source_target_pairs={{0,64},{64,128},{128,192},{192,0},{1,65},{65,129},{129,193},{193,1... | collective-permute-start | bytes 196616 | tf_op jit(solution)/shard_map/ppermute | solution.py:303
  29.5 0.0 collective-permute-done.7
  29.5 2.3 %collective-permute-start.12 = (f32[2,32,256]{2,1,0:T(8,128)S(1)}, f32[2,32,256]{2,1,0:T(8,128)S(1)}, u32[]{:S(2)}, u32[]{:S(2)}) collective-permute-start(f32[2,32,256]{2,1,0:T(8,128)S(1)} %get-tuple-element.36), channel_id=1, source_target_pairs={{0,192},{64,0},{128,64},{192,128},{1,193},{65,1},{129,65},{193,129... | collective-permute-start | bytes 196616 | tf_op jit(solution)/shard_map/ppermute | solution.py:303
  31.7 0.0 collective-permute-done.8
  31.7 0.0 collective-permute-done.9
  31.8 6.3 %collective-permute-start.15 = (f32[1,32,256]{2,1,0:T(8,128)S(1)}, f32[1,32,256]{2,1,0:T(8,128)S(1)}, u32[]{:S(2)}, u32[]{:S(2)}) collective-permute-start(f32[1,32,256]{2,1,0:T(8,128)S(1)} %fusion), channel_id=1, source_target_pairs={{0,48},{16,0},{32,16},{48,32},{1,49},{17,1},{33,17},{49,33},{2,50}... | collective-permute-start | bytes 98312 | tf_op jit(solution)/shard_map/ppermute | solution.py:306
  38.1 0.0 collective-permute-done.10
  38.1 0.0 collective-permute-done.11
  38.1 0.0 collective-permute-done.12
  38.2 3.8 %collective-permute-start.13 = (f32[1,32,256]{2,1,0:T(8,128)S(1)}, f32[1,32,256]{2,1,0:T(8,128)S(1)}, u32[]{:S(2)}, u32[]{:S(2)}) collective-permute-start(f32[1,32,256]{2,1,0:T(8,128)S(1)} %get-tuple-element.44), channel_id=1, source_target_pairs={{0,32},{16,48},{32,0},{48,16},{1,33},{17,49},{33,1},{49,17},{2,34}... | collective-permute-start | bytes 98312 | tf_op jit(solution)/shard_map/ppermute | solution.py:306
  42.0 1.5 %collective-permute-start.14 = (f32[1,32,256]{2,1,0:T(8,128)S(1)}, f32[1,32,256]{2,1,0:T(8,128)S(1)}, u32[]{:S(2)}, u32[]{:S(2)}) collective-permute-start(f32[1,32,256]{2,1,0:T(8,128)S(1)} %get-tuple-element.43), channel_id=1, source_target_pairs={{0,16},{16,32},{32,48},{48,0},{1,17},{17,33},{33,49},{49,1},{2,18}... | collective-permute-start | bytes 98312 | tf_op jit(solution)/shard_map/ppermute | solution.py:306
  43.4 0.0 collective-permute-done.15
  43.4 2.6 %collective-permute-done.13 = f32[1,32,256]{2,1,0:T(8,128)S(1)} collective-permute-done((f32[1,32,256]{2,1,0:T(8,128)S(1)}, f32[1,32,256]{2,1,0:T(8,128)S(1)}, u32[]{:S(2)}, u32[]{:S(2)}) %collective-permute-start.13) | collective-permute-done | bytes 32800 | tf_op jit(solution)/shard_map/ppermute | solution.py:306
  46.1 1.9 %collective-permute-done.14 = f32[1,32,256]{2,1,0:T(8,128)S(1)} collective-permute-done((f32[1,32,256]{2,1,0:T(8,128)S(1)}, f32[1,32,256]{2,1,0:T(8,128)S(1)}, u32[]{:S(2)}, u32[]{:S(2)}) %collective-permute-start.14) | collective-permute-done | bytes 32800 | tf_op jit(solution)/shard_map/ppermute | solution.py:306
  48.0 0.6 %fusion.6 = f32[1,32,256]{2,1,0:T(8,128)} fusion(f32[1,32,256]{2,1,0:T(8,128)S(1)} %collective-permute-done.13, f32[2,32,256]{2,1,0:T(8,128)S(1)} %collective-permute-done.9, f32[2,32,256]{2,1,0:T(8,128)S(1)} %collective-permute-done.8, f32[2,32,256]{2,1,0:T(8,128)S(1)} %collective-permute-done.7, f32[2,32,256]{2,1,0:T(8,128)S(1)} %get-tuple-element.35, ...), kind=kLoop, calls=%fused_computation.21 | loop fusion | flops 57344 | bytes 262144 | tf_op jit(solution)/shard_map/mul | solution.py:307
  (6 shorter events, 0.1 us)
Async XLA Ops:
  2.2 14.4 %collective-permute-start = (f32[32,16,256]{2,1,0:T(8,128)S(1)}, f32[32,16,256]{2,1,0:T(8,128)S(1)}, u32[]{:S(2)}, u32[]{:S(2)}) collective-permute-start(f32[32,16,256]{2,1,0:T(8,128)S(1)} %get-tuple-element.21.bottom_ref), channel_id=1, source_target_pairs={{0,2},{2,4},{4,6},{6,0},{1,3},{3,5},{5,7},{7,1},{8,10},{10,12},{12... | collective-permute-start | bytes 1572872 | tf_op jit(solution)/shard_map/ppermute | solution.py:269
  3.9 6.1 %copy-start = (bf16[2,2,4,32,128]{4,3,2,1,0:T(8,128)(2,1)S(1)}, bf16[2,2,4,32,128]{4,3,2,1,0:T(8,128)(2,1)}, u32[]{:S(2)}) copy-start(bf16[2,2,4,32,128]{4,3,2,1,0:T(8,128)(2,1)} %constant.36.clone.patch_ref) | copy-start | bytes 393220
  3.9 6.1 %copy-start.1 = (bf16[2,2,64,128]{3,2,1,0:T(8,128)(2,1)S(1)}, bf16[2,2,64,128]{3,2,1,0:T(8,128)(2,1)}, u32[]{:S(2)}) copy-start(bf16[2,2,64,128]{3,2,1,0:T(8,128)(2,1)} %constant.38.clone.edge_ref) | copy-start | bytes 196612
  3.9 14.1 %collective-permute-start.1 = (f32[32,16,256]{2,1,0:T(8,128)S(1)}, f32[32,16,256]{2,1,0:T(8,128)S(1)}, u32[]{:S(2)}, u32[]{:S(2)}) collective-permute-start(f32[32,16,256]{2,1,0:T(8,128)S(1)} %get-tuple-element.22.top_ref), channel_id=1, source_target_pairs={{0,6},{2,0},{4,2},{6,4},{1,7},{3,1},{5,3},{7,5},{8,14},{10,8},{12,... | collective-permute-start | bytes 1572872 | tf_op jit(solution)/shard_map/ppermute | solution.py:270
  5.3 7.9 %collective-permute-start.3 = (f32[2,32,256]{2,1,0:T(8,128)S(1)}, f32[2,32,256]{2,1,0:T(8,128)S(1)}, u32[]{:S(2)}, u32[]{:S(2)}) collective-permute-start(f32[2,32,256]{2,1,0:T(8,128)S(1)} %get-tuple-element.25), channel_id=1, source_target_pairs={{0,1},{1,0},{2,3},{3,2},{4,5},{5,4},{6,7},{7,6},{8,9},{9,8},{10,11... | collective-permute-start | bytes 196616 | tf_op jit(solution)/shard_map/ppermute | solution.py:277
  7.1 6.0 %collective-permute-start.2 = (f32[2,16,256]{2,1,0:T(8,128)S(1)}, f32[2,16,256]{2,1,0:T(8,128)S(1)}, u32[]{:S(2)}, u32[]{:S(2)}) collective-permute-start(f32[2,16,256]{2,1,0:T(8,128)S(1)} %get-tuple-element.24), channel_id=1, source_target_pairs={{0,3},{1,2},{2,5},{3,4},{4,7},{5,6},{6,1},{7,0},{8,11},{9,10},{10,... | collective-permute-start | bytes 98312 | tf_op jit(solution)/shard_map/ppermute | solution.py:275
  8.2 5.0 %copy-start.2 = (bf16[4,96,192]{2,1,0:T(8,128)(2,1)S(1)}, bf16[4,96,192]{2,1,0:T(8,128)(2,1)}, u32[]{:S(2)}) copy-start(bf16[4,96,192]{2,1,0:T(8,128)(2,1)} %constant.33.clone.left_ref) | copy-start | bytes 442372
  8.2 5.0 %copy-start.4 = (bf16[4,16,96]{2,1,0:T(8,128)(2,1)S(1)}, bf16[4,16,96]{2,1,0:T(8,128)(2,1)}, u32[]{:S(2)}) copy-start(bf16[4,16,96]{2,1,0:T(8,128)(2,1)} %constant.34.clone.inner_ref) | copy-start | bytes 36868
  8.2 5.0 %collective-permute-start.4 = (f32[2,16,256]{2,1,0:T(8,128)S(1)}, f32[2,16,256]{2,1,0:T(8,128)S(1)}, u32[]{:S(2)}, u32[]{:S(2)}) collective-permute-start(f32[2,16,256]{2,1,0:T(8,128)S(1)} %get-tuple-element.26), channel_id=1, source_target_pairs={{0,7},{1,6},{2,1},{3,0},{4,3},{5,2},{6,5},{7,4},{8,15},{9,14},{10,... | collective-permute-start | bytes 98312 | tf_op jit(solution)/shard_map/ppermute | solution.py:276
  13.2 4.8 %copy-start.3 = (bf16[4,80,192]{2,1,0:T(8,128)(2,1)S(1)}, bf16[4,80,192]{2,1,0:T(8,128)(2,1)}, u32[]{:S(2)}) copy-start(bf16[4,80,192]{2,1,0:T(8,128)(2,1)} %constant.35.clone.left_ref) | copy-start | bytes 368644
  19.6 2.3 %collective-permute-start.6 = (f32[8,32,256]{2,1,0:T(8,128)S(1)}, f32[8,32,256]{2,1,0:T(8,128)S(1)}, u32[]{:S(2)}, u32[]{:S(2)}) collective-permute-start(f32[8,32,256]{2,1,0:T(8,128)S(1)} %get-tuple-element.34), channel_id=1, source_target_pairs={{0,8},{8,0},{1,9},{9,1},{2,10},{10,2},{3,11},{11,3},{4,12},{12,4},... | collective-permute-start | bytes 786440 | tf_op jit(solution)/shard_map/ppermute | solution.py:296
  21.4 4.3 %collective-permute-start.5 = (f32[8,32,256]{2,1,0:T(8,128)S(1)}, f32[8,32,256]{2,1,0:T(8,128)S(1)}, u32[]{:S(2)}, u32[]{:S(2)}) collective-permute-start(f32[8,32,256]{2,1,0:T(8,128)S(1)} %get-tuple-element.32), channel_id=1, source_target_pairs={{0,8},{8,0},{1,9},{9,1},{2,10},{10,2},{3,11},{11,3},{4,12},{12,4},... | collective-permute-start | bytes 786440 | tf_op jit(solution)/shard_map/ppermute | solution.py:296
  22.0 7.5 %collective-permute-start.7 = (f32[2,32,256]{2,1,0:T(8,128)S(1)}, f32[2,32,256]{2,1,0:T(8,128)S(1)}, u32[]{:S(2)}, u32[]{:S(2)}) collective-permute-start(f32[2,32,256]{2,1,0:T(8,128)S(1)} %get-tuple-element.39), channel_id=1, source_target_pairs={{0,128},{64,192},{128,0},{192,64},{1,129},{65,193},{129,1},{193,65... | collective-permute-start | bytes 196616 | tf_op jit(solution)/shard_map/ppermute | solution.py:303
  25.1 6.6 %collective-permute-start.8 = (f32[2,32,256]{2,1,0:T(8,128)S(1)}, f32[2,32,256]{2,1,0:T(8,128)S(1)}, u32[]{:S(2)}, u32[]{:S(2)}) collective-permute-start(f32[2,32,256]{2,1,0:T(8,128)S(1)} %get-tuple-element.42), channel_id=1, source_target_pairs={{0,64},{64,128},{128,192},{192,0},{1,65},{65,129},{129,193},{193,1... | collective-permute-start | bytes 196616 | tf_op jit(solution)/shard_map/ppermute | solution.py:303
  25.7 6.0 %collective-permute-start.9 = (f32[2,32,256]{2,1,0:T(8,128)S(1)}, f32[2,32,256]{2,1,0:T(8,128)S(1)}, u32[]{:S(2)}, u32[]{:S(2)}) collective-permute-start(f32[2,32,256]{2,1,0:T(8,128)S(1)} %get-tuple-element.38), channel_id=1, source_target_pairs={{0,192},{64,0},{128,64},{192,128},{1,193},{65,1},{129,65},{193,129... | collective-permute-start | bytes 196616 | tf_op jit(solution)/shard_map/ppermute | solution.py:303
  28.5 9.6 %collective-permute-start.10 = (f32[2,32,256]{2,1,0:T(8,128)S(1)}, f32[2,32,256]{2,1,0:T(8,128)S(1)}, u32[]{:S(2)}, u32[]{:S(2)}) collective-permute-start(f32[2,32,256]{2,1,0:T(8,128)S(1)} %get-tuple-element.41), channel_id=1, source_target_pairs={{0,128},{64,192},{128,0},{192,64},{1,129},{65,193},{129,1},{193,65... | collective-permute-start | bytes 196616 | tf_op jit(solution)/shard_map/ppermute | solution.py:303
  28.5 9.6 %collective-permute-start.11 = (f32[2,32,256]{2,1,0:T(8,128)S(1)}, f32[2,32,256]{2,1,0:T(8,128)S(1)}, u32[]{:S(2)}, u32[]{:S(2)}) collective-permute-start(f32[2,32,256]{2,1,0:T(8,128)S(1)} %get-tuple-element.40), channel_id=1, source_target_pairs={{0,64},{64,128},{128,192},{192,0},{1,65},{65,129},{129,193},{193,1... | collective-permute-start | bytes 196616 | tf_op jit(solution)/shard_map/ppermute | solution.py:303
  29.5 8.7 %collective-permute-start.12 = (f32[2,32,256]{2,1,0:T(8,128)S(1)}, f32[2,32,256]{2,1,0:T(8,128)S(1)}, u32[]{:S(2)}, u32[]{:S(2)}) collective-permute-start(f32[2,32,256]{2,1,0:T(8,128)S(1)} %get-tuple-element.36), channel_id=1, source_target_pairs={{0,192},{64,0},{128,64},{192,128},{1,193},{65,1},{129,65},{193,129... | collective-permute-start | bytes 196616 | tf_op jit(solution)/shard_map/ppermute | solution.py:303
  31.8 11.7 %collective-permute-start.15 = (f32[1,32,256]{2,1,0:T(8,128)S(1)}, f32[1,32,256]{2,1,0:T(8,128)S(1)}, u32[]{:S(2)}, u32[]{:S(2)}) collective-permute-start(f32[1,32,256]{2,1,0:T(8,128)S(1)} %fusion), channel_id=1, source_target_pairs={{0,48},{16,0},{32,16},{48,32},{1,49},{17,1},{33,17},{49,33},{2,50}... | collective-permute-start | bytes 98312 | tf_op jit(solution)/shard_map/ppermute | solution.py:306
  38.2 7.9 %collective-permute-start.13 = (f32[1,32,256]{2,1,0:T(8,128)S(1)}, f32[1,32,256]{2,1,0:T(8,128)S(1)}, u32[]{:S(2)}, u32[]{:S(2)}) collective-permute-start(f32[1,32,256]{2,1,0:T(8,128)S(1)} %get-tuple-element.44), channel_id=1, source_target_pairs={{0,32},{16,48},{32,0},{48,16},{1,33},{17,49},{33,1},{49,17},{2,34}... | collective-permute-start | bytes 98312 | tf_op jit(solution)/shard_map/ppermute | solution.py:306
  42.0 6.0 %collective-permute-start.14 = (f32[1,32,256]{2,1,0:T(8,128)S(1)}, f32[1,32,256]{2,1,0:T(8,128)S(1)}, u32[]{:S(2)}, u32[]{:S(2)}) collective-permute-start(f32[1,32,256]{2,1,0:T(8,128)S(1)} %get-tuple-element.43), channel_id=1, source_target_pairs={{0,16},{16,32},{32,48},{48,0},{1,17},{17,33},{33,49},{49,1},{2,18}... | collective-permute-start | bytes 98312 | tf_op jit(solution)/shard_map/ppermute | solution.py:306

commit v14 on v13

--- a/solution.py
+++ b/solution.py
@@ -192,13 +192,13 @@
         v = stack3([r[16 * part + f] for r in (above_ref, top_ref, bottom_ref, below_ref)])
         u = jnp.dot(left, v, preferred_element_type=F32)
         at = slice(16 * f, 16 * f + 16)
-        fh_ref[at, :256], fl_ref[at, :256] = split(u[:16])
-        fh_ref[at, 256:], fl_ref[at, 256:] = split(u[16:32])
-        mh_ref[at], ml_ref[at] = split(u[32:48])
+        fh_ref[at], fl_ref[at] = split(u[:16])
+        both = slice(32 * f, 32 * f + 32)
+        mh_ref[both], ml_ref[both] = split(u[16:48])
         ch_ref[at, :256], cl_ref[at, :256] = split(u[48:64])
         ch_ref[at, 256:], cl_ref[at, 256:] = split(u[64:])
 
-    outer_ref[...] = dot3((fh_ref[...], fl_ref[...]), (right_ref[0, :512], right_ref[1, :512]))
+    outer_ref[...] = dot3((fh_ref[...], fl_ref[...]), (right_ref[0, :256], right_ref[1, :256]))
     middle_ref[...] = dot3((mh_ref[...], ml_ref[...]), (right_ref[0, 256:512], right_ref[1, 256:512]))
     pairs = dot3((ch_ref[...], cl_ref[...]), (right_ref[0, 512:], right_ref[1, 512:]))
     for h in range(2):
@@ -215,9 +215,8 @@
         rows = []
         for f in range(4 * g, 4 * g + 4):
             own = own_ref[16 * (16 * part + f) : 16 * (16 * part + f) + 16]
-            rows += [outer_ref[16 * f : 16 * f + 8], middle_ref[16 * f : 16 * f + 16] + own]
-            rows += [outer_ref[16 * f + 8 : 16 * f + 16]]
-        alpha = jnp.concatenate(rows) + jnp.concatenate([low, high], axis=1)
+            rows += [outer_ref[16 * f : 16 * f + 8], own, outer_ref[16 * f + 8 : 16 * f + 16]]
+        alpha = (jnp.concatenate(rows) + middle_ref[at]) + jnp.concatenate([low, high], axis=1)
         first = 16 * part + 4 * g
         q = p_ref[first : first + 4] * alpha.reshape(4, 32, 256)
         for j in range(2):
@@ -252,7 +251,7 @@
     whole = slice(0, 64)
     left = three(slice(0, 96), whole)
     inner = three(slice(8, 24), slice(HALO, 48))
-    rows = np.r_[0:8, 24:32, 32:40, 56:64, 40:56, 64:96]
+    rows = np.r_[0:8, 24:32, 32:96]
     left_rest = three(rows, whole)
     right, edge = (halves(t) for t in right_tables(512, 2))
     blocks = right[1].reshape(2, 4, 256, 256)
@@ -289,8 +288,8 @@
         keep, give = call(
             functools.partial(filter_kernel, part), [(8, 32, 256)] * 2,
             where, near_p, above, top, bottom, below, left_rest, right, near, own,
-            scratch=[vmem((256, 512), BF16)] * 2 + [vmem((256, 256), BF16)] * 2 + [vmem((256, 512), BF16)] * 2
-            + [vmem((256, 256), F32)] * 2 + [vmem((2, 512, 128), F32)],
+            scratch=[vmem((256, 256), BF16)] * 2 + [vmem((512, 256), BF16)] * 2 + [vmem((256, 512), BF16)] * 2
+            + [vmem((256, 256), F32), vmem((512, 256), F32), vmem((2, 512, 128), F32)],
             cost=2 * 10**9,
         )
         got = lax.ppermute(give, "core", swap)

time: 48.8 us -> 48.7 us (level)
  transfers between devices with their start and end apart: 16 -> 16, of which waited for: 6 -> 6; matrix products, arithmetic and copies ran while one was open for 0% -> 0% of each run, Pallas kernels for 12% -> 11%
where the time goes in v14:
time: 48.7 us; the launch traced here: 48.5 us
  starting transfers between devices  29 us (60%)
  Pallas kernels  9.27 us (19%)
  waiting for transfers between devices  9.23 us (19%)
  other arithmetic  0.73 us (1%)
    ppermute x3, starting transfers between devices, body(): lax.ppermute(cell, 'z', ring(e))  11.6 us
    ppermute x6, starting transfers between devices, body(): x2, x1, x3 = (lax.ppermute(piece[d, wave], 'x', ring(d)) for d in (2, 1, 3))  9.67 us
    pallas_call x6, Pallas kernels, call(): pl.pallas_call(kernel, out_shape=[o if isinstance(o, jax.ShapeDtypeStruct...  9.27 us
    ppermute x3, waiting for transfers between devices, body(): lax.ppermute(cell, 'z', ring(e))  4.55 us
    ppermute x1, waiting for transfers between devices, body(): above = lax.ppermute(bottom, 'gx', ring(1))  2.09 us
    ppermute x1, starting transfers between devices, body(): side_below = lax.ppermute(edge_top, ('gx', 'gy'), diagonal(3))  1.8 us
    ppermute x1, starting transfers between devices, body(): side = lax.ppermute(edges, 'gy', swap)  1.76 us
    ppermute x1, starting transfers between devices, body(): above = lax.ppermute(bottom, 'gx', ring(1))  1.65 us
  transfers between devices with their start and end apart: 16, of which 6 were waited for; matrix products, arithmetic and copies ran while one was open for 0% of the time, Pallas kernels for 11%

profile of v14, /device:TPU:8, one launch (start us, length us, event | category | flops | bytes accessed | tf_op | source)
XLA Modules:
  0.0 48.5 jit_solution(1133378021519455339)
XLA Ops:
  0.0 0.1 stack.23.where
  0.1 2.1 %shard_map.82 = (f32[32,32,256]{2,1,0:T(8,128)S(1)}, f32[32,16,256]{2,1,0:T(8,128)S(1)}, f32[32,16,256]{2,1,0:T(8,128)S(1)}) custom-call(s32[5]{0:T(128)S(1)} %stack.23.where, f32[1,32,32,256]{3,2,1,0:T(8,128)} %p_hbm.1, f32[32,32,256]{2,1,0:T(8,128)} %c_hbm.1), custom_call_target="tpu_custom_call" | custom-call | bytes 1048576 | tf_op jit(solution)/shard_map/pallas_call | solution.py:233
  2.2 1.7 %collective-permute-start = (f32[32,16,256]{2,1,0:T(8,128)S(1)}, f32[32,16,256]{2,1,0:T(8,128)S(1)}, u32[]{:S(2)}, u32[]{:S(2)}) collective-permute-start(f32[32,16,256]{2,1,0:T(8,128)S(1)} %get-tuple-element.21.bottom_ref), channel_id=1, source_target_pairs={{0,2},{2,4},{4,6},{6,0},{1,3},{3,5},{5,7},{7,1},{8,10},{10,12},{12... | collective-permute-start | bytes 1572872 | tf_op jit(solution)/shard_map/ppermute | solution.py:268
  3.9 0.0 copy-start
  3.9 0.0 copy-start.1
  3.9 0.7 %collective-permute-start.1 = (f32[32,16,256]{2,1,0:T(8,128)S(1)}, f32[32,16,256]{2,1,0:T(8,128)S(1)}, u32[]{:S(2)}, u32[]{:S(2)}) collective-permute-start(f32[32,16,256]{2,1,0:T(8,128)S(1)} %get-tuple-element.22.top_ref), channel_id=1, source_target_pairs={{0,6},{2,0},{4,2},{6,4},{1,7},{3,1},{5,3},{7,5},{8,14},{10,8},{12,... | collective-permute-start | bytes 1572872 | tf_op jit(solution)/shard_map/ppermute | solution.py:269
  4.6 0.7 %shard_map.84 = (f32[2,32,256]{2,1,0:T(8,128)S(1)}, f32[2,16,256]{2,1,0:T(8,128)S(1)}, f32[2,16,256]{2,1,0:T(8,128)S(1)}) custom-call(s32[5]{0:T(128)S(1)} %stack.23.where, f32[32,16,256]{2,1,0:T(8,128)S(1)} %get-tuple-element.22.top_ref, f32[32,16,256]{2,1,0:T(8,128)S(1)} %get-tuple-element.21.bottom_ref), custom_call_target="tpu_custom_call" | custom-call | bytes 1048576 | tf_op jit(solution)/shard_map/pallas_call | solution.py:233
  5.3 1.8 %collective-permute-start.3 = (f32[2,32,256]{2,1,0:T(8,128)S(1)}, f32[2,32,256]{2,1,0:T(8,128)S(1)}, u32[]{:S(2)}, u32[]{:S(2)}) collective-permute-start(f32[2,32,256]{2,1,0:T(8,128)S(1)} %get-tuple-element.25), channel_id=1, source_target_pairs={{0,1},{1,0},{2,3},{3,2},{4,5},{5,4},{6,7},{7,6},{8,9},{9,8},{10,11... | collective-permute-start | bytes 196616 | tf_op jit(solution)/shard_map/ppermute | solution.py:276
  7.1 1.1 %collective-permute-start.2 = (f32[2,16,256]{2,1,0:T(8,128)S(1)}, f32[2,16,256]{2,1,0:T(8,128)S(1)}, u32[]{:S(2)}, u32[]{:S(2)}) collective-permute-start(f32[2,16,256]{2,1,0:T(8,128)S(1)} %get-tuple-element.24), channel_id=1, source_target_pairs={{0,3},{1,2},{2,5},{3,4},{4,7},{5,6},{6,1},{7,0},{8,11},{9,10},{10,... | collective-permute-start | bytes 98312 | tf_op jit(solution)/shard_map/ppermute | solution.py:274
  8.2 1.8 %collective-permute-start.4 = (f32[2,16,256]{2,1,0:T(8,128)S(1)}, f32[2,16,256]{2,1,0:T(8,128)S(1)}, u32[]{:S(2)}, u32[]{:S(2)}) collective-permute-start(f32[2,16,256]{2,1,0:T(8,128)S(1)} %get-tuple-element.26), channel_id=1, source_target_pairs={{0,7},{1,6},{2,1},{3,0},{4,3},{5,2},{6,5},{7,4},{8,15},{9,14},{10,... | collective-permute-start | bytes 98312 | tf_op jit(solution)/shard_map/ppermute | solution.py:275
  10.0 0.0 copy-done
  10.0 0.0 copy-done.1
  10.0 1.9 %shard_map.83 = (bf16[512,128]{1,0:T(8,128)(2,1)S(1)}, bf16[512,128]{1,0:T(8,128)(2,1)S(1)}, bf16[2,1024,256]{2,1,0:T(8,128)(2,1)S(1)}) custom-call(s32[5]{0:T(128)S(1)} %stack.23.where, bf16[2,2,64,128]{3,2,1,0:T(8,128)(2,1)S(1)} %copy-done.1, bf16[2,2,4,32,128]{4,3,2,1,0:T(8,128)(2,1)S(1)} %copy-done, bf16[2,1024,256]{2,1,0:T(8,128)(2,1)} %constant.37.clone.right_hbm), custom_call_target="tpu_custom_call" | custom-call | bytes 1048576 | tf_op jit(solution)/shard_map/pallas_call | solution.py:233
  11.9 1.1 %collective-permute-done.2.side_above_ref = f32[2,16,256]{2,1,0:T(8,128)S(1)} collective-permute-done((f32[2,16,256]{2,1,0:T(8,128)S(1)}, f32[2,16,256]{2,1,0:T(8,128)S(1)}, u32[]{:S(2)}, u32[]{:S(2)}) %collective-permute-start.2) | collective-permute-done | bytes 32800 | tf_op jit(solution)/shard_map/ppermute | solution.py:274
  13.0 0.1 collective-permute-done.4.side_below_ref
  13.2 0.0 collective-permute-done.3.side_ref
  13.2 0.0 copy-done.2
  13.2 0.0 copy-done.4
  13.2 0.0 copy-start.3
  13.2 1.4 %shard_map.85 = (f32[128,128]{1,0:T(8,128)S(1)}, f32[512,256]{1,0:T(8,128)S(1)}) custom-call(s32[5]{0:T(128)S(1)} %stack.23.where, f32[32,16,256]{2,1,0:T(8,128)S(1)} %get-tuple-element.22.top_ref, f32[32,16,256]{2,1,0:T(8,128)S(1)} %get-tuple-element.21.bottom_ref, f32[2,16,256]{2,1,0:T(8,128)S(1)} %collective-permute-done.2.side_above_ref, ...), custom_call_target="tpu_custom_call" | custom-call | flops 1000000000 | bytes 1048576 | tf_op jit(solution)/shard_map/pallas_call | solution.py:233
  14.6 2.1 %collective-permute-done.above_ref = f32[32,16,256]{2,1,0:T(8,128)S(1)} collective-permute-done((f32[32,16,256]{2,1,0:T(8,128)S(1)}, f32[32,16,256]{2,1,0:T(8,128)S(1)}, u32[]{:S(2)}, u32[]{:S(2)}) %collective-permute-start) | collective-permute-done | bytes 524320 | tf_op jit(solution)/shard_map/ppermute | solution.py:268
  16.7 1.3 %collective-permute-done.1.below_ref = f32[32,16,256]{2,1,0:T(8,128)S(1)} collective-permute-done((f32[32,16,256]{2,1,0:T(8,128)S(1)}, f32[32,16,256]{2,1,0:T(8,128)S(1)}, u32[]{:S(2)}, u32[]{:S(2)}) %collective-permute-start.1) | collective-permute-done | bytes 524320 | tf_op jit(solution)/shard_map/ppermute | solution.py:269
  18.0 0.0 copy-done.3
  18.0 1.6 %shard_map.87 = (f32[8,32,256]{2,1,0:T(8,128)S(1)}, f32[8,32,256]{2,1,0:T(8,128)S(1)}) custom-call(s32[5]{0:T(128)S(1)} %stack.23.where, f32[32,32,256]{2,1,0:T(8,128)S(1)} %get-tuple-element.20.p_ref, f32[32,16,256]{2,1,0:T(8,128)S(1)} %collective-permute-done.above_ref, f32[32,16,256]{2,1,0:T(8,128)S(1)} %get-tuple-element.22.top_ref, ...), custom_call_target="tpu_custom_call" | custom-call | flops 2000000000 | bytes 1048576 | tf_op jit(solution)/shard_map/pallas_call | solution.py:233
  19.6 0.1 collective-permute-start.6
  19.7 1.6 %shard_map.86 = (f32[8,32,256]{2,1,0:T(8,128)S(1)}, f32[8,32,256]{2,1,0:T(8,128)S(1)}) custom-call(s32[5]{0:T(128)S(1)} %stack.23.where, f32[32,32,256]{2,1,0:T(8,128)S(1)} %get-tuple-element.20.p_ref, f32[32,16,256]{2,1,0:T(8,128)S(1)} %collective-permute-done.above_ref, f32[32,16,256]{2,1,0:T(8,128)S(1)} %get-tuple-element.22.top_ref, ...), custom_call_target="tpu_custom_call" | custom-call | flops 2000000000 | bytes 1048576 | tf_op jit(solution)/shard_map/pallas_call | solution.py:233
  21.2 0.6 %collective-permute-start.5 = (f32[8,32,256]{2,1,0:T(8,128)S(1)}, f32[8,32,256]{2,1,0:T(8,128)S(1)}, u32[]{:S(2)}, u32[]{:S(2)}) collective-permute-start(f32[8,32,256]{2,1,0:T(8,128)S(1)} %get-tuple-element.32), channel_id=1, source_target_pairs={{0,8},{8,0},{1,9},{9,1},{2,10},{10,2},{3,11},{11,3},{4,12},{12,4},... | collective-permute-start | bytes 786440 | tf_op jit(solution)/shard_map/ppermute | solution.py:295
  21.8 0.0 collective-permute-done.6
  21.9 3.1 %collective-permute-start.7 = (f32[2,32,256]{2,1,0:T(8,128)S(1)}, f32[2,32,256]{2,1,0:T(8,128)S(1)}, u32[]{:S(2)}, u32[]{:S(2)}) collective-permute-start(f32[2,32,256]{2,1,0:T(8,128)S(1)} %get-tuple-element.39), channel_id=1, source_target_pairs={{0,128},{64,192},{128,0},{192,64},{1,129},{65,193},{129,1},{193,65... | collective-permute-start | bytes 196616 | tf_op jit(solution)/shard_map/ppermute | solution.py:302
  25.0 0.6 %collective-permute-start.8 = (f32[2,32,256]{2,1,0:T(8,128)S(1)}, f32[2,32,256]{2,1,0:T(8,128)S(1)}, u32[]{:S(2)}, u32[]{:S(2)}) collective-permute-start(f32[2,32,256]{2,1,0:T(8,128)S(1)} %get-tuple-element.42), channel_id=1, source_target_pairs={{0,64},{64,128},{128,192},{192,0},{1,65},{65,129},{129,193},{193,1... | collective-permute-start | bytes 196616 | tf_op jit(solution)/shard_map/ppermute | solution.py:302
  25.6 0.0 collective-permute-done.5
  25.6 2.7 %collective-permute-start.9 = (f32[2,32,256]{2,1,0:T(8,128)S(1)}, f32[2,32,256]{2,1,0:T(8,128)S(1)}, u32[]{:S(2)}, u32[]{:S(2)}) collective-permute-start(f32[2,32,256]{2,1,0:T(8,128)S(1)} %get-tuple-element.38), channel_id=1, source_target_pairs={{0,192},{64,0},{128,64},{192,128},{1,193},{65,1},{129,65},{193,129... | collective-permute-start | bytes 196616 | tf_op jit(solution)/shard_map/ppermute | solution.py:302
  28.3 0.0 collective-permute-start.10
  28.3 1.0 %collective-permute-start.11 = (f32[2,32,256]{2,1,0:T(8,128)S(1)}, f32[2,32,256]{2,1,0:T(8,128)S(1)}, u32[]{:S(2)}, u32[]{:S(2)}) collective-permute-start(f32[2,32,256]{2,1,0:T(8,128)S(1)} %get-tuple-element.40), channel_id=1, source_target_pairs={{0,64},{64,128},{128,192},{192,0},{1,65},{65,129},{129,193},{193,1... | collective-permute-start | bytes 196616 | tf_op jit(solution)/shard_map/ppermute | solution.py:302
  29.3 0.0 collective-permute-done.7
  29.3 2.3 %collective-permute-start.12 = (f32[2,32,256]{2,1,0:T(8,128)S(1)}, f32[2,32,256]{2,1,0:T(8,128)S(1)}, u32[]{:S(2)}, u32[]{:S(2)}) collective-permute-start(f32[2,32,256]{2,1,0:T(8,128)S(1)} %get-tuple-element.36), channel_id=1, source_target_pairs={{0,192},{64,0},{128,64},{192,128},{1,193},{65,1},{129,65},{193,129... | collective-permute-start | bytes 196616 | tf_op jit(solution)/shard_map/ppermute | solution.py:302
  31.6 0.0 collective-permute-done.8
  31.6 0.0 collective-permute-done.9
  31.6 6.4 %collective-permute-start.15 = (f32[1,32,256]{2,1,0:T(8,128)S(1)}, f32[1,32,256]{2,1,0:T(8,128)S(1)}, u32[]{:S(2)}, u32[]{:S(2)}) collective-permute-start(f32[1,32,256]{2,1,0:T(8,128)S(1)} %fusion), channel_id=1, source_target_pairs={{0,48},{16,0},{32,16},{48,32},{1,49},{17,1},{33,17},{49,33},{2,50}... | collective-permute-start | bytes 98312 | tf_op jit(solution)/shard_map/ppermute | solution.py:305
  38.0 0.0 collective-permute-done.10
  38.0 0.0 collective-permute-done.11
  38.0 0.0 collective-permute-done.12
  38.0 3.8 %collective-permute-start.13 = (f32[1,32,256]{2,1,0:T(8,128)S(1)}, f32[1,32,256]{2,1,0:T(8,128)S(1)}, u32[]{:S(2)}, u32[]{:S(2)}) collective-permute-start(f32[1,32,256]{2,1,0:T(8,128)S(1)} %get-tuple-element.44), channel_id=1, source_target_pairs={{0,32},{16,48},{32,0},{48,16},{1,33},{17,49},{33,1},{49,17},{2,34}... | collective-permute-start | bytes 98312 | tf_op jit(solution)/shard_map/ppermute | solution.py:305
  41.8 1.5 %collective-permute-start.14 = (f32[1,32,256]{2,1,0:T(8,128)S(1)}, f32[1,32,256]{2,1,0:T(8,128)S(1)}, u32[]{:S(2)}, u32[]{:S(2)}) collective-permute-start(f32[1,32,256]{2,1,0:T(8,128)S(1)} %get-tuple-element.43), channel_id=1, source_target_pairs={{0,16},{16,32},{32,48},{48,0},{1,17},{17,33},{33,49},{49,1},{2,18}... | collective-permute-start | bytes 98312 | tf_op jit(solution)/shard_map/ppermute | solution.py:305
  43.3 0.0 collective-permute-done.15
  43.3 2.6 %collective-permute-done.13 = f32[1,32,256]{2,1,0:T(8,128)S(1)} collective-permute-done((f32[1,32,256]{2,1,0:T(8,128)S(1)}, f32[1,32,256]{2,1,0:T(8,128)S(1)}, u32[]{:S(2)}, u32[]{:S(2)}) %collective-permute-start.13) | collective-permute-done | bytes 32800 | tf_op jit(solution)/shard_map/ppermute | solution.py:305
  45.9 1.9 %collective-permute-done.14 = f32[1,32,256]{2,1,0:T(8,128)S(1)} collective-permute-done((f32[1,32,256]{2,1,0:T(8,128)S(1)}, f32[1,32,256]{2,1,0:T(8,128)S(1)}, u32[]{:S(2)}, u32[]{:S(2)}) %collective-permute-start.14) | collective-permute-done | bytes 32800 | tf_op jit(solution)/shard_map/ppermute | solution.py:305
  47.8 0.6 %fusion.6 = f32[1,32,256]{2,1,0:T(8,128)} fusion(f32[1,32,256]{2,1,0:T(8,128)S(1)} %collective-permute-done.13, f32[2,32,256]{2,1,0:T(8,128)S(1)} %collective-permute-done.9, f32[2,32,256]{2,1,0:T(8,128)S(1)} %collective-permute-done.8, f32[2,32,256]{2,1,0:T(8,128)S(1)} %collective-permute-done.7, f32[2,32,256]{2,1,0:T(8,128)S(1)} %get-tuple-element.35, ...), kind=kLoop, calls=%fused_computation.21 | loop fusion | flops 57344 | bytes 262144 | tf_op jit(solution)/shard_map/mul | solution.py:306
  (6 shorter events, 0.1 us)
Async XLA Ops:
  2.2 14.4 %collective-permute-start = (f32[32,16,256]{2,1,0:T(8,128)S(1)}, f32[32,16,256]{2,1,0:T(8,128)S(1)}, u32[]{:S(2)}, u32[]{:S(2)}) collective-permute-start(f32[32,16,256]{2,1,0:T(8,128)S(1)} %get-tuple-element.21.bottom_ref), channel_id=1, source_target_pairs={{0,2},{2,4},{4,6},{6,0},{1,3},{3,5},{5,7},{7,1},{8,10},{10,12},{12... | collective-permute-start | bytes 1572872 | tf_op jit(solution)/shard_map/ppermute | solution.py:268
  3.9 6.1 %copy-start = (bf16[2,2,4,32,128]{4,3,2,1,0:T(8,128)(2,1)S(1)}, bf16[2,2,4,32,128]{4,3,2,1,0:T(8,128)(2,1)}, u32[]{:S(2)}) copy-start(bf16[2,2,4,32,128]{4,3,2,1,0:T(8,128)(2,1)} %constant.36.clone.patch_ref) | copy-start | bytes 393220
  3.9 6.1 %copy-start.1 = (bf16[2,2,64,128]{3,2,1,0:T(8,128)(2,1)S(1)}, bf16[2,2,64,128]{3,2,1,0:T(8,128)(2,1)}, u32[]{:S(2)}) copy-start(bf16[2,2,64,128]{3,2,1,0:T(8,128)(2,1)} %constant.38.clone.edge_ref) | copy-start | bytes 196612
  3.9 14.1 %collective-permute-start.1 = (f32[32,16,256]{2,1,0:T(8,128)S(1)}, f32[32,16,256]{2,1,0:T(8,128)S(1)}, u32[]{:S(2)}, u32[]{:S(2)}) collective-permute-start(f32[32,16,256]{2,1,0:T(8,128)S(1)} %get-tuple-element.22.top_ref), channel_id=1, source_target_pairs={{0,6},{2,0},{4,2},{6,4},{1,7},{3,1},{5,3},{7,5},{8,14},{10,8},{12,... | collective-permute-start | bytes 1572872 | tf_op jit(solution)/shard_map/ppermute | solution.py:269
  5.3 7.9 %collective-permute-start.3 = (f32[2,32,256]{2,1,0:T(8,128)S(1)}, f32[2,32,256]{2,1,0:T(8,128)S(1)}, u32[]{:S(2)}, u32[]{:S(2)}) collective-permute-start(f32[2,32,256]{2,1,0:T(8,128)S(1)} %get-tuple-element.25), channel_id=1, source_target_pairs={{0,1},{1,0},{2,3},{3,2},{4,5},{5,4},{6,7},{7,6},{8,9},{9,8},{10,11... | collective-permute-start | bytes 196616 | tf_op jit(solution)/shard_map/ppermute | solution.py:276
  7.1 6.0 %collective-permute-start.2 = (f32[2,16,256]{2,1,0:T(8,128)S(1)}, f32[2,16,256]{2,1,0:T(8,128)S(1)}, u32[]{:S(2)}, u32[]{:S(2)}) collective-permute-start(f32[2,16,256]{2,1,0:T(8,128)S(1)} %get-tuple-element.24), channel_id=1, source_target_pairs={{0,3},{1,2},{2,5},{3,4},{4,7},{5,6},{6,1},{7,0},{8,11},{9,10},{10,... | collective-permute-start | bytes 98312 | tf_op jit(solution)/shard_map/ppermute | solution.py:274
  8.2 5.0 %copy-start.2 = (bf16[4,96,192]{2,1,0:T(8,128)(2,1)S(1)}, bf16[4,96,192]{2,1,0:T(8,128)(2,1)}, u32[]{:S(2)}) copy-start(bf16[4,96,192]{2,1,0:T(8,128)(2,1)} %constant.33.clone.left_ref) | copy-start | bytes 442372
  8.2 5.0 %copy-start.4 = (bf16[4,16,96]{2,1,0:T(8,128)(2,1)S(1)}, bf16[4,16,96]{2,1,0:T(8,128)(2,1)}, u32[]{:S(2)}) copy-start(bf16[4,16,96]{2,1,0:T(8,128)(2,1)} %constant.34.clone.inner_ref) | copy-start | bytes 36868
  8.2 5.0 %collective-permute-start.4 = (f32[2,16,256]{2,1,0:T(8,128)S(1)}, f32[2,16,256]{2,1,0:T(8,128)S(1)}, u32[]{:S(2)}, u32[]{:S(2)}) collective-permute-start(f32[2,16,256]{2,1,0:T(8,128)S(1)} %get-tuple-element.26), channel_id=1, source_target_pairs={{0,7},{1,6},{2,1},{3,0},{4,3},{5,2},{6,5},{7,4},{8,15},{9,14},{10,... | collective-permute-start | bytes 98312 | tf_op jit(solution)/shard_map/ppermute | solution.py:275
  13.2 4.8 %copy-start.3 = (bf16[4,80,192]{2,1,0:T(8,128)(2,1)S(1)}, bf16[4,80,192]{2,1,0:T(8,128)(2,1)}, u32[]{:S(2)}) copy-start(bf16[4,80,192]{2,1,0:T(8,128)(2,1)} %constant.35.clone.left_ref) | copy-start | bytes 368644
  19.6 2.3 %collective-permute-start.6 = (f32[8,32,256]{2,1,0:T(8,128)S(1)}, f32[8,32,256]{2,1,0:T(8,128)S(1)}, u32[]{:S(2)}, u32[]{:S(2)}) collective-permute-start(f32[8,32,256]{2,1,0:T(8,128)S(1)} %get-tuple-element.34), channel_id=1, source_target_pairs={{0,8},{8,0},{1,9},{9,1},{2,10},{10,2},{3,11},{11,3},{4,12},{12,4},... | collective-permute-start | bytes 786440 | tf_op jit(solution)/shard_map/ppermute | solution.py:295
  21.2 4.3 %collective-permute-start.5 = (f32[8,32,256]{2,1,0:T(8,128)S(1)}, f32[8,32,256]{2,1,0:T(8,128)S(1)}, u32[]{:S(2)}, u32[]{:S(2)}) collective-permute-start(f32[8,32,256]{2,1,0:T(8,128)S(1)} %get-tuple-element.32), channel_id=1, source_target_pairs={{0,8},{8,0},{1,9},{9,1},{2,10},{10,2},{3,11},{11,3},{4,12},{12,4},... | collective-permute-start | bytes 786440 | tf_op jit(solution)/shard_map/ppermute | solution.py:295
  21.9 7.4 %collective-permute-start.7 = (f32[2,32,256]{2,1,0:T(8,128)S(1)}, f32[2,32,256]{2,1,0:T(8,128)S(1)}, u32[]{:S(2)}, u32[]{:S(2)}) collective-permute-start(f32[2,32,256]{2,1,0:T(8,128)S(1)} %get-tuple-element.39), channel_id=1, source_target_pairs={{0,128},{64,192},{128,0},{192,64},{1,129},{65,193},{129,1},{193,65... | collective-permute-start | bytes 196616 | tf_op jit(solution)/shard_map/ppermute | solution.py:302
  25.0 6.6 %collective-permute-start.8 = (f32[2,32,256]{2,1,0:T(8,128)S(1)}, f32[2,32,256]{2,1,0:T(8,128)S(1)}, u32[]{:S(2)}, u32[]{:S(2)}) collective-permute-start(f32[2,32,256]{2,1,0:T(8,128)S(1)} %get-tuple-element.42), channel_id=1, source_target_pairs={{0,64},{64,128},{128,192},{192,0},{1,65},{65,129},{129,193},{193,1... | collective-permute-start | bytes 196616 | tf_op jit(solution)/shard_map/ppermute | solution.py:302
  25.6 6.0 %collective-permute-start.9 = (f32[2,32,256]{2,1,0:T(8,128)S(1)}, f32[2,32,256]{2,1,0:T(8,128)S(1)}, u32[]{:S(2)}, u32[]{:S(2)}) collective-permute-start(f32[2,32,256]{2,1,0:T(8,128)S(1)} %get-tuple-element.38), channel_id=1, source_target_pairs={{0,192},{64,0},{128,64},{192,128},{1,193},{65,1},{129,65},{193,129... | collective-permute-start | bytes 196616 | tf_op jit(solution)/shard_map/ppermute | solution.py:302
  28.3 9.6 %collective-permute-start.10 = (f32[2,32,256]{2,1,0:T(8,128)S(1)}, f32[2,32,256]{2,1,0:T(8,128)S(1)}, u32[]{:S(2)}, u32[]{:S(2)}) collective-permute-start(f32[2,32,256]{2,1,0:T(8,128)S(1)} %get-tuple-element.41), channel_id=1, source_target_pairs={{0,128},{64,192},{128,0},{192,64},{1,129},{65,193},{129,1},{193,65... | collective-permute-start | bytes 196616 | tf_op jit(solution)/shard_map/ppermute | solution.py:302
  28.3 9.6 %collective-permute-start.11 = (f32[2,32,256]{2,1,0:T(8,128)S(1)}, f32[2,32,256]{2,1,0:T(8,128)S(1)}, u32[]{:S(2)}, u32[]{:S(2)}) collective-permute-start(f32[2,32,256]{2,1,0:T(8,128)S(1)} %get-tuple-element.40), channel_id=1, source_target_pairs={{0,64},{64,128},{128,192},{192,0},{1,65},{65,129},{129,193},{193,1... | collective-permute-start | bytes 196616 | tf_op jit(solution)/shard_map/ppermute | solution.py:302
  29.3 8.7 %collective-permute-start.12 = (f32[2,32,256]{2,1,0:T(8,128)S(1)}, f32[2,32,256]{2,1,0:T(8,128)S(1)}, u32[]{:S(2)}, u32[]{:S(2)}) collective-permute-start(f32[2,32,256]{2,1,0:T(8,128)S(1)} %get-tuple-element.36), channel_id=1, source_target_pairs={{0,192},{64,0},{128,64},{192,128},{1,193},{65,1},{129,65},{193,129... | collective-permute-start | bytes 196616 | tf_op jit(solution)/shard_map/ppermute | solution.py:302
  31.6 11.7 %collective-permute-start.15 = (f32[1,32,256]{2,1,0:T(8,128)S(1)}, f32[1,32,256]{2,1,0:T(8,128)S(1)}, u32[]{:S(2)}, u32[]{:S(2)}) collective-permute-start(f32[1,32,256]{2,1,0:T(8,128)S(1)} %fusion), channel_id=1, source_target_pairs={{0,48},{16,0},{32,16},{48,32},{1,49},{17,1},{33,17},{49,33},{2,50}... | collective-permute-start | bytes 98312 | tf_op jit(solution)/shard_map/ppermute | solution.py:305
  38.0 7.9 %collective-permute-start.13 = (f32[1,32,256]{2,1,0:T(8,128)S(1)}, f32[1,32,256]{2,1,0:T(8,128)S(1)}, u32[]{:S(2)}, u32[]{:S(2)}) collective-permute-start(f32[1,32,256]{2,1,0:T(8,128)S(1)} %get-tuple-element.44), channel_id=1, source_target_pairs={{0,32},{16,48},{32,0},{48,16},{1,33},{17,49},{33,1},{49,17},{2,34}... | collective-permute-start | bytes 98312 | tf_op jit(solution)/shard_map/ppermute | solution.py:305
  41.8 6.0 %collective-permute-start.14 = (f32[1,32,256]{2,1,0:T(8,128)S(1)}, f32[1,32,256]{2,1,0:T(8,128)S(1)}, u32[]{:S(2)}, u32[]{:S(2)}) collective-permute-start(f32[1,32,256]{2,1,0:T(8,128)S(1)} %get-tuple-element.43), channel_id=1, source_target_pairs={{0,16},{16,32},{32,48},{48,0},{1,17},{17,33},{33,49},{49,1},{2,18}... | collective-permute-start | bytes 98312 | tf_op jit(solution)/shard_map/ppermute | solution.py:305
